TPU v7x, 256 devices: a whole 4x4x8 slice. The times are simulated.
256 devices in a mesh: seq: 16 (over y_lo, z), head: 16 (over y_hi, x, core).
Axes of the slice: x: 4, y: 4 (y_hi: 2, y_lo: 2; y = y_hi * 2 + y_lo), z: 8, core: 2. Of those that a mesh axis runs over, the one named last changes fastest.
Arguments:
- queries: bfloat16 [57344, 4096], P('seq', 'head'), may hold values from -6 to 6
- key_rows: bfloat16 [57344, 4096], P('seq', 'head'), may hold values from -6 to 6
- value_rows: bfloat16 [57344, 4096], P('seq', 'head'), may hold values from -6 to 6
- band_reach: int32 [224], P('seq'), may hold values from 1 to 3, as said below
- far_list: int32 [224, 2], P('seq'), may hold values from 0 to 223, as said below
- slopes: float32 [32], P('head'), may hold values from 1e-05 to 0.08
Outputs:
- mixed: bfloat16 [57344, 4096], P(('seq', 'head'))
Inputs may be any that keep to these rules, and one draw needn't show every extreme that they name: Some query block has band_reach exactly 3. `far_list`: block g lies on index g // 14 of seq. Of the 28 far blocks listed for the query blocks of one index of seq, at most 2 lie on any one index, and exactly 2 on some index.
All inputs are finite; a program needn't handle non-finite values.
Results may differ from a plain program's by a relative error of at most 0.0049.
Values may be sent and summed in bfloat16 or wider, within the bound.
No kernel may reach another device: no remote copies, remote signals or barrier semaphores. Data moves between devices by JAX's collectives and lax.ppermute only.
A program may use at most 128 MiB of HBM per device.

v0:
```python
import math

import jax
import jax.numpy as jnp
from jax import lax
from jax.sharding import PartitionSpec as P

BT = 256
BAND = 3
FAR = 2


def padded(x, sides, width):
    for axis, dim in sides:
        size, length = (lax.axis_size(axis), x.shape[dim])
        up = [(i, (i + 1) % size) for i in range(size - 1)]
        down = [(j, i) for i, j in up]
        last = lax.slice_in_dim(x, length - width, length, axis=dim)
        first = lax.slice_in_dim(x, 0, width, axis=dim)
        before = lax.ppermute(last, axis, up)
        after = lax.ppermute(first, axis, down)
        x = jnp.concatenate([before, x, after], axis=dim)
    return x


def block_attention(query_rows, key_value, key_pos, key_mask, query_pos, slopes):
    head_count = slopes.shape[0]
    head_size = query_rows.shape[1] // head_count
    queries_h = query_rows.reshape(query_rows.shape[0], head_count, head_size)
    keys_h = key_value[0].reshape(key_value.shape[1], head_count, head_size)
    values_h = key_value[1].reshape(key_value.shape[1], head_count, head_size)
    scores = jnp.einsum("qhd,khd->hqk", queries_h, keys_h, preferred_element_type=jnp.float32) * (
        1.0 / math.sqrt(head_size)
    )
    distance = jnp.abs(query_pos[:, None] - key_pos[None, :]).astype(jnp.float32)
    scores = scores - slopes[:, None, None] * distance[None, :, :]
    scores = jnp.where(key_mask[None, None, :], scores, -jnp.inf)
    row_max = jnp.max(scores, axis=2, keepdims=True)
    raised = jnp.exp(scores - row_max)
    weights = (raised / jnp.sum(raised, axis=2, keepdims=True)).astype(jnp.bfloat16)
    attended = jnp.einsum("hqk,khd->qhd", weights, values_h, preferred_element_type=jnp.float32)
    return attended.astype(jnp.bfloat16).reshape(query_rows.shape[0], head_count * head_size)


def body(queries, key_rows, value_rows, band_reach, far_list, slopes):
    myself = lax.axis_index("seq")
    devices_seq = lax.axis_size("seq")
    tok_rows, channels = key_rows.shape
    blk_dev = tok_rows // BT
    total_blocks = blk_dev * devices_seq
    margin = BAND * BT
    key_value_pair = jnp.stack([key_rows, value_rows])
    requests = far_list.reshape(-1)
    request_count = requests.shape[0]
    capacity = max(2, (request_count + devices_seq - 1) // devices_seq)
    source = requests // blk_dev
    local_blk = requests % blk_dev
    per_source = (source[:, None] == jnp.arange(devices_seq)[None, :]).astype(jnp.int32)
    slot_rank = jnp.sum((jnp.cumsum(per_source, axis=0) - 1) * per_source, axis=1)
    extended = padded(key_value_pair, (("seq", 1),), margin)
    slot_ids = jnp.arange(capacity)
    placed = (per_source[:, :, None] == 1) & (slot_rank[:, None, None] == slot_ids[None, None, :])
    request_table = jnp.sum(jnp.where(placed, local_blk[:, None, None], 0), axis=0)
    asked_for = lax.all_to_all(request_table, "seq", split_axis=0, concat_axis=0, tiled=True)
    local_blocks = key_value_pair.reshape(2, blk_dev, BT, channels)
    outgoing = jnp.take(local_blocks, asked_for, axis=1)
    incoming = lax.all_to_all(outgoing, "seq", split_axis=1, concat_axis=1, tiled=True)
    far_pair = incoming[:, source, slot_rank]
    query_blocks = queries.reshape(blk_dev, BT, channels)
    band_span = 2 * BAND + 1
    offsets = jnp.arange(band_span) - BAND
    within = jnp.arange(BT)

    def attend(local_block):
        block_id = myself * blk_dev + local_block
        band_pair = lax.dynamic_slice_in_dim(extended, local_block * BT, band_span * BT, 1)
        far_part = lax.dynamic_slice_in_dim(far_pair, local_block * FAR, FAR, 1).reshape(
            2, FAR * BT, channels
        )
        key_value = jnp.concatenate([band_pair, far_part], axis=1)
        band_blocks = block_id + offsets
        band_ok = (
            (jnp.abs(offsets) <= band_reach[local_block])
            & (band_blocks >= 0)
            & (band_blocks < total_blocks)
        )
        key_blocks = jnp.concatenate([band_blocks, far_list[local_block]])
        key_ok = jnp.concatenate([band_ok, jnp.ones((FAR,), jnp.bool_)])
        key_pos = (key_blocks[:, None] * BT + within[None, :]).reshape(-1)
        key_mask = jnp.repeat(key_ok, BT)
        return block_attention(
            query_blocks[local_block], key_value, key_pos, key_mask, block_id * BT + within, slopes
        )

    attended = lax.map(attend, jnp.arange(blk_dev))
    mixed_out = attended.reshape(tok_rows, channels)
    return lax.all_to_all(mixed_out, "head", split_axis=0, concat_axis=1, tiled=True)


def solution(mesh):
    in_specs = (
        P("seq", "head"),
        P("seq", "head"),
        P("seq", "head"),
        P("seq"),
        P("seq", None),
        P("head"),
    )
    out_specs = P(("seq", "head"), None)
    return jax.shard_map(body, mesh=mesh, in_specs=in_specs, out_specs=out_specs, check_vma=False)
```

profile of v0, /device:TPU:160, one launch (start us, length us, event | category | flops | bytes accessed | tf_op | source)
XLA Modules:
  0.0 704.8 jit_solution(5672250290825670350)
XLA Ops:
  3.2 7.8 %all-to-all-start = ((s32[16,1,2]{2,1,0:T(1,128)}), s32[16,1,2]{2,1,0:T(1,128)S(1)}, u32[]{:S(2)}, u32[]{:S(2)}) async-start(s32[16,1,2]{2,1,0:T(1,128)} %copy.77), calls=%async_computation | async-start | bytes 16384 | tf_op jit(solution)/shard_map/all_to_all | solution.py:64
  11.0 4.2 pad_maximum_fusion.2
  15.6 7.0 gather_fusion
  22.6 7.5 %fusion.19 = bf16[2,16,2,256,256]{4,3,2,0,1:T(8,128)(2,1)} fusion(bf16[16,2,2,256,256]{4,3,2,1,0:T(8,128)(2,1)} %bitcast.72, pred[16,2]{1,0:T(8,128)(4,1)S(1)} %copy.79), kind=kLoop, calls=%fused_computation.35 | loop fusion | flops 4194304 | bytes 16777248 | tf_op jit(solution)/shard_map/jit(_take)/select_n | solution.py:66
  30.1 8.7 %all-to-all-start.1 = ((bf16[2,16,2,256,256]{4,3,2,0,1:T(8,128)(2,1)}), bf16[2,16,2,256,256]{4,3,2,0,1:T(8,128)(2,1)}, u32[]{:S(2)}, u32[]{:S(2)}) async-start(bf16[2,16,2,256,256]{4,3,2,0,1:T(8,128)(2,1)} %fusion.19), calls=%async_computation.1 | async-start | bytes 16777216 | tf_op jit(solution)/shard_map/all_to_all | solution.py:67
  53.8 182.9 %collective-permute-done = bf16[2,768,256]{1,2,0:T(8,128)(2,1)S(1)} collective-permute-done((bf16[2,768,256]{1,2,0:T(8,128)(2,1)}, bf16[2,768,256]{1,2,0:T(8,128)(2,1)S(1)}, u32[]{:S(2)}, u32[]{:S(2)}) %collective-permute-start) | collective-permute-done | bytes 786464 | tf_op jit(solution)/shard_map/ppermute | solution.py:20
  236.8 12.5 %collective-permute-done.1 = bf16[2,768,256]{1,2,0:T(8,128)(2,1)} collective-permute-done((bf16[2,768,256]{1,2,0:T(8,128)(2,1)S(1)}, bf16[2,768,256]{1,2,0:T(8,128)(2,1)}, u32[]{:S(2)}, u32[]{:S(2)}) %collective-permute-start.1) | collective-permute-done | bytes 786464 | tf_op jit(solution)/shard_map/ppermute | solution.py:21
  249.3 4.6 pad_maximum_fusion.1
  253.8 7.6 %copy.85 = bf16[2,16,2,256,256]{4,3,2,1,0:T(8,128)(2,1)} copy(bf16[2,16,2,256,256]{4,3,2,0,1:T(8,128)(2,1)} %all-to-all-done.1) | data formatting | bytes 16777216 | tf_op jit(solution)/shard_map/all_to_all | solution.py:67
  261.4 8.5 %gather_fusion.1 = bf16[28,2,256,256]{3,2,1,0:T(8,128)(2,1)} fusion(bf16[2,16,2,256,256]{4,3,2,1,0:T(8,128)(2,1)} %copy.85, s32[28]{0:T(128)S(1)} %fusion.24), kind=kCustom, calls=%fused_computation.1 | custom fusion | bytes 14680288 | tf_op jit(solution)/shard_map/gather | solution.py:68
  270.0 400.5 %while.14 = (s32[]{:T(128)}, bf16[14,256,256]{2,1,0:T(8,128)(2,1)}, s32[14]{0:T(128)S(1)}, bf16[2,5120,256]{1,2,0:T(8,128)(2,1)}, bf16[2,28,256,256]{3,2,0,1:T(8...) while((s32[]{:T(128)}, bf16[14,256,256]{2,1,0:T(8,128)(2,1)}, ...), condition=%wide.region_6.7_spmd.clone.clone, body=%wide.region_3.6_spmd.clone.clone.sunk | while | flops 927866496 | bytes 33087212 | solution.py:95
  292.1 5.7 fusion.53
  313.5 4.0 fusion.52
  320.7 5.7 fusion.53
  342.1 4.0 fusion.52
  349.3 5.7 fusion.53
  370.7 4.0 fusion.52
  378.0 5.7 fusion.53
  406.6 5.7 fusion.53
  435.2 5.7 fusion.53
  456.5 4.0 fusion.52
  463.8 5.7 fusion.53
  485.1 4.0 fusion.52
  492.4 5.7 fusion.53
  513.7 4.0 fusion.52
  521.0 5.7 fusion.53
  549.6 5.7 fusion.53
  578.2 5.7 fusion.53
  606.8 5.7 fusion.53
  635.4 5.7 fusion.53
  664.0 5.7 fusion.53
  670.5 32.9 %all_to_all.39 = bf16[16,224,256]{2,1,0:T(8,128)(2,1)S(1)} all-to-all(bf16[16,224,256]{2,1,0:T(8,128)(2,1)} %bitcast.85), channel_id=1, replica_groups=mesh['seq'=16,'head'=16] {'head'}, dimensions={0} | all-to-all | bytes 3670016 | tf_op jit(solution)/shard_map/all_to_all | solution.py:97
  (484 shorter events, 264.8 us)
Async XLA Ops:
  3.2 12.0 %all-to-all-start = ((s32[16,1,2]{2,1,0:T(1,128)}), s32[16,1,2]{2,1,0:T(1,128)S(1)}, u32[]{:S(2)}, u32[]{:S(2)}) async-start(s32[16,1,2]{2,1,0:T(1,128)} %copy.77), calls=%async_computation | async-start | bytes 16384 | tf_op jit(solution)/shard_map/all_to_all | solution.py:64
  30.1 223.8 %all-to-all-start.1 = ((bf16[2,16,2,256,256]{4,3,2,0,1:T(8,128)(2,1)}), bf16[2,16,2,256,256]{4,3,2,0,1:T(8,128)(2,1)}, u32[]{:S(2)}, u32[]{:S(2)}) async-start(bf16[2,16,2,256,256]{4,3,2,0,1:T(8,128)(2,1)} %fusion.19), calls=%async_computation.1 | async-start | bytes 16777216 | tf_op jit(solution)/shard_map/all_to_all | solution.py:67
  41.6 11.9 %copy-start.1 = (s32[14,2]{0,1:T(2,128)S(1)}, s32[14,2]{0,1:T(2,128)}, u32[]{:S(2)}) copy-start(s32[14,2]{0,1:T(2,128)} %param.12) | copy-start | bytes 340
  47.5 189.2 %collective-permute-start = (bf16[2,768,256]{1,2,0:T(8,128)(2,1)}, bf16[2,768,256]{1,2,0:T(8,128)(2,1)S(1)}, u32[]{:S(2)}, u32[]{:S(2)}) collective-permute-start(bf16[2,768,256]{1,2,0:T(8,128)(2,1)} %get-tuple-element.281), channel_id=1, source_target_pairs={{0,16},{16,32},{32,48},{48,64},{64,80},{80,96},{96,112},{112,128},... | collective-permute-start | bytes 2359304 | tf_op jit(solution)/shard_map/ppermute | solution.py:20
  50.0 199.3 %collective-permute-start.1 = (bf16[2,768,256]{1,2,0:T(8,128)(2,1)S(1)}, bf16[2,768,256]{1,2,0:T(8,128)(2,1)}, u32[]{:S(2)}, u32[]{:S(2)}) collective-permute-start(bf16[2,768,256]{1,2,0:T(8,128)(2,1)S(1)} %get-tuple-element.282), channel_id=1, source_target_pairs={{16,0},{32,16},{48,32},{64,48},{80,64},{96,80},{112,96},{128,112},... | collective-permute-start | bytes 2359304 | tf_op jit(solution)/shard_map/ppermute | solution.py:21
  261.4 8.5 %copy-start = (f32[2]{0:T(128)S(1)}, f32[2]{0:T(128)}, u32[]{:S(2)}) copy-start(f32[2]{0:T(128)} %param.13) | copy-start | bytes 28
  270.0 6.6 copy-start.4
  270.0 8.4 %copy-start.2 = (s32[14,2]{1,0:T(8,128)}, s32[14,2]{1,0:T(8,128)S(1)}, u32[]{:S(2)}) copy-start(s32[14,2]{1,0:T(8,128)S(1)} %get-tuple-element.399) | copy-start | bytes 340 | tf_op jit(solution)/shard_map/while
  298.6 6.6 copy-start.4
  298.6 8.4 %copy-start.2 = (s32[14,2]{1,0:T(8,128)}, s32[14,2]{1,0:T(8,128)S(1)}, u32[]{:S(2)}) copy-start(s32[14,2]{1,0:T(8,128)S(1)} %get-tuple-element.399) | copy-start | bytes 340 | tf_op jit(solution)/shard_map/while
  327.2 6.6 copy-start.4
  327.2 8.4 %copy-start.2 = (s32[14,2]{1,0:T(8,128)}, s32[14,2]{1,0:T(8,128)S(1)}, u32[]{:S(2)}) copy-start(s32[14,2]{1,0:T(8,128)S(1)} %get-tuple-element.399) | copy-start | bytes 340 | tf_op jit(solution)/shard_map/while
  355.8 6.6 copy-start.4
  355.8 8.4 %copy-start.2 = (s32[14,2]{1,0:T(8,128)}, s32[14,2]{1,0:T(8,128)S(1)}, u32[]{:S(2)}) copy-start(s32[14,2]{1,0:T(8,128)S(1)} %get-tuple-element.399) | copy-start | bytes 340 | tf_op jit(solution)/shard_map/while
  384.4 6.6 copy-start.4
  384.4 8.4 %copy-start.2 = (s32[14,2]{1,0:T(8,128)}, s32[14,2]{1,0:T(8,128)S(1)}, u32[]{:S(2)}) copy-start(s32[14,2]{1,0:T(8,128)S(1)} %get-tuple-element.399) | copy-start | bytes 340 | tf_op jit(solution)/shard_map/while
  413.0 6.6 copy-start.4
  413.0 8.4 %copy-start.2 = (s32[14,2]{1,0:T(8,128)}, s32[14,2]{1,0:T(8,128)S(1)}, u32[]{:S(2)}) copy-start(s32[14,2]{1,0:T(8,128)S(1)} %get-tuple-element.399) | copy-start | bytes 340 | tf_op jit(solution)/shard_map/while
  441.6 6.6 copy-start.4
  441.6 8.4 %copy-start.2 = (s32[14,2]{1,0:T(8,128)}, s32[14,2]{1,0:T(8,128)S(1)}, u32[]{:S(2)}) copy-start(s32[14,2]{1,0:T(8,128)S(1)} %get-tuple-element.399) | copy-start | bytes 340 | tf_op jit(solution)/shard_map/while
  470.2 6.6 copy-start.4
  470.2 8.4 %copy-start.2 = (s32[14,2]{1,0:T(8,128)}, s32[14,2]{1,0:T(8,128)S(1)}, u32[]{:S(2)}) copy-start(s32[14,2]{1,0:T(8,128)S(1)} %get-tuple-element.399) | copy-start | bytes 340 | tf_op jit(solution)/shard_map/while
  498.8 6.6 copy-start.4
  498.8 8.4 %copy-start.2 = (s32[14,2]{1,0:T(8,128)}, s32[14,2]{1,0:T(8,128)S(1)}, u32[]{:S(2)}) copy-start(s32[14,2]{1,0:T(8,128)S(1)} %get-tuple-element.399) | copy-start | bytes 340 | tf_op jit(solution)/shard_map/while
  527.4 6.6 copy-start.4
  527.4 8.4 %copy-start.2 = (s32[14,2]{1,0:T(8,128)}, s32[14,2]{1,0:T(8,128)S(1)}, u32[]{:S(2)}) copy-start(s32[14,2]{1,0:T(8,128)S(1)} %get-tuple-element.399) | copy-start | bytes 340 | tf_op jit(solution)/shard_map/while
  556.0 6.6 copy-start.4
  556.0 8.4 %copy-start.2 = (s32[14,2]{1,0:T(8,128)}, s32[14,2]{1,0:T(8,128)S(1)}, u32[]{:S(2)}) copy-start(s32[14,2]{1,0:T(8,128)S(1)} %get-tuple-element.399) | copy-start | bytes 340 | tf_op jit(solution)/shard_map/while
  584.6 8.4 %copy-start.2 = (s32[14,2]{1,0:T(8,128)}, s32[14,2]{1,0:T(8,128)S(1)}, u32[]{:S(2)}) copy-start(s32[14,2]{1,0:T(8,128)S(1)} %get-tuple-element.399) | copy-start | bytes 340 | tf_op jit(solution)/shard_map/while
  613.2 8.4 %copy-start.2 = (s32[14,2]{1,0:T(8,128)}, s32[14,2]{1,0:T(8,128)S(1)}, u32[]{:S(2)}) copy-start(s32[14,2]{1,0:T(8,128)S(1)} %get-tuple-element.399) | copy-start | bytes 340 | tf_op jit(solution)/shard_map/while
  641.9 6.6 copy-start.4
  641.9 8.4 %copy-start.2 = (s32[14,2]{1,0:T(8,128)}, s32[14,2]{1,0:T(8,128)S(1)}, u32[]{:S(2)}) copy-start(s32[14,2]{1,0:T(8,128)S(1)} %get-tuple-element.399) | copy-start | bytes 340 | tf_op jit(solution)/shard_map/while
  (30 other events, 193.6 us)
where the time goes:
time: 708 us; the launch traced here: 705 us
  waiting for transfers between devices  195 us (28%)
  matrix products  181 us (26%)
  local copies, waits for them, and re-layouts  166 us (23%)
  other arithmetic  54.3 us (8%)
  loops' own time  52.6 us (7%)
  blocking collectives  32.9 us (5%)
  starting transfers between devices  22.3 us (3%)
    ppermute x1, waiting for transfers between devices, padded(): before = lax.ppermute(last, axis, up)  183 us
    dot_general x14, matrix products, block_attention(): jnp.einsum('hqk,khd->qhd', weights, values_h, preferred_element_type=jnp....  79.1 us
    dot_general x14, matrix products, block_attention(): jnp.einsum('qhd,khd->hqk', queries_h, keys_h, preferred_element_type=jnp....  55.6 us
    another operation x1, loops' own time, body(): attended = lax.map(attend, jnp.arange(blk_dev))  52.6 us
    sub x14, matrix products, block_attention(): raised = jnp.exp(scores - row_max)  45.9 us
    dynamic_slice x28, local copies, waits for them, and re-layouts, attend(): query_blocks[local_block]  45.3 us
    all_to_all x1, blocking collectives, body(): lax.all_to_all(mixed_out, 'head', split_axis=0, concat_axis=1, tiled=True)  32.9 us
    dynamic_slice x14, local copies, waits for them, and re-layouts, attend(): lax.dynamic_slice_in_dim(extended, local_block * BT, band_span * BT, 1)  22.7 us
  transfers between devices with their start and end apart: 4, of which 2 were waited for; matrix products, arithmetic and copies ran while one was open for 3% of the time, Pallas kernels for 0%

commit v1 on v0

v1 whole, which is shorter than its diff:
```python
import functools
import math

import jax
import jax.numpy as jnp
from jax import lax
from jax.experimental import pallas as pl
from jax.experimental.pallas import tpu as pltpu
from jax.sharding import PartitionSpec as P


BT = 256
BAND = 3
FAR = 2
CAP = 2
DH = 128
LOG2E = 1.4426950408889634
FAR_AWAY = 1e30
MIB = 1 << 20


def route_kernel(far_ref, table_ref, slot_ref, count_ref, *, sources, blk_dev):
    for s in range(sources):
        count_ref[s] = 0
        for r in range(CAP):
            table_ref[s, r] = 0

    def step(i, carry):
        for f in range(FAR):
            block = far_ref[f, i]
            s = lax.div(block, blk_dev)
            r = jnp.minimum(count_ref[s], CAP - 1)
            count_ref[s] = r + 1
            table_ref[s, r] = block - s * blk_dev
            slot_ref[f, i] = s * CAP + r
        return carry

    lax.fori_loop(0, blk_dev, step, 0)


def route(far_list, sources):
    blk_dev = far_list.shape[0]
    smem = pl.BlockSpec(memory_space=pltpu.SMEM)
    return pl.pallas_call(
        functools.partial(route_kernel, sources=sources, blk_dev=blk_dev),
        out_shape=(
            jax.ShapeDtypeStruct((sources, CAP), jnp.int32),
            jax.ShapeDtypeStruct((FAR, blk_dev), jnp.int32),
        ),
        in_specs=[smem],
        out_specs=(smem, smem),
        scratch_shapes=[pltpu.SMEM((sources,), jnp.int32)],
        name="route",
    )(far_list.T)


def pack_kernel(asked_ref, me_ref, keys_ref, values_ref, *refs, shifts, head):
    out_refs, sems = refs[:-1], refs[-1]
    column = pl.ds(head * DH, DH)
    copies = []
    for shift in range(shifts):
        target = me_ref[0] + shift
        target = jnp.where(target >= shifts, target - shifts, target)
        for r in range(CAP):
            rows = pl.ds(pl.multiple_of(asked_ref[target, r] * BT, BT), BT)
            for which, ref in enumerate((keys_ref, values_ref)):
                slot = r * 2 + which
                if len(out_refs) == 1:
                    dst = out_refs[0].at[target, slot]
                else:
                    dst = out_refs[shift].at[slot]
                copy = pltpu.make_async_copy(ref.at[rows, column], dst, sems.at[shift, slot])
                copy.start()
                copies.append(copy)
    for copy in copies:
        copy.wait()


def pack(asked, me, key_rows, value_rows, head, split):
    shifts = asked.shape[0]
    smem = pl.BlockSpec(memory_space=pltpu.SMEM)
    hbm = pl.BlockSpec(memory_space=pltpu.HBM)
    one = jax.ShapeDtypeStruct((CAP * 2, BT, DH), jnp.bfloat16)
    if split:
        out_shape = (one,) * shifts
    else:
        out_shape = (jax.ShapeDtypeStruct((shifts,) + one.shape, one.dtype),)
    return pl.pallas_call(
        functools.partial(pack_kernel, shifts=shifts, head=head),
        out_shape=out_shape,
        in_specs=[smem, smem, hbm, hbm],
        out_specs=(hbm,) * len(out_shape),
        scratch_shapes=[pltpu.SemaphoreType.DMA((shifts, CAP * 2))],
        name="pack",
    )(asked, me, key_rows, value_rows)


def distances():
    rows = lax.broadcasted_iota(jnp.int32, (BT, BT), 0)
    columns = lax.broadcasted_iota(jnp.int32, (BT, BT), 1)
    return (rows - columns).astype(jnp.float32)


def pair_scores(query, key, offset, slope, gap):
    product = lax.dot_general(
        query, key, (((1,), (1,)), ((), ())), preferred_element_type=jnp.float32
    )
    return product * (LOG2E / math.sqrt(DH)) - slope * jnp.abs(gap + offset)


def weighted(weights, value):
    return lax.dot_general(
        weights.astype(jnp.bfloat16), value, (((1,), (0,)), ((), ())),
        preferred_element_type=jnp.float32,
    )


def row_max(scores):
    return jnp.max(scores, axis=1, keepdims=True)


def row_sum(scores):
    return jnp.sum(scores, axis=1, keepdims=True)


def band_kernel(
    meta_ref, slopes_ref, query_ref, keys_hbm, values_hbm, before_hbm, after_hbm,
    acc_ref, stat_ref,
    keys_ref, values_ref, gap_ref, max_ref, sum_ref, sems, *, blk_dev, total_blocks,
):
    head = pl.program_id(0)
    local = pl.program_id(1)
    margin = BAND * BT
    tok_rows = blk_dev * BT

    @pl.when(local == 0)
    def _():
        column = pl.ds(pl.multiple_of(head * DH, DH), DH)
        copies = []
        for which, (ref, whole) in enumerate(((keys_ref, keys_hbm), (values_ref, values_hbm))):
            copies += [
                pltpu.make_async_copy(
                    before_hbm.at[which, :, column], ref.at[pl.ds(0, margin)], sems.at[which, 0]
                ),
                pltpu.make_async_copy(
                    whole.at[:, column], ref.at[pl.ds(margin, tok_rows)], sems.at[which, 1]
                ),
                pltpu.make_async_copy(
                    after_hbm.at[which, :, column],
                    ref.at[pl.ds(margin + tok_rows, margin)],
                    sems.at[which, 2],
                ),
            ]
        for copy in copies:
            copy.start()
        gap_ref[...] = distances()
        for copy in copies:
            copy.wait()

    slope = slopes_ref[head] * LOG2E
    reach = meta_ref[local]
    block = meta_ref[blk_dev] * blk_dev + local
    query = query_ref[...]

    def rows_of(offset):
        return pl.ds(pl.multiple_of((local + BAND + offset) * BT, BT), BT)

    scores = pair_scores(query, keys_ref[rows_of(0), :], 0.0, slope, gap_ref[...])
    top = row_max(scores)
    weights = jnp.exp2(scores - top)
    max_ref[...] = top
    sum_ref[...] = row_sum(weights)
    acc_ref[...] = weighted(weights, values_ref[rows_of(0), :])

    for distance in range(1, BAND + 1):

        @pl.when(reach >= distance)
        def _():
            low = jnp.where(block >= distance, float(distance * BT), FAR_AWAY)
            high = jnp.where(block + distance < total_blocks, -float(distance * BT), -FAR_AWAY)
            gap = gap_ref[...]
            first = pair_scores(query, keys_ref[rows_of(-distance), :], low, slope, gap)
            second = pair_scores(query, keys_ref[rows_of(distance), :], high, slope, gap)
            old = max_ref[...]
            top = jnp.maximum(old, row_max(jnp.maximum(first, second)))
            shrink = jnp.exp2(old - top)
            first = jnp.exp2(first - top)
            second = jnp.exp2(second - top)
            max_ref[...] = top
            sum_ref[...] = sum_ref[...] * shrink + row_sum(first + second)
            acc_ref[...] = (
                acc_ref[...] * shrink
                + weighted(first, values_ref[rows_of(-distance), :])
                + weighted(second, values_ref[rows_of(distance), :])
            )

    lane = lax.broadcasted_iota(jnp.int32, (BT, DH), 1)
    stat_ref[...] = jnp.where(lane < DH // 2, max_ref[...], sum_ref[...])


def band_attention(meta, slopes, queries, key_rows, value_rows, before, after, total_blocks):
    tok_rows, channels = queries.shape
    blk_dev = tok_rows // BT
    heads = channels // DH
    any_spec = pl.BlockSpec(memory_space=pltpu.HBM)
    tile = pl.BlockSpec((BT, DH), lambda h, i, *_: (i, h))
    ext = tok_rows + 2 * BAND * BT
    return pl.pallas_call(
        functools.partial(band_kernel, blk_dev=blk_dev, total_blocks=total_blocks),
        out_shape=(
            jax.ShapeDtypeStruct((tok_rows, channels), jnp.float32),
            jax.ShapeDtypeStruct((tok_rows, channels), jnp.float32),
        ),
        grid_spec=pltpu.PrefetchScalarGridSpec(
            num_scalar_prefetch=2,
            grid=(heads, blk_dev),
            in_specs=[tile, any_spec, any_spec, any_spec, any_spec],
            out_specs=(tile, tile),
            scratch_shapes=[
                pltpu.VMEM((ext, DH), jnp.bfloat16),
                pltpu.VMEM((ext, DH), jnp.bfloat16),
                pltpu.VMEM((BT, BT), jnp.float32),
                pltpu.VMEM((BT, 1), jnp.float32),
                pltpu.VMEM((BT, 1), jnp.float32),
                pltpu.SemaphoreType.DMA((2, 3)),
            ],
        ),
        compiler_params=pltpu.CompilerParams(vmem_limit_bytes=24 * MIB),
        cost_estimate=pl.CostEstimate(
            flops=7 * 4 * tok_rows * BT * channels,
            transcendentals=7 * tok_rows * BT * heads,
            bytes_accessed=30 * MIB,
        ),
        name="band",
    )(meta, slopes, queries, key_rows, value_rows, before, after)


def far_kernel(
    meta_ref, slot_ref, block_ref, slopes_ref, query_ref, acc_ref, stat_ref, *refs, head, blk_dev,
    sources,
):
    pieces = refs[:-4]
    out_ref, buffer_ref, gap_ref, sems = refs[-4:]
    local = pl.program_id(0)

    @pl.when(local == 0)
    def _():
        if len(pieces) == 1:
            copies = [
                pltpu.make_async_copy(pieces[0].at[s], buffer_ref.at[s], sems.at[s])
                for s in range(sources)
            ]
        else:
            copies = [
                pltpu.make_async_copy(piece, buffer_ref.at[s], sems.at[s])
                for s, piece in enumerate(pieces)
            ]
        for copy in copies:
            copy.start()
        gap_ref[...] = distances()
        for copy in copies:
            copy.wait()

    slope = slopes_ref[head] * LOG2E
    me = meta_ref[blk_dev]
    block = me * blk_dev + local
    query = query_ref[...]
    gap = gap_ref[...]
    scores = []
    values = []
    for f in range(FAR):
        offset = ((block - block_ref[f, local]) * BT).astype(jnp.float32)
        slot = slot_ref[f, local]
        source = lax.div(slot, CAP)
        if len(pieces) > 1:
            source = me - source
            source = jnp.where(source < 0, source + sources, source)
        rank = lax.rem(slot, CAP)
        scores.append(pair_scores(query, buffer_ref[source, rank * 2], offset, slope, gap))
        values.append(buffer_ref[source, rank * 2 + 1])
    old = stat_ref[:, 0:1]
    old_sum = stat_ref[:, DH // 2 : DH // 2 + 1]
    top = jnp.maximum(old, row_max(jnp.maximum(scores[0], scores[1])))
    shrink = jnp.exp2(old - top)
    first = jnp.exp2(scores[0] - top)
    second = jnp.exp2(scores[1] - top)
    total = old_sum * shrink + row_sum(first + second)
    acc = acc_ref[...] * shrink + weighted(first, values[0]) + weighted(second, values[1])
    out_ref[...] = (acc / total).astype(jnp.bfloat16)


def far_attention(meta, slots, far_blocks, slopes, queries, acc, stat, pieces, head, sources):
    tok_rows = queries.shape[0]
    blk_dev = tok_rows // BT
    tile = pl.BlockSpec((BT, DH), lambda i, *_: (i, head))
    any_spec = pl.BlockSpec(memory_space=pltpu.HBM)
    return pl.pallas_call(
        functools.partial(far_kernel, head=head, blk_dev=blk_dev, sources=sources),
        out_shape=jax.ShapeDtypeStruct((tok_rows, DH), jnp.bfloat16),
        grid_spec=pltpu.PrefetchScalarGridSpec(
            num_scalar_prefetch=4,
            grid=(blk_dev,),
            in_specs=[tile, tile, tile] + [any_spec] * len(pieces),
            out_specs=pl.BlockSpec((BT, DH), lambda i, *_: (i, 0)),
            scratch_shapes=[
                pltpu.VMEM((sources, CAP * 2, BT, DH), jnp.bfloat16),
                pltpu.VMEM((BT, BT), jnp.float32),
                pltpu.SemaphoreType.DMA((sources,)),
            ],
        ),
        compiler_params=pltpu.CompilerParams(vmem_limit_bytes=16 * MIB),
        cost_estimate=pl.CostEstimate(
            flops=2 * 4 * tok_rows * BT * DH,
            transcendentals=2 * tok_rows * BT,
            bytes_accessed=14 * MIB,
        ),
        name="far",
    )(meta, slots, far_blocks, slopes, queries, acc, stat, *pieces)


def body(queries, key_rows, value_rows, band_reach, far_list, slopes):
    myself = lax.axis_index("seq")
    sources = lax.axis_size("seq")
    tok_rows, channels = key_rows.shape
    blk_dev = tok_rows // BT
    margin = BAND * BT
    heads = channels // DH
    up = [(i, i + 1) for i in range(sources - 1)]
    down = [(i + 1, i) for i in range(sources - 1)]

    table, slots = route(far_list, sources)
    asked = lax.all_to_all(table, "seq", split_axis=0, concat_axis=0, tiled=True)
    last = jnp.stack([key_rows[tok_rows - margin :], value_rows[tok_rows - margin :]])
    first = jnp.stack([key_rows[:margin], value_rows[:margin]])
    before = lax.ppermute(last, "seq", up)
    after = lax.ppermute(first, "seq", down)

    me = myself[None].astype(jnp.int32)
    incoming = []
    for head in range(heads):
        split = head == heads - 1
        outgoing = pack(asked, me, key_rows, value_rows, head, split)
        if split:
            pieces = [outgoing[0]]
            for shift in range(1, sources):
                ring = [(i, (i + shift) % sources) for i in range(sources)]
                pieces.append(lax.ppermute(outgoing[shift], "seq", ring))
            incoming.append(pieces)
        else:
            incoming.append(
                [lax.all_to_all(outgoing[0], "seq", split_axis=0, concat_axis=0, tiled=True)]
            )

    meta = jnp.concatenate([band_reach, me])
    acc, stat = band_attention(
        meta, slopes, queries, key_rows, value_rows, before, after, blk_dev * sources
    )
    acc, stat, queries = (
        pltpu.with_memory_space_constraint(x, pltpu.HBM) for x in (acc, stat, queries)
    )
    parts = []
    for head in range(heads):
        attended = far_attention(
            meta, slots, far_list.T, slopes, queries, acc, stat, incoming[head], head, sources
        )
        parts.append(
            lax.all_to_all(
                attended.reshape(lax.axis_size("head"), -1, DH), "head",
                split_axis=0, concat_axis=0, tiled=True,
            )
        )
    mixed = jnp.stack(parts, axis=1)
    return mixed.transpose(2, 0, 1, 3).reshape(mixed.shape[2], -1)


def solution(mesh):
    in_specs = (
        P("seq", "head"),
        P("seq", "head"),
        P("seq", "head"),
        P("seq"),
        P("seq", None),
        P("head"),
    )
    out_specs = P(("seq", "head"), None)

    return jax.shard_map(body, mesh=mesh, in_specs=in_specs, out_specs=out_specs, check_vma=False)
```

time: 708 us -> 535 us (0.76)
  the two profiles are of different devices: /device:TPU:160 before, /device:TPU:64 now
where the time goes in v1:
time: 535 us; the launch traced here: 534 us
  Pallas kernels  351 us (66%)
  starting transfers between devices  89.9 us (17%)
  waiting for transfers between devices  59.3 us (11%)
  blocking collectives  22 us (4%)
  local copies, waits for them, and re-layouts  11.4 us (2%)
    pallas_call x2, Pallas kernels, pack(): pl.pallas_call(functools.partial(pack_kernel, shifts=shifts, head=head),...  259 us
    pallas_call x1, Pallas kernels, band_attention(): pl.pallas_call(functools.partial(band_kernel, blk_dev=blk_dev, total_bloc...  60.4 us
    ppermute x15, starting transfers between devices, body(): pieces.append(lax.ppermute(outgoing[shift], 'seq', ring))  59.8 us
    ppermute x15, waiting for transfers between devices, body(): pieces.append(lax.ppermute(outgoing[shift], 'seq', ring))  51.9 us
    pallas_call x2, Pallas kernels, far_attention(): pl.pallas_call(functools.partial(far_kernel, head=head, blk_dev=blk_dev,...  29.4 us
    all_to_all x1, blocking collectives, body(): lax.all_to_all(attended.reshape(lax.axis_size('head'), -1, DH), 'head', s...  22 us
  transfers between devices with their start and end apart: 20, of which 10 were waited for; matrix products, arithmetic and copies ran while one was open for 0% of the time, Pallas kernels for 41%

profile of v1, /device:TPU:64, one launch (start us, length us, event | category | flops | bytes accessed | tf_op | source)
XLA Modules:
  0.0 534.2 jit_solution(16383881716386674959)
XLA Ops:
  1.8 9.2 %all-to-all-start = ((s32[16,1,2]{2,1,0:T(1,128)}), s32[16,1,2]{2,1,0:T(1,128)S(1)}, u32[]{:S(2)}, u32[]{:S(2)}) async-start(s32[16,1,2]{2,1,0:T(1,128)} %bitcast.28), calls=%async_computation | async-start | bytes 16384 | tf_op jit(solution)/shard_map/all_to_all | solution.py:332
  10.9 6.2 %all-to-all-done = s32[16,1,2]{2,1,0:T(1,128)S(1)} async-done(((s32[16,1,2]{2,1,0:T(1,128)}), s32[16,1,2]{2,1,0:T(1,128)S(1)}, u32[]{:S(2)}, u32[]{:S(2)}) %all-to-all-start) | async-done | bytes 160 | tf_op jit(solution)/shard_map/all_to_all | solution.py:332
  17.8 129.5 %pack.2 = bf16[16,4,256,128]{3,2,1,0:T(8,128)(2,1)} custom-call(s32[16,2]{1,0:T(8,128)} %bitcast.26, s32[1]{0:T(128)} %bitcast.me_ref, bf16[3584,256]{1,0:T(8,128)(2,1)} %keys_ref.3, bf16[3584,256]{1,0:T(8,128)(2,1)} %values_ref.3), custom_call_target="tpu_custom_call" | custom-call | tf_op jit(solution)/shard_map/pack/pallas_call | solution.py:88
  147.3 6.6 %all-to-all-start.1 = ((bf16[16,4,256,128]{3,2,1,0:T(8,128)(2,1)}), bf16[16,4,256,128]{3,2,1,0:T(8,128)(2,1)}, u32[]{:S(2)}, u32[]{:S(2)}) async-start(bf16[16,4,256,128]{3,2,1,0:T(8,128)(2,1)} %pack.2), calls=%async_computation.1 | async-start | bytes 8388608 | tf_op jit(solution)/shard_map/all_to_all | solution.py:351
  155.3 129.7 %pack.3 = (bf16[4,256,128]{2,1,0:T(8,128)(2,1)}, bf16[4,256,128]{2,1,0:T(8,128)(2,1)}, bf16[4,256,128]{2,1,0:T(8,128)(2,1)}, bf16[4,256,128]{2,1,0:T(8,128)(2,1)...) custom-call(s32[16,2]{1,0:T(8,128)} %bitcast.27, ...), custom_call_target="tpu_custom_call" | custom-call | tf_op jit(solution)/shard_map/pack/pallas_call | solution.py:88
  285.1 2.5 collective-permute-start.10
  287.7 2.5 collective-permute-start.1
  290.2 4.8 collective-permute-start.11
  295.3 3.9 collective-permute-start.13
  299.3 5.1 collective-permute-start
  304.4 6.9 %collective-permute-done.11.refs_10_ = bf16[4,256,128]{2,1,0:T(8,128)(2,1)S(1)} collective-permute-done((bf16[4,256,128]{2,1,0:T(8,128)(2,1)}, bf16[4,256,128]{2,1,0:T(8,128)(2,1)S(1)}, u32[]{:S(2)}, u32[]{:S(2)}) %collective-permute-start.11) | collective-permute-done | bytes 262176 | tf_op jit(solution)/shard_map/ppermute | solution.py:347
  311.3 4.7 collective-permute-start.14
  316.0 7.1 %collective-permute-done.12.refs_11_ = bf16[4,256,128]{2,1,0:T(8,128)(2,1)S(1)} collective-permute-done((bf16[4,256,128]{2,1,0:T(8,128)(2,1)}, bf16[4,256,128]{2,1,0:T(8,128)(2,1)S(1)}, u32[]{:S(2)}, u32[]{:S(2)}) %collective-permute-start.12) | collective-permute-done | bytes 262176 | tf_op jit(solution)/shard_map/ppermute | solution.py:347
  323.2 9.6 %collective-permute-start.15 = (bf16[4,256,128]{2,1,0:T(8,128)(2,1)}, bf16[4,256,128]{2,1,0:T(8,128)(2,1)S(1)}, u32[]{:S(2)}, u32[]{:S(2)}) collective-permute-start(bf16[4,256,128]{2,1,0:T(8,128)(2,1)} %get-tuple-element.43), channel_id=1, source_target_pairs={{0,224},{16,240},{32,0},{48,16},{64,32},{80,48},{96,64},{112,80},{... | collective-permute-start | bytes 786440 | tf_op jit(solution)/shard_map/ppermute | solution.py:347
  332.8 3.8 collective-permute-done.13.refs_12_
  336.6 9.2 %collective-permute-start.2 = (bf16[4,256,128]{2,1,0:T(8,128)(2,1)}, bf16[4,256,128]{2,1,0:T(8,128)(2,1)S(1)}, u32[]{:S(2)}, u32[]{:S(2)}) collective-permute-start(bf16[4,256,128]{2,1,0:T(8,128)(2,1)} %get-tuple-element.30), channel_id=1, source_target_pairs={{0,16},{16,32},{32,48},{48,64},{64,80},{80,96},{96,112},{112,128},... | collective-permute-start | bytes 786440 | tf_op jit(solution)/shard_map/ppermute | solution.py:347
  345.8 6.5 %collective-permute-done.15.refs_14_ = bf16[4,256,128]{2,1,0:T(8,128)(2,1)S(1)} collective-permute-done((bf16[4,256,128]{2,1,0:T(8,128)(2,1)}, bf16[4,256,128]{2,1,0:T(8,128)(2,1)S(1)}, u32[]{:S(2)}, u32[]{:S(2)}) %collective-permute-start.15) | collective-permute-done | bytes 262176 | tf_op jit(solution)/shard_map/ppermute | solution.py:347
  352.8 5.1 collective-permute-start.4
  358.0 5.1 collective-permute-done.2.refs_1_
  363.9 7.6 %collective-permute-done.3.refs_2_ = bf16[4,256,128]{2,1,0:T(8,128)(2,1)S(1)} collective-permute-done((bf16[4,256,128]{2,1,0:T(8,128)(2,1)}, bf16[4,256,128]{2,1,0:T(8,128)(2,1)S(1)}, u32[]{:S(2)}, u32[]{:S(2)}) %collective-permute-start.3) | collective-permute-done | bytes 262176 | tf_op jit(solution)/shard_map/ppermute | solution.py:347
  371.5 3.5 collective-permute-start.6
  375.0 14.3 %collective-permute-done.4.refs_3_ = bf16[4,256,128]{2,1,0:T(8,128)(2,1)S(1)} collective-permute-done((bf16[4,256,128]{2,1,0:T(8,128)(2,1)}, bf16[4,256,128]{2,1,0:T(8,128)(2,1)S(1)}, u32[]{:S(2)}, u32[]{:S(2)}) %collective-permute-start.4) | collective-permute-done | bytes 262176 | tf_op jit(solution)/shard_map/ppermute | solution.py:347
  389.3 7.5 %collective-permute-start.7 = (bf16[4,256,128]{2,1,0:T(8,128)(2,1)S(1)}, bf16[4,256,128]{2,1,0:T(8,128)(2,1)S(1)}, u32[]{:S(2)}, u32[]{:S(2)}) collective-permute-start(bf16[4,256,128]{2,1,0:T(8,128)(2,1)S(1)} %copy-done.12), channel_id=1, source_target_pairs={{0,96},{16,112},{32,128},{48,144},{64,160},{80,176},{96,192},{112,... | collective-permute-start | bytes 786440 | tf_op jit(solution)/shard_map/ppermute | solution.py:347
  397.3 7.4 %collective-permute-start.9 = (bf16[4,256,128]{2,1,0:T(8,128)(2,1)S(1)}, bf16[4,256,128]{2,1,0:T(8,128)(2,1)S(1)}, u32[]{:S(2)}, u32[]{:S(2)}) collective-permute-start(bf16[4,256,128]{2,1,0:T(8,128)(2,1)S(1)} %copy-done.10), channel_id=1, source_target_pairs={{0,128},{16,144},{32,160},{48,176},{64,192},{80,208},{96,224},{112... | collective-permute-start | bytes 786440 | tf_op jit(solution)/shard_map/ppermute | solution.py:347
  406.2 60.4 %band.1 = (f32[3584,256]{1,0:T(8,128)S(1)}, f32[3584,256]{1,0:T(8,128)S(1)}) custom-call(s32[15]{0:T(128)S(1)} %pad_add_fusion.meta_ref, f32[2]{0:T(128)S(1)} %copy-done.8, bf16[3584,256]{1,0:T(8,128)(2,1)S(1)} %copy-done.4, bf16[3584,256]{1,0:T(8,128)(2,1)S(1)} %copy-done.2, bf16[3584,256]{1,0:T(8,128)(2,1)S(1)} %copy-done.3, ...), custom_call_target="tpu_custom_call" | custom-call | flops 6576668672 | bytes 31457280 | tf_op jit(solution)/shard_map/band/pallas_call | solution.py:208
  466.7 1.8 copy-done
  470.3 14.1 %far.3 = bf16[3584,128]{1,0:T(8,128)(2,1)} custom-call(s32[15]{0:T(128)S(1)} %pad_add_fusion.meta_ref, s32[2,14]{1,0:T(2,128)S(1)} %copy-done.7, s32[2,14]{1,0:T(2,128)S(1)} %bitcast.22, f32[2]{0:T(128)S(1)} %copy-done.8, bf16[3584,256]{1,0:T(8,128)(2,1)} %query_ref.5, f32[3584,256]{1,0:T(8,128)} %copy-done, f32[3584,256]{1,0:T(8,128)} %copy-done.1, ...), custom_call_target="tpu_custom_call" | custom-call | flops 939524096 | bytes 14680064 | tf_op jit(solution)/shard_map/far/pallas_call | solution.py:297
  484.4 6.8 %all-to-all-start.3 = ((bf16[16,224,128]{2,1,0:T(8,128)(2,1)}), bf16[16,224,128]{2,1,0:T(8,128)(2,1)S(1)}, u32[]{:S(2)}, u32[]{:S(2)}) async-start(bf16[16,224,128]{2,1,0:T(8,128)(2,1)} %bitcast.10), calls=%async_computation.3 | async-start | bytes 1835008 | tf_op jit(solution)/shard_map/all_to_all | solution.py:367
  491.2 15.3 %far.2 = bf16[3584,128]{1,0:T(8,128)(2,1)S(1)} custom-call(s32[15]{0:T(128)S(1)} %pad_add_fusion.meta_ref, s32[2,14]{1,0:T(2,128)S(1)} %copy-done.7, s32[2,14]{1,0:T(2,128)S(1)} %bitcast.23, f32[2]{0:T(128)S(1)} %copy-done.8, bf16[3584,256]{1,0:T(8,128)(2,1)} %query_ref.5, f32[3584,256]{1,0:T(8,128)} %copy-done, f32[3584,256]{1,0:T(8,128)} %copy-done.1, ...), custom_call_target="tpu_custom_call" | custom-call | flops 939524096 | bytes 14680064 | tf_op jit(solution)/shard_map/far/pallas_call | solution.py:297
  507.7 22.0 %all_to_all.26 = bf16[16,224,128]{2,1,0:T(8,128)(2,1)S(1)} all-to-all(bf16[16,224,128]{2,1,0:T(8,128)(2,1)S(1)} %bitcast.20), channel_id=1, replica_groups=mesh['seq'=16,'head'=16] {'head'}, dimensions={0} | all-to-all | bytes 1835008 | tf_op jit(solution)/shard_map/all_to_all | solution.py:367
  530.0 1.9 copy.16
  531.8 2.3 reshape.13
  (54 shorter events, 11.0 us)
Async XLA Ops:
  1.8 15.4 %all-to-all-start = ((s32[16,1,2]{2,1,0:T(1,128)}), s32[16,1,2]{2,1,0:T(1,128)S(1)}, u32[]{:S(2)}, u32[]{:S(2)}) async-start(s32[16,1,2]{2,1,0:T(1,128)} %bitcast.28), calls=%async_computation | async-start | bytes 16384 | tf_op jit(solution)/shard_map/all_to_all | solution.py:332
  147.3 337.1 %all-to-all-start.1 = ((bf16[16,4,256,128]{3,2,1,0:T(8,128)(2,1)}), bf16[16,4,256,128]{3,2,1,0:T(8,128)(2,1)}, u32[]{:S(2)}, u32[]{:S(2)}) async-start(bf16[16,4,256,128]{3,2,1,0:T(8,128)(2,1)} %pack.2), calls=%async_computation.1 | async-start | bytes 8388608 | tf_op jit(solution)/shard_map/all_to_all | solution.py:351
  155.3 249.4 %copy-start.3 = (bf16[3584,256]{1,0:T(8,128)(2,1)S(1)}, bf16[3584,256]{1,0:T(8,128)(2,1)}, u32[]{:S(2)}) copy-start(bf16[3584,256]{1,0:T(8,128)(2,1)} %values_ref.3) | copy-start | bytes 5505028
  285.0 72.9 %copy-start.15 = (s32[14]{0:T(128)S(1)}, s32[14]{0:T(128)}, u32[]{:S(2)}) copy-start(s32[14]{0:T(128)} %param.9) | copy-start | bytes 172
  285.0 78.0 %copy-start.14 = (bf16[4,256,128]{2,1,0:T(8,128)(2,1)S(1)}, bf16[4,256,128]{2,1,0:T(8,128)(2,1)}, u32[]{:S(2)}) copy-start(bf16[4,256,128]{2,1,0:T(8,128)(2,1)} %get-tuple-element.33) | copy-start | bytes 786436
  285.0 86.4 %copy-start.13 = (bf16[4,256,128]{2,1,0:T(8,128)(2,1)S(1)}, bf16[4,256,128]{2,1,0:T(8,128)(2,1)}, u32[]{:S(2)}) copy-start(bf16[4,256,128]{2,1,0:T(8,128)(2,1)} %get-tuple-element.34) | copy-start | bytes 786436
  285.1 104.3 %copy-start.12 = (bf16[4,256,128]{2,1,0:T(8,128)(2,1)S(1)}, bf16[4,256,128]{2,1,0:T(8,128)(2,1)}, u32[]{:S(2)}) copy-start(bf16[4,256,128]{2,1,0:T(8,128)(2,1)} %get-tuple-element.35) | copy-start | bytes 786436
  285.1 111.7 %copy-start.11 = (bf16[4,256,128]{2,1,0:T(8,128)(2,1)S(1)}, bf16[4,256,128]{2,1,0:T(8,128)(2,1)}, u32[]{:S(2)}) copy-start(bf16[4,256,128]{2,1,0:T(8,128)(2,1)} %get-tuple-element.36) | copy-start | bytes 786436
  285.1 112.2 %copy-start.10 = (bf16[4,256,128]{2,1,0:T(8,128)(2,1)S(1)}, bf16[4,256,128]{2,1,0:T(8,128)(2,1)}, u32[]{:S(2)}) copy-start(bf16[4,256,128]{2,1,0:T(8,128)(2,1)} %get-tuple-element.37) | copy-start | bytes 786436
  285.1 119.6 %copy-start.2 = (bf16[3584,256]{1,0:T(8,128)(2,1)S(1)}, bf16[3584,256]{1,0:T(8,128)(2,1)}, u32[]{:S(2)}) copy-start(bf16[3584,256]{1,0:T(8,128)(2,1)} %keys_ref.3) | copy-start | bytes 5505028
  285.1 119.6 %copy-start.8 = (f32[2]{0:T(128)S(1)}, f32[2]{0:T(128)}, u32[]{:S(2)}) copy-start(f32[2]{0:T(128)} %slopes_ref.5) | copy-start | bytes 28
  285.1 14.2 %collective-permute-start.10 = (bf16[4,256,128]{2,1,0:T(8,128)(2,1)}, bf16[4,256,128]{2,1,0:T(8,128)(2,1)S(1)}, u32[]{:S(2)}, u32[]{:S(2)}) collective-permute-start(bf16[4,256,128]{2,1,0:T(8,128)(2,1)} %get-tuple-element.38), channel_id=1, source_target_pairs={{0,144},{16,160},{32,176},{48,192},{64,208},{80,224},{96,240},{112... | collective-permute-start | bytes 786440 | tf_op jit(solution)/shard_map/ppermute | solution.py:347
  287.7 109.1 %collective-permute-start.1 = (bf16[2,768,256]{2,1,0:T(8,128)(2,1)S(1)}, bf16[2,768,256]{2,1,0:T(8,128)(2,1)S(1)}, u32[]{:S(2)}, u32[]{:S(2)}) collective-permute-start(bf16[2,768,256]{2,1,0:T(8,128)(2,1)S(1)} %pad_maximum_fusion.1), channel_id=1, source_target_pairs={{16,0},{32,16},{48,32},{64,48},{80,64},{96,80},{112,96},{128,112},... | collective-permute-start | bytes 2359304 | tf_op jit(solution)/shard_map/ppermute | solution.py:336
  290.2 21.1 %collective-permute-start.11 = (bf16[4,256,128]{2,1,0:T(8,128)(2,1)}, bf16[4,256,128]{2,1,0:T(8,128)(2,1)S(1)}, u32[]{:S(2)}, u32[]{:S(2)}) collective-permute-start(bf16[4,256,128]{2,1,0:T(8,128)(2,1)} %get-tuple-element.39), channel_id=1, source_target_pairs={{0,160},{16,176},{32,192},{48,208},{64,224},{80,240},{96,0},{112,1... | collective-permute-start | bytes 786440 | tf_op jit(solution)/shard_map/ppermute | solution.py:347
  295.0 28.2 %collective-permute-start.12 = (bf16[4,256,128]{2,1,0:T(8,128)(2,1)}, bf16[4,256,128]{2,1,0:T(8,128)(2,1)S(1)}, u32[]{:S(2)}, u32[]{:S(2)}) collective-permute-start(bf16[4,256,128]{2,1,0:T(8,128)(2,1)} %get-tuple-element.40), channel_id=1, source_target_pairs={{0,176},{16,192},{32,208},{48,224},{64,240},{80,0},{96,16},{112,32... | collective-permute-start | bytes 786440 | tf_op jit(solution)/shard_map/ppermute | solution.py:347
  295.3 41.3 %collective-permute-start.13 = (bf16[4,256,128]{2,1,0:T(8,128)(2,1)}, bf16[4,256,128]{2,1,0:T(8,128)(2,1)S(1)}, u32[]{:S(2)}, u32[]{:S(2)}) collective-permute-start(bf16[4,256,128]{2,1,0:T(8,128)(2,1)} %get-tuple-element.41), channel_id=1, source_target_pairs={{0,192},{16,208},{32,224},{48,240},{64,0},{80,16},{96,32},{112,48}... | collective-permute-start | bytes 786440 | tf_op jit(solution)/shard_map/ppermute | solution.py:347
  299.3 98.0 %collective-permute-start = (bf16[2,768,256]{2,1,0:T(8,128)(2,1)S(1)}, bf16[2,768,256]{2,1,0:T(8,128)(2,1)S(1)}, u32[]{:S(2)}, u32[]{:S(2)}) collective-permute-start(bf16[2,768,256]{2,1,0:T(8,128)(2,1)S(1)} %pad_maximum_fusion), channel_id=1, source_target_pairs={{0,16},{16,32},{32,48},{48,64},{64,80},{80,96},{96,112},{112,128},... | collective-permute-start | bytes 2359304 | tf_op jit(solution)/shard_map/ppermute | solution.py:335
  311.3 25.3 %collective-permute-start.14 = (bf16[4,256,128]{2,1,0:T(8,128)(2,1)}, bf16[4,256,128]{2,1,0:T(8,128)(2,1)S(1)}, u32[]{:S(2)}, u32[]{:S(2)}) collective-permute-start(bf16[4,256,128]{2,1,0:T(8,128)(2,1)} %get-tuple-element.42), channel_id=1, source_target_pairs={{0,208},{16,224},{32,240},{48,0},{64,16},{80,32},{96,48},{112,64},... | collective-permute-start | bytes 786440 | tf_op jit(solution)/shard_map/ppermute | solution.py:347
  323.2 29.2 %collective-permute-start.15 = (bf16[4,256,128]{2,1,0:T(8,128)(2,1)}, bf16[4,256,128]{2,1,0:T(8,128)(2,1)S(1)}, u32[]{:S(2)}, u32[]{:S(2)}) collective-permute-start(bf16[4,256,128]{2,1,0:T(8,128)(2,1)} %get-tuple-element.43), channel_id=1, source_target_pairs={{0,224},{16,240},{32,0},{48,16},{64,32},{80,48},{96,64},{112,80},{... | collective-permute-start | bytes 786440 | tf_op jit(solution)/shard_map/ppermute | solution.py:347
  336.6 16.2 %collective-permute-start.16 = (bf16[4,256,128]{2,1,0:T(8,128)(2,1)}, bf16[4,256,128]{2,1,0:T(8,128)(2,1)S(1)}, u32[]{:S(2)}, u32[]{:S(2)}) collective-permute-start(bf16[4,256,128]{2,1,0:T(8,128)(2,1)} %get-tuple-element.44), channel_id=1, source_target_pairs={{0,240},{16,0},{32,16},{48,32},{64,48},{80,64},{96,80},{112,96},{1... | collective-permute-start | bytes 786440 | tf_op jit(solution)/shard_map/ppermute | solution.py:347
  336.6 26.5 %collective-permute-start.2 = (bf16[4,256,128]{2,1,0:T(8,128)(2,1)}, bf16[4,256,128]{2,1,0:T(8,128)(2,1)S(1)}, u32[]{:S(2)}, u32[]{:S(2)}) collective-permute-start(bf16[4,256,128]{2,1,0:T(8,128)(2,1)} %get-tuple-element.30), channel_id=1, source_target_pairs={{0,16},{16,32},{32,48},{48,64},{64,80},{80,96},{96,112},{112,128},... | collective-permute-start | bytes 786440 | tf_op jit(solution)/shard_map/ppermute | solution.py:347
  352.3 19.1 %collective-permute-start.3 = (bf16[4,256,128]{2,1,0:T(8,128)(2,1)}, bf16[4,256,128]{2,1,0:T(8,128)(2,1)S(1)}, u32[]{:S(2)}, u32[]{:S(2)}) collective-permute-start(bf16[4,256,128]{2,1,0:T(8,128)(2,1)} %get-tuple-element.31), channel_id=1, source_target_pairs={{0,32},{16,48},{32,64},{48,80},{64,96},{80,112},{96,128},{112,144}... | collective-permute-start | bytes 786440 | tf_op jit(solution)/shard_map/ppermute | solution.py:347
  352.8 36.5 %collective-permute-start.4 = (bf16[4,256,128]{2,1,0:T(8,128)(2,1)}, bf16[4,256,128]{2,1,0:T(8,128)(2,1)S(1)}, u32[]{:S(2)}, u32[]{:S(2)}) collective-permute-start(bf16[4,256,128]{2,1,0:T(8,128)(2,1)} %get-tuple-element.32), channel_id=1, source_target_pairs={{0,48},{16,64},{32,80},{48,96},{64,112},{80,128},{96,144},{112,160... | collective-permute-start | bytes 786440 | tf_op jit(solution)/shard_map/ppermute | solution.py:347
  363.1 107.2 %collective-permute-start.5 = (bf16[4,256,128]{2,1,0:T(8,128)(2,1)S(1)}, bf16[4,256,128]{2,1,0:T(8,128)(2,1)S(1)}, u32[]{:S(2)}, u32[]{:S(2)}) collective-permute-start(bf16[4,256,128]{2,1,0:T(8,128)(2,1)S(1)} %copy-done.14), channel_id=1, source_target_pairs={{0,64},{16,80},{32,96},{48,112},{64,128},{80,144},{96,160},{112,17... | collective-permute-start | bytes 786440 | tf_op jit(solution)/shard_map/ppermute | solution.py:347
  371.5 98.8 %collective-permute-start.6 = (bf16[4,256,128]{2,1,0:T(8,128)(2,1)S(1)}, bf16[4,256,128]{2,1,0:T(8,128)(2,1)S(1)}, u32[]{:S(2)}, u32[]{:S(2)}) collective-permute-start(bf16[4,256,128]{2,1,0:T(8,128)(2,1)S(1)} %copy-done.13), channel_id=1, source_target_pairs={{0,80},{16,96},{32,112},{48,128},{64,144},{80,160},{96,176},{112,1... | collective-permute-start | bytes 786440 | tf_op jit(solution)/shard_map/ppermute | solution.py:347
  389.3 81.0 %collective-permute-start.7 = (bf16[4,256,128]{2,1,0:T(8,128)(2,1)S(1)}, bf16[4,256,128]{2,1,0:T(8,128)(2,1)S(1)}, u32[]{:S(2)}, u32[]{:S(2)}) collective-permute-start(bf16[4,256,128]{2,1,0:T(8,128)(2,1)S(1)} %copy-done.12), channel_id=1, source_target_pairs={{0,96},{16,112},{32,128},{48,144},{64,160},{80,176},{96,192},{112,... | collective-permute-start | bytes 786440 | tf_op jit(solution)/shard_map/ppermute | solution.py:347
  396.8 73.5 %collective-permute-start.8 = (bf16[4,256,128]{2,1,0:T(8,128)(2,1)S(1)}, bf16[4,256,128]{2,1,0:T(8,128)(2,1)S(1)}, u32[]{:S(2)}, u32[]{:S(2)}) collective-permute-start(bf16[4,256,128]{2,1,0:T(8,128)(2,1)S(1)} %copy-done.11), channel_id=1, source_target_pairs={{0,112},{16,128},{32,144},{48,160},{64,176},{80,192},{96,208},{112... | collective-permute-start | bytes 786440 | tf_op jit(solution)/shard_map/ppermute | solution.py:347
  397.3 73.0 %collective-permute-start.9 = (bf16[4,256,128]{2,1,0:T(8,128)(2,1)S(1)}, bf16[4,256,128]{2,1,0:T(8,128)(2,1)S(1)}, u32[]{:S(2)}, u32[]{:S(2)}) collective-permute-start(bf16[4,256,128]{2,1,0:T(8,128)(2,1)S(1)} %copy-done.10), channel_id=1, source_target_pairs={{0,128},{16,144},{32,160},{48,176},{64,192},{80,208},{96,224},{112... | collective-permute-start | bytes 786440 | tf_op jit(solution)/shard_map/ppermute | solution.py:347
  406.2 64.1 %copy-start.5 = (bf16[4,256,128]{2,1,0:T(8,128)(2,1)S(1)}, bf16[4,256,128]{2,1,0:T(8,128)(2,1)}, u32[]{:S(2)}) copy-start(bf16[4,256,128]{2,1,0:T(8,128)(2,1)} %get-tuple-element.29.refs_0_) | copy-start | bytes 786436
  406.2 64.1 %copy-start.6 = (s32[14,2]{0,1:T(2,128)S(1)}, s32[14,2]{0,1:T(2,128)}, u32[]{:S(2)}) copy-start(s32[14,2]{0,1:T(2,128)} %param.10) | copy-start | bytes 340
  406.2 64.1 %copy-start.7 = (s32[2,14]{1,0:T(2,128)S(1)}, s32[2,14]{1,0:T(2,128)}, u32[]{:S(2)}) copy-start(s32[2,14]{1,0:T(2,128)} %get-tuple-element.25.slot_ref) | copy-start | bytes 340
  484.4 23.3 %all-to-all-start.3 = ((bf16[16,224,128]{2,1,0:T(8,128)(2,1)}), bf16[16,224,128]{2,1,0:T(8,128)(2,1)S(1)}, u32[]{:S(2)}, u32[]{:S(2)}) async-start(bf16[16,224,128]{2,1,0:T(8,128)(2,1)} %bitcast.10), calls=%async_computation.3 | async-start | bytes 1835008 | tf_op jit(solution)/shard_map/all_to_all | solution.py:367
  (4 other events, 5.7 us)

commit v2 on v1

--- a/solution.py
+++ b/solution.py
@@ -54,9 +54,8 @@
     )(far_list.T)
 
 
-def pack_kernel(asked_ref, me_ref, keys_ref, values_ref, *refs, shifts, head):
+def pack_kernel(asked_ref, me_ref, keys_ref, values_ref, *refs, shifts):
     out_refs, sems = refs[:-1], refs[-1]
-    column = pl.ds(head * DH, DH)
     copies = []
     for shift in range(shifts):
         target = me_ref[0] + shift
@@ -69,7 +68,7 @@
                     dst = out_refs[0].at[target, slot]
                 else:
                     dst = out_refs[shift].at[slot]
-                copy = pltpu.make_async_copy(ref.at[rows, column], dst, sems.at[shift, slot])
+                copy = pltpu.make_async_copy(ref.at[rows, :], dst, sems.at[shift, slot])
                 copy.start()
                 copies.append(copy)
     for copy in copies:
@@ -78,19 +77,25 @@
 
 def pack(asked, me, key_rows, value_rows, head, split):
     shifts = asked.shape[0]
-    smem = pl.BlockSpec(memory_space=pltpu.SMEM)
+    tok_rows = key_rows.shape[0]
     hbm = pl.BlockSpec(memory_space=pltpu.HBM)
-    one = jax.ShapeDtypeStruct((CAP * 2, BT, DH), jnp.bfloat16)
+    column = pl.BlockSpec((tok_rows, DH), lambda i, *_: (0, head))
+    one = (CAP * 2, BT, DH)
     if split:
-        out_shape = (one,) * shifts
+        out_shape = (pltpu.HBM(one, key_rows.dtype),) * shifts
     else:
-        out_shape = (jax.ShapeDtypeStruct((shifts,) + one.shape, one.dtype),)
+        out_shape = (pltpu.HBM((shifts,) + one, key_rows.dtype),)
     return pl.pallas_call(
-        functools.partial(pack_kernel, shifts=shifts, head=head),
+        functools.partial(pack_kernel, shifts=shifts),
         out_shape=out_shape,
-        in_specs=[smem, smem, hbm, hbm],
-        out_specs=(hbm,) * len(out_shape),
-        scratch_shapes=[pltpu.SemaphoreType.DMA((shifts, CAP * 2))],
+        grid_spec=pltpu.PrefetchScalarGridSpec(
+            num_scalar_prefetch=2,
+            grid=(1,),
+            in_specs=[column, column],
+            out_specs=(hbm,) * len(out_shape),
+            scratch_shapes=[pltpu.SemaphoreType.DMA((shifts, CAP * 2))],
+        ),
+        compiler_params=pltpu.CompilerParams(vmem_limit_bytes=16 * MIB),
         name="pack",
     )(asked, me, key_rows, value_rows)
 
@@ -194,8 +199,9 @@
                 + weighted(second, values_ref[rows_of(distance), :])
             )
 
-    lane = lax.broadcasted_iota(jnp.int32, (BT, DH), 1)
-    stat_ref[...] = jnp.where(lane < DH // 2, max_ref[...], sum_ref[...])
+    total = sum_ref[...]
+    acc_ref[...] = acc_ref[...] / total
+    stat_ref[...] = jnp.broadcast_to(max_ref[...] + jnp.log2(total), (BT, DH))
 
 
 def band_attention(meta, slopes, queries, key_rows, value_rows, before, after, total_blocks):
@@ -237,7 +243,7 @@
 
 def far_kernel(
     meta_ref, slot_ref, block_ref, slopes_ref, query_ref, acc_ref, stat_ref, *refs, head, blk_dev,
-    sources,
+    sources, group,
 ):
     pieces = refs[:-4]
     out_ref, buffer_ref, gap_ref, sems = refs[-4:]
@@ -263,45 +269,48 @@
 
     slope = slopes_ref[head] * LOG2E
     me = meta_ref[blk_dev]
-    block = me * blk_dev + local
-    query = query_ref[...]
     gap = gap_ref[...]
-    scores = []
-    values = []
-    for f in range(FAR):
-        offset = ((block - block_ref[f, local]) * BT).astype(jnp.float32)
-        slot = slot_ref[f, local]
-        source = lax.div(slot, CAP)
-        if len(pieces) > 1:
-            source = me - source
-            source = jnp.where(source < 0, source + sources, source)
-        rank = lax.rem(slot, CAP)
-        scores.append(pair_scores(query, buffer_ref[source, rank * 2], offset, slope, gap))
-        values.append(buffer_ref[source, rank * 2 + 1])
-    old = stat_ref[:, 0:1]
-    old_sum = stat_ref[:, DH // 2 : DH // 2 + 1]
-    top = jnp.maximum(old, row_max(jnp.maximum(scores[0], scores[1])))
-    shrink = jnp.exp2(old - top)
-    first = jnp.exp2(scores[0] - top)
-    second = jnp.exp2(scores[1] - top)
-    total = old_sum * shrink + row_sum(first + second)
-    acc = acc_ref[...] * shrink + weighted(first, values[0]) + weighted(second, values[1])
-    out_ref[...] = (acc / total).astype(jnp.bfloat16)
+    ones = jnp.ones((BT, DH), jnp.bfloat16)
+    for part in range(group):
+        i = local * group + part
+        rows = pl.ds(part * BT, BT)
+        block = me * blk_dev + i
+        query = query_ref[rows, :]
+        scores = []
+        values = []
+        for f in range(FAR):
+            offset = ((block - block_ref[f, i]) * BT).astype(jnp.float32)
+            slot = slot_ref[f, i]
+            source = lax.div(slot, CAP)
+            if len(pieces) > 1:
+                source = me - source
+                source = jnp.where(source < 0, source + sources, source)
+            rank = lax.rem(slot, CAP)
+            scores.append(pair_scores(query, buffer_ref[source, rank * 2], offset, slope, gap))
+            values.append(jnp.concatenate([buffer_ref[source, rank * 2 + 1], ones], axis=1))
+        band = stat_ref[rows, :]
+        top = jnp.maximum(band[:, 0:1], row_max(jnp.maximum(scores[0], scores[1])))
+        weights = [jnp.exp2(score - top) for score in scores]
+        far = weighted(weights[0], values[0]) + weighted(weights[1], values[1])
+        share = jnp.exp2(band - top)
+        acc = acc_ref[rows, :] * share + far[:, :DH]
+        out_ref[rows, :] = (acc / (share + far[:, DH:])).astype(jnp.bfloat16)
 
 
 def far_attention(meta, slots, far_blocks, slopes, queries, acc, stat, pieces, head, sources):
     tok_rows = queries.shape[0]
     blk_dev = tok_rows // BT
-    tile = pl.BlockSpec((BT, DH), lambda i, *_: (i, head))
-    any_spec = pl.BlockSpec(memory_space=pltpu.HBM)
+    group = 2 if blk_dev % 2 == 0 else 1
+    tile = pl.BlockSpec((group * BT, DH), lambda i, *_: (i, head))
+    hbm = pl.BlockSpec(memory_space=pltpu.HBM)
     return pl.pallas_call(
-        functools.partial(far_kernel, head=head, blk_dev=blk_dev, sources=sources),
+        functools.partial(far_kernel, head=head, blk_dev=blk_dev, sources=sources, group=group),
         out_shape=jax.ShapeDtypeStruct((tok_rows, DH), jnp.bfloat16),
         grid_spec=pltpu.PrefetchScalarGridSpec(
             num_scalar_prefetch=4,
-            grid=(blk_dev,),
-            in_specs=[tile, tile, tile] + [any_spec] * len(pieces),
-            out_specs=pl.BlockSpec((BT, DH), lambda i, *_: (i, 0)),
+            grid=(blk_dev // group,),
+            in_specs=[tile, tile, tile] + [hbm] * len(pieces),
+            out_specs=pl.BlockSpec((group * BT, DH), lambda i, *_: (i, 0)),
             scratch_shapes=[
                 pltpu.VMEM((sources, CAP * 2, BT, DH), jnp.bfloat16),
                 pltpu.VMEM((BT, BT), jnp.float32),
@@ -316,6 +325,48 @@
         ),
         name="far",
     )(meta, slots, far_blocks, slopes, queries, acc, stat, *pieces)
+
+
+def place_kernel(part_ref, *refs, head):
+    out_ref, buffer_ref, in_sems, out_sems = refs[-4:]
+    peers = part_ref.shape[0]
+    width = out_ref.shape[1] // peers
+    loads = [
+        pltpu.make_async_copy(part_ref.at[g], buffer_ref.at[g], in_sems.at[g])
+        for g in range(peers)
+    ]
+    stores = [
+        pltpu.make_async_copy(
+            buffer_ref.at[g], out_ref.at[:, pl.ds(g * width + head * DH, DH)], out_sems.at[g]
+        )
+        for g in range(peers)
+    ]
+    for load in loads:
+        load.start()
+    for load, store in zip(loads, stores):
+        load.wait()
+        store.start()
+    for store in stores:
+        store.wait()
+
+
+def place(part, so_far, head, heads):
+    peers, rows, _ = part.shape
+    hbm = pl.BlockSpec(memory_space=pltpu.HBM)
+    args = (part,) if so_far is None else (part, so_far)
+    return pl.pallas_call(
+        functools.partial(place_kernel, head=head),
+        out_shape=jax.ShapeDtypeStruct((rows, peers * heads * DH), part.dtype),
+        in_specs=[hbm] * len(args),
+        out_specs=hbm,
+        scratch_shapes=[
+            pltpu.VMEM(part.shape, part.dtype),
+            pltpu.SemaphoreType.DMA((peers,)),
+            pltpu.SemaphoreType.DMA((peers,)),
+        ],
+        input_output_aliases={} if so_far is None else {1: 0},
+        name="place",
+    )(*args)
 
 
 def body(queries, key_rows, value_rows, band_reach, far_list, slopes):
@@ -336,10 +387,13 @@
     after = lax.ppermute(first, "seq", down)
 
     me = myself[None].astype(jnp.int32)
+    keys_hbm, values_hbm = (
+        pltpu.with_memory_space_constraint(x, pltpu.HBM) for x in (key_rows, value_rows)
+    )
     incoming = []
     for head in range(heads):
         split = head == heads - 1
-        outgoing = pack(asked, me, key_rows, value_rows, head, split)
+        outgoing = pack(asked, me, keys_hbm, values_hbm, head, split)
         if split:
             pieces = [outgoing[0]]
             for shift in range(1, sources):
@@ -358,19 +412,17 @@
     acc, stat, queries = (
         pltpu.with_memory_space_constraint(x, pltpu.HBM) for x in (acc, stat, queries)
     )
-    parts = []
+    mixed = None
     for head in range(heads):
         attended = far_attention(
             meta, slots, far_list.T, slopes, queries, acc, stat, incoming[head], head, sources
         )
-        parts.append(
-            lax.all_to_all(
-                attended.reshape(lax.axis_size("head"), -1, DH), "head",
-                split_axis=0, concat_axis=0, tiled=True,
-            )
+        part = lax.all_to_all(
+            attended.reshape(lax.axis_size("head"), -1, DH), "head",
+            split_axis=0, concat_axis=0, tiled=True,
         )
-    mixed = jnp.stack(parts, axis=1)
-    return mixed.transpose(2, 0, 1, 3).reshape(mixed.shape[2], -1)
+        mixed = place(part, mixed, head, heads)
+    return mixed
 
 
 def solution(mesh):

time: 535 us -> 336 us (0.63)
  Pallas kernels: 351 us -> 97.9 us
  waiting for transfers between devices: 59.3 us -> 136 us
  blocking collectives: 22 us -> 0 us
  local copies, waits for them, and re-layouts: 11.4 us -> 6.04 us
    pallas_call x2 -> x4, Pallas kernels: 259 us -> 13.9 us  [the longest x2 9.69 us: pack(): pl.pallas_call(functools.partial(pack_kernel, shifts=shifts), out_shape=o...]
    ppermute x1, waiting for transfers between devices: 0.01 us -> 88.7 us  [body(): after = lax.ppermute(first, 'seq', down)]
    ppermute x15, waiting for transfers between devices: 51.9 us -> 27.2 us  [body(): pieces.append(lax.ppermute(outgoing[shift], 'seq', ring))]
    all_to_all x1 -> x0, blocking collectives: 22 us -> none  [body(): lax.all_to_all(attended.reshape(lax.axis_size('head'), -1, DH), 'head', s...]
    all_to_all x1 -> x2, waiting for transfers between devices: 1.26 us -> 14.4 us  [body(): lax.all_to_all(attended.reshape(lax.axis_size('head'), -1, DH), 'head', s...]
    pallas_call x2, Pallas kernels: 29.4 us -> 21.7 us  [far_attention(): pl.pallas_call(functools.partial(far_kernel, head=head, blk_dev=blk_dev,...]
    all_to_all x1 -> x2, starting transfers between devices: 6.75 us -> 13.2 us  [body(): lax.all_to_all(attended.reshape(lax.axis_size('head'), -1, DH), 'head', s...]
  transfers between devices with their start and end apart: 20 -> 21, of which waited for: 10 -> 10; matrix products, arithmetic and copies ran while one was open for 0% -> 1% of each run, Pallas kernels for 41% -> 27%
where the time goes in v2:
time: 336 us
  waiting for transfers between devices  136 us (40%)
  Pallas kernels  97.9 us (29%)
  starting transfers between devices  94.4 us (28%)
  local copies, waits for them, and re-layouts  6.04 us (2%)
    ppermute x1, waiting for transfers between devices, body(): after = lax.ppermute(first, 'seq', down)  88.7 us
    pallas_call x1, Pallas kernels, band_attention(): pl.pallas_call(functools.partial(band_kernel, blk_dev=blk_dev, total_bloc...  60.6 us
    ppermute x15, starting transfers between devices, body(): pieces.append(lax.ppermute(outgoing[shift], 'seq', ring))  59.5 us
    ppermute x15, waiting for transfers between devices, body(): pieces.append(lax.ppermute(outgoing[shift], 'seq', ring))  27.2 us
    pallas_call x2, Pallas kernels, far_attention(): pl.pallas_call(functools.partial(far_kernel, head=head, blk_dev=blk_dev,...  21.7 us
    all_to_all x2, waiting for transfers between devices, body(): lax.all_to_all(attended.reshape(lax.axis_size('head'), -1, DH), 'head', s...  14.4 us
    all_to_all x2, starting transfers between devices, body(): lax.all_to_all(attended.reshape(lax.axis_size('head'), -1, DH), 'head', s...  13.2 us
    pallas_call x2, Pallas kernels, pack(): pl.pallas_call(functools.partial(pack_kernel, shifts=shifts), out_shape=o...  9.69 us
  transfers between devices with their start and end apart: 21, of which 10 were waited for; matrix products, arithmetic and copies ran while one was open for 1% of the time, Pallas kernels for 27%

profile of v2, /device:TPU:64, one launch (start us, length us, event | category | flops | bytes accessed | tf_op | source)
XLA Modules:
  0.0 335.5 jit_solution(4004407011761446838)
XLA Ops:
  1.8 9.2 %all-to-all-start = ((s32[16,1,2]{2,1,0:T(1,128)}), s32[16,1,2]{2,1,0:T(1,128)S(1)}, u32[]{:S(2)}, u32[]{:S(2)}) async-start(s32[16,1,2]{2,1,0:T(1,128)} %bitcast.21), calls=%async_computation | async-start | bytes 16384 | tf_op jit(solution)/shard_map/all_to_all | solution.py:383
  10.9 6.2 %all-to-all-done = s32[16,1,2]{2,1,0:T(1,128)S(1)} async-done(((s32[16,1,2]{2,1,0:T(1,128)}), s32[16,1,2]{2,1,0:T(1,128)S(1)}, u32[]{:S(2)}, u32[]{:S(2)}) %all-to-all-start) | async-done | bytes 160 | tf_op jit(solution)/shard_map/all_to_all | solution.py:383
  17.1 4.7 %pack.3 = bf16[16,4,256,128]{3,2,1,0:T(8,128)(2,1)} custom-call(s32[16,2]{1,0:T(8,128)S(1)} %bitcast.16, s32[1]{0:T(128)} %bitcast.me_ref, bf16[3584,256]{1,0:T(8,128)(2,1)} %keys_ref.3, bf16[3584,256]{1,0:T(8,128)(2,1)} %values_ref.3), custom_call_target="tpu_custom_call" | custom-call | tf_op jit(solution)/shard_map/pack/pallas_call | solution.py:88
  21.9 6.6 %all-to-all-start.2 = ((bf16[16,4,256,128]{3,2,1,0:T(8,128)(2,1)}), bf16[16,4,256,128]{3,2,1,0:T(8,128)(2,1)}, u32[]{:S(2)}, u32[]{:S(2)}) async-start(bf16[16,4,256,128]{3,2,1,0:T(8,128)(2,1)} %pack.3), calls=%async_computation.2 | async-start | bytes 8388608 | tf_op jit(solution)/shard_map/all_to_all | solution.py:405
  30.0 2.6 collective-permute-start.1
  32.7 3.4 %collective-permute-start = (bf16[2,768,256]{2,1,0:T(8,128)(2,1)S(1)}, bf16[2,768,256]{2,1,0:T(8,128)(2,1)S(1)}, u32[]{:S(2)}, u32[]{:S(2)}) collective-permute-start(bf16[2,768,256]{2,1,0:T(8,128)(2,1)S(1)} %pad_maximum_fusion), channel_id=1, source_target_pairs={{0,16},{16,32},{32,48},{48,64},{64,80},{80,96},{96,112},{112,128},... | collective-permute-start | bytes 2359304 | tf_op jit(solution)/shard_map/ppermute | solution.py:386
  36.2 5.0 %pack.2 = (bf16[4,256,128]{2,1,0:T(8,128)(2,1)}, bf16[4,256,128]{2,1,0:T(8,128)(2,1)}, bf16[4,256,128]{2,1,0:T(8,128)(2,1)}, bf16[4,256,128]{2,1,0:T(8,128)(2,1)...) custom-call(s32[16,2]{1,0:T(8,128)S(1)} %bitcast.17, ...), custom_call_target="tpu_custom_call" | custom-call | tf_op jit(solution)/shard_map/pack/pallas_call | solution.py:88
  41.2 3.7 %collective-permute-start.10 = (bf16[4,256,128]{2,1,0:T(8,128)(2,1)}, bf16[4,256,128]{2,1,0:T(8,128)(2,1)S(1)}, u32[]{:S(2)}, u32[]{:S(2)}) collective-permute-start(bf16[4,256,128]{2,1,0:T(8,128)(2,1)} %get-tuple-element.38), channel_id=1, source_target_pairs={{0,144},{16,160},{32,176},{48,192},{64,208},{80,224},{96,240},{112... | collective-permute-start | bytes 786440 | tf_op jit(solution)/shard_map/ppermute | solution.py:401
  46.3 2.2 collective-permute-start.12
  48.5 88.7 %collective-permute-done.1.after_hbm = bf16[2,768,256]{2,1,0:T(8,128)(2,1)S(1)} collective-permute-done((bf16[2,768,256]{2,1,0:T(8,128)(2,1)S(1)}, bf16[2,768,256]{2,1,0:T(8,128)(2,1)S(1)}, u32[]{:S(2)}, u32[]{:S(2)}) %collective-permute-start.1) | collective-permute-done | bytes 786464 | tf_op jit(solution)/shard_map/ppermute | solution.py:387
  137.2 5.7 %collective-permute-start.13 = (bf16[4,256,128]{2,1,0:T(8,128)(2,1)}, bf16[4,256,128]{2,1,0:T(8,128)(2,1)S(1)}, u32[]{:S(2)}, u32[]{:S(2)}) collective-permute-start(bf16[4,256,128]{2,1,0:T(8,128)(2,1)} %get-tuple-element.41), channel_id=1, source_target_pairs={{0,192},{16,208},{32,224},{48,240},{64,0},{80,16},{96,32},{112,48}... | collective-permute-start | bytes 786440 | tf_op jit(solution)/shard_map/ppermute | solution.py:401
  143.0 2.5 collective-permute-start.14
  145.4 60.6 %band.1 = (f32[3584,256]{1,0:T(8,128)S(1)}, f32[3584,256]{1,0:T(8,128)S(1)}) custom-call(s32[15]{0:T(128)S(1)} %pad_add_fusion.meta_ref, f32[2]{0:T(128)S(1)} %copy-done.8, bf16[3584,256]{1,0:T(8,128)(2,1)S(1)} %copy-done.4, bf16[3584,256]{1,0:T(8,128)(2,1)S(1)} %copy-done.2, bf16[3584,256]{1,0:T(8,128)(2,1)S(1)} %copy-done.3, ...), custom_call_target="tpu_custom_call" | custom-call | flops 6576668672 | bytes 31457280 | tf_op jit(solution)/shard_map/band/pallas_call | solution.py:214
  209.6 11.8 %far.3 = bf16[3584,128]{1,0:T(8,128)(2,1)} custom-call(s32[15]{0:T(128)S(1)} %pad_add_fusion.meta_ref, s32[2,14]{1,0:T(2,128)S(1)} %copy-done.7, s32[2,14]{1,0:T(2,128)S(1)} %bitcast.19, f32[2]{0:T(128)S(1)} %copy-done.8, bf16[3584,256]{1,0:T(8,128)(2,1)} %query_ref.5, f32[3584,256]{1,0:T(8,128)} %copy-done, f32[3584,256]{1,0:T(8,128)} %copy-done.1, ...), custom_call_target="tpu_custom_call" | custom-call | flops 939524096 | bytes 14680064 | tf_op jit(solution)/shard_map/far/pallas_call | solution.py:306
  221.4 6.9 %all-to-all-start.3 = ((bf16[16,224,128]{2,1,0:T(8,128)(2,1)}), bf16[16,224,128]{2,1,0:T(8,128)(2,1)S(1)}, u32[]{:S(2)}, u32[]{:S(2)}) async-start(bf16[16,224,128]{2,1,0:T(8,128)(2,1)} %bitcast.9), calls=%async_computation.3 | async-start | bytes 1835008 | tf_op jit(solution)/shard_map/all_to_all | solution.py:420
  228.6 2.0 collective-permute-start.2
  230.6 4.0 %collective-permute-start.3 = (bf16[4,256,128]{2,1,0:T(8,128)(2,1)}, bf16[4,256,128]{2,1,0:T(8,128)(2,1)S(1)}, u32[]{:S(2)}, u32[]{:S(2)}) collective-permute-start(bf16[4,256,128]{2,1,0:T(8,128)(2,1)} %get-tuple-element.31), channel_id=1, source_target_pairs={{0,32},{16,48},{32,64},{48,80},{64,96},{80,112},{96,128},{112,144}... | collective-permute-start | bytes 786440 | tf_op jit(solution)/shard_map/ppermute | solution.py:401
  234.6 5.6 %collective-permute-done.15.refs_14_ = bf16[4,256,128]{2,1,0:T(8,128)(2,1)S(1)} collective-permute-done((bf16[4,256,128]{2,1,0:T(8,128)(2,1)}, bf16[4,256,128]{2,1,0:T(8,128)(2,1)S(1)}, u32[]{:S(2)}, u32[]{:S(2)}) %collective-permute-start.15) | collective-permute-done | bytes 262176 | tf_op jit(solution)/shard_map/ppermute | solution.py:401
  241.1 1.9 collective-permute-done.16.refs_15_
  243.0 4.1 %collective-permute-start.6 = (bf16[4,256,128]{2,1,0:T(8,128)(2,1)S(1)}, bf16[4,256,128]{2,1,0:T(8,128)(2,1)S(1)}, u32[]{:S(2)}, u32[]{:S(2)}) collective-permute-start(bf16[4,256,128]{2,1,0:T(8,128)(2,1)S(1)} %copy-done.14), channel_id=1, source_target_pairs={{0,80},{16,96},{32,112},{48,128},{64,144},{80,160},{96,176},{112,1... | collective-permute-start | bytes 786440 | tf_op jit(solution)/shard_map/ppermute | solution.py:401
  248.0 11.7 %collective-permute-start.7 = (bf16[4,256,128]{2,1,0:T(8,128)(2,1)S(1)}, bf16[4,256,128]{2,1,0:T(8,128)(2,1)S(1)}, u32[]{:S(2)}, u32[]{:S(2)}) collective-permute-start(bf16[4,256,128]{2,1,0:T(8,128)(2,1)S(1)} %copy-done.13), channel_id=1, source_target_pairs={{0,96},{16,112},{32,128},{48,144},{64,160},{80,176},{96,192},{112,... | collective-permute-start | bytes 786440 | tf_op jit(solution)/shard_map/ppermute | solution.py:401
  259.7 6.8 %collective-permute-start.8 = (bf16[4,256,128]{2,1,0:T(8,128)(2,1)S(1)}, bf16[4,256,128]{2,1,0:T(8,128)(2,1)S(1)}, u32[]{:S(2)}, u32[]{:S(2)}) collective-permute-start(bf16[4,256,128]{2,1,0:T(8,128)(2,1)S(1)} %copy-done.12), channel_id=1, source_target_pairs={{0,112},{16,128},{32,144},{48,160},{64,176},{80,192},{96,208},{112... | collective-permute-start | bytes 786440 | tf_op jit(solution)/shard_map/ppermute | solution.py:401
  266.5 4.7 %collective-permute-done.4.refs_3_ = bf16[4,256,128]{2,1,0:T(8,128)(2,1)S(1)} collective-permute-done((bf16[4,256,128]{2,1,0:T(8,128)(2,1)}, bf16[4,256,128]{2,1,0:T(8,128)(2,1)S(1)}, u32[]{:S(2)}, u32[]{:S(2)}) %collective-permute-start.4) | collective-permute-done | bytes 262176 | tf_op jit(solution)/shard_map/ppermute | solution.py:401
  271.3 14.2 %collective-permute-start.9 = (bf16[4,256,128]{2,1,0:T(8,128)(2,1)S(1)}, bf16[4,256,128]{2,1,0:T(8,128)(2,1)S(1)}, u32[]{:S(2)}, u32[]{:S(2)}) collective-permute-start(bf16[4,256,128]{2,1,0:T(8,128)(2,1)S(1)} %copy-done.11), channel_id=1, source_target_pairs={{0,128},{16,144},{32,160},{48,176},{64,192},{80,208},{96,224},{112... | collective-permute-start | bytes 786440 | tf_op jit(solution)/shard_map/ppermute | solution.py:401
  285.5 6.8 %collective-permute-done.7.refs_6_ = bf16[4,256,128]{2,1,0:T(8,128)(2,1)S(1)} collective-permute-done((bf16[4,256,128]{2,1,0:T(8,128)(2,1)S(1)}, bf16[4,256,128]{2,1,0:T(8,128)(2,1)S(1)}, u32[]{:S(2)}, u32[]{:S(2)}) %collective-permute-start.7) | collective-permute-done | bytes 262176 | tf_op jit(solution)/shard_map/ppermute | solution.py:401
  292.3 1.8 collective-permute-done.8.refs_7_
  294.1 5.4 %collective-permute-done.9.refs_8_ = bf16[4,256,128]{2,1,0:T(8,128)(2,1)S(1)} collective-permute-done((bf16[4,256,128]{2,1,0:T(8,128)(2,1)S(1)}, bf16[4,256,128]{2,1,0:T(8,128)(2,1)S(1)}, u32[]{:S(2)}, u32[]{:S(2)}) %collective-permute-start.9) | collective-permute-done | bytes 262176 | tf_op jit(solution)/shard_map/ppermute | solution.py:401
  299.5 9.9 %far.2 = bf16[3584,128]{1,0:T(8,128)(2,1)} custom-call(s32[15]{0:T(128)S(1)} %pad_add_fusion.meta_ref, s32[2,14]{1,0:T(2,128)S(1)} %copy-done.7, s32[2,14]{1,0:T(2,128)S(1)} %bitcast.20, f32[2]{0:T(128)S(1)} %copy-done.8, bf16[3584,256]{1,0:T(8,128)(2,1)} %query_ref.5, f32[3584,256]{1,0:T(8,128)} %copy-done, f32[3584,256]{1,0:T(8,128)} %copy-done.1, ...), custom_call_target="tpu_custom_call" | custom-call | flops 939524096 | bytes 14680064 | tf_op jit(solution)/shard_map/far/pallas_call | solution.py:306
  309.4 6.3 %all-to-all-start.1 = ((bf16[16,224,128]{2,1,0:T(8,128)(2,1)}), bf16[16,224,128]{2,1,0:T(8,128)(2,1)S(1)}, u32[]{:S(2)}, u32[]{:S(2)}) async-start(bf16[16,224,128]{2,1,0:T(8,128)(2,1)} %bitcast.8), calls=%async_computation.1 | async-start | bytes 1835008 | tf_op jit(solution)/shard_map/all_to_all | solution.py:420
  315.8 2.1 place.2.refs_0_
  317.9 14.4 %all-to-all-done.1.part_ref = bf16[16,224,128]{2,1,0:T(8,128)(2,1)S(1)} async-done(((bf16[16,224,128]{2,1,0:T(8,128)(2,1)}), bf16[16,224,128]{2,1,0:T(8,128)(2,1)S(1)}, u32[]{:S(2)}, u32[]{:S(2)}) %all-to-all-start.1) | async-done | bytes 917536 | tf_op jit(solution)/shard_map/all_to_all | solution.py:420
  333.2 2.1 place.3
  (54 shorter events, 11.5 us)
Async XLA Ops:
  1.8 15.4 %all-to-all-start = ((s32[16,1,2]{2,1,0:T(1,128)}), s32[16,1,2]{2,1,0:T(1,128)S(1)}, u32[]{:S(2)}, u32[]{:S(2)}) async-start(s32[16,1,2]{2,1,0:T(1,128)} %bitcast.21), calls=%async_computation | async-start | bytes 16384 | tf_op jit(solution)/shard_map/all_to_all | solution.py:383
  21.9 187.7 %all-to-all-start.2 = ((bf16[16,4,256,128]{3,2,1,0:T(8,128)(2,1)}), bf16[16,4,256,128]{3,2,1,0:T(8,128)(2,1)}, u32[]{:S(2)}, u32[]{:S(2)}) async-start(bf16[16,4,256,128]{3,2,1,0:T(8,128)(2,1)} %pack.3), calls=%async_computation.2 | async-start | bytes 8388608 | tf_op jit(solution)/shard_map/all_to_all | solution.py:405
  29.9 115.5 %copy-start.4 = (bf16[3584,256]{1,0:T(8,128)(2,1)S(1)}, bf16[3584,256]{1,0:T(8,128)(2,1)}, u32[]{:S(2)}) copy-start(bf16[3584,256]{1,0:T(8,128)(2,1)} %query_ref.5) | copy-start | bytes 5505028
  30.0 107.2 %collective-permute-start.1 = (bf16[2,768,256]{2,1,0:T(8,128)(2,1)S(1)}, bf16[2,768,256]{2,1,0:T(8,128)(2,1)S(1)}, u32[]{:S(2)}, u32[]{:S(2)}) collective-permute-start(bf16[2,768,256]{2,1,0:T(8,128)(2,1)S(1)} %pad_maximum_fusion.1), channel_id=1, source_target_pairs={{16,0},{32,16},{48,32},{64,48},{80,64},{96,80},{112,96},{128,112},... | collective-permute-start | bytes 2359304 | tf_op jit(solution)/shard_map/ppermute | solution.py:387
  32.7 110.2 %collective-permute-start = (bf16[2,768,256]{2,1,0:T(8,128)(2,1)S(1)}, bf16[2,768,256]{2,1,0:T(8,128)(2,1)S(1)}, u32[]{:S(2)}, u32[]{:S(2)}) collective-permute-start(bf16[2,768,256]{2,1,0:T(8,128)(2,1)S(1)} %pad_maximum_fusion), channel_id=1, source_target_pairs={{0,16},{16,32},{32,48},{48,64},{64,80},{80,96},{96,112},{112,128},... | collective-permute-start | bytes 2359304 | tf_op jit(solution)/shard_map/ppermute | solution.py:386
  36.2 109.2 %copy-start.2 = (bf16[3584,256]{1,0:T(8,128)(2,1)S(1)}, bf16[3584,256]{1,0:T(8,128)(2,1)}, u32[]{:S(2)}) copy-start(bf16[3584,256]{1,0:T(8,128)(2,1)} %keys_ref.3) | copy-start | bytes 5505028
  36.2 109.2 %copy-start.3 = (bf16[3584,256]{1,0:T(8,128)(2,1)S(1)}, bf16[3584,256]{1,0:T(8,128)(2,1)}, u32[]{:S(2)}) copy-start(bf16[3584,256]{1,0:T(8,128)(2,1)} %values_ref.3) | copy-start | bytes 5505028
  36.2 109.2 %copy-start.8 = (f32[2]{0:T(128)S(1)}, f32[2]{0:T(128)}, u32[]{:S(2)}) copy-start(f32[2]{0:T(128)} %slopes_ref.5) | copy-start | bytes 28
  41.2 187.2 %collective-permute-start.10 = (bf16[4,256,128]{2,1,0:T(8,128)(2,1)}, bf16[4,256,128]{2,1,0:T(8,128)(2,1)S(1)}, u32[]{:S(2)}, u32[]{:S(2)}) collective-permute-start(bf16[4,256,128]{2,1,0:T(8,128)(2,1)} %get-tuple-element.38), channel_id=1, source_target_pairs={{0,144},{16,160},{32,176},{48,192},{64,208},{80,224},{96,240},{112... | collective-permute-start | bytes 786440 | tf_op jit(solution)/shard_map/ppermute | solution.py:401
  44.9 183.6 %collective-permute-start.11 = (bf16[4,256,128]{2,1,0:T(8,128)(2,1)}, bf16[4,256,128]{2,1,0:T(8,128)(2,1)S(1)}, u32[]{:S(2)}, u32[]{:S(2)}) collective-permute-start(bf16[4,256,128]{2,1,0:T(8,128)(2,1)} %get-tuple-element.39), channel_id=1, source_target_pairs={{0,160},{16,176},{32,192},{48,208},{64,224},{80,240},{96,0},{112,1... | collective-permute-start | bytes 786440 | tf_op jit(solution)/shard_map/ppermute | solution.py:401
  46.3 182.2 %collective-permute-start.12 = (bf16[4,256,128]{2,1,0:T(8,128)(2,1)}, bf16[4,256,128]{2,1,0:T(8,128)(2,1)S(1)}, u32[]{:S(2)}, u32[]{:S(2)}) collective-permute-start(bf16[4,256,128]{2,1,0:T(8,128)(2,1)} %get-tuple-element.40), channel_id=1, source_target_pairs={{0,176},{16,192},{32,208},{48,224},{64,240},{80,0},{96,16},{112,32... | collective-permute-start | bytes 786440 | tf_op jit(solution)/shard_map/ppermute | solution.py:401
  137.2 93.3 %collective-permute-start.13 = (bf16[4,256,128]{2,1,0:T(8,128)(2,1)}, bf16[4,256,128]{2,1,0:T(8,128)(2,1)S(1)}, u32[]{:S(2)}, u32[]{:S(2)}) collective-permute-start(bf16[4,256,128]{2,1,0:T(8,128)(2,1)} %get-tuple-element.41), channel_id=1, source_target_pairs={{0,192},{16,208},{32,224},{48,240},{64,0},{80,16},{96,32},{112,48}... | collective-permute-start | bytes 786440 | tf_op jit(solution)/shard_map/ppermute | solution.py:401
  143.0 66.7 %copy-start.6 = (s32[14,2]{0,1:T(2,128)S(1)}, s32[14,2]{0,1:T(2,128)}, u32[]{:S(2)}) copy-start(s32[14,2]{0,1:T(2,128)} %param.10) | copy-start | bytes 340
  143.0 66.7 %copy-start.7 = (s32[2,14]{1,0:T(2,128)S(1)}, s32[2,14]{1,0:T(2,128)}, u32[]{:S(2)}) copy-start(s32[2,14]{1,0:T(2,128)} %get-tuple-element.25.slot_ref) | copy-start | bytes 340
  143.0 91.6 %collective-permute-start.14 = (bf16[4,256,128]{2,1,0:T(8,128)(2,1)}, bf16[4,256,128]{2,1,0:T(8,128)(2,1)S(1)}, u32[]{:S(2)}, u32[]{:S(2)}) collective-permute-start(bf16[4,256,128]{2,1,0:T(8,128)(2,1)} %get-tuple-element.42), channel_id=1, source_target_pairs={{0,208},{16,224},{32,240},{48,0},{64,16},{80,32},{96,48},{112,64},... | collective-permute-start | bytes 786440 | tf_op jit(solution)/shard_map/ppermute | solution.py:401
  221.4 21.6 %copy-start.14 = (bf16[4,256,128]{2,1,0:T(8,128)(2,1)S(1)}, bf16[4,256,128]{2,1,0:T(8,128)(2,1)}, u32[]{:S(2)}) copy-start(bf16[4,256,128]{2,1,0:T(8,128)(2,1)} %get-tuple-element.34) | copy-start | bytes 786436
  221.4 26.6 %copy-start.13 = (bf16[4,256,128]{2,1,0:T(8,128)(2,1)S(1)}, bf16[4,256,128]{2,1,0:T(8,128)(2,1)}, u32[]{:S(2)}) copy-start(bf16[4,256,128]{2,1,0:T(8,128)(2,1)} %get-tuple-element.35) | copy-start | bytes 786436
  221.4 38.3 %copy-start.12 = (bf16[4,256,128]{2,1,0:T(8,128)(2,1)S(1)}, bf16[4,256,128]{2,1,0:T(8,128)(2,1)}, u32[]{:S(2)}) copy-start(bf16[4,256,128]{2,1,0:T(8,128)(2,1)} %get-tuple-element.36) | copy-start | bytes 786436
  221.4 49.8 %copy-start.11 = (bf16[4,256,128]{2,1,0:T(8,128)(2,1)S(1)}, bf16[4,256,128]{2,1,0:T(8,128)(2,1)}, u32[]{:S(2)}) copy-start(bf16[4,256,128]{2,1,0:T(8,128)(2,1)} %get-tuple-element.37) | copy-start | bytes 786436
  221.4 78.0 %copy-start.5 = (bf16[4,256,128]{2,1,0:T(8,128)(2,1)S(1)}, bf16[4,256,128]{2,1,0:T(8,128)(2,1)}, u32[]{:S(2)}) copy-start(bf16[4,256,128]{2,1,0:T(8,128)(2,1)} %get-tuple-element.29.refs_0_) | copy-start | bytes 786436
  221.4 88.0 %all-to-all-start.3 = ((bf16[16,224,128]{2,1,0:T(8,128)(2,1)}), bf16[16,224,128]{2,1,0:T(8,128)(2,1)S(1)}, u32[]{:S(2)}, u32[]{:S(2)}) async-start(bf16[16,224,128]{2,1,0:T(8,128)(2,1)} %bitcast.9), calls=%async_computation.3 | async-start | bytes 1835008 | tf_op jit(solution)/shard_map/all_to_all | solution.py:420
  228.3 11.9 %collective-permute-start.15 = (bf16[4,256,128]{2,1,0:T(8,128)(2,1)}, bf16[4,256,128]{2,1,0:T(8,128)(2,1)S(1)}, u32[]{:S(2)}, u32[]{:S(2)}) collective-permute-start(bf16[4,256,128]{2,1,0:T(8,128)(2,1)} %get-tuple-element.43), channel_id=1, source_target_pairs={{0,224},{16,240},{32,0},{48,16},{64,32},{80,48},{96,64},{112,80},{... | collective-permute-start | bytes 786440 | tf_op jit(solution)/shard_map/ppermute | solution.py:401
  228.4 14.5 %collective-permute-start.16 = (bf16[4,256,128]{2,1,0:T(8,128)(2,1)}, bf16[4,256,128]{2,1,0:T(8,128)(2,1)S(1)}, u32[]{:S(2)}, u32[]{:S(2)}) collective-permute-start(bf16[4,256,128]{2,1,0:T(8,128)(2,1)} %get-tuple-element.44), channel_id=1, source_target_pairs={{0,240},{16,0},{32,16},{48,32},{64,48},{80,64},{96,80},{112,96},{1... | collective-permute-start | bytes 786440 | tf_op jit(solution)/shard_map/ppermute | solution.py:401
  228.6 19.5 %collective-permute-start.2 = (bf16[4,256,128]{2,1,0:T(8,128)(2,1)}, bf16[4,256,128]{2,1,0:T(8,128)(2,1)S(1)}, u32[]{:S(2)}, u32[]{:S(2)}) collective-permute-start(bf16[4,256,128]{2,1,0:T(8,128)(2,1)} %get-tuple-element.30), channel_id=1, source_target_pairs={{0,16},{16,32},{32,48},{48,64},{64,80},{80,96},{96,112},{112,128},... | collective-permute-start | bytes 786440 | tf_op jit(solution)/shard_map/ppermute | solution.py:401
  230.6 29.1 %collective-permute-start.3 = (bf16[4,256,128]{2,1,0:T(8,128)(2,1)}, bf16[4,256,128]{2,1,0:T(8,128)(2,1)S(1)}, u32[]{:S(2)}, u32[]{:S(2)}) collective-permute-start(bf16[4,256,128]{2,1,0:T(8,128)(2,1)} %get-tuple-element.31), channel_id=1, source_target_pairs={{0,32},{16,48},{32,64},{48,80},{64,96},{80,112},{96,128},{112,144}... | collective-permute-start | bytes 786440 | tf_op jit(solution)/shard_map/ppermute | solution.py:401
  234.6 36.7 %collective-permute-start.4 = (bf16[4,256,128]{2,1,0:T(8,128)(2,1)}, bf16[4,256,128]{2,1,0:T(8,128)(2,1)S(1)}, u32[]{:S(2)}, u32[]{:S(2)}) collective-permute-start(bf16[4,256,128]{2,1,0:T(8,128)(2,1)} %get-tuple-element.32), channel_id=1, source_target_pairs={{0,48},{16,64},{32,80},{48,96},{64,112},{80,128},{96,144},{112,160... | collective-permute-start | bytes 786440 | tf_op jit(solution)/shard_map/ppermute | solution.py:401
  240.2 45.3 %collective-permute-start.5 = (bf16[4,256,128]{2,1,0:T(8,128)(2,1)}, bf16[4,256,128]{2,1,0:T(8,128)(2,1)S(1)}, u32[]{:S(2)}, u32[]{:S(2)}) collective-permute-start(bf16[4,256,128]{2,1,0:T(8,128)(2,1)} %get-tuple-element.33), channel_id=1, source_target_pairs={{0,64},{16,80},{32,96},{48,112},{64,128},{80,144},{96,160},{112,17... | collective-permute-start | bytes 786440 | tf_op jit(solution)/shard_map/ppermute | solution.py:401
  243.0 42.5 %collective-permute-start.6 = (bf16[4,256,128]{2,1,0:T(8,128)(2,1)S(1)}, bf16[4,256,128]{2,1,0:T(8,128)(2,1)S(1)}, u32[]{:S(2)}, u32[]{:S(2)}) collective-permute-start(bf16[4,256,128]{2,1,0:T(8,128)(2,1)S(1)} %copy-done.14), channel_id=1, source_target_pairs={{0,80},{16,96},{32,112},{48,128},{64,144},{80,160},{96,176},{112,1... | collective-permute-start | bytes 786440 | tf_op jit(solution)/shard_map/ppermute | solution.py:401
  248.0 44.3 %collective-permute-start.7 = (bf16[4,256,128]{2,1,0:T(8,128)(2,1)S(1)}, bf16[4,256,128]{2,1,0:T(8,128)(2,1)S(1)}, u32[]{:S(2)}, u32[]{:S(2)}) collective-permute-start(bf16[4,256,128]{2,1,0:T(8,128)(2,1)S(1)} %copy-done.13), channel_id=1, source_target_pairs={{0,96},{16,112},{32,128},{48,144},{64,160},{80,176},{96,192},{112,... | collective-permute-start | bytes 786440 | tf_op jit(solution)/shard_map/ppermute | solution.py:401
  259.7 34.4 %collective-permute-start.8 = (bf16[4,256,128]{2,1,0:T(8,128)(2,1)S(1)}, bf16[4,256,128]{2,1,0:T(8,128)(2,1)S(1)}, u32[]{:S(2)}, u32[]{:S(2)}) collective-permute-start(bf16[4,256,128]{2,1,0:T(8,128)(2,1)S(1)} %copy-done.12), channel_id=1, source_target_pairs={{0,112},{16,128},{32,144},{48,160},{64,176},{80,192},{96,208},{112... | collective-permute-start | bytes 786440 | tf_op jit(solution)/shard_map/ppermute | solution.py:401
  271.3 28.2 %collective-permute-start.9 = (bf16[4,256,128]{2,1,0:T(8,128)(2,1)S(1)}, bf16[4,256,128]{2,1,0:T(8,128)(2,1)S(1)}, u32[]{:S(2)}, u32[]{:S(2)}) collective-permute-start(bf16[4,256,128]{2,1,0:T(8,128)(2,1)S(1)} %copy-done.11), channel_id=1, source_target_pairs={{0,128},{16,144},{32,160},{48,176},{64,192},{80,208},{96,224},{112... | collective-permute-start | bytes 786440 | tf_op jit(solution)/shard_map/ppermute | solution.py:401
  309.4 22.9 %all-to-all-start.1 = ((bf16[16,224,128]{2,1,0:T(8,128)(2,1)}), bf16[16,224,128]{2,1,0:T(8,128)(2,1)S(1)}, u32[]{:S(2)}, u32[]{:S(2)}) async-start(bf16[16,224,128]{2,1,0:T(8,128)(2,1)} %bitcast.8), calls=%async_computation.1 | async-start | bytes 1835008 | tf_op jit(solution)/shard_map/all_to_all | solution.py:420
  (5 other events, 17.1 us)

commit v3 on v2

--- a/solution.py
+++ b/solution.py
@@ -57,17 +57,17 @@
 def pack_kernel(asked_ref, me_ref, keys_ref, values_ref, *refs, shifts):
     out_refs, sems = refs[:-1], refs[-1]
     copies = []
-    for shift in range(shifts):
-        target = me_ref[0] + shift
-        target = jnp.where(target >= shifts, target - shifts, target)
-        for r in range(CAP):
-            rows = pl.ds(pl.multiple_of(asked_ref[target, r] * BT, BT), BT)
-            for which, ref in enumerate((keys_ref, values_ref)):
+    for which, ref in enumerate((keys_ref, values_ref)):
+        for shift in range(shifts):
+            target = me_ref[0] + shift
+            target = jnp.where(target >= shifts, target - shifts, target)
+            for r in range(CAP):
+                rows = pl.ds(pl.multiple_of(asked_ref[target, r] * BT, BT), BT)
                 slot = r * 2 + which
                 if len(out_refs) == 1:
                     dst = out_refs[0].at[target, slot]
                 else:
-                    dst = out_refs[shift].at[slot]
+                    dst = out_refs[which * shifts + shift].at[r]
                 copy = pltpu.make_async_copy(ref.at[rows, :], dst, sems.at[shift, slot])
                 copy.start()
                 copies.append(copy)
@@ -80,11 +80,10 @@
     tok_rows = key_rows.shape[0]
     hbm = pl.BlockSpec(memory_space=pltpu.HBM)
     column = pl.BlockSpec((tok_rows, DH), lambda i, *_: (0, head))
-    one = (CAP * 2, BT, DH)
     if split:
-        out_shape = (pltpu.HBM(one, key_rows.dtype),) * shifts
+        out_shape = (pltpu.HBM((CAP, BT, DH), key_rows.dtype),) * (2 * shifts)
     else:
-        out_shape = (pltpu.HBM((shifts,) + one, key_rows.dtype),)
+        out_shape = (pltpu.HBM((shifts, CAP * 2, BT, DH), key_rows.dtype),)
     return pl.pallas_call(
         functools.partial(pack_kernel, shifts=shifts),
         out_shape=out_shape,
@@ -241,28 +240,41 @@
     )(meta, slopes, queries, key_rows, value_rows, before, after)
 
 
+def gather_pieces(pieces, buffer_ref, sems, sources):
+    if len(pieces) == 1:
+        pieces = [pieces[0].at[s] for s in range(sources)]
+    copies = [
+        pltpu.make_async_copy(piece, buffer_ref.at[s], sems.at[s])
+        for s, piece in enumerate(pieces)
+    ]
+    for copy in copies:
+        copy.start()
+    return copies
+
+
+def place_of(slot, me, sources, split):
+    source = lax.div(slot, CAP)
+    if split:
+        source = me - source
+        source = jnp.where(source < 0, source + sources, source)
+    return source, lax.rem(slot, CAP)
+
+
 def far_kernel(
     meta_ref, slot_ref, block_ref, slopes_ref, query_ref, acc_ref, stat_ref, *refs, head, blk_dev,
-    sources, group,
+    sources, group, split,
 ):
-    pieces = refs[:-4]
-    out_ref, buffer_ref, gap_ref, sems = refs[-4:]
+    if split:
+        pieces = refs[:-5]
+        weights_ref, out_ref, buffer_ref, gap_ref, sems = refs[-5:]
+    else:
+        pieces = refs[:-4]
+        out_ref, buffer_ref, gap_ref, sems = refs[-4:]
     local = pl.program_id(0)
 
     @pl.when(local == 0)
     def _():
-        if len(pieces) == 1:
-            copies = [
-                pltpu.make_async_copy(pieces[0].at[s], buffer_ref.at[s], sems.at[s])
-                for s in range(sources)
-            ]
-        else:
-            copies = [
-                pltpu.make_async_copy(piece, buffer_ref.at[s], sems.at[s])
-                for s, piece in enumerate(pieces)
-            ]
-        for copy in copies:
-            copy.start()
+        copies = gather_pieces(pieces, buffer_ref, sems, sources)
         gap_ref[...] = distances()
         for copy in copies:
             copy.wait()
@@ -280,44 +292,55 @@
         values = []
         for f in range(FAR):
             offset = ((block - block_ref[f, i]) * BT).astype(jnp.float32)
-            slot = slot_ref[f, i]
-            source = lax.div(slot, CAP)
-            if len(pieces) > 1:
-                source = me - source
-                source = jnp.where(source < 0, source + sources, source)
-            rank = lax.rem(slot, CAP)
-            scores.append(pair_scores(query, buffer_ref[source, rank * 2], offset, slope, gap))
-            values.append(jnp.concatenate([buffer_ref[source, rank * 2 + 1], ones], axis=1))
+            source, rank = place_of(slot_ref[f, i], me, sources, split)
+            key = buffer_ref[source, rank if split else rank * 2]
+            scores.append(pair_scores(query, key, offset, slope, gap))
+            if not split:
+                values.append(jnp.concatenate([buffer_ref[source, rank * 2 + 1], ones], axis=1))
         band = stat_ref[rows, :]
         top = jnp.maximum(band[:, 0:1], row_max(jnp.maximum(scores[0], scores[1])))
         weights = [jnp.exp2(score - top) for score in scores]
-        far = weighted(weights[0], values[0]) + weighted(weights[1], values[1])
         share = jnp.exp2(band - top)
-        acc = acc_ref[rows, :] * share + far[:, :DH]
-        out_ref[rows, :] = (acc / (share + far[:, DH:])).astype(jnp.bfloat16)
+        if split:
+            scale = 1.0 / (share[:, 0:1] + row_sum(weights[0] + weights[1]))
+            for f in range(FAR):
+                weights_ref[rows, f * BT : (f + 1) * BT] = (weights[f] * scale).astype(jnp.bfloat16)
+            out_ref[rows, :] = acc_ref[rows, :] * (share * scale)
+        else:
+            far = weighted(weights[0], values[0]) + weighted(weights[1], values[1])
+            acc = acc_ref[rows, :] * share + far[:, :DH]
+            out_ref[rows, :] = (acc / (share + far[:, DH:])).astype(jnp.bfloat16)
 
 
 def far_attention(meta, slots, far_blocks, slopes, queries, acc, stat, pieces, head, sources):
     tok_rows = queries.shape[0]
     blk_dev = tok_rows // BT
+    split = len(pieces) > 1
     group = 2 if blk_dev % 2 == 0 else 1
     tile = pl.BlockSpec((group * BT, DH), lambda i, *_: (i, head))
     hbm = pl.BlockSpec(memory_space=pltpu.HBM)
+    out_shape = [jax.ShapeDtypeStruct((tok_rows, DH), jnp.float32 if split else jnp.bfloat16)]
+    out_specs = [pl.BlockSpec((group * BT, DH), lambda i, *_: (i, 0))]
+    if split:
+        out_shape.insert(0, jax.ShapeDtypeStruct((tok_rows, FAR * BT), jnp.bfloat16))
+        out_specs.insert(0, pl.BlockSpec((group * BT, FAR * BT), lambda i, *_: (i, 0)))
     return pl.pallas_call(
-        functools.partial(far_kernel, head=head, blk_dev=blk_dev, sources=sources, group=group),
-        out_shape=jax.ShapeDtypeStruct((tok_rows, DH), jnp.bfloat16),
+        functools.partial(
+            far_kernel, head=head, blk_dev=blk_dev, sources=sources, group=group, split=split
+        ),
+        out_shape=out_shape,
         grid_spec=pltpu.PrefetchScalarGridSpec(
             num_scalar_prefetch=4,
             grid=(blk_dev // group,),
             in_specs=[tile, tile, tile] + [hbm] * len(pieces),
-            out_specs=pl.BlockSpec((group * BT, DH), lambda i, *_: (i, 0)),
+            out_specs=out_specs,
             scratch_shapes=[
-                pltpu.VMEM((sources, CAP * 2, BT, DH), jnp.bfloat16),
+                pltpu.VMEM((sources, CAP if split else CAP * 2, BT, DH), jnp.bfloat16),
                 pltpu.VMEM((BT, BT), jnp.float32),
                 pltpu.SemaphoreType.DMA((sources,)),
             ],
         ),
-        compiler_params=pltpu.CompilerParams(vmem_limit_bytes=16 * MIB),
+        compiler_params=pltpu.CompilerParams(vmem_limit_bytes=24 * MIB),
         cost_estimate=pl.CostEstimate(
             flops=2 * 4 * tok_rows * BT * DH,
             transcendentals=2 * tok_rows * BT,
@@ -327,46 +350,101 @@
     )(meta, slots, far_blocks, slopes, queries, acc, stat, *pieces)
 
 
-def place_kernel(part_ref, *refs, head):
-    out_ref, buffer_ref, in_sems, out_sems = refs[-4:]
-    peers = part_ref.shape[0]
-    width = out_ref.shape[1] // peers
+def value_kernel(me_ref, slot_ref, weights_ref, acc_ref, *refs, sources, group):
+    pieces = refs[:-3]
+    out_ref, buffer_ref, sems = refs[-3:]
+    local = pl.program_id(0)
+
+    @pl.when(local == 0)
+    def _():
+        for copy in gather_pieces(pieces, buffer_ref, sems, sources):
+            copy.wait()
+
+    for part in range(group):
+        rows = pl.ds(part * BT, BT)
+        acc = acc_ref[rows, :]
+        for f in range(FAR):
+            source, rank = place_of(slot_ref[f, local * group + part], me_ref[0], sources, True)
+            acc = acc + weighted(
+                weights_ref[rows, f * BT : (f + 1) * BT], buffer_ref[source, rank]
+            )
+        out_ref[rows, :] = acc.astype(jnp.bfloat16)
+
+
+def far_values(me, slots, weights, acc, pieces, sources):
+    tok_rows = acc.shape[0]
+    blk_dev = tok_rows // BT
+    group = 2 if blk_dev % 2 == 0 else 1
+    hbm = pl.BlockSpec(memory_space=pltpu.HBM)
+    return pl.pallas_call(
+        functools.partial(value_kernel, sources=sources, group=group),
+        out_shape=jax.ShapeDtypeStruct((tok_rows, DH), jnp.bfloat16),
+        grid_spec=pltpu.PrefetchScalarGridSpec(
+            num_scalar_prefetch=2,
+            grid=(blk_dev // group,),
+            in_specs=[
+                pl.BlockSpec((group * BT, FAR * BT), lambda i, *_: (i, 0)),
+                pl.BlockSpec((group * BT, DH), lambda i, *_: (i, 0)),
+            ]
+            + [hbm] * len(pieces),
+            out_specs=pl.BlockSpec((group * BT, DH), lambda i, *_: (i, 0)),
+            scratch_shapes=[
+                pltpu.VMEM((sources, CAP, BT, DH), jnp.bfloat16),
+                pltpu.SemaphoreType.DMA((sources,)),
+            ],
+        ),
+        compiler_params=pltpu.CompilerParams(vmem_limit_bytes=16 * MIB),
+        name="values",
+    )(me, slots, weights, acc, *pieces)
+
+
+def place_kernel(*refs, heads):
+    parts = refs[:heads]
+    out_ref, buffer_ref, in_sems, out_sems = refs[heads:]
+    peers = parts[0].shape[0]
+    width = heads * DH
     loads = [
-        pltpu.make_async_copy(part_ref.at[g], buffer_ref.at[g], in_sems.at[g])
+        [
+            pltpu.make_async_copy(
+                part.at[g], buffer_ref.at[g, :, pl.ds(head * DH, DH)], in_sems.at[g, head]
+            )
+            for head, part in enumerate(parts)
+        ]
         for g in range(peers)
     ]
     stores = [
         pltpu.make_async_copy(
-            buffer_ref.at[g], out_ref.at[:, pl.ds(g * width + head * DH, DH)], out_sems.at[g]
+            buffer_ref.at[g], out_ref.at[:, pl.ds(g * width, width)], out_sems.at[g]
         )
         for g in range(peers)
     ]
-    for load in loads:
-        load.start()
-    for load, store in zip(loads, stores):
-        load.wait()
+    for pair in loads:
+        for load in pair:
+            load.start()
+    for pair, store in zip(loads, stores):
+        for load in pair:
+            load.wait()
         store.start()
     for store in stores:
         store.wait()
 
 
-def place(part, so_far, head, heads):
-    peers, rows, _ = part.shape
-    hbm = pl.BlockSpec(memory_space=pltpu.HBM)
-    args = (part,) if so_far is None else (part, so_far)
+def place(parts):
+    peers, rows, _ = parts[0].shape
+    heads = len(parts)
+    any_spec = pl.BlockSpec(memory_space=pl.ANY)
     return pl.pallas_call(
-        functools.partial(place_kernel, head=head),
-        out_shape=jax.ShapeDtypeStruct((rows, peers * heads * DH), part.dtype),
-        in_specs=[hbm] * len(args),
-        out_specs=hbm,
+        functools.partial(place_kernel, heads=heads),
+        out_shape=jax.ShapeDtypeStruct((rows, peers * heads * DH), parts[0].dtype),
+        in_specs=[any_spec] * heads,
+        out_specs=pl.BlockSpec(memory_space=pltpu.HBM),
         scratch_shapes=[
-            pltpu.VMEM(part.shape, part.dtype),
-            pltpu.SemaphoreType.DMA((peers,)),
+            pltpu.VMEM((peers, rows, heads * DH), parts[0].dtype),
+            pltpu.SemaphoreType.DMA((peers, heads)),
             pltpu.SemaphoreType.DMA((peers,)),
         ],
-        input_output_aliases={} if so_far is None else {1: 0},
         name="place",
-    )(*args)
+    )(*parts)
 
 
 def body(queries, key_rows, value_rows, band_reach, far_list, slopes):
@@ -395,10 +473,13 @@
         split = head == heads - 1
         outgoing = pack(asked, me, keys_hbm, values_hbm, head, split)
         if split:
-            pieces = [outgoing[0]]
-            for shift in range(1, sources):
-                ring = [(i, (i + shift) % sources) for i in range(sources)]
-                pieces.append(lax.ppermute(outgoing[shift], "seq", ring))
+            pieces = []
+            for which in range(2):
+                arrays = list(outgoing[which * sources : (which + 1) * sources])
+                for shift in range(1, sources):
+                    ring = [(i, (i + shift) % sources) for i in range(sources)]
+                    arrays[shift] = lax.ppermute(arrays[shift], "seq", ring)
+                pieces.append(arrays)
             incoming.append(pieces)
         else:
             incoming.append(
@@ -412,17 +493,24 @@
     acc, stat, queries = (
         pltpu.with_memory_space_constraint(x, pltpu.HBM) for x in (acc, stat, queries)
     )
-    mixed = None
+    parts = []
     for head in range(heads):
+        split = head == heads - 1
+        pieces = incoming[head][0] if split else incoming[head]
         attended = far_attention(
-            meta, slots, far_list.T, slopes, queries, acc, stat, incoming[head], head, sources
+            meta, slots, far_list.T, slopes, queries, acc, stat, pieces, head, sources
         )
-        part = lax.all_to_all(
-            attended.reshape(lax.axis_size("head"), -1, DH), "head",
-            split_axis=0, concat_axis=0, tiled=True,
+        if split:
+            attended = far_values(me, slots, *attended, incoming[head][1], sources)
+        else:
+            attended = attended[0]
+        parts.append(
+            lax.all_to_all(
+                attended.reshape(lax.axis_size("head"), -1, DH), "head",
+                split_axis=0, concat_axis=0, tiled=True,
+            )
         )
-        mixed = place(part, mixed, head, heads)
-    return mixed
+    return place(parts)
 
 
 def solution(mesh):

time: 336 us -> 389 us (1.16)
  the two profiles are of different devices: /device:TPU:64 before, /device:TPU:40 now
where the time goes in v3:
time: 389 us; the launch traced here: 388 us
  waiting for transfers between devices  149 us (38%)
  starting transfers between devices  108 us (28%)
  Pallas kernels  107 us (28%)
  blocking collectives  19.6 us (5%)
  local copies, waits for them, and re-layouts  3.94 us (1%)
    ppermute x30, waiting for transfers between devices, body(): arrays[shift] = lax.ppermute(arrays[shift], 'seq', ring)  137 us
    ppermute x30, starting transfers between devices, body(): arrays[shift] = lax.ppermute(arrays[shift], 'seq', ring)  79 us
    pallas_call x1, Pallas kernels, band_attention(): pl.pallas_call(functools.partial(band_kernel, blk_dev=blk_dev, total_bloc...  58.1 us
    pallas_call x2, Pallas kernels, far_attention(): pl.pallas_call(functools.partial(far_kernel, head=head, blk_dev=blk_dev,...  27.2 us
    all_to_all x1, blocking collectives, body(): lax.all_to_all(attended.reshape(lax.axis_size('head'), -1, DH), 'head', s...  19.6 us
    pallas_call x2, Pallas kernels, pack(): pl.pallas_call(functools.partial(pack_kernel, shifts=shifts), out_shape=o...  9.71 us
    all_to_all x1, starting transfers between devices, body(): lax.all_to_all(table, 'seq', split_axis=0, concat_axis=0, tiled=True)  9.5 us
  transfers between devices with their start and end apart: 35, of which 15 were waited for; matrix products, arithmetic and copies ran while one was open for 0% of the time, Pallas kernels for 25%

profile of v3, /device:TPU:40, one launch (start us, length us, event | category | flops | bytes accessed | tf_op | source)
XLA Modules:
  0.0 387.8 jit_solution(2361741315389698229)
XLA Ops:
  1.8 9.5 %all-to-all-start = ((s32[16,1,2]{2,1,0:T(1,128)}), s32[16,1,2]{2,1,0:T(1,128)S(1)}, u32[]{:S(2)}, u32[]{:S(2)}) async-start(s32[16,1,2]{2,1,0:T(1,128)} %bitcast.22), calls=%async_computation | async-start | bytes 16384 | tf_op jit(solution)/shard_map/all_to_all | solution.py:461
  11.3 6.2 %all-to-all-done = s32[16,1,2]{2,1,0:T(1,128)S(1)} async-done(((s32[16,1,2]{2,1,0:T(1,128)}), s32[16,1,2]{2,1,0:T(1,128)S(1)}, u32[]{:S(2)}, u32[]{:S(2)}) %all-to-all-start) | async-done | bytes 160 | tf_op jit(solution)/shard_map/all_to_all | solution.py:461
  17.5 4.7 %pack.2 = bf16[16,4,256,128]{3,2,1,0:T(8,128)(2,1)} custom-call(s32[16,2]{1,0:T(8,128)S(1)} %bitcast.17, s32[1]{0:T(128)} %bitcast.me_ref, bf16[3584,256]{1,0:T(8,128)(2,1)} %keys_ref.3, bf16[3584,256]{1,0:T(8,128)(2,1)} %values_ref.3), custom_call_target="tpu_custom_call" | custom-call | tf_op jit(solution)/shard_map/pack/pallas_call | solution.py:87
  22.1 6.7 %all-to-all-start.1 = ((bf16[16,4,256,128]{3,2,1,0:T(8,128)(2,1)}), bf16[16,4,256,128]{3,2,1,0:T(8,128)(2,1)}, u32[]{:S(2)}, u32[]{:S(2)}) async-start(bf16[16,4,256,128]{3,2,1,0:T(8,128)(2,1)} %pack.2), calls=%async_computation.1 | async-start | bytes 8388608 | tf_op jit(solution)/shard_map/all_to_all | solution.py:486
  28.9 5.0 %pack.3 = (bf16[2,256,128]{2,1,0:T(8,128)(2,1)}, bf16[2,256,128]{2,1,0:T(8,128)(2,1)}, bf16[2,256,128]{2,1,0:T(8,128)(2,1)}, bf16[2,256,128]{2,1,0:T(8,128)(2,1)...) custom-call(s32[16,2]{1,0:T(8,128)S(1)} %bitcast.18, ...), custom_call_target="tpu_custom_call" | custom-call | tf_op jit(solution)/shard_map/pack/pallas_call | solution.py:87
  35.9 4.6 %collective-permute-start.11 = (bf16[2,256,128]{2,1,0:T(8,128)(2,1)S(1)}, bf16[2,256,128]{2,1,0:T(8,128)(2,1)S(1)}, u32[]{:S(2)}, u32[]{:S(2)}) collective-permute-start(bf16[2,256,128]{2,1,0:T(8,128)(2,1)S(1)} %copy-done.39), channel_id=1, source_target_pairs={{0,160},{16,176},{32,192},{48,208},{64,224},{80,240},{96,0},{112,1... | collective-permute-start | bytes 393224 | tf_op jit(solution)/shard_map/ppermute | solution.py:481
  41.0 3.2 collective-permute-start.13
  45.8 79.2 %collective-permute-done.10.refs_9_ = bf16[2,256,128]{2,1,0:T(8,128)(2,1)S(1)} collective-permute-done((bf16[2,256,128]{2,1,0:T(8,128)(2,1)}, bf16[2,256,128]{2,1,0:T(8,128)(2,1)S(1)}, u32[]{:S(2)}, u32[]{:S(2)}) %collective-permute-start.10) | collective-permute-done | bytes 131104 | tf_op jit(solution)/shard_map/ppermute | solution.py:481
  127.6 3.2 collective-permute-done.11.refs_10_
  130.8 4.4 %collective-permute-start.1 = (bf16[2,768,256]{2,1,0:T(8,128)(2,1)S(1)}, bf16[2,768,256]{2,1,0:T(8,128)(2,1)S(1)}, u32[]{:S(2)}, u32[]{:S(2)}) collective-permute-start(bf16[2,768,256]{2,1,0:T(8,128)(2,1)S(1)} %pad_maximum_fusion.1), channel_id=1, source_target_pairs={{16,0},{32,16},{48,32},{64,48},{80,64},{96,80},{112,96},{128,112},... | collective-permute-start | bytes 2359304 | tf_op jit(solution)/shard_map/ppermute | solution.py:465
  135.3 3.9 %collective-permute-done.12.refs_11_ = bf16[2,256,128]{2,1,0:T(8,128)(2,1)S(1)} collective-permute-done((bf16[2,256,128]{2,1,0:T(8,128)(2,1)S(1)}, bf16[2,256,128]{2,1,0:T(8,128)(2,1)S(1)}, u32[]{:S(2)}, u32[]{:S(2)}) %collective-permute-start.12) | collective-permute-done | bytes 131104 | tf_op jit(solution)/shard_map/ppermute | solution.py:481
  139.2 3.6 collective-permute-start.16
  145.9 6.4 %collective-permute-start.4 = (bf16[2,256,128]{2,1,0:T(8,128)(2,1)S(1)}, bf16[2,256,128]{2,1,0:T(8,128)(2,1)S(1)}, u32[]{:S(2)}, u32[]{:S(2)}) collective-permute-start(bf16[2,256,128]{2,1,0:T(8,128)(2,1)S(1)} %copy-done.31), channel_id=1, source_target_pairs={{0,48},{16,64},{32,80},{48,96},{64,112},{80,128},{96,144},{112,160... | collective-permute-start | bytes 393224 | tf_op jit(solution)/shard_map/ppermute | solution.py:481
  152.3 9.3 %collective-permute-done.16.refs_15_ = bf16[2,256,128]{2,1,0:T(8,128)(2,1)S(1)} collective-permute-done((bf16[2,256,128]{2,1,0:T(8,128)(2,1)S(1)}, bf16[2,256,128]{2,1,0:T(8,128)(2,1)S(1)}, u32[]{:S(2)}, u32[]{:S(2)}) %collective-permute-start.16) | collective-permute-done | bytes 131104 | tf_op jit(solution)/shard_map/ppermute | solution.py:481
  163.8 4.6 %collective-permute-start.5 = (bf16[2,256,128]{2,1,0:T(8,128)(2,1)S(1)}, bf16[2,256,128]{2,1,0:T(8,128)(2,1)S(1)}, u32[]{:S(2)}, u32[]{:S(2)}) collective-permute-start(bf16[2,256,128]{2,1,0:T(8,128)(2,1)S(1)} %copy-done.30), channel_id=1, source_target_pairs={{0,64},{16,80},{32,96},{48,112},{64,128},{80,144},{96,160},{112,17... | collective-permute-start | bytes 393224 | tf_op jit(solution)/shard_map/ppermute | solution.py:481
  168.4 4.6 %collective-permute-start.6 = (bf16[2,256,128]{2,1,0:T(8,128)(2,1)S(1)}, bf16[2,256,128]{2,1,0:T(8,128)(2,1)S(1)}, u32[]{:S(2)}, u32[]{:S(2)}) collective-permute-start(bf16[2,256,128]{2,1,0:T(8,128)(2,1)S(1)} %copy-done.29), channel_id=1, source_target_pairs={{0,80},{16,96},{32,112},{48,128},{64,144},{80,160},{96,176},{112,1... | collective-permute-start | bytes 393224 | tf_op jit(solution)/shard_map/ppermute | solution.py:481
  173.8 17.3 %collective-permute-start.8 = (bf16[2,256,128]{2,1,0:T(8,128)(2,1)S(1)}, bf16[2,256,128]{2,1,0:T(8,128)(2,1)S(1)}, u32[]{:S(2)}, u32[]{:S(2)}) collective-permute-start(bf16[2,256,128]{2,1,0:T(8,128)(2,1)S(1)} %copy-done.27), channel_id=1, source_target_pairs={{0,112},{16,128},{32,144},{48,160},{64,176},{80,192},{96,208},{112... | collective-permute-start | bytes 393224 | tf_op jit(solution)/shard_map/ppermute | solution.py:481
  195.1 3.1 collective-permute-done.8.refs_7_
  201.8 5.0 %collective-permute-start.20 = (bf16[2,256,128]{2,1,0:T(8,128)(2,1)S(1)}, bf16[2,256,128]{2,1,0:T(8,128)(2,1)S(1)}, u32[]{:S(2)}, u32[]{:S(2)}) collective-permute-start(bf16[2,256,128]{2,1,0:T(8,128)(2,1)S(1)} %copy-done.22), channel_id=1, source_target_pairs={{0,64},{16,80},{32,96},{48,112},{64,128},{80,144},{96,160},{112,17... | collective-permute-start | bytes 393224 | tf_op jit(solution)/shard_map/ppermute | solution.py:481
  206.8 12.1 %collective-permute-done.18.refs_2_ = bf16[2,256,128]{2,1,0:T(8,128)(2,1)S(1)} collective-permute-done((bf16[2,256,128]{2,1,0:T(8,128)(2,1)S(1)}, bf16[2,256,128]{2,1,0:T(8,128)(2,1)S(1)}, u32[]{:S(2)}, u32[]{:S(2)}) %collective-permute-start.18) | collective-permute-done | bytes 131104 | tf_op jit(solution)/shard_map/ppermute | solution.py:481
  221.4 12.2 %collective-permute-done.21.refs_5_ = bf16[2,256,128]{2,1,0:T(8,128)(2,1)S(1)} collective-permute-done((bf16[2,256,128]{2,1,0:T(8,128)(2,1)S(1)}, bf16[2,256,128]{2,1,0:T(8,128)(2,1)S(1)}, u32[]{:S(2)}, u32[]{:S(2)}) %collective-permute-start.21) | collective-permute-done | bytes 131104 | tf_op jit(solution)/shard_map/ppermute | solution.py:481
  235.0 4.1 %collective-permute-done.24.refs_8_ = bf16[2,256,128]{2,1,0:T(8,128)(2,1)S(1)} collective-permute-done((bf16[2,256,128]{2,1,0:T(8,128)(2,1)S(1)}, bf16[2,256,128]{2,1,0:T(8,128)(2,1)S(1)}, u32[]{:S(2)}, u32[]{:S(2)}) %collective-permute-start.24) | collective-permute-done | bytes 131104 | tf_op jit(solution)/shard_map/ppermute | solution.py:481
  239.1 4.0 %collective-permute-done.25.refs_9_ = bf16[2,256,128]{2,1,0:T(8,128)(2,1)S(1)} collective-permute-done((bf16[2,256,128]{2,1,0:T(8,128)(2,1)S(1)}, bf16[2,256,128]{2,1,0:T(8,128)(2,1)S(1)}, u32[]{:S(2)}, u32[]{:S(2)}) %collective-permute-start.25) | collective-permute-done | bytes 131104 | tf_op jit(solution)/shard_map/ppermute | solution.py:481
  243.0 4.6 %collective-permute-done.26.refs_10_ = bf16[2,256,128]{2,1,0:T(8,128)(2,1)S(1)} collective-permute-done((bf16[2,256,128]{2,1,0:T(8,128)(2,1)S(1)}, bf16[2,256,128]{2,1,0:T(8,128)(2,1)S(1)}, u32[]{:S(2)}, u32[]{:S(2)}) %collective-permute-start.26) | collective-permute-done | bytes 131104 | tf_op jit(solution)/shard_map/ppermute | solution.py:481
  247.7 8.1 %collective-permute-start.30 = (bf16[2,256,128]{2,1,0:T(8,128)(2,1)S(1)}, bf16[2,256,128]{2,1,0:T(8,128)(2,1)S(1)}, u32[]{:S(2)}, u32[]{:S(2)}) collective-permute-start(bf16[2,256,128]{2,1,0:T(8,128)(2,1)S(1)} %copy-done.12), channel_id=1, source_target_pairs={{0,224},{16,240},{32,0},{48,16},{64,32},{80,48},{96,64},{112,80},{... | collective-permute-start | bytes 393224 | tf_op jit(solution)/shard_map/ppermute | solution.py:481
  257.2 58.1 %band.1 = (f32[3584,256]{1,0:T(8,128)S(1)}, f32[3584,256]{1,0:T(8,128)S(1)}) custom-call(s32[15]{0:T(128)S(1)} %pad_add_fusion.meta_ref, f32[2]{0:T(128)S(1)} %copy-done.9, bf16[3584,256]{1,0:T(8,128)(2,1)S(1)} %copy-done.4, bf16[3584,256]{1,0:T(8,128)(2,1)S(1)} %copy-done.2, bf16[3584,256]{1,0:T(8,128)(2,1)S(1)} %copy-done.3, ...), custom_call_target="tpu_custom_call" | custom-call | flops 6576668672 | bytes 31457280 | tf_op jit(solution)/shard_map/band/pallas_call | solution.py:213
  319.0 16.2 %far.3 = (bf16[3584,512]{1,0:T(8,128)(2,1)S(1)}, f32[3584,128]{1,0:T(8,128)S(1)}) custom-call(s32[15]{0:T(128)S(1)} %pad_add_fusion.meta_ref, s32[2,14]{1,0:T(2,128)S(1)} %copy-done.7, s32[2,14]{1,0:T(2,128)S(1)} %bitcast.20, f32[2]{0:T(128)S(1)} %copy-done.9, bf16[3584,256]{1,0:T(8,128)(2,1)} %query_ref.5, f32[3584,256]{1,0:T(8,128)} %copy-done, ...), custom_call_target="tpu_custom_call" | custom-call | flops 939524096 | bytes 14680064 | tf_op jit(solution)/shard_map/far/pallas_call | solution.py:327
  335.2 7.6 %values.1 = bf16[3584,128]{1,0:T(8,128)(2,1)} custom-call(s32[1]{0:T(128)} %bitcast.me_ref, s32[2,14]{1,0:T(2,128)S(1)} %copy-done.7, bf16[3584,512]{1,0:T(8,128)(2,1)S(1)} %get-tuple-element.63.weights_ref, f32[3584,128]{1,0:T(8,128)S(1)} %get-tuple-element.64.acc_ref, bf16[2,256,128]{2,1,0:T(8,128)(2,1)S(1)} %copy-done.5, ...), custom_call_target="tpu_custom_call" | custom-call | tf_op jit(solution)/shard_map/values/pallas_call | solution.py:379
  342.8 6.1 %all-to-all-start.3 = ((bf16[16,224,128]{2,1,0:T(8,128)(2,1)}), bf16[16,224,128]{2,1,0:T(8,128)(2,1)S(1)}, u32[]{:S(2)}, u32[]{:S(2)}) async-start(bf16[16,224,128]{2,1,0:T(8,128)(2,1)} %bitcast.9), calls=%async_computation.3 | async-start | bytes 1835008 | tf_op jit(solution)/shard_map/all_to_all | solution.py:508
  349.0 11.0 %far.2 = bf16[3584,128]{1,0:T(8,128)(2,1)S(1)} custom-call(s32[15]{0:T(128)S(1)} %pad_add_fusion.meta_ref, s32[2,14]{1,0:T(2,128)S(1)} %copy-done.7, s32[2,14]{1,0:T(2,128)S(1)} %bitcast.21, f32[2]{0:T(128)S(1)} %copy-done.9, bf16[3584,256]{1,0:T(8,128)(2,1)} %query_ref.5, f32[3584,256]{1,0:T(8,128)} %copy-done, f32[3584,256]{1,0:T(8,128)} %copy-done.1, ...), custom_call_target="tpu_custom_call" | custom-call | flops 939524096 | bytes 14680064 | tf_op jit(solution)/shard_map/far/pallas_call | solution.py:327
  360.0 5.5 %all-to-all-done.3.refs_1_ = bf16[16,224,128]{2,1,0:T(8,128)(2,1)S(1)} async-done(((bf16[16,224,128]{2,1,0:T(8,128)(2,1)}), bf16[16,224,128]{2,1,0:T(8,128)(2,1)S(1)}, u32[]{:S(2)}, u32[]{:S(2)}) %all-to-all-start.3) | async-done | bytes 917536 | tf_op jit(solution)/shard_map/all_to_all | solution.py:508
  365.5 19.6 %all_to_all.26.refs_0_ = bf16[16,224,128]{2,1,0:T(8,128)(2,1)} all-to-all(bf16[16,224,128]{2,1,0:T(8,128)(2,1)S(1)} %bitcast.16), channel_id=1, replica_groups=mesh['seq'=16,'head'=16] {'head'}, dimensions={0} | all-to-all | bytes 1835008 | tf_op jit(solution)/shard_map/all_to_all | solution.py:508
  (133 shorter events, 33.2 us)
Async XLA Ops:
  1.8 15.7 %all-to-all-start = ((s32[16,1,2]{2,1,0:T(1,128)}), s32[16,1,2]{2,1,0:T(1,128)S(1)}, u32[]{:S(2)}, u32[]{:S(2)}) async-start(s32[16,1,2]{2,1,0:T(1,128)} %bitcast.22), calls=%async_computation | async-start | bytes 16384 | tf_op jit(solution)/shard_map/all_to_all | solution.py:461
  22.1 320.7 %all-to-all-start.1 = ((bf16[16,4,256,128]{3,2,1,0:T(8,128)(2,1)}), bf16[16,4,256,128]{3,2,1,0:T(8,128)(2,1)}, u32[]{:S(2)}, u32[]{:S(2)}) async-start(bf16[16,4,256,128]{3,2,1,0:T(8,128)(2,1)} %pack.2), calls=%async_computation.1 | async-start | bytes 8388608 | tf_op jit(solution)/shard_map/all_to_all | solution.py:486
  34.0 91.0 %collective-permute-start.10 = (bf16[2,256,128]{2,1,0:T(8,128)(2,1)}, bf16[2,256,128]{2,1,0:T(8,128)(2,1)S(1)}, u32[]{:S(2)}, u32[]{:S(2)}) collective-permute-start(bf16[2,256,128]{2,1,0:T(8,128)(2,1)} %get-tuple-element.56), channel_id=1, source_target_pairs={{0,144},{16,160},{32,176},{48,192},{64,208},{80,224},{96,240},{112... | collective-permute-start | bytes 393224 | tf_op jit(solution)/shard_map/ppermute | solution.py:481
  35.9 95.0 %collective-permute-start.11 = (bf16[2,256,128]{2,1,0:T(8,128)(2,1)S(1)}, bf16[2,256,128]{2,1,0:T(8,128)(2,1)S(1)}, u32[]{:S(2)}, u32[]{:S(2)}) collective-permute-start(bf16[2,256,128]{2,1,0:T(8,128)(2,1)S(1)} %copy-done.39), channel_id=1, source_target_pairs={{0,160},{16,176},{32,192},{48,208},{64,224},{80,240},{96,0},{112,1... | collective-permute-start | bytes 393224 | tf_op jit(solution)/shard_map/ppermute | solution.py:481
  40.5 98.7 %collective-permute-start.12 = (bf16[2,256,128]{2,1,0:T(8,128)(2,1)S(1)}, bf16[2,256,128]{2,1,0:T(8,128)(2,1)S(1)}, u32[]{:S(2)}, u32[]{:S(2)}) collective-permute-start(bf16[2,256,128]{2,1,0:T(8,128)(2,1)S(1)} %copy-done.38), channel_id=1, source_target_pairs={{0,176},{16,192},{32,208},{48,224},{64,240},{80,0},{96,16},{112,32... | collective-permute-start | bytes 393224 | tf_op jit(solution)/shard_map/ppermute | solution.py:481
  41.0 101.8 %collective-permute-start.13 = (bf16[2,256,128]{2,1,0:T(8,128)(2,1)S(1)}, bf16[2,256,128]{2,1,0:T(8,128)(2,1)S(1)}, u32[]{:S(2)}, u32[]{:S(2)}) collective-permute-start(bf16[2,256,128]{2,1,0:T(8,128)(2,1)S(1)} %copy-done.37), channel_id=1, source_target_pairs={{0,192},{16,208},{32,224},{48,240},{64,0},{80,16},{96,32},{112,48}... | collective-permute-start | bytes 393224 | tf_op jit(solution)/shard_map/ppermute | solution.py:481
  44.3 101.6 %collective-permute-start.14 = (bf16[2,256,128]{2,1,0:T(8,128)(2,1)S(1)}, bf16[2,256,128]{2,1,0:T(8,128)(2,1)S(1)}, u32[]{:S(2)}, u32[]{:S(2)}) collective-permute-start(bf16[2,256,128]{2,1,0:T(8,128)(2,1)S(1)} %copy-done.36), channel_id=1, source_target_pairs={{0,208},{16,224},{32,240},{48,0},{64,16},{80,32},{96,48},{112,64},... | collective-permute-start | bytes 393224 | tf_op jit(solution)/shard_map/ppermute | solution.py:481
  125.0 20.8 %collective-permute-start.15 = (bf16[2,256,128]{2,1,0:T(8,128)(2,1)S(1)}, bf16[2,256,128]{2,1,0:T(8,128)(2,1)S(1)}, u32[]{:S(2)}, u32[]{:S(2)}) collective-permute-start(bf16[2,256,128]{2,1,0:T(8,128)(2,1)S(1)} %copy-done.35), channel_id=1, source_target_pairs={{0,224},{16,240},{32,0},{48,16},{64,32},{80,48},{96,64},{112,80},{... | collective-permute-start | bytes 393224 | tf_op jit(solution)/shard_map/ppermute | solution.py:481
  130.8 116.8 %collective-permute-start.1 = (bf16[2,768,256]{2,1,0:T(8,128)(2,1)S(1)}, bf16[2,768,256]{2,1,0:T(8,128)(2,1)S(1)}, u32[]{:S(2)}, u32[]{:S(2)}) collective-permute-start(bf16[2,768,256]{2,1,0:T(8,128)(2,1)S(1)} %pad_maximum_fusion.1), channel_id=1, source_target_pairs={{16,0},{32,16},{48,32},{64,48},{80,64},{96,80},{112,96},{128,112},... | collective-permute-start | bytes 2359304 | tf_op jit(solution)/shard_map/ppermute | solution.py:465
  139.2 22.5 %collective-permute-start.16 = (bf16[2,256,128]{2,1,0:T(8,128)(2,1)S(1)}, bf16[2,256,128]{2,1,0:T(8,128)(2,1)S(1)}, u32[]{:S(2)}, u32[]{:S(2)}) collective-permute-start(bf16[2,256,128]{2,1,0:T(8,128)(2,1)S(1)} %copy-done.34), channel_id=1, source_target_pairs={{0,240},{16,0},{32,16},{48,32},{64,48},{80,64},{96,80},{112,96},{1... | collective-permute-start | bytes 393224 | tf_op jit(solution)/shard_map/ppermute | solution.py:481
  142.9 20.9 %collective-permute-start.2 = (bf16[2,256,128]{2,1,0:T(8,128)(2,1)S(1)}, bf16[2,256,128]{2,1,0:T(8,128)(2,1)S(1)}, u32[]{:S(2)}, u32[]{:S(2)}) collective-permute-start(bf16[2,256,128]{2,1,0:T(8,128)(2,1)S(1)} %copy-done.33), channel_id=1, source_target_pairs={{0,16},{16,32},{32,48},{48,64},{64,80},{80,96},{96,112},{112,128},... | collective-permute-start | bytes 393224 | tf_op jit(solution)/shard_map/ppermute | solution.py:481
  145.9 22.5 %collective-permute-start.3 = (bf16[2,256,128]{2,1,0:T(8,128)(2,1)S(1)}, bf16[2,256,128]{2,1,0:T(8,128)(2,1)S(1)}, u32[]{:S(2)}, u32[]{:S(2)}) collective-permute-start(bf16[2,256,128]{2,1,0:T(8,128)(2,1)S(1)} %copy-done.32), channel_id=1, source_target_pairs={{0,32},{16,48},{32,64},{48,80},{64,96},{80,112},{96,128},{112,144}... | collective-permute-start | bytes 393224 | tf_op jit(solution)/shard_map/ppermute | solution.py:481
  145.9 27.1 %collective-permute-start.4 = (bf16[2,256,128]{2,1,0:T(8,128)(2,1)S(1)}, bf16[2,256,128]{2,1,0:T(8,128)(2,1)S(1)}, u32[]{:S(2)}, u32[]{:S(2)}) collective-permute-start(bf16[2,256,128]{2,1,0:T(8,128)(2,1)S(1)} %copy-done.31), channel_id=1, source_target_pairs={{0,48},{16,64},{32,80},{48,96},{64,112},{80,128},{96,144},{112,160... | collective-permute-start | bytes 393224 | tf_op jit(solution)/shard_map/ppermute | solution.py:481
  161.7 94.1 %collective-permute-start = (bf16[2,768,256]{2,1,0:T(8,128)(2,1)S(1)}, bf16[2,768,256]{2,1,0:T(8,128)(2,1)S(1)}, u32[]{:S(2)}, u32[]{:S(2)}) collective-permute-start(bf16[2,768,256]{2,1,0:T(8,128)(2,1)S(1)} %pad_maximum_fusion), channel_id=1, source_target_pairs={{0,16},{16,32},{32,48},{48,64},{64,80},{80,96},{96,112},{112,128},... | collective-permute-start | bytes 2359304 | tf_op jit(solution)/shard_map/ppermute | solution.py:464
  163.8 10.0 %collective-permute-start.5 = (bf16[2,256,128]{2,1,0:T(8,128)(2,1)S(1)}, bf16[2,256,128]{2,1,0:T(8,128)(2,1)S(1)}, u32[]{:S(2)}, u32[]{:S(2)}) collective-permute-start(bf16[2,256,128]{2,1,0:T(8,128)(2,1)S(1)} %copy-done.30), channel_id=1, source_target_pairs={{0,64},{16,80},{32,96},{48,112},{64,128},{80,144},{96,160},{112,17... | collective-permute-start | bytes 393224 | tf_op jit(solution)/shard_map/ppermute | solution.py:481
  168.4 22.7 %collective-permute-start.6 = (bf16[2,256,128]{2,1,0:T(8,128)(2,1)S(1)}, bf16[2,256,128]{2,1,0:T(8,128)(2,1)S(1)}, u32[]{:S(2)}, u32[]{:S(2)}) collective-permute-start(bf16[2,256,128]{2,1,0:T(8,128)(2,1)S(1)} %copy-done.29), channel_id=1, source_target_pairs={{0,80},{16,96},{32,112},{48,128},{64,144},{80,160},{96,176},{112,1... | collective-permute-start | bytes 393224 | tf_op jit(solution)/shard_map/ppermute | solution.py:481
  173.0 20.4 %collective-permute-start.7 = (bf16[2,256,128]{2,1,0:T(8,128)(2,1)S(1)}, bf16[2,256,128]{2,1,0:T(8,128)(2,1)S(1)}, u32[]{:S(2)}, u32[]{:S(2)}) collective-permute-start(bf16[2,256,128]{2,1,0:T(8,128)(2,1)S(1)} %copy-done.28), channel_id=1, source_target_pairs={{0,96},{16,112},{32,128},{48,144},{64,160},{80,176},{96,192},{112,... | collective-permute-start | bytes 393224 | tf_op jit(solution)/shard_map/ppermute | solution.py:481
  173.8 24.5 %collective-permute-start.8 = (bf16[2,256,128]{2,1,0:T(8,128)(2,1)S(1)}, bf16[2,256,128]{2,1,0:T(8,128)(2,1)S(1)}, u32[]{:S(2)}, u32[]{:S(2)}) collective-permute-start(bf16[2,256,128]{2,1,0:T(8,128)(2,1)S(1)} %copy-done.27), channel_id=1, source_target_pairs={{0,112},{16,128},{32,144},{48,160},{64,176},{80,192},{96,208},{112... | collective-permute-start | bytes 393224 | tf_op jit(solution)/shard_map/ppermute | solution.py:481
  198.3 20.7 %collective-permute-start.18 = (bf16[2,256,128]{2,1,0:T(8,128)(2,1)S(1)}, bf16[2,256,128]{2,1,0:T(8,128)(2,1)S(1)}, u32[]{:S(2)}, u32[]{:S(2)}) collective-permute-start(bf16[2,256,128]{2,1,0:T(8,128)(2,1)S(1)} %copy-done.24), channel_id=1, source_target_pairs={{0,32},{16,48},{32,64},{48,80},{64,96},{80,112},{96,128},{112,144}... | collective-permute-start | bytes 393224 | tf_op jit(solution)/shard_map/ppermute | solution.py:481
  199.2 19.8 %collective-permute-start.19 = (bf16[2,256,128]{2,1,0:T(8,128)(2,1)S(1)}, bf16[2,256,128]{2,1,0:T(8,128)(2,1)S(1)}, u32[]{:S(2)}, u32[]{:S(2)}) collective-permute-start(bf16[2,256,128]{2,1,0:T(8,128)(2,1)S(1)} %copy-done.23), channel_id=1, source_target_pairs={{0,48},{16,64},{32,80},{48,96},{64,112},{80,128},{96,144},{112,160... | collective-permute-start | bytes 393224 | tf_op jit(solution)/shard_map/ppermute | solution.py:481
  201.8 19.2 %collective-permute-start.20 = (bf16[2,256,128]{2,1,0:T(8,128)(2,1)S(1)}, bf16[2,256,128]{2,1,0:T(8,128)(2,1)S(1)}, u32[]{:S(2)}, u32[]{:S(2)}) collective-permute-start(bf16[2,256,128]{2,1,0:T(8,128)(2,1)S(1)} %copy-done.22), channel_id=1, source_target_pairs={{0,64},{16,80},{32,96},{48,112},{64,128},{80,144},{96,160},{112,17... | collective-permute-start | bytes 393224 | tf_op jit(solution)/shard_map/ppermute | solution.py:481
  219.0 14.6 %collective-permute-start.21 = (bf16[2,256,128]{2,1,0:T(8,128)(2,1)S(1)}, bf16[2,256,128]{2,1,0:T(8,128)(2,1)S(1)}, u32[]{:S(2)}, u32[]{:S(2)}) collective-permute-start(bf16[2,256,128]{2,1,0:T(8,128)(2,1)S(1)} %copy-done.21), channel_id=1, source_target_pairs={{0,80},{16,96},{32,112},{48,128},{64,144},{80,160},{96,176},{112,1... | collective-permute-start | bytes 393224 | tf_op jit(solution)/shard_map/ppermute | solution.py:481
  219.0 14.5 %collective-permute-start.22 = (bf16[2,256,128]{2,1,0:T(8,128)(2,1)S(1)}, bf16[2,256,128]{2,1,0:T(8,128)(2,1)S(1)}, u32[]{:S(2)}, u32[]{:S(2)}) collective-permute-start(bf16[2,256,128]{2,1,0:T(8,128)(2,1)S(1)} %copy-done.20), channel_id=1, source_target_pairs={{0,96},{16,112},{32,128},{48,144},{64,160},{80,176},{96,192},{112,... | collective-permute-start | bytes 393224 | tf_op jit(solution)/shard_map/ppermute | solution.py:481
  221.1 13.1 %collective-permute-start.23 = (bf16[2,256,128]{2,1,0:T(8,128)(2,1)S(1)}, bf16[2,256,128]{2,1,0:T(8,128)(2,1)S(1)}, u32[]{:S(2)}, u32[]{:S(2)}) collective-permute-start(bf16[2,256,128]{2,1,0:T(8,128)(2,1)S(1)} %copy-done.19), channel_id=1, source_target_pairs={{0,112},{16,128},{32,144},{48,160},{64,176},{80,192},{96,208},{112... | collective-permute-start | bytes 393224 | tf_op jit(solution)/shard_map/ppermute | solution.py:481
  233.6 9.5 %collective-permute-start.25 = (bf16[2,256,128]{2,1,0:T(8,128)(2,1)S(1)}, bf16[2,256,128]{2,1,0:T(8,128)(2,1)S(1)}, u32[]{:S(2)}, u32[]{:S(2)}) collective-permute-start(bf16[2,256,128]{2,1,0:T(8,128)(2,1)S(1)} %copy-done.17), channel_id=1, source_target_pairs={{0,144},{16,160},{32,176},{48,192},{64,208},{80,224},{96,240},{112... | collective-permute-start | bytes 393224 | tf_op jit(solution)/shard_map/ppermute | solution.py:481
  234.2 13.5 %collective-permute-start.26 = (bf16[2,256,128]{2,1,0:T(8,128)(2,1)S(1)}, bf16[2,256,128]{2,1,0:T(8,128)(2,1)S(1)}, u32[]{:S(2)}, u32[]{:S(2)}) collective-permute-start(bf16[2,256,128]{2,1,0:T(8,128)(2,1)S(1)} %copy-done.16), channel_id=1, source_target_pairs={{0,160},{16,176},{32,192},{48,208},{64,224},{80,240},{96,0},{112,1... | collective-permute-start | bytes 393224 | tf_op jit(solution)/shard_map/ppermute | solution.py:481
  239.1 96.1 %collective-permute-start.27 = (bf16[2,256,128]{2,1,0:T(8,128)(2,1)S(1)}, bf16[2,256,128]{2,1,0:T(8,128)(2,1)S(1)}, u32[]{:S(2)}, u32[]{:S(2)}) collective-permute-start(bf16[2,256,128]{2,1,0:T(8,128)(2,1)S(1)} %copy-done.15), channel_id=1, source_target_pairs={{0,176},{16,192},{32,208},{48,224},{64,240},{80,0},{96,16},{112,32... | collective-permute-start | bytes 393224 | tf_op jit(solution)/shard_map/ppermute | solution.py:481
  243.0 92.1 %collective-permute-start.28 = (bf16[2,256,128]{2,1,0:T(8,128)(2,1)S(1)}, bf16[2,256,128]{2,1,0:T(8,128)(2,1)S(1)}, u32[]{:S(2)}, u32[]{:S(2)}) collective-permute-start(bf16[2,256,128]{2,1,0:T(8,128)(2,1)S(1)} %copy-done.14), channel_id=1, source_target_pairs={{0,192},{16,208},{32,224},{48,240},{64,0},{80,16},{96,32},{112,48}... | collective-permute-start | bytes 393224 | tf_op jit(solution)/shard_map/ppermute | solution.py:481
  247.7 87.5 %collective-permute-start.29 = (bf16[2,256,128]{2,1,0:T(8,128)(2,1)S(1)}, bf16[2,256,128]{2,1,0:T(8,128)(2,1)S(1)}, u32[]{:S(2)}, u32[]{:S(2)}) collective-permute-start(bf16[2,256,128]{2,1,0:T(8,128)(2,1)S(1)} %copy-done.13), channel_id=1, source_target_pairs={{0,208},{16,224},{32,240},{48,0},{64,16},{80,32},{96,48},{112,64},... | collective-permute-start | bytes 393224 | tf_op jit(solution)/shard_map/ppermute | solution.py:481
  247.7 87.5 %collective-permute-start.30 = (bf16[2,256,128]{2,1,0:T(8,128)(2,1)S(1)}, bf16[2,256,128]{2,1,0:T(8,128)(2,1)S(1)}, u32[]{:S(2)}, u32[]{:S(2)}) collective-permute-start(bf16[2,256,128]{2,1,0:T(8,128)(2,1)S(1)} %copy-done.12), channel_id=1, source_target_pairs={{0,224},{16,240},{32,0},{48,16},{64,32},{80,48},{96,64},{112,80},{... | collective-permute-start | bytes 393224 | tf_op jit(solution)/shard_map/ppermute | solution.py:481
  255.8 79.4 %collective-permute-start.31 = (bf16[2,256,128]{2,1,0:T(8,128)(2,1)S(1)}, bf16[2,256,128]{2,1,0:T(8,128)(2,1)S(1)}, u32[]{:S(2)}, u32[]{:S(2)}) collective-permute-start(bf16[2,256,128]{2,1,0:T(8,128)(2,1)S(1)} %copy-done.11), channel_id=1, source_target_pairs={{0,240},{16,0},{32,16},{48,32},{64,48},{80,64},{96,80},{112,96},{1... | collective-permute-start | bytes 393224 | tf_op jit(solution)/shard_map/ppermute | solution.py:481
  342.8 22.7 %all-to-all-start.3 = ((bf16[16,224,128]{2,1,0:T(8,128)(2,1)}), bf16[16,224,128]{2,1,0:T(8,128)(2,1)S(1)}, u32[]{:S(2)}, u32[]{:S(2)}) async-start(bf16[16,224,128]{2,1,0:T(8,128)(2,1)} %bitcast.9), calls=%async_computation.3 | async-start | bytes 1835008 | tf_op jit(solution)/shard_map/all_to_all | solution.py:508
  (44 other events, 5003.4 us)

commit v4 on v3

--- a/solution.py
+++ b/solution.py
@@ -128,10 +128,10 @@
 
 
 def band_kernel(
-    meta_ref, slopes_ref, query_ref, keys_hbm, values_hbm, before_hbm, after_hbm,
-    acc_ref, stat_ref,
-    keys_ref, values_ref, gap_ref, max_ref, sum_ref, sems, *, blk_dev, total_blocks,
+    meta_ref, slopes_ref, query_ref, keys_hbm, values_hbm, *refs, blk_dev, total_blocks,
 ):
+    before_hbm, after_hbm = refs[0:2], refs[2:4]
+    acc_ref, stat_ref, keys_ref, values_ref, gap_ref, max_ref, sum_ref, sems = refs[4:]
     head = pl.program_id(0)
     local = pl.program_id(1)
     margin = BAND * BT
@@ -144,13 +144,13 @@
         for which, (ref, whole) in enumerate(((keys_ref, keys_hbm), (values_ref, values_hbm))):
             copies += [
                 pltpu.make_async_copy(
-                    before_hbm.at[which, :, column], ref.at[pl.ds(0, margin)], sems.at[which, 0]
+                    before_hbm[which].at[:, column], ref.at[pl.ds(0, margin)], sems.at[which, 0]
                 ),
                 pltpu.make_async_copy(
                     whole.at[:, column], ref.at[pl.ds(margin, tok_rows)], sems.at[which, 1]
                 ),
                 pltpu.make_async_copy(
-                    after_hbm.at[which, :, column],
+                    after_hbm[which].at[:, column],
                     ref.at[pl.ds(margin + tok_rows, margin)],
                     sems.at[which, 2],
                 ),
@@ -219,7 +219,7 @@
         grid_spec=pltpu.PrefetchScalarGridSpec(
             num_scalar_prefetch=2,
             grid=(heads, blk_dev),
-            in_specs=[tile, any_spec, any_spec, any_spec, any_spec],
+            in_specs=[tile] + [any_spec] * 6,
             out_specs=(tile, tile),
             scratch_shapes=[
                 pltpu.VMEM((ext, DH), jnp.bfloat16),
@@ -237,7 +237,7 @@
             bytes_accessed=30 * MIB,
         ),
         name="band",
-    )(meta, slopes, queries, key_rows, value_rows, before, after)
+    )(meta, slopes, queries, key_rows, value_rows, *before, *after)
 
 
 def gather_pieces(pieces, buffer_ref, sems, sources):
@@ -350,50 +350,56 @@
     )(meta, slots, far_blocks, slopes, queries, acc, stat, *pieces)
 
 
-def value_kernel(me_ref, slot_ref, weights_ref, acc_ref, *refs, sources, group):
-    pieces = refs[:-3]
-    out_ref, buffer_ref, sems = refs[-3:]
-    local = pl.program_id(0)
-
-    @pl.when(local == 0)
-    def _():
-        for copy in gather_pieces(pieces, buffer_ref, sems, sources):
-            copy.wait()
-
-    for part in range(group):
-        rows = pl.ds(part * BT, BT)
-        acc = acc_ref[rows, :]
+def value_kernel(me_ref, slot_ref, weights_hbm, acc_hbm, *refs, sources, blk_dev):
+    pieces = refs[:-7]
+    out_ref, weights_ref, acc_ref, buffer_ref, sems, weight_sems, acc_sems = refs[-7:]
+    copies = gather_pieces(pieces, buffer_ref, sems, sources)
+    rows = [pl.ds(i * BT, BT) for i in range(blk_dev)]
+    weight_copies = [
+        pltpu.make_async_copy(weights_hbm.at[r], weights_ref.at[r], weight_sems.at[i])
+        for i, r in enumerate(rows)
+    ]
+    acc_copies = [
+        pltpu.make_async_copy(acc_hbm.at[r], acc_ref.at[r], acc_sems.at[i])
+        for i, r in enumerate(rows)
+    ]
+    for weight_copy, acc_copy in zip(weight_copies, acc_copies):
+        weight_copy.start()
+        acc_copy.start()
+    for copy in copies:
+        copy.wait()
+    for i, r in enumerate(rows):
+        weight_copies[i].wait()
+        acc_copies[i].wait()
+        acc = acc_ref[r, :]
         for f in range(FAR):
-            source, rank = place_of(slot_ref[f, local * group + part], me_ref[0], sources, True)
-            acc = acc + weighted(
-                weights_ref[rows, f * BT : (f + 1) * BT], buffer_ref[source, rank]
-            )
-        out_ref[rows, :] = acc.astype(jnp.bfloat16)
+            source, rank = place_of(slot_ref[f, i], me_ref[0], sources, True)
+            acc = acc + weighted(weights_ref[r, f * BT : (f + 1) * BT], buffer_ref[source, rank])
+        out_ref[r, :] = acc.astype(jnp.bfloat16)
 
 
 def far_values(me, slots, weights, acc, pieces, sources):
     tok_rows = acc.shape[0]
     blk_dev = tok_rows // BT
-    group = 2 if blk_dev % 2 == 0 else 1
-    hbm = pl.BlockSpec(memory_space=pltpu.HBM)
+    any_spec = pl.BlockSpec(memory_space=pl.ANY)
     return pl.pallas_call(
-        functools.partial(value_kernel, sources=sources, group=group),
+        functools.partial(value_kernel, sources=sources, blk_dev=blk_dev),
         out_shape=jax.ShapeDtypeStruct((tok_rows, DH), jnp.bfloat16),
         grid_spec=pltpu.PrefetchScalarGridSpec(
             num_scalar_prefetch=2,
-            grid=(blk_dev // group,),
-            in_specs=[
-                pl.BlockSpec((group * BT, FAR * BT), lambda i, *_: (i, 0)),
-                pl.BlockSpec((group * BT, DH), lambda i, *_: (i, 0)),
-            ]
-            + [hbm] * len(pieces),
-            out_specs=pl.BlockSpec((group * BT, DH), lambda i, *_: (i, 0)),
+            grid=(1,),
+            in_specs=[any_spec] * (2 + len(pieces)),
+            out_specs=pl.BlockSpec((tok_rows, DH), lambda i, *_: (0, 0)),
             scratch_shapes=[
+                pltpu.VMEM(weights.shape, weights.dtype),
+                pltpu.VMEM(acc.shape, acc.dtype),
                 pltpu.VMEM((sources, CAP, BT, DH), jnp.bfloat16),
                 pltpu.SemaphoreType.DMA((sources,)),
+                pltpu.SemaphoreType.DMA((blk_dev,)),
+                pltpu.SemaphoreType.DMA((blk_dev,)),
             ],
         ),
-        compiler_params=pltpu.CompilerParams(vmem_limit_bytes=16 * MIB),
+        compiler_params=pltpu.CompilerParams(vmem_limit_bytes=20 * MIB),
         name="values",
     )(me, slots, weights, acc, *pieces)
 
@@ -457,13 +463,12 @@
     up = [(i, i + 1) for i in range(sources - 1)]
     down = [(i + 1, i) for i in range(sources - 1)]
 
+    before, after = [], []
+    for rows in (key_rows, value_rows):
+        before.append(lax.ppermute(rows[tok_rows - margin :], "seq", up))
+        after.append(lax.ppermute(rows[:margin], "seq", down))
     table, slots = route(far_list, sources)
     asked = lax.all_to_all(table, "seq", split_axis=0, concat_axis=0, tiled=True)
-    last = jnp.stack([key_rows[tok_rows - margin :], value_rows[tok_rows - margin :]])
-    first = jnp.stack([key_rows[:margin], value_rows[:margin]])
-    before = lax.ppermute(last, "seq", up)
-    after = lax.ppermute(first, "seq", down)
-
     me = myself[None].astype(jnp.int32)
     keys_hbm, values_hbm = (
         pltpu.with_memory_space_constraint(x, pltpu.HBM) for x in (key_rows, value_rows)
@@ -479,7 +484,7 @@
                 for shift in range(1, sources):
                     ring = [(i, (i + shift) % sources) for i in range(sources)]
                     arrays[shift] = lax.ppermute(arrays[shift], "seq", ring)
-                pieces.append(arrays)
+                pieces.append([pltpu.with_memory_space_constraint(x, pltpu.HBM) for x in arrays])
             incoming.append(pieces)
         else:
             incoming.append(

time: 389 us -> 378 us (0.972)
  the two profiles are of different devices: /device:TPU:40 before, /device:TPU:64 now
where the time goes in v4:
time: 378 us
  waiting for transfers between devices  157 us (42%)
  Pallas kernels  108 us (29%)
  starting transfers between devices  86.7 us (23%)
  blocking collectives  19.6 us (5%)
  local copies, waits for them, and re-layouts  4.75 us (1%)
    ppermute x30, waiting for transfers between devices, body(): arrays[shift] = lax.ppermute(arrays[shift], 'seq', ring)  146 us
    pallas_call x1, Pallas kernels, band_attention(): pl.pallas_call(functools.partial(band_kernel, blk_dev=blk_dev, total_bloc...  60.5 us
    ppermute x30, starting transfers between devices, body(): arrays[shift] = lax.ppermute(arrays[shift], 'seq', ring)  52.9 us
    pallas_call x2, Pallas kernels, far_attention(): pl.pallas_call(functools.partial(far_kernel, head=head, blk_dev=blk_dev,...  25.5 us
    all_to_all x1, blocking collectives, body(): lax.all_to_all(attended.reshape(lax.axis_size('head'), -1, DH), 'head', s...  19.6 us
    pallas_call x2, Pallas kernels, pack(): pl.pallas_call(functools.partial(pack_kernel, shifts=shifts), out_shape=o...  9.74 us
    all_to_all x1, starting transfers between devices, body(): lax.all_to_all(table, 'seq', split_axis=0, concat_axis=0, tiled=True)  9.16 us
    pallas_call x1, Pallas kernels, far_values(): pl.pallas_call(functools.partial(value_kernel, sources=sources, blk_dev=b...  8.2 us
  transfers between devices with their start and end apart: 37, of which 15 were waited for; matrix products, arithmetic and copies ran while one was open for 0% of the time, Pallas kernels for 26%

profile of v4, /device:TPU:64, one launch (start us, length us, event | category | flops | bytes accessed | tf_op | source)
XLA Modules:
  0.0 377.6 jit_solution(17696654240773424579)
XLA Ops:
  1.8 9.2 %all-to-all-start = ((s32[16,1,2]{2,1,0:T(1,128)}), s32[16,1,2]{2,1,0:T(1,128)S(1)}, u32[]{:S(2)}, u32[]{:S(2)}) async-start(s32[16,1,2]{2,1,0:T(1,128)} %bitcast.14), calls=%async_computation | async-start | bytes 16384 | tf_op jit(solution)/shard_map/all_to_all | solution.py:471
  10.9 6.2 %all-to-all-done = s32[16,1,2]{2,1,0:T(1,128)S(1)} async-done(((s32[16,1,2]{2,1,0:T(1,128)}), s32[16,1,2]{2,1,0:T(1,128)S(1)}, u32[]{:S(2)}, u32[]{:S(2)}) %all-to-all-start) | async-done | bytes 160 | tf_op jit(solution)/shard_map/all_to_all | solution.py:471
  17.1 4.7 %pack.2 = bf16[16,4,256,128]{3,2,1,0:T(8,128)(2,1)} custom-call(s32[16,2]{1,0:T(8,128)S(1)} %bitcast.9, s32[1]{0:T(128)} %bitcast.me_ref, bf16[3584,256]{1,0:T(8,128)(2,1)} %keys_ref.3, bf16[3584,256]{1,0:T(8,128)(2,1)} %values_ref.3), custom_call_target="tpu_custom_call" | custom-call | tf_op jit(solution)/shard_map/pack/pallas_call | solution.py:87
  21.8 6.6 %all-to-all-start.1 = ((bf16[16,4,256,128]{3,2,1,0:T(8,128)(2,1)}), bf16[16,4,256,128]{3,2,1,0:T(8,128)(2,1)}, u32[]{:S(2)}, u32[]{:S(2)}) async-start(bf16[16,4,256,128]{3,2,1,0:T(8,128)(2,1)} %pack.2), calls=%async_computation.1 | async-start | bytes 8388608 | tf_op jit(solution)/shard_map/all_to_all | solution.py:491
  28.5 5.1 %pack.3 = (bf16[2,256,128]{2,1,0:T(8,128)(2,1)}, bf16[2,256,128]{2,1,0:T(8,128)(2,1)}, bf16[2,256,128]{2,1,0:T(8,128)(2,1)}, bf16[2,256,128]{2,1,0:T(8,128)(2,1)...) custom-call(s32[16,2]{1,0:T(8,128)S(1)} %bitcast.10, ...), custom_call_target="tpu_custom_call" | custom-call | tf_op jit(solution)/shard_map/pack/pallas_call | solution.py:87
  38.2 3.5 collective-permute-start.13
  43.5 82.0 %collective-permute-done.10.refs_7_ = bf16[2,256,128]{2,1,0:T(8,128)(2,1)S(1)} collective-permute-done((bf16[2,256,128]{2,1,0:T(8,128)(2,1)}, bf16[2,256,128]{2,1,0:T(8,128)(2,1)S(1)}, u32[]{:S(2)}, u32[]{:S(2)}) %collective-permute-start.10) | collective-permute-done | bytes 131104 | tf_op jit(solution)/shard_map/ppermute | solution.py:486
  125.6 4.9 %collective-permute-start.15 = (bf16[2,256,128]{2,1,0:T(8,128)(2,1)}, bf16[2,256,128]{2,1,0:T(8,128)(2,1)S(1)}, u32[]{:S(2)}, u32[]{:S(2)}) collective-permute-start(bf16[2,256,128]{2,1,0:T(8,128)(2,1)} %get-tuple-element.59), channel_id=1, source_target_pairs={{0,192},{16,208},{32,224},{48,240},{64,0},{80,16},{96,32},{112,48}... | collective-permute-start | bytes 393224 | tf_op jit(solution)/shard_map/ppermute | solution.py:486
  132.7 7.4 %collective-permute-done.13.refs_10_ = bf16[2,256,128]{2,1,0:T(8,128)(2,1)S(1)} collective-permute-done((bf16[2,256,128]{2,1,0:T(8,128)(2,1)}, bf16[2,256,128]{2,1,0:T(8,128)(2,1)S(1)}, u32[]{:S(2)}, u32[]{:S(2)}) %collective-permute-start.13) | collective-permute-done | bytes 131104 | tf_op jit(solution)/shard_map/ppermute | solution.py:486
  140.1 2.8 collective-permute-done.14.refs_11_
  145.7 4.5 %collective-permute-start.5 = (bf16[2,256,128]{2,1,0:T(8,128)(2,1)}, bf16[2,256,128]{2,1,0:T(8,128)(2,1)S(1)}, u32[]{:S(2)}, u32[]{:S(2)}) collective-permute-start(bf16[2,256,128]{2,1,0:T(8,128)(2,1)} %get-tuple-element.49), channel_id=1, source_target_pairs={{0,32},{16,48},{32,64},{48,80},{64,96},{80,112},{96,128},{112,144}... | collective-permute-start | bytes 393224 | tf_op jit(solution)/shard_map/ppermute | solution.py:486
  150.2 4.6 %collective-permute-start.7 = (bf16[2,256,128]{2,1,0:T(8,128)(2,1)}, bf16[2,256,128]{2,1,0:T(8,128)(2,1)S(1)}, u32[]{:S(2)}, u32[]{:S(2)}) collective-permute-start(bf16[2,256,128]{2,1,0:T(8,128)(2,1)} %get-tuple-element.51), channel_id=1, source_target_pairs={{0,64},{16,80},{32,96},{48,112},{64,128},{80,144},{96,160},{112,17... | collective-permute-start | bytes 393224 | tf_op jit(solution)/shard_map/ppermute | solution.py:486
  154.8 4.9 %collective-permute-start.8 = (bf16[2,256,128]{2,1,0:T(8,128)(2,1)}, bf16[2,256,128]{2,1,0:T(8,128)(2,1)S(1)}, u32[]{:S(2)}, u32[]{:S(2)}) collective-permute-start(bf16[2,256,128]{2,1,0:T(8,128)(2,1)} %get-tuple-element.52), channel_id=1, source_target_pairs={{0,80},{16,96},{32,112},{48,128},{64,144},{80,160},{96,176},{112,1... | collective-permute-start | bytes 393224 | tf_op jit(solution)/shard_map/ppermute | solution.py:486
  159.7 3.8 collective-permute-start.9
  163.5 3.1 collective-permute-done.6.refs_3_
  166.6 3.3 collective-permute-start.20
  169.9 7.0 %collective-permute-done.7.refs_4_ = bf16[2,256,128]{2,1,0:T(8,128)(2,1)S(1)} collective-permute-done((bf16[2,256,128]{2,1,0:T(8,128)(2,1)}, bf16[2,256,128]{2,1,0:T(8,128)(2,1)S(1)}, u32[]{:S(2)}, u32[]{:S(2)}) %collective-permute-start.7) | collective-permute-done | bytes 131104 | tf_op jit(solution)/shard_map/ppermute | solution.py:486
  179.7 6.2 %collective-permute-start.23 = (bf16[2,256,128]{2,1,0:T(8,128)(2,1)}, bf16[2,256,128]{2,1,0:T(8,128)(2,1)S(1)}, u32[]{:S(2)}, u32[]{:S(2)}) collective-permute-start(bf16[2,256,128]{2,1,0:T(8,128)(2,1)} %get-tuple-element.70), channel_id=1, source_target_pairs={{0,80},{16,96},{32,112},{48,128},{64,144},{80,160},{96,176},{112,1... | collective-permute-start | bytes 393224 | tf_op jit(solution)/shard_map/ppermute | solution.py:486
  186.1 3.3 collective-permute-done.21.refs_3_
  189.6 8.4 %collective-permute-done.22.refs_4_ = bf16[2,256,128]{2,1,0:T(8,128)(2,1)S(1)} collective-permute-done((bf16[2,256,128]{2,1,0:T(8,128)(2,1)}, bf16[2,256,128]{2,1,0:T(8,128)(2,1)S(1)}, u32[]{:S(2)}, u32[]{:S(2)}) %collective-permute-start.22) | collective-permute-done | bytes 131104 | tf_op jit(solution)/shard_map/ppermute | solution.py:486
  202.3 4.0 %collective-permute-start.2 = (bf16[768,256]{1,0:T(8,128)(2,1)S(1)}, bf16[768,256]{1,0:T(8,128)(2,1)S(1)}, u32[]{:S(2)}, u32[]{:S(2)}) collective-permute-start(bf16[768,256]{1,0:T(8,128)(2,1)S(1)} %get-tuple-element.83), channel_id=1, source_target_pairs={{16,0},{32,16},{48,32},{64,48},{80,64},{96,80},{112,96},{128,112},... | collective-permute-start | bytes 1179656 | tf_op jit(solution)/shard_map/ppermute | solution.py:469
  206.3 3.4 collective-permute-start.3
  209.9 11.9 %collective-permute-done.27.refs_9_ = bf16[2,256,128]{2,1,0:T(8,128)(2,1)S(1)} collective-permute-done((bf16[2,256,128]{2,1,0:T(8,128)(2,1)S(1)}, bf16[2,256,128]{2,1,0:T(8,128)(2,1)S(1)}, u32[]{:S(2)}, u32[]{:S(2)}) %collective-permute-start.27) | collective-permute-done | bytes 131104 | tf_op jit(solution)/shard_map/ppermute | solution.py:486
  221.9 13.7 %collective-permute-done.28.refs_10_ = bf16[2,256,128]{2,1,0:T(8,128)(2,1)S(1)} collective-permute-done((bf16[2,256,128]{2,1,0:T(8,128)(2,1)S(1)}, bf16[2,256,128]{2,1,0:T(8,128)(2,1)S(1)}, u32[]{:S(2)}, u32[]{:S(2)}) %collective-permute-start.28) | collective-permute-done | bytes 131104 | tf_op jit(solution)/shard_map/ppermute | solution.py:486
  238.0 4.1 %collective-permute-start.31 = (bf16[2,256,128]{2,1,0:T(8,128)(2,1)S(1)}, bf16[2,256,128]{2,1,0:T(8,128)(2,1)S(1)}, u32[]{:S(2)}, u32[]{:S(2)}) collective-permute-start(bf16[2,256,128]{2,1,0:T(8,128)(2,1)S(1)} %copy-done.41), channel_id=1, source_target_pairs={{0,208},{16,224},{32,240},{48,0},{64,16},{80,32},{96,48},{112,64},... | collective-permute-start | bytes 393224 | tf_op jit(solution)/shard_map/ppermute | solution.py:486
  244.0 60.5 %band.1 = (f32[3584,256]{1,0:T(8,128)S(1)}, f32[3584,256]{1,0:T(8,128)S(1)}) custom-call(s32[15]{0:T(128)S(1)} %pad_add_fusion.meta_ref, f32[2]{0:T(128)S(1)} %copy-done.7, bf16[3584,256]{1,0:T(8,128)(2,1)S(1)} %copy-done.4, bf16[3584,256]{1,0:T(8,128)(2,1)S(1)} %copy-done.2, bf16[3584,256]{1,0:T(8,128)(2,1)S(1)} %copy-done.3, ...), custom_call_target="tpu_custom_call" | custom-call | flops 6576668672 | bytes 31457280 | tf_op jit(solution)/shard_map/band/pallas_call | solution.py:213
  308.5 14.4 %far.3 = (bf16[3584,512]{1,0:T(8,128)(2,1)S(1)}, f32[3584,128]{1,0:T(8,128)S(1)}) custom-call(s32[15]{0:T(128)S(1)} %pad_add_fusion.meta_ref, s32[2,14]{1,0:T(2,128)S(1)} %copy-done.5, s32[2,14]{1,0:T(2,128)S(1)} %bitcast.12, f32[2]{0:T(128)S(1)} %copy-done.7, bf16[3584,256]{1,0:T(8,128)(2,1)} %query_ref.5, f32[3584,256]{1,0:T(8,128)} %copy-done, ...), custom_call_target="tpu_custom_call" | custom-call | flops 939524096 | bytes 14680064 | tf_op jit(solution)/shard_map/far/pallas_call | solution.py:327
  323.8 8.2 %values.1 = bf16[3584,128]{1,0:T(8,128)(2,1)} custom-call(s32[1]{0:T(128)} %bitcast.me_ref, s32[2,14]{1,0:T(2,128)S(1)} %copy-done.5, bf16[3584,512]{1,0:T(8,128)(2,1)S(1)} %get-tuple-element.63.weights_hbm, f32[3584,128]{1,0:T(8,128)S(1)} %get-tuple-element.64.acc_hbm, bf16[2,256,128]{2,1,0:T(8,128)(2,1)} %get-tuple-element.65.refs_0_, ...), custom_call_target="tpu_custom_call" | custom-call | tf_op jit(solution)/shard_map/values/pallas_call | solution.py:385
  332.0 6.8 %all-to-all-start.3 = ((bf16[16,224,128]{2,1,0:T(8,128)(2,1)}), bf16[16,224,128]{2,1,0:T(8,128)(2,1)S(1)}, u32[]{:S(2)}, u32[]{:S(2)}) async-start(bf16[16,224,128]{2,1,0:T(8,128)(2,1)} %bitcast.5), calls=%async_computation.3 | async-start | bytes 1835008 | tf_op jit(solution)/shard_map/all_to_all | solution.py:513
  338.8 11.0 %far.2 = bf16[3584,128]{1,0:T(8,128)(2,1)S(1)} custom-call(s32[15]{0:T(128)S(1)} %pad_add_fusion.meta_ref, s32[2,14]{1,0:T(2,128)S(1)} %copy-done.5, s32[2,14]{1,0:T(2,128)S(1)} %bitcast.13, f32[2]{0:T(128)S(1)} %copy-done.7, bf16[3584,256]{1,0:T(8,128)(2,1)} %query_ref.5, f32[3584,256]{1,0:T(8,128)} %copy-done, f32[3584,256]{1,0:T(8,128)} %copy-done.1, ...), custom_call_target="tpu_custom_call" | custom-call | flops 939524096 | bytes 14680064 | tf_op jit(solution)/shard_map/far/pallas_call | solution.py:327
  349.8 5.5 %all-to-all-done.3.refs_1_ = bf16[16,224,128]{2,1,0:T(8,128)(2,1)S(1)} async-done(((bf16[16,224,128]{2,1,0:T(8,128)(2,1)}), bf16[16,224,128]{2,1,0:T(8,128)(2,1)S(1)}, u32[]{:S(2)}, u32[]{:S(2)}) %all-to-all-start.3) | async-done | bytes 917536 | tf_op jit(solution)/shard_map/all_to_all | solution.py:513
  355.3 19.6 %all_to_all.26.refs_0_ = bf16[16,224,128]{2,1,0:T(8,128)(2,1)} all-to-all(bf16[16,224,128]{2,1,0:T(8,128)(2,1)S(1)} %bitcast.8), channel_id=1, replica_groups=mesh['seq'=16,'head'=16] {'head'}, dimensions={0} | all-to-all | bytes 1835008 | tf_op jit(solution)/shard_map/all_to_all | solution.py:513
  (148 shorter events, 32.3 us)
Async XLA Ops:
  21.8 310.2 %all-to-all-start.1 = ((bf16[16,4,256,128]{3,2,1,0:T(8,128)(2,1)}), bf16[16,4,256,128]{3,2,1,0:T(8,128)(2,1)}, u32[]{:S(2)}, u32[]{:S(2)}) async-start(bf16[16,4,256,128]{3,2,1,0:T(8,128)(2,1)} %pack.2), calls=%async_computation.1 | async-start | bytes 8388608 | tf_op jit(solution)/shard_map/all_to_all | solution.py:491
  33.6 91.9 %collective-permute-start.10 = (bf16[2,256,128]{2,1,0:T(8,128)(2,1)}, bf16[2,256,128]{2,1,0:T(8,128)(2,1)S(1)}, u32[]{:S(2)}, u32[]{:S(2)}) collective-permute-start(bf16[2,256,128]{2,1,0:T(8,128)(2,1)} %get-tuple-element.54), channel_id=1, source_target_pairs={{0,112},{16,128},{32,144},{48,160},{64,176},{80,192},{96,208},{112... | collective-permute-start | bytes 393224 | tf_op jit(solution)/shard_map/ppermute | solution.py:486
  35.2 95.2 %collective-permute-start.11 = (bf16[2,256,128]{2,1,0:T(8,128)(2,1)}, bf16[2,256,128]{2,1,0:T(8,128)(2,1)S(1)}, u32[]{:S(2)}, u32[]{:S(2)}) collective-permute-start(bf16[2,256,128]{2,1,0:T(8,128)(2,1)} %get-tuple-element.55), channel_id=1, source_target_pairs={{0,128},{16,144},{32,160},{48,176},{64,192},{80,208},{96,224},{112... | collective-permute-start | bytes 393224 | tf_op jit(solution)/shard_map/ppermute | solution.py:486
  35.7 97.0 %collective-permute-start.12 = (bf16[2,256,128]{2,1,0:T(8,128)(2,1)}, bf16[2,256,128]{2,1,0:T(8,128)(2,1)S(1)}, u32[]{:S(2)}, u32[]{:S(2)}) collective-permute-start(bf16[2,256,128]{2,1,0:T(8,128)(2,1)} %get-tuple-element.56), channel_id=1, source_target_pairs={{0,144},{16,160},{32,176},{48,192},{64,208},{80,224},{96,240},{112... | collective-permute-start | bytes 393224 | tf_op jit(solution)/shard_map/ppermute | solution.py:486
  38.2 101.9 %collective-permute-start.13 = (bf16[2,256,128]{2,1,0:T(8,128)(2,1)}, bf16[2,256,128]{2,1,0:T(8,128)(2,1)S(1)}, u32[]{:S(2)}, u32[]{:S(2)}) collective-permute-start(bf16[2,256,128]{2,1,0:T(8,128)(2,1)} %get-tuple-element.57), channel_id=1, source_target_pairs={{0,160},{16,176},{32,192},{48,208},{64,224},{80,240},{96,0},{112,1... | collective-permute-start | bytes 393224 | tf_op jit(solution)/shard_map/ppermute | solution.py:486
  41.7 101.2 %collective-permute-start.14 = (bf16[2,256,128]{2,1,0:T(8,128)(2,1)}, bf16[2,256,128]{2,1,0:T(8,128)(2,1)S(1)}, u32[]{:S(2)}, u32[]{:S(2)}) collective-permute-start(bf16[2,256,128]{2,1,0:T(8,128)(2,1)} %get-tuple-element.58), channel_id=1, source_target_pairs={{0,176},{16,192},{32,208},{48,224},{64,240},{80,0},{96,16},{112,32... | collective-permute-start | bytes 393224 | tf_op jit(solution)/shard_map/ppermute | solution.py:486
  125.6 20.1 %collective-permute-start.15 = (bf16[2,256,128]{2,1,0:T(8,128)(2,1)}, bf16[2,256,128]{2,1,0:T(8,128)(2,1)S(1)}, u32[]{:S(2)}, u32[]{:S(2)}) collective-permute-start(bf16[2,256,128]{2,1,0:T(8,128)(2,1)} %get-tuple-element.59), channel_id=1, source_target_pairs={{0,192},{16,208},{32,224},{48,240},{64,0},{80,16},{96,32},{112,48}... | collective-permute-start | bytes 393224 | tf_op jit(solution)/shard_map/ppermute | solution.py:486
  130.5 19.7 %collective-permute-start.16 = (bf16[2,256,128]{2,1,0:T(8,128)(2,1)}, bf16[2,256,128]{2,1,0:T(8,128)(2,1)S(1)}, u32[]{:S(2)}, u32[]{:S(2)}) collective-permute-start(bf16[2,256,128]{2,1,0:T(8,128)(2,1)} %get-tuple-element.60), channel_id=1, source_target_pairs={{0,208},{16,224},{32,240},{48,0},{64,16},{80,32},{96,48},{112,64},... | collective-permute-start | bytes 393224 | tf_op jit(solution)/shard_map/ppermute | solution.py:486
  132.7 17.5 %collective-permute-start.17 = (bf16[2,256,128]{2,1,0:T(8,128)(2,1)}, bf16[2,256,128]{2,1,0:T(8,128)(2,1)S(1)}, u32[]{:S(2)}, u32[]{:S(2)}) collective-permute-start(bf16[2,256,128]{2,1,0:T(8,128)(2,1)} %get-tuple-element.61), channel_id=1, source_target_pairs={{0,224},{16,240},{32,0},{48,16},{64,32},{80,48},{96,64},{112,80},{... | collective-permute-start | bytes 393224 | tf_op jit(solution)/shard_map/ppermute | solution.py:486
  142.9 16.8 %collective-permute-start.4 = (bf16[2,256,128]{2,1,0:T(8,128)(2,1)}, bf16[2,256,128]{2,1,0:T(8,128)(2,1)S(1)}, u32[]{:S(2)}, u32[]{:S(2)}) collective-permute-start(bf16[2,256,128]{2,1,0:T(8,128)(2,1)} %get-tuple-element.48), channel_id=1, source_target_pairs={{0,16},{16,32},{32,48},{48,64},{64,80},{80,96},{96,112},{112,128},... | collective-permute-start | bytes 393224 | tf_op jit(solution)/shard_map/ppermute | solution.py:486
  145.7 17.8 %collective-permute-start.5 = (bf16[2,256,128]{2,1,0:T(8,128)(2,1)}, bf16[2,256,128]{2,1,0:T(8,128)(2,1)S(1)}, u32[]{:S(2)}, u32[]{:S(2)}) collective-permute-start(bf16[2,256,128]{2,1,0:T(8,128)(2,1)} %get-tuple-element.49), channel_id=1, source_target_pairs={{0,32},{16,48},{32,64},{48,80},{64,96},{80,112},{96,128},{112,144}... | collective-permute-start | bytes 393224 | tf_op jit(solution)/shard_map/ppermute | solution.py:486
  150.2 16.4 %collective-permute-start.6 = (bf16[2,256,128]{2,1,0:T(8,128)(2,1)}, bf16[2,256,128]{2,1,0:T(8,128)(2,1)S(1)}, u32[]{:S(2)}, u32[]{:S(2)}) collective-permute-start(bf16[2,256,128]{2,1,0:T(8,128)(2,1)} %get-tuple-element.50), channel_id=1, source_target_pairs={{0,48},{16,64},{32,80},{48,96},{64,112},{80,128},{96,144},{112,160... | collective-permute-start | bytes 393224 | tf_op jit(solution)/shard_map/ppermute | solution.py:486
  150.2 26.6 %collective-permute-start.7 = (bf16[2,256,128]{2,1,0:T(8,128)(2,1)}, bf16[2,256,128]{2,1,0:T(8,128)(2,1)S(1)}, u32[]{:S(2)}, u32[]{:S(2)}) collective-permute-start(bf16[2,256,128]{2,1,0:T(8,128)(2,1)} %get-tuple-element.51), channel_id=1, source_target_pairs={{0,64},{16,80},{32,96},{48,112},{64,128},{80,144},{96,160},{112,17... | collective-permute-start | bytes 393224 | tf_op jit(solution)/shard_map/ppermute | solution.py:486
  154.8 23.3 %collective-permute-start.8 = (bf16[2,256,128]{2,1,0:T(8,128)(2,1)}, bf16[2,256,128]{2,1,0:T(8,128)(2,1)S(1)}, u32[]{:S(2)}, u32[]{:S(2)}) collective-permute-start(bf16[2,256,128]{2,1,0:T(8,128)(2,1)} %get-tuple-element.52), channel_id=1, source_target_pairs={{0,80},{16,96},{32,112},{48,128},{64,144},{80,160},{96,176},{112,1... | collective-permute-start | bytes 393224 | tf_op jit(solution)/shard_map/ppermute | solution.py:486
  159.7 20.0 %collective-permute-start.9 = (bf16[2,256,128]{2,1,0:T(8,128)(2,1)}, bf16[2,256,128]{2,1,0:T(8,128)(2,1)S(1)}, u32[]{:S(2)}, u32[]{:S(2)}) collective-permute-start(bf16[2,256,128]{2,1,0:T(8,128)(2,1)} %get-tuple-element.53), channel_id=1, source_target_pairs={{0,96},{16,112},{32,128},{48,144},{64,160},{80,176},{96,192},{112,... | collective-permute-start | bytes 393224 | tf_op jit(solution)/shard_map/ppermute | solution.py:486
  163.5 22.4 %collective-permute-start.19 = (bf16[2,256,128]{2,1,0:T(8,128)(2,1)}, bf16[2,256,128]{2,1,0:T(8,128)(2,1)S(1)}, u32[]{:S(2)}, u32[]{:S(2)}) collective-permute-start(bf16[2,256,128]{2,1,0:T(8,128)(2,1)} %get-tuple-element.66), channel_id=1, source_target_pairs={{0,16},{16,32},{32,48},{48,64},{64,80},{80,96},{96,112},{112,128},... | collective-permute-start | bytes 393224 | tf_op jit(solution)/shard_map/ppermute | solution.py:486
  166.6 19.3 %collective-permute-start.20 = (bf16[2,256,128]{2,1,0:T(8,128)(2,1)}, bf16[2,256,128]{2,1,0:T(8,128)(2,1)S(1)}, u32[]{:S(2)}, u32[]{:S(2)}) collective-permute-start(bf16[2,256,128]{2,1,0:T(8,128)(2,1)} %get-tuple-element.67), channel_id=1, source_target_pairs={{0,32},{16,48},{32,64},{48,80},{64,96},{80,112},{96,128},{112,144}... | collective-permute-start | bytes 393224 | tf_op jit(solution)/shard_map/ppermute | solution.py:486
  178.1 19.9 %collective-permute-start.22 = (bf16[2,256,128]{2,1,0:T(8,128)(2,1)}, bf16[2,256,128]{2,1,0:T(8,128)(2,1)S(1)}, u32[]{:S(2)}, u32[]{:S(2)}) collective-permute-start(bf16[2,256,128]{2,1,0:T(8,128)(2,1)} %get-tuple-element.69), channel_id=1, source_target_pairs={{0,64},{16,80},{32,96},{48,112},{64,128},{80,144},{96,160},{112,17... | collective-permute-start | bytes 393224 | tf_op jit(solution)/shard_map/ppermute | solution.py:486
  179.7 20.2 %collective-permute-start.23 = (bf16[2,256,128]{2,1,0:T(8,128)(2,1)}, bf16[2,256,128]{2,1,0:T(8,128)(2,1)S(1)}, u32[]{:S(2)}, u32[]{:S(2)}) collective-permute-start(bf16[2,256,128]{2,1,0:T(8,128)(2,1)} %get-tuple-element.70), channel_id=1, source_target_pairs={{0,80},{16,96},{32,112},{48,128},{64,144},{80,160},{96,176},{112,1... | collective-permute-start | bytes 393224 | tf_op jit(solution)/shard_map/ppermute | solution.py:486
  185.9 16.4 %collective-permute-start.24 = (bf16[2,256,128]{2,1,0:T(8,128)(2,1)}, bf16[2,256,128]{2,1,0:T(8,128)(2,1)S(1)}, u32[]{:S(2)}, u32[]{:S(2)}) collective-permute-start(bf16[2,256,128]{2,1,0:T(8,128)(2,1)} %get-tuple-element.71), channel_id=1, source_target_pairs={{0,96},{16,112},{32,128},{48,144},{64,160},{80,176},{96,192},{112,... | collective-permute-start | bytes 393224 | tf_op jit(solution)/shard_map/ppermute | solution.py:486
  185.9 20.3 %collective-permute-start.25 = (bf16[2,256,128]{2,1,0:T(8,128)(2,1)}, bf16[2,256,128]{2,1,0:T(8,128)(2,1)S(1)}, u32[]{:S(2)}, u32[]{:S(2)}) collective-permute-start(bf16[2,256,128]{2,1,0:T(8,128)(2,1)} %get-tuple-element.72), channel_id=1, source_target_pairs={{0,112},{16,128},{32,144},{48,160},{64,176},{80,192},{96,208},{112... | collective-permute-start | bytes 393224 | tf_op jit(solution)/shard_map/ppermute | solution.py:486
  189.5 20.3 %collective-permute-start.26 = (bf16[2,256,128]{2,1,0:T(8,128)(2,1)}, bf16[2,256,128]{2,1,0:T(8,128)(2,1)S(1)}, u32[]{:S(2)}, u32[]{:S(2)}) collective-permute-start(bf16[2,256,128]{2,1,0:T(8,128)(2,1)} %get-tuple-element.73), channel_id=1, source_target_pairs={{0,128},{16,144},{32,160},{48,176},{64,192},{80,208},{96,224},{112... | collective-permute-start | bytes 393224 | tf_op jit(solution)/shard_map/ppermute | solution.py:486
  197.9 37.7 %collective-permute-start = (bf16[768,256]{1,0:T(8,128)(2,1)S(1)}, bf16[768,256]{1,0:T(8,128)(2,1)S(1)}, u32[]{:S(2)}, u32[]{:S(2)}) collective-permute-start(bf16[768,256]{1,0:T(8,128)(2,1)S(1)} %get-tuple-element.84), channel_id=1, source_target_pairs={{0,16},{16,32},{32,48},{48,64},{64,80},{80,96},{96,112},{112,128},... | collective-permute-start | bytes 1179656 | tf_op jit(solution)/shard_map/ppermute | solution.py:468
  199.9 38.1 %collective-permute-start.1 = (bf16[768,256]{1,0:T(8,128)(2,1)S(1)}, bf16[768,256]{1,0:T(8,128)(2,1)S(1)}, u32[]{:S(2)}, u32[]{:S(2)}) collective-permute-start(bf16[768,256]{1,0:T(8,128)(2,1)S(1)} %get-tuple-element.82), channel_id=1, source_target_pairs={{0,16},{16,32},{32,48},{48,64},{64,80},{80,96},{96,112},{112,128},... | collective-permute-start | bytes 1179656 | tf_op jit(solution)/shard_map/ppermute | solution.py:468
  202.3 39.9 %collective-permute-start.2 = (bf16[768,256]{1,0:T(8,128)(2,1)S(1)}, bf16[768,256]{1,0:T(8,128)(2,1)S(1)}, u32[]{:S(2)}, u32[]{:S(2)}) collective-permute-start(bf16[768,256]{1,0:T(8,128)(2,1)S(1)} %get-tuple-element.83), channel_id=1, source_target_pairs={{16,0},{32,16},{48,32},{64,48},{80,64},{96,80},{112,96},{128,112},... | collective-permute-start | bytes 1179656 | tf_op jit(solution)/shard_map/ppermute | solution.py:469
  206.3 35.9 %collective-permute-start.3 = (bf16[768,256]{1,0:T(8,128)(2,1)S(1)}, bf16[768,256]{1,0:T(8,128)(2,1)S(1)}, u32[]{:S(2)}, u32[]{:S(2)}) collective-permute-start(bf16[768,256]{1,0:T(8,128)(2,1)S(1)} %get-tuple-element.81), channel_id=1, source_target_pairs={{16,0},{32,16},{48,32},{64,48},{80,64},{96,80},{112,96},{128,112},... | collective-permute-start | bytes 1179656 | tf_op jit(solution)/shard_map/ppermute | solution.py:469
  235.6 87.3 %collective-permute-start.29 = (bf16[2,256,128]{2,1,0:T(8,128)(2,1)S(1)}, bf16[2,256,128]{2,1,0:T(8,128)(2,1)S(1)}, u32[]{:S(2)}, u32[]{:S(2)}) collective-permute-start(bf16[2,256,128]{2,1,0:T(8,128)(2,1)S(1)} %copy-done.43), channel_id=1, source_target_pairs={{0,176},{16,192},{32,208},{48,224},{64,240},{80,0},{96,16},{112,32... | collective-permute-start | bytes 393224 | tf_op jit(solution)/shard_map/ppermute | solution.py:486
  235.6 87.3 %collective-permute-start.30 = (bf16[2,256,128]{2,1,0:T(8,128)(2,1)S(1)}, bf16[2,256,128]{2,1,0:T(8,128)(2,1)S(1)}, u32[]{:S(2)}, u32[]{:S(2)}) collective-permute-start(bf16[2,256,128]{2,1,0:T(8,128)(2,1)S(1)} %copy-done.42), channel_id=1, source_target_pairs={{0,192},{16,208},{32,224},{48,240},{64,0},{80,16},{96,32},{112,48}... | collective-permute-start | bytes 393224 | tf_op jit(solution)/shard_map/ppermute | solution.py:486
  238.0 84.9 %collective-permute-start.31 = (bf16[2,256,128]{2,1,0:T(8,128)(2,1)S(1)}, bf16[2,256,128]{2,1,0:T(8,128)(2,1)S(1)}, u32[]{:S(2)}, u32[]{:S(2)}) collective-permute-start(bf16[2,256,128]{2,1,0:T(8,128)(2,1)S(1)} %copy-done.41), channel_id=1, source_target_pairs={{0,208},{16,224},{32,240},{48,0},{64,16},{80,32},{96,48},{112,64},... | collective-permute-start | bytes 393224 | tf_op jit(solution)/shard_map/ppermute | solution.py:486
  242.1 80.8 %collective-permute-start.32 = (bf16[2,256,128]{2,1,0:T(8,128)(2,1)S(1)}, bf16[2,256,128]{2,1,0:T(8,128)(2,1)S(1)}, u32[]{:S(2)}, u32[]{:S(2)}) collective-permute-start(bf16[2,256,128]{2,1,0:T(8,128)(2,1)S(1)} %copy-done.40), channel_id=1, source_target_pairs={{0,224},{16,240},{32,0},{48,16},{64,32},{80,48},{96,64},{112,80},{... | collective-permute-start | bytes 393224 | tf_op jit(solution)/shard_map/ppermute | solution.py:486
  242.2 80.8 %collective-permute-start.33 = (bf16[2,256,128]{2,1,0:T(8,128)(2,1)S(1)}, bf16[2,256,128]{2,1,0:T(8,128)(2,1)S(1)}, u32[]{:S(2)}, u32[]{:S(2)}) collective-permute-start(bf16[2,256,128]{2,1,0:T(8,128)(2,1)S(1)} %copy-done.39), channel_id=1, source_target_pairs={{0,240},{16,0},{32,16},{48,32},{64,48},{80,64},{96,80},{112,96},{1... | collective-permute-start | bytes 393224 | tf_op jit(solution)/shard_map/ppermute | solution.py:486
  332.0 23.3 %all-to-all-start.3 = ((bf16[16,224,128]{2,1,0:T(8,128)(2,1)}), bf16[16,224,128]{2,1,0:T(8,128)(2,1)S(1)}, u32[]{:S(2)}, u32[]{:S(2)}) async-start(bf16[16,224,128]{2,1,0:T(8,128)(2,1)} %bitcast.5), calls=%async_computation.3 | async-start | bytes 1835008 | tf_op jit(solution)/shard_map/all_to_all | solution.py:513
  (52 other events, 5820.9 us)

commit v5 on v3

--- a/solution.py
+++ b/solution.py
@@ -230,7 +230,7 @@
                 pltpu.SemaphoreType.DMA((2, 3)),
             ],
         ),
-        compiler_params=pltpu.CompilerParams(vmem_limit_bytes=24 * MIB),
+        compiler_params=pltpu.CompilerParams(vmem_limit_bytes=12 * MIB),
         cost_estimate=pl.CostEstimate(
             flops=7 * 4 * tok_rows * BT * channels,
             transcendentals=7 * tok_rows * BT * heads,
@@ -322,7 +322,10 @@
     out_shape = [jax.ShapeDtypeStruct((tok_rows, DH), jnp.float32 if split else jnp.bfloat16)]
     out_specs = [pl.BlockSpec((group * BT, DH), lambda i, *_: (i, 0))]
     if split:
-        out_shape.insert(0, jax.ShapeDtypeStruct((tok_rows, FAR * BT), jnp.bfloat16))
+        out_shape = [
+            pltpu.VMEM((tok_rows, FAR * BT), jnp.bfloat16),
+            pltpu.VMEM((tok_rows, DH), jnp.float32),
+        ]
         out_specs.insert(0, pl.BlockSpec((group * BT, FAR * BT), lambda i, *_: (i, 0)))
     return pl.pallas_call(
         functools.partial(
@@ -340,7 +343,7 @@
                 pltpu.SemaphoreType.DMA((sources,)),
             ],
         ),
-        compiler_params=pltpu.CompilerParams(vmem_limit_bytes=24 * MIB),
+        compiler_params=pltpu.CompilerParams(vmem_limit_bytes=12 * MIB),
         cost_estimate=pl.CostEstimate(
             flops=2 * 4 * tok_rows * BT * DH,
             transcendentals=2 * tok_rows * BT,
@@ -350,101 +353,65 @@
     )(meta, slots, far_blocks, slopes, queries, acc, stat, *pieces)
 
 
-def value_kernel(me_ref, slot_ref, weights_ref, acc_ref, *refs, sources, group):
-    pieces = refs[:-3]
-    out_ref, buffer_ref, sems = refs[-3:]
-    local = pl.program_id(0)
-
-    @pl.when(local == 0)
-    def _():
-        for copy in gather_pieces(pieces, buffer_ref, sems, sources):
-            copy.wait()
-
-    for part in range(group):
-        rows = pl.ds(part * BT, BT)
-        acc = acc_ref[rows, :]
+def value_kernel(me_ref, slot_ref, weights_ref, acc_ref, *refs, sources, blk_dev):
+    pieces = refs[:-2]
+    out_ref, buffer_ref = refs[-2:]
+    for s, piece in enumerate(pieces):
+        buffer_ref[s] = piece[...]
+    for i in range(blk_dev):
+        r = pl.ds(i * BT, BT)
+        acc = acc_ref[r, :]
         for f in range(FAR):
-            source, rank = place_of(slot_ref[f, local * group + part], me_ref[0], sources, True)
-            acc = acc + weighted(
-                weights_ref[rows, f * BT : (f + 1) * BT], buffer_ref[source, rank]
-            )
-        out_ref[rows, :] = acc.astype(jnp.bfloat16)
+            source, rank = place_of(slot_ref[f, i], me_ref[0], sources, True)
+            acc = acc + weighted(weights_ref[r, f * BT : (f + 1) * BT], buffer_ref[source, rank])
+        out_ref[r, :] = acc.astype(jnp.bfloat16)
 
 
 def far_values(me, slots, weights, acc, pieces, sources):
     tok_rows = acc.shape[0]
     blk_dev = tok_rows // BT
-    group = 2 if blk_dev % 2 == 0 else 1
-    hbm = pl.BlockSpec(memory_space=pltpu.HBM)
-    return pl.pallas_call(
-        functools.partial(value_kernel, sources=sources, group=group),
-        out_shape=jax.ShapeDtypeStruct((tok_rows, DH), jnp.bfloat16),
-        grid_spec=pltpu.PrefetchScalarGridSpec(
-            num_scalar_prefetch=2,
-            grid=(blk_dev // group,),
-            in_specs=[
-                pl.BlockSpec((group * BT, FAR * BT), lambda i, *_: (i, 0)),
-                pl.BlockSpec((group * BT, DH), lambda i, *_: (i, 0)),
-            ]
-            + [hbm] * len(pieces),
-            out_specs=pl.BlockSpec((group * BT, DH), lambda i, *_: (i, 0)),
-            scratch_shapes=[
-                pltpu.VMEM((sources, CAP, BT, DH), jnp.bfloat16),
-                pltpu.SemaphoreType.DMA((sources,)),
-            ],
-        ),
-        compiler_params=pltpu.CompilerParams(vmem_limit_bytes=16 * MIB),
+    smem = pl.BlockSpec(memory_space=pltpu.SMEM)
+    vmem = pl.BlockSpec(memory_space=pltpu.VMEM)
+    return pl.pallas_call(
+        functools.partial(value_kernel, sources=sources, blk_dev=blk_dev),
+        out_shape=pltpu.VMEM((tok_rows, DH), jnp.bfloat16),
+        in_specs=[smem, smem] + [vmem] * (2 + len(pieces)),
+        out_specs=vmem,
+        scratch_shapes=[pltpu.VMEM((sources, CAP, BT, DH), jnp.bfloat16)],
+        compiler_params=pltpu.CompilerParams(vmem_limit_bytes=4 * MIB),
         name="values",
     )(me, slots, weights, acc, *pieces)
 
 
 def place_kernel(*refs, heads):
     parts = refs[:heads]
-    out_ref, buffer_ref, in_sems, out_sems = refs[heads:]
+    out_ref, sems = refs[heads:]
     peers = parts[0].shape[0]
     width = heads * DH
-    loads = [
-        [
-            pltpu.make_async_copy(
-                part.at[g], buffer_ref.at[g, :, pl.ds(head * DH, DH)], in_sems.at[g, head]
-            )
-            for head, part in enumerate(parts)
-        ]
+    copies = [
+        pltpu.make_async_copy(
+            part.at[g], out_ref.at[:, pl.ds(g * width + head * DH, DH)], sems.at[g, head]
+        )
+        for head, part in enumerate(parts)
         for g in range(peers)
     ]
-    stores = [
-        pltpu.make_async_copy(
-            buffer_ref.at[g], out_ref.at[:, pl.ds(g * width, width)], out_sems.at[g]
-        )
-        for g in range(peers)
-    ]
-    for pair in loads:
-        for load in pair:
-            load.start()
-    for pair, store in zip(loads, stores):
-        for load in pair:
-            load.wait()
-        store.start()
-    for store in stores:
-        store.wait()
+    for copy in copies:
+        copy.start()
+    for copy in copies:
+        copy.wait()
 
 
 def place(parts):
     peers, rows, _ = parts[0].shape
     heads = len(parts)
-    any_spec = pl.BlockSpec(memory_space=pl.ANY)
     return pl.pallas_call(
         functools.partial(place_kernel, heads=heads),
         out_shape=jax.ShapeDtypeStruct((rows, peers * heads * DH), parts[0].dtype),
-        in_specs=[any_spec] * heads,
+        in_specs=[pl.BlockSpec(memory_space=pltpu.VMEM)] * heads,
         out_specs=pl.BlockSpec(memory_space=pltpu.HBM),
-        scratch_shapes=[
-            pltpu.VMEM((peers, rows, heads * DH), parts[0].dtype),
-            pltpu.SemaphoreType.DMA((peers, heads)),
-            pltpu.SemaphoreType.DMA((peers,)),
-        ],
+        scratch_shapes=[pltpu.SemaphoreType.DMA((peers, heads))],
         name="place",
-    )(*parts)
+    )(*(pltpu.with_memory_space_constraint(part, pltpu.VMEM) for part in parts))
 
 
 def body(queries, key_rows, value_rows, band_reach, far_list, slopes):
@@ -474,12 +441,13 @@
         outgoing = pack(asked, me, keys_hbm, values_hbm, head, split)
         if split:
             pieces = []
-            for which in range(2):
+            for which, kind in enumerate(("key", "value")):
                 arrays = list(outgoing[which * sources : (which + 1) * sources])
                 for shift in range(1, sources):
                     ring = [(i, (i + shift) % sources) for i in range(sources)]
                     arrays[shift] = lax.ppermute(arrays[shift], "seq", ring)
-                pieces.append(arrays)
+                space = pltpu.HBM if kind == "key" else pltpu.VMEM
+                pieces.append([pltpu.with_memory_space_constraint(x, space) for x in arrays])
             incoming.append(pieces)
         else:
             incoming.append(

time: 389 us -> 382 us (0.982)
  starting transfers between devices: 108 us -> 117 us
  waiting for transfers between devices: 149 us -> 141 us
  Pallas kernels: 107 us -> 99.3 us
    ppermute x30, starting transfers between devices: 79 us -> 87.7 us  [body(): arrays[shift] = lax.ppermute(arrays[shift], 'seq', ring)]
    ppermute x30, waiting for transfers between devices: 137 us -> 130 us  [body(): arrays[shift] = lax.ppermute(arrays[shift], 'seq', ring)]
    pallas_call x1, Pallas kernels: 7.58 us -> 2.74 us  [far_values(): pl.pallas_call(functools.partial(value_kernel, sources=sources, blk_dev=b...]
  transfers between devices with their start and end apart: 35 -> 35, of which waited for: 15 -> 14; matrix products, arithmetic and copies ran while one was open for 0% -> 0% of each run, Pallas kernels for 25% -> 24%
where the time goes in v5:
time: 382 us; the launch traced here: 381 us
  waiting for transfers between devices  141 us (37%)
  starting transfers between devices  117 us (31%)
  Pallas kernels  99.3 us (26%)
  blocking collectives  18.9 us (5%)
  local copies, waits for them, and re-layouts  4.01 us (1%)
    ppermute x30, waiting for transfers between devices, body(): arrays[shift] = lax.ppermute(arrays[shift], 'seq', ring)  130 us
    ppermute x30, starting transfers between devices, body(): arrays[shift] = lax.ppermute(arrays[shift], 'seq', ring)  87.7 us
    pallas_call x1, Pallas kernels, band_attention(): pl.pallas_call(functools.partial(band_kernel, blk_dev=blk_dev, total_bloc...  58.1 us
    pallas_call x2, Pallas kernels, far_attention(): pl.pallas_call(functools.partial(far_kernel, head=head, blk_dev=blk_dev,...  25.5 us
    all_to_all x1, blocking collectives, body(): lax.all_to_all(attended.reshape(lax.axis_size('head'), -1, DH), 'head', s...  18.9 us
    pallas_call x2, Pallas kernels, pack(): pl.pallas_call(functools.partial(pack_kernel, shifts=shifts), out_shape=o...  9.74 us
    all_to_all x1, starting transfers between devices, body(): lax.all_to_all(table, 'seq', split_axis=0, concat_axis=0, tiled=True)  9.5 us
  transfers between devices with their start and end apart: 35, of which 14 were waited for; matrix products, arithmetic and copies ran while one was open for 0% of the time, Pallas kernels for 24%

profile of v5, /device:TPU:40, one launch (start us, length us, event | category | flops | bytes accessed | tf_op | source)
XLA Modules:
  0.0 381.1 jit_solution(6626394222083734846)
XLA Ops:
  1.8 9.5 %all-to-all-start = ((s32[16,1,2]{2,1,0:T(1,128)}), s32[16,1,2]{2,1,0:T(1,128)S(1)}, u32[]{:S(2)}, u32[]{:S(2)}) async-start(s32[16,1,2]{2,1,0:T(1,128)} %bitcast.22), calls=%async_computation | async-start | bytes 16384 | tf_op jit(solution)/shard_map/all_to_all | solution.py:428
  11.3 6.2 %all-to-all-done = s32[16,1,2]{2,1,0:T(1,128)S(1)} async-done(((s32[16,1,2]{2,1,0:T(1,128)}), s32[16,1,2]{2,1,0:T(1,128)S(1)}, u32[]{:S(2)}, u32[]{:S(2)}) %all-to-all-start) | async-done | bytes 160 | tf_op jit(solution)/shard_map/all_to_all | solution.py:428
  17.5 4.7 %pack.2 = bf16[16,4,256,128]{3,2,1,0:T(8,128)(2,1)} custom-call(s32[16,2]{1,0:T(8,128)S(1)} %bitcast.17, s32[1]{0:T(128)} %bitcast.me_ref, bf16[3584,256]{1,0:T(8,128)(2,1)} %keys_ref.3, bf16[3584,256]{1,0:T(8,128)(2,1)} %values_ref.3), custom_call_target="tpu_custom_call" | custom-call | tf_op jit(solution)/shard_map/pack/pallas_call | solution.py:87
  22.2 6.7 %all-to-all-start.1 = ((bf16[16,4,256,128]{3,2,1,0:T(8,128)(2,1)}), bf16[16,4,256,128]{3,2,1,0:T(8,128)(2,1)}, u32[]{:S(2)}, u32[]{:S(2)}) async-start(bf16[16,4,256,128]{3,2,1,0:T(8,128)(2,1)} %pack.2), calls=%async_computation.1 | async-start | bytes 8388608 | tf_op jit(solution)/shard_map/all_to_all | solution.py:454
  28.9 5.1 %pack.3 = (bf16[2,256,128]{2,1,0:T(8,128)(2,1)}, bf16[2,256,128]{2,1,0:T(8,128)(2,1)}, bf16[2,256,128]{2,1,0:T(8,128)(2,1)}, bf16[2,256,128]{2,1,0:T(8,128)(2,1)...) custom-call(s32[16,2]{1,0:T(8,128)S(1)} %bitcast.18, ...), custom_call_target="tpu_custom_call" | custom-call | tf_op jit(solution)/shard_map/pack/pallas_call | solution.py:87
  35.9 4.6 %collective-permute-start.11 = (bf16[2,256,128]{2,1,0:T(8,128)(2,1)S(1)}, bf16[2,256,128]{2,1,0:T(8,128)(2,1)S(1)}, u32[]{:S(2)}, u32[]{:S(2)}) collective-permute-start(bf16[2,256,128]{2,1,0:T(8,128)(2,1)S(1)} %copy-done.52), channel_id=1, source_target_pairs={{0,160},{16,176},{32,192},{48,208},{64,224},{80,240},{96,0},{112,1... | collective-permute-start | bytes 393224 | tf_op jit(solution)/shard_map/ppermute | solution.py:448
  41.0 3.2 collective-permute-start.13
  45.8 79.2 %collective-permute-done.10.refs_9_ = bf16[2,256,128]{2,1,0:T(8,128)(2,1)S(1)} collective-permute-done((bf16[2,256,128]{2,1,0:T(8,128)(2,1)}, bf16[2,256,128]{2,1,0:T(8,128)(2,1)S(1)}, u32[]{:S(2)}, u32[]{:S(2)}) %collective-permute-start.10) | collective-permute-done | bytes 131104 | tf_op jit(solution)/shard_map/ppermute | solution.py:448
  127.6 3.2 collective-permute-done.11.refs_10_
  130.8 4.4 %collective-permute-start.1 = (bf16[2,768,256]{2,1,0:T(8,128)(2,1)S(1)}, bf16[2,768,256]{2,1,0:T(8,128)(2,1)S(1)}, u32[]{:S(2)}, u32[]{:S(2)}) collective-permute-start(bf16[2,768,256]{2,1,0:T(8,128)(2,1)S(1)} %pad_maximum_fusion.1), channel_id=1, source_target_pairs={{16,0},{32,16},{48,32},{64,48},{80,64},{96,80},{112,96},{128,112},... | collective-permute-start | bytes 2359304 | tf_op jit(solution)/shard_map/ppermute | solution.py:432
  135.3 3.9 %collective-permute-done.12.refs_11_ = bf16[2,256,128]{2,1,0:T(8,128)(2,1)S(1)} collective-permute-done((bf16[2,256,128]{2,1,0:T(8,128)(2,1)S(1)}, bf16[2,256,128]{2,1,0:T(8,128)(2,1)S(1)}, u32[]{:S(2)}, u32[]{:S(2)}) %collective-permute-start.12) | collective-permute-done | bytes 131104 | tf_op jit(solution)/shard_map/ppermute | solution.py:448
  139.2 3.6 collective-permute-start.16
  142.8 3.0 collective-permute-start.2
  146.0 6.4 %collective-permute-start.4 = (bf16[2,256,128]{2,1,0:T(8,128)(2,1)S(1)}, bf16[2,256,128]{2,1,0:T(8,128)(2,1)S(1)}, u32[]{:S(2)}, u32[]{:S(2)}) collective-permute-start(bf16[2,256,128]{2,1,0:T(8,128)(2,1)S(1)} %copy-done.44), channel_id=1, source_target_pairs={{0,48},{16,64},{32,80},{48,96},{64,112},{80,128},{96,144},{112,160... | collective-permute-start | bytes 393224 | tf_op jit(solution)/shard_map/ppermute | solution.py:448
  152.4 9.2 %collective-permute-done.16.refs_15_ = bf16[2,256,128]{2,1,0:T(8,128)(2,1)S(1)} collective-permute-done((bf16[2,256,128]{2,1,0:T(8,128)(2,1)S(1)}, bf16[2,256,128]{2,1,0:T(8,128)(2,1)S(1)}, u32[]{:S(2)}, u32[]{:S(2)}) %collective-permute-start.16) | collective-permute-done | bytes 131104 | tf_op jit(solution)/shard_map/ppermute | solution.py:448
  163.8 4.6 %collective-permute-start.5 = (bf16[2,256,128]{2,1,0:T(8,128)(2,1)S(1)}, bf16[2,256,128]{2,1,0:T(8,128)(2,1)S(1)}, u32[]{:S(2)}, u32[]{:S(2)}) collective-permute-start(bf16[2,256,128]{2,1,0:T(8,128)(2,1)S(1)} %copy-done.43), channel_id=1, source_target_pairs={{0,64},{16,80},{32,96},{48,112},{64,128},{80,144},{96,160},{112,17... | collective-permute-start | bytes 393224 | tf_op jit(solution)/shard_map/ppermute | solution.py:448
  168.4 4.7 %collective-permute-start.6 = (bf16[2,256,128]{2,1,0:T(8,128)(2,1)S(1)}, bf16[2,256,128]{2,1,0:T(8,128)(2,1)S(1)}, u32[]{:S(2)}, u32[]{:S(2)}) collective-permute-start(bf16[2,256,128]{2,1,0:T(8,128)(2,1)S(1)} %copy-done.42), channel_id=1, source_target_pairs={{0,80},{16,96},{32,112},{48,128},{64,144},{80,160},{96,176},{112,1... | collective-permute-start | bytes 393224 | tf_op jit(solution)/shard_map/ppermute | solution.py:448
  173.7 17.3 %collective-permute-start.8 = (bf16[2,256,128]{2,1,0:T(8,128)(2,1)S(1)}, bf16[2,256,128]{2,1,0:T(8,128)(2,1)S(1)}, u32[]{:S(2)}, u32[]{:S(2)}) collective-permute-start(bf16[2,256,128]{2,1,0:T(8,128)(2,1)S(1)} %copy-done.40), channel_id=1, source_target_pairs={{0,112},{16,128},{32,144},{48,160},{64,176},{80,192},{96,208},{112... | collective-permute-start | bytes 393224 | tf_op jit(solution)/shard_map/ppermute | solution.py:448
  195.2 3.0 collective-permute-done.8.refs_7_
  201.9 5.0 %collective-permute-start.20 = (bf16[2,256,128]{2,1,0:T(8,128)(2,1)S(1)}, bf16[2,256,128]{2,1,0:T(8,128)(2,1)S(1)}, u32[]{:S(2)}, u32[]{:S(2)}) collective-permute-start(bf16[2,256,128]{2,1,0:T(8,128)(2,1)S(1)} %copy-done.35), channel_id=1, source_target_pairs={{0,64},{16,80},{32,96},{48,112},{64,128},{80,144},{96,160},{112,17... | collective-permute-start | bytes 393224 | tf_op jit(solution)/shard_map/ppermute | solution.py:448
  206.9 11.6 %collective-permute-done.18.refs_2_ = bf16[2,256,128]{2,1,0:T(8,128)(2,1)S(1)} collective-permute-done((bf16[2,256,128]{2,1,0:T(8,128)(2,1)S(1)}, bf16[2,256,128]{2,1,0:T(8,128)(2,1)S(1)}, u32[]{:S(2)}, u32[]{:S(2)}) %collective-permute-start.18) | collective-permute-done | bytes 131104 | tf_op jit(solution)/shard_map/ppermute | solution.py:448
  221.3 10.2 %collective-permute-done.21.refs_5_ = bf16[2,256,128]{2,1,0:T(8,128)(2,1)S(1)} collective-permute-done((bf16[2,256,128]{2,1,0:T(8,128)(2,1)S(1)}, bf16[2,256,128]{2,1,0:T(8,128)(2,1)S(1)}, u32[]{:S(2)}, u32[]{:S(2)}) %collective-permute-start.21) | collective-permute-done | bytes 131104 | tf_op jit(solution)/shard_map/ppermute | solution.py:448
  234.9 2.8 collective-permute-done.24.refs_8_
  238.2 3.7 collective-permute-start.28
  241.9 5.4 %collective-permute-done.26.refs_10_ = bf16[2,256,128]{2,1,0:T(8,128)(2,1)S(1)} collective-permute-done((bf16[2,256,128]{2,1,0:T(8,128)(2,1)S(1)}, bf16[2,256,128]{2,1,0:T(8,128)(2,1)S(1)}, u32[]{:S(2)}, u32[]{:S(2)}) %collective-permute-start.26) | collective-permute-done | bytes 131104 | tf_op jit(solution)/shard_map/ppermute | solution.py:448
  247.3 11.0 %collective-permute-start.30 = (bf16[2,256,128]{2,1,0:T(8,128)(2,1)S(1)}, bf16[2,256,128]{2,1,0:T(8,128)(2,1)S(1)}, u32[]{:S(2)}, u32[]{:S(2)}) collective-permute-start(bf16[2,256,128]{2,1,0:T(8,128)(2,1)S(1)} %copy-done.25), channel_id=1, source_target_pairs={{0,224},{16,240},{32,0},{48,16},{64,32},{80,48},{96,64},{112,80},{... | collective-permute-start | bytes 393224 | tf_op jit(solution)/shard_map/ppermute | solution.py:448
  258.7 58.1 %band.1 = (f32[3584,256]{1,0:T(8,128)S(1)}, f32[3584,256]{1,0:T(8,128)S(1)}) custom-call(s32[15]{0:T(128)S(1)} %pad_add_fusion.meta_ref, f32[2]{0:T(128)S(1)} %copy-done.8, bf16[3584,256]{1,0:T(8,128)(2,1)S(1)} %copy-done.4, bf16[3584,256]{1,0:T(8,128)(2,1)S(1)} %copy-done.2, bf16[3584,256]{1,0:T(8,128)(2,1)S(1)} %copy-done.3, ...), custom_call_target="tpu_custom_call" | custom-call | flops 6576668672 | bytes 31457280 | tf_op jit(solution)/shard_map/band/pallas_call | solution.py:213
  320.7 14.4 %far.3 = (bf16[3584,512]{1,0:T(8,128)(2,1)S(1)}, f32[3584,128]{1,0:T(8,128)S(1)}) custom-call(s32[15]{0:T(128)S(1)} %pad_add_fusion.meta_ref, s32[2,14]{1,0:T(2,128)S(1)} %copy-done.6, s32[2,14]{1,0:T(2,128)S(1)} %bitcast.20, f32[2]{0:T(128)S(1)} %copy-done.8, bf16[3584,256]{1,0:T(8,128)(2,1)} %query_ref.5, f32[3584,256]{1,0:T(8,128)} %copy-done, ...), custom_call_target="tpu_custom_call" | custom-call | flops 939524096 | bytes 14680064 | tf_op jit(solution)/shard_map/far/pallas_call | solution.py:330
  337.9 6.1 %all-to-all-start.3 = ((bf16[16,224,128]{2,1,0:T(8,128)(2,1)}), bf16[16,224,128]{2,1,0:T(8,128)(2,1)S(1)}, u32[]{:S(2)}, u32[]{:S(2)}) async-start(bf16[16,224,128]{2,1,0:T(8,128)(2,1)} %bitcast.9), calls=%async_computation.3 | async-start | bytes 1835008 | tf_op jit(solution)/shard_map/all_to_all | solution.py:476
  344.1 11.0 %far.2 = bf16[3584,128]{1,0:T(8,128)(2,1)S(1)} custom-call(s32[15]{0:T(128)S(1)} %pad_add_fusion.meta_ref, s32[2,14]{1,0:T(2,128)S(1)} %copy-done.6, s32[2,14]{1,0:T(2,128)S(1)} %bitcast.21, f32[2]{0:T(128)S(1)} %copy-done.8, bf16[3584,256]{1,0:T(8,128)(2,1)} %query_ref.5, f32[3584,256]{1,0:T(8,128)} %copy-done, f32[3584,256]{1,0:T(8,128)} %copy-done.1, ...), custom_call_target="tpu_custom_call" | custom-call | flops 939524096 | bytes 14680064 | tf_op jit(solution)/shard_map/far/pallas_call | solution.py:330
  355.1 5.5 %all-to-all-done.3.refs_1_ = bf16[16,224,128]{2,1,0:T(8,128)(2,1)S(1)} async-done(((bf16[16,224,128]{2,1,0:T(8,128)(2,1)}), bf16[16,224,128]{2,1,0:T(8,128)(2,1)S(1)}, u32[]{:S(2)}, u32[]{:S(2)}) %all-to-all-start.3) | async-done | bytes 917536 | tf_op jit(solution)/shard_map/all_to_all | solution.py:476
  360.6 18.9 %all_to_all.26.refs_0_ = bf16[16,224,128]{2,1,0:T(8,128)(2,1)S(1)} all-to-all(bf16[16,224,128]{2,1,0:T(8,128)(2,1)S(1)} %bitcast.16), channel_id=1, replica_groups=mesh['seq'=16,'head'=16] {'head'}, dimensions={0} | all-to-all | bytes 1835008 | tf_op jit(solution)/shard_map/all_to_all | solution.py:476
  (159 shorter events, 33.8 us)
Async XLA Ops:
  1.8 15.7 %all-to-all-start = ((s32[16,1,2]{2,1,0:T(1,128)}), s32[16,1,2]{2,1,0:T(1,128)S(1)}, u32[]{:S(2)}, u32[]{:S(2)}) async-start(s32[16,1,2]{2,1,0:T(1,128)} %bitcast.22), calls=%async_computation | async-start | bytes 16384 | tf_op jit(solution)/shard_map/all_to_all | solution.py:428
  22.2 315.8 %all-to-all-start.1 = ((bf16[16,4,256,128]{3,2,1,0:T(8,128)(2,1)}), bf16[16,4,256,128]{3,2,1,0:T(8,128)(2,1)}, u32[]{:S(2)}, u32[]{:S(2)}) async-start(bf16[16,4,256,128]{3,2,1,0:T(8,128)(2,1)} %pack.2), calls=%async_computation.1 | async-start | bytes 8388608 | tf_op jit(solution)/shard_map/all_to_all | solution.py:454
  34.0 91.0 %collective-permute-start.10 = (bf16[2,256,128]{2,1,0:T(8,128)(2,1)}, bf16[2,256,128]{2,1,0:T(8,128)(2,1)S(1)}, u32[]{:S(2)}, u32[]{:S(2)}) collective-permute-start(bf16[2,256,128]{2,1,0:T(8,128)(2,1)} %get-tuple-element.56), channel_id=1, source_target_pairs={{0,144},{16,160},{32,176},{48,192},{64,208},{80,224},{96,240},{112... | collective-permute-start | bytes 393224 | tf_op jit(solution)/shard_map/ppermute | solution.py:448
  35.9 94.9 %collective-permute-start.11 = (bf16[2,256,128]{2,1,0:T(8,128)(2,1)S(1)}, bf16[2,256,128]{2,1,0:T(8,128)(2,1)S(1)}, u32[]{:S(2)}, u32[]{:S(2)}) collective-permute-start(bf16[2,256,128]{2,1,0:T(8,128)(2,1)S(1)} %copy-done.52), channel_id=1, source_target_pairs={{0,160},{16,176},{32,192},{48,208},{64,224},{80,240},{96,0},{112,1... | collective-permute-start | bytes 393224 | tf_op jit(solution)/shard_map/ppermute | solution.py:448
  40.5 98.7 %collective-permute-start.12 = (bf16[2,256,128]{2,1,0:T(8,128)(2,1)S(1)}, bf16[2,256,128]{2,1,0:T(8,128)(2,1)S(1)}, u32[]{:S(2)}, u32[]{:S(2)}) collective-permute-start(bf16[2,256,128]{2,1,0:T(8,128)(2,1)S(1)} %copy-done.51), channel_id=1, source_target_pairs={{0,176},{16,192},{32,208},{48,224},{64,240},{80,0},{96,16},{112,32... | collective-permute-start | bytes 393224 | tf_op jit(solution)/shard_map/ppermute | solution.py:448
  41.0 101.8 %collective-permute-start.13 = (bf16[2,256,128]{2,1,0:T(8,128)(2,1)S(1)}, bf16[2,256,128]{2,1,0:T(8,128)(2,1)S(1)}, u32[]{:S(2)}, u32[]{:S(2)}) collective-permute-start(bf16[2,256,128]{2,1,0:T(8,128)(2,1)S(1)} %copy-done.50), channel_id=1, source_target_pairs={{0,192},{16,208},{32,224},{48,240},{64,0},{80,16},{96,32},{112,48}... | collective-permute-start | bytes 393224 | tf_op jit(solution)/shard_map/ppermute | solution.py:448
  44.3 101.6 %collective-permute-start.14 = (bf16[2,256,128]{2,1,0:T(8,128)(2,1)S(1)}, bf16[2,256,128]{2,1,0:T(8,128)(2,1)S(1)}, u32[]{:S(2)}, u32[]{:S(2)}) collective-permute-start(bf16[2,256,128]{2,1,0:T(8,128)(2,1)S(1)} %copy-done.49), channel_id=1, source_target_pairs={{0,208},{16,224},{32,240},{48,0},{64,16},{80,32},{96,48},{112,64},... | collective-permute-start | bytes 393224 | tf_op jit(solution)/shard_map/ppermute | solution.py:448
  125.0 20.9 %collective-permute-start.15 = (bf16[2,256,128]{2,1,0:T(8,128)(2,1)S(1)}, bf16[2,256,128]{2,1,0:T(8,128)(2,1)S(1)}, u32[]{:S(2)}, u32[]{:S(2)}) collective-permute-start(bf16[2,256,128]{2,1,0:T(8,128)(2,1)S(1)} %copy-done.48), channel_id=1, source_target_pairs={{0,224},{16,240},{32,0},{48,16},{64,32},{80,48},{96,64},{112,80},{... | collective-permute-start | bytes 393224 | tf_op jit(solution)/shard_map/ppermute | solution.py:448
  130.8 116.5 %collective-permute-start.1 = (bf16[2,768,256]{2,1,0:T(8,128)(2,1)S(1)}, bf16[2,768,256]{2,1,0:T(8,128)(2,1)S(1)}, u32[]{:S(2)}, u32[]{:S(2)}) collective-permute-start(bf16[2,768,256]{2,1,0:T(8,128)(2,1)S(1)} %pad_maximum_fusion.1), channel_id=1, source_target_pairs={{16,0},{32,16},{48,32},{64,48},{80,64},{96,80},{112,96},{128,112},... | collective-permute-start | bytes 2359304 | tf_op jit(solution)/shard_map/ppermute | solution.py:432
  139.2 22.5 %collective-permute-start.16 = (bf16[2,256,128]{2,1,0:T(8,128)(2,1)S(1)}, bf16[2,256,128]{2,1,0:T(8,128)(2,1)S(1)}, u32[]{:S(2)}, u32[]{:S(2)}) collective-permute-start(bf16[2,256,128]{2,1,0:T(8,128)(2,1)S(1)} %copy-done.47), channel_id=1, source_target_pairs={{0,240},{16,0},{32,16},{48,32},{64,48},{80,64},{96,80},{112,96},{1... | collective-permute-start | bytes 393224 | tf_op jit(solution)/shard_map/ppermute | solution.py:448
  142.8 20.9 %collective-permute-start.2 = (bf16[2,256,128]{2,1,0:T(8,128)(2,1)S(1)}, bf16[2,256,128]{2,1,0:T(8,128)(2,1)S(1)}, u32[]{:S(2)}, u32[]{:S(2)}) collective-permute-start(bf16[2,256,128]{2,1,0:T(8,128)(2,1)S(1)} %copy-done.46), channel_id=1, source_target_pairs={{0,16},{16,32},{32,48},{48,64},{64,80},{80,96},{96,112},{112,128},... | collective-permute-start | bytes 393224 | tf_op jit(solution)/shard_map/ppermute | solution.py:448
  145.8 22.5 %collective-permute-start.3 = (bf16[2,256,128]{2,1,0:T(8,128)(2,1)S(1)}, bf16[2,256,128]{2,1,0:T(8,128)(2,1)S(1)}, u32[]{:S(2)}, u32[]{:S(2)}) collective-permute-start(bf16[2,256,128]{2,1,0:T(8,128)(2,1)S(1)} %copy-done.45), channel_id=1, source_target_pairs={{0,32},{16,48},{32,64},{48,80},{64,96},{80,112},{96,128},{112,144}... | collective-permute-start | bytes 393224 | tf_op jit(solution)/shard_map/ppermute | solution.py:448
  146.0 27.1 %collective-permute-start.4 = (bf16[2,256,128]{2,1,0:T(8,128)(2,1)S(1)}, bf16[2,256,128]{2,1,0:T(8,128)(2,1)S(1)}, u32[]{:S(2)}, u32[]{:S(2)}) collective-permute-start(bf16[2,256,128]{2,1,0:T(8,128)(2,1)S(1)} %copy-done.44), channel_id=1, source_target_pairs={{0,48},{16,64},{32,80},{48,96},{64,112},{80,128},{96,144},{112,160... | collective-permute-start | bytes 393224 | tf_op jit(solution)/shard_map/ppermute | solution.py:448
  161.6 96.7 %collective-permute-start = (bf16[2,768,256]{2,1,0:T(8,128)(2,1)S(1)}, bf16[2,768,256]{2,1,0:T(8,128)(2,1)S(1)}, u32[]{:S(2)}, u32[]{:S(2)}) collective-permute-start(bf16[2,768,256]{2,1,0:T(8,128)(2,1)S(1)} %pad_maximum_fusion), channel_id=1, source_target_pairs={{0,16},{16,32},{32,48},{48,64},{64,80},{80,96},{96,112},{112,128},... | collective-permute-start | bytes 2359304 | tf_op jit(solution)/shard_map/ppermute | solution.py:431
  163.8 10.0 %collective-permute-start.5 = (bf16[2,256,128]{2,1,0:T(8,128)(2,1)S(1)}, bf16[2,256,128]{2,1,0:T(8,128)(2,1)S(1)}, u32[]{:S(2)}, u32[]{:S(2)}) collective-permute-start(bf16[2,256,128]{2,1,0:T(8,128)(2,1)S(1)} %copy-done.43), channel_id=1, source_target_pairs={{0,64},{16,80},{32,96},{48,112},{64,128},{80,144},{96,160},{112,17... | collective-permute-start | bytes 393224 | tf_op jit(solution)/shard_map/ppermute | solution.py:448
  168.4 22.7 %collective-permute-start.6 = (bf16[2,256,128]{2,1,0:T(8,128)(2,1)S(1)}, bf16[2,256,128]{2,1,0:T(8,128)(2,1)S(1)}, u32[]{:S(2)}, u32[]{:S(2)}) collective-permute-start(bf16[2,256,128]{2,1,0:T(8,128)(2,1)S(1)} %copy-done.42), channel_id=1, source_target_pairs={{0,80},{16,96},{32,112},{48,128},{64,144},{80,160},{96,176},{112,1... | collective-permute-start | bytes 393224 | tf_op jit(solution)/shard_map/ppermute | solution.py:448
  173.1 20.4 %collective-permute-start.7 = (bf16[2,256,128]{2,1,0:T(8,128)(2,1)S(1)}, bf16[2,256,128]{2,1,0:T(8,128)(2,1)S(1)}, u32[]{:S(2)}, u32[]{:S(2)}) collective-permute-start(bf16[2,256,128]{2,1,0:T(8,128)(2,1)S(1)} %copy-done.41), channel_id=1, source_target_pairs={{0,96},{16,112},{32,128},{48,144},{64,160},{80,176},{96,192},{112,... | collective-permute-start | bytes 393224 | tf_op jit(solution)/shard_map/ppermute | solution.py:448
  173.7 24.5 %collective-permute-start.8 = (bf16[2,256,128]{2,1,0:T(8,128)(2,1)S(1)}, bf16[2,256,128]{2,1,0:T(8,128)(2,1)S(1)}, u32[]{:S(2)}, u32[]{:S(2)}) collective-permute-start(bf16[2,256,128]{2,1,0:T(8,128)(2,1)S(1)} %copy-done.40), channel_id=1, source_target_pairs={{0,112},{16,128},{32,144},{48,160},{64,176},{80,192},{96,208},{112... | collective-permute-start | bytes 393224 | tf_op jit(solution)/shard_map/ppermute | solution.py:448
  193.5 8.4 %collective-permute-start.17 = (bf16[2,256,128]{2,1,0:T(8,128)(2,1)S(1)}, bf16[2,256,128]{2,1,0:T(8,128)(2,1)S(1)}, u32[]{:S(2)}, u32[]{:S(2)}) collective-permute-start(bf16[2,256,128]{2,1,0:T(8,128)(2,1)S(1)} %copy-done.38), channel_id=1, source_target_pairs={{0,16},{16,32},{32,48},{48,64},{64,80},{80,96},{96,112},{112,128},... | collective-permute-start | bytes 393224 | tf_op jit(solution)/shard_map/ppermute | solution.py:448
  198.2 20.3 %collective-permute-start.18 = (bf16[2,256,128]{2,1,0:T(8,128)(2,1)S(1)}, bf16[2,256,128]{2,1,0:T(8,128)(2,1)S(1)}, u32[]{:S(2)}, u32[]{:S(2)}) collective-permute-start(bf16[2,256,128]{2,1,0:T(8,128)(2,1)S(1)} %copy-done.37), channel_id=1, source_target_pairs={{0,32},{16,48},{32,64},{48,80},{64,96},{80,112},{96,128},{112,144}... | collective-permute-start | bytes 393224 | tf_op jit(solution)/shard_map/ppermute | solution.py:448
  199.3 19.3 %collective-permute-start.19 = (bf16[2,256,128]{2,1,0:T(8,128)(2,1)S(1)}, bf16[2,256,128]{2,1,0:T(8,128)(2,1)S(1)}, u32[]{:S(2)}, u32[]{:S(2)}) collective-permute-start(bf16[2,256,128]{2,1,0:T(8,128)(2,1)S(1)} %copy-done.36), channel_id=1, source_target_pairs={{0,48},{16,64},{32,80},{48,96},{64,112},{80,128},{96,144},{112,160... | collective-permute-start | bytes 393224 | tf_op jit(solution)/shard_map/ppermute | solution.py:448
  201.9 19.0 %collective-permute-start.20 = (bf16[2,256,128]{2,1,0:T(8,128)(2,1)S(1)}, bf16[2,256,128]{2,1,0:T(8,128)(2,1)S(1)}, u32[]{:S(2)}, u32[]{:S(2)}) collective-permute-start(bf16[2,256,128]{2,1,0:T(8,128)(2,1)S(1)} %copy-done.35), channel_id=1, source_target_pairs={{0,64},{16,80},{32,96},{48,112},{64,128},{80,144},{96,160},{112,17... | collective-permute-start | bytes 393224 | tf_op jit(solution)/shard_map/ppermute | solution.py:448
  218.5 13.0 %collective-permute-start.21 = (bf16[2,256,128]{2,1,0:T(8,128)(2,1)S(1)}, bf16[2,256,128]{2,1,0:T(8,128)(2,1)S(1)}, u32[]{:S(2)}, u32[]{:S(2)}) collective-permute-start(bf16[2,256,128]{2,1,0:T(8,128)(2,1)S(1)} %copy-done.34), channel_id=1, source_target_pairs={{0,80},{16,96},{32,112},{48,128},{64,144},{80,160},{96,176},{112,1... | collective-permute-start | bytes 393224 | tf_op jit(solution)/shard_map/ppermute | solution.py:448
  218.5 13.0 %collective-permute-start.22 = (bf16[2,256,128]{2,1,0:T(8,128)(2,1)S(1)}, bf16[2,256,128]{2,1,0:T(8,128)(2,1)S(1)}, u32[]{:S(2)}, u32[]{:S(2)}) collective-permute-start(bf16[2,256,128]{2,1,0:T(8,128)(2,1)S(1)} %copy-done.33), channel_id=1, source_target_pairs={{0,96},{16,112},{32,128},{48,144},{64,160},{80,176},{96,192},{112,... | collective-permute-start | bytes 393224 | tf_op jit(solution)/shard_map/ppermute | solution.py:448
  220.9 12.6 %collective-permute-start.23 = (bf16[2,256,128]{2,1,0:T(8,128)(2,1)S(1)}, bf16[2,256,128]{2,1,0:T(8,128)(2,1)S(1)}, u32[]{:S(2)}, u32[]{:S(2)}) collective-permute-start(bf16[2,256,128]{2,1,0:T(8,128)(2,1)S(1)} %copy-done.32), channel_id=1, source_target_pairs={{0,112},{16,128},{32,144},{48,160},{64,176},{80,192},{96,208},{112... | collective-permute-start | bytes 393224 | tf_op jit(solution)/shard_map/ppermute | solution.py:448
  233.5 13.8 %collective-permute-start.26 = (bf16[2,256,128]{2,1,0:T(8,128)(2,1)S(1)}, bf16[2,256,128]{2,1,0:T(8,128)(2,1)S(1)}, u32[]{:S(2)}, u32[]{:S(2)}) collective-permute-start(bf16[2,256,128]{2,1,0:T(8,128)(2,1)S(1)} %copy-done.29), channel_id=1, source_target_pairs={{0,160},{16,176},{32,192},{48,208},{64,224},{80,240},{96,0},{112,1... | collective-permute-start | bytes 393224 | tf_op jit(solution)/shard_map/ppermute | solution.py:448
  237.7 97.4 %collective-permute-start.27 = (bf16[2,256,128]{2,1,0:T(8,128)(2,1)S(1)}, bf16[2,256,128]{2,1,0:T(8,128)(2,1)S(1)}, u32[]{:S(2)}, u32[]{:S(2)}) collective-permute-start(bf16[2,256,128]{2,1,0:T(8,128)(2,1)S(1)} %copy-done.28), channel_id=1, source_target_pairs={{0,176},{16,192},{32,208},{48,224},{64,240},{80,0},{96,16},{112,32... | collective-permute-start | bytes 393224 | tf_op jit(solution)/shard_map/ppermute | solution.py:448
  238.2 97.0 %collective-permute-start.28 = (bf16[2,256,128]{2,1,0:T(8,128)(2,1)S(1)}, bf16[2,256,128]{2,1,0:T(8,128)(2,1)S(1)}, u32[]{:S(2)}, u32[]{:S(2)}) collective-permute-start(bf16[2,256,128]{2,1,0:T(8,128)(2,1)S(1)} %copy-done.27), channel_id=1, source_target_pairs={{0,192},{16,208},{32,224},{48,240},{64,0},{80,16},{96,32},{112,48}... | collective-permute-start | bytes 393224 | tf_op jit(solution)/shard_map/ppermute | solution.py:448
  247.3 87.9 %collective-permute-start.29 = (bf16[2,256,128]{2,1,0:T(8,128)(2,1)S(1)}, bf16[2,256,128]{2,1,0:T(8,128)(2,1)S(1)}, u32[]{:S(2)}, u32[]{:S(2)}) collective-permute-start(bf16[2,256,128]{2,1,0:T(8,128)(2,1)S(1)} %copy-done.26), channel_id=1, source_target_pairs={{0,208},{16,224},{32,240},{48,0},{64,16},{80,32},{96,48},{112,64},... | collective-permute-start | bytes 393224 | tf_op jit(solution)/shard_map/ppermute | solution.py:448
  247.3 87.9 %collective-permute-start.30 = (bf16[2,256,128]{2,1,0:T(8,128)(2,1)S(1)}, bf16[2,256,128]{2,1,0:T(8,128)(2,1)S(1)}, u32[]{:S(2)}, u32[]{:S(2)}) collective-permute-start(bf16[2,256,128]{2,1,0:T(8,128)(2,1)S(1)} %copy-done.25), channel_id=1, source_target_pairs={{0,224},{16,240},{32,0},{48,16},{64,32},{80,48},{96,64},{112,80},{... | collective-permute-start | bytes 393224 | tf_op jit(solution)/shard_map/ppermute | solution.py:448
  258.4 76.8 %collective-permute-start.31 = (bf16[2,256,128]{2,1,0:T(8,128)(2,1)S(1)}, bf16[2,256,128]{2,1,0:T(8,128)(2,1)S(1)}, u32[]{:S(2)}, u32[]{:S(2)}) collective-permute-start(bf16[2,256,128]{2,1,0:T(8,128)(2,1)S(1)} %copy-done.24), channel_id=1, source_target_pairs={{0,240},{16,0},{32,16},{48,32},{64,48},{80,64},{96,80},{112,96},{1... | collective-permute-start | bytes 393224 | tf_op jit(solution)/shard_map/ppermute | solution.py:448
  337.9 22.7 %all-to-all-start.3 = ((bf16[16,224,128]{2,1,0:T(8,128)(2,1)}), bf16[16,224,128]{2,1,0:T(8,128)(2,1)S(1)}, u32[]{:S(2)}, u32[]{:S(2)}) async-start(bf16[16,224,128]{2,1,0:T(8,128)(2,1)} %bitcast.9), calls=%async_computation.3 | async-start | bytes 1835008 | tf_op jit(solution)/shard_map/all_to_all | solution.py:476
  (57 other events, 7210.7 us)

commit v6 on v5

--- a/solution.py
+++ b/solution.py
@@ -99,17 +99,20 @@
     )(asked, me, key_rows, value_rows)
 
 
-def distances():
+def fill_bias(bias_ref, slope):
     rows = lax.broadcasted_iota(jnp.int32, (BT, BT), 0)
     columns = lax.broadcasted_iota(jnp.int32, (BT, BT), 1)
-    return (rows - columns).astype(jnp.float32)
-
-
-def pair_scores(query, key, offset, slope, gap):
+    gap = (rows - columns).astype(jnp.float32) * slope
+    bias_ref[0] = gap
+    bias_ref[1] = -gap
+    bias_ref[2] = jnp.abs(gap)
+
+
+def pair_scores(query, key, bias):
     product = lax.dot_general(
         query, key, (((1,), (1,)), ((), ())), preferred_element_type=jnp.float32
     )
-    return product * (LOG2E / math.sqrt(DH)) - slope * jnp.abs(gap + offset)
+    return product * (LOG2E / math.sqrt(DH)) - bias
 
 
 def weighted(weights, value):
@@ -123,19 +126,16 @@
     return jnp.max(scores, axis=1, keepdims=True)
 
 
-def row_sum(scores):
-    return jnp.sum(scores, axis=1, keepdims=True)
-
-
 def band_kernel(
     meta_ref, slopes_ref, query_ref, keys_hbm, values_hbm, before_hbm, after_hbm,
     acc_ref, stat_ref,
-    keys_ref, values_ref, gap_ref, max_ref, sum_ref, sems, *, blk_dev, total_blocks,
+    keys_ref, values_ref, bias_ref, max_ref, acc_ref2, sems, *, blk_dev, total_blocks,
 ):
     head = pl.program_id(0)
     local = pl.program_id(1)
     margin = BAND * BT
     tok_rows = blk_dev * BT
+    slope = slopes_ref[head] * LOG2E
 
     @pl.when(local == 0)
     def _():
@@ -157,50 +157,47 @@
             ]
         for copy in copies:
             copy.start()
-        gap_ref[...] = distances()
+        fill_bias(bias_ref, slope)
         for copy in copies:
             copy.wait()
 
-    slope = slopes_ref[head] * LOG2E
     reach = meta_ref[local]
     block = meta_ref[blk_dev] * blk_dev + local
     query = query_ref[...]
+    ones = jnp.ones((BT, DH), jnp.bfloat16)
 
     def rows_of(offset):
         return pl.ds(pl.multiple_of((local + BAND + offset) * BT, BT), BT)
 
-    scores = pair_scores(query, keys_ref[rows_of(0), :], 0.0, slope, gap_ref[...])
+    def value_of(offset):
+        return jnp.concatenate([values_ref[rows_of(offset), :], ones], axis=1)
+
+    scores = pair_scores(query, keys_ref[rows_of(0), :], bias_ref[2])
     top = row_max(scores)
-    weights = jnp.exp2(scores - top)
     max_ref[...] = top
-    sum_ref[...] = row_sum(weights)
-    acc_ref[...] = weighted(weights, values_ref[rows_of(0), :])
+    acc_ref2[...] = weighted(jnp.exp2(scores - top), value_of(0))
 
     for distance in range(1, BAND + 1):
 
         @pl.when(reach >= distance)
         def _():
-            low = jnp.where(block >= distance, float(distance * BT), FAR_AWAY)
-            high = jnp.where(block + distance < total_blocks, -float(distance * BT), -FAR_AWAY)
-            gap = gap_ref[...]
-            first = pair_scores(query, keys_ref[rows_of(-distance), :], low, slope, gap)
-            second = pair_scores(query, keys_ref[rows_of(distance), :], high, slope, gap)
+            low = slope * jnp.where(block >= distance, float(distance * BT), FAR_AWAY)
+            high = slope * jnp.where(block + distance < total_blocks, float(distance * BT), FAR_AWAY)
+            first = pair_scores(query, keys_ref[rows_of(-distance), :], bias_ref[0])
+            second = pair_scores(query, keys_ref[rows_of(distance), :], bias_ref[1])
             old = max_ref[...]
-            top = jnp.maximum(old, row_max(jnp.maximum(first, second)))
+            top = jnp.maximum(old, jnp.maximum(row_max(first) - low, row_max(second) - high))
             shrink = jnp.exp2(old - top)
-            first = jnp.exp2(first - top)
-            second = jnp.exp2(second - top)
             max_ref[...] = top
-            sum_ref[...] = sum_ref[...] * shrink + row_sum(first + second)
-            acc_ref[...] = (
-                acc_ref[...] * shrink
-                + weighted(first, values_ref[rows_of(-distance), :])
-                + weighted(second, values_ref[rows_of(distance), :])
+            acc_ref2[...] = (
+                acc_ref2[...] * shrink
+                + weighted(jnp.exp2(first - (top + low)), value_of(-distance))
+                + weighted(jnp.exp2(second - (top + high)), value_of(distance))
             )
 
-    total = sum_ref[...]
-    acc_ref[...] = acc_ref[...] / total
-    stat_ref[...] = jnp.broadcast_to(max_ref[...] + jnp.log2(total), (BT, DH))
+    total = acc_ref2[:, DH:]
+    acc_ref[...] = acc_ref2[:, :DH] / total
+    stat_ref[...] = max_ref[...] + jnp.log2(total)
 
 
 def band_attention(meta, slopes, queries, key_rows, value_rows, before, after, total_blocks):
@@ -224,9 +221,9 @@
             scratch_shapes=[
                 pltpu.VMEM((ext, DH), jnp.bfloat16),
                 pltpu.VMEM((ext, DH), jnp.bfloat16),
-                pltpu.VMEM((BT, BT), jnp.float32),
+                pltpu.VMEM((3, BT, BT), jnp.float32),
                 pltpu.VMEM((BT, 1), jnp.float32),
-                pltpu.VMEM((BT, 1), jnp.float32),
+                pltpu.VMEM((BT, 2 * DH), jnp.float32),
                 pltpu.SemaphoreType.DMA((2, 3)),
             ],
         ),
@@ -265,51 +262,60 @@
     sources, group, split,
 ):
     if split:
-        pieces = refs[:-5]
-        weights_ref, out_ref, buffer_ref, gap_ref, sems = refs[-5:]
+        pieces = refs[:-6]
+        weights_ref, out_ref, scale_ref, buffer_ref, bias_ref, sems = refs[-6:]
     else:
         pieces = refs[:-4]
-        out_ref, buffer_ref, gap_ref, sems = refs[-4:]
+        out_ref, buffer_ref, bias_ref, sems = refs[-4:]
     local = pl.program_id(0)
+    slope = slopes_ref[head] * LOG2E
 
     @pl.when(local == 0)
     def _():
         copies = gather_pieces(pieces, buffer_ref, sems, sources)
-        gap_ref[...] = distances()
+        fill_bias(bias_ref, slope)
         for copy in copies:
             copy.wait()
 
-    slope = slopes_ref[head] * LOG2E
     me = meta_ref[blk_dev]
-    gap = gap_ref[...]
     ones = jnp.ones((BT, DH), jnp.bfloat16)
     for part in range(group):
         i = local * group + part
         rows = pl.ds(part * BT, BT)
         block = me * blk_dev + i
         query = query_ref[rows, :]
-        scores = []
-        values = []
+        scores, values, shifts = [], [], []
         for f in range(FAR):
-            offset = ((block - block_ref[f, i]) * BT).astype(jnp.float32)
+            apart = block - block_ref[f, i]
+            sign = jnp.where(apart > 0, 0, jnp.where(apart < 0, 1, 2))
+            shifts.append(slope * (jnp.abs(apart) * BT).astype(jnp.float32))
             source, rank = place_of(slot_ref[f, i], me, sources, split)
             key = buffer_ref[source, rank if split else rank * 2]
-            scores.append(pair_scores(query, key, offset, slope, gap))
-            if not split:
+            scores.append(pair_scores(query, key, bias_ref[sign]))
+            if split:
+                values.append(ones)
+            else:
                 values.append(jnp.concatenate([buffer_ref[source, rank * 2 + 1], ones], axis=1))
         band = stat_ref[rows, :]
-        top = jnp.maximum(band[:, 0:1], row_max(jnp.maximum(scores[0], scores[1])))
-        weights = [jnp.exp2(score - top) for score in scores]
+        top = jnp.maximum(
+            band[:, 0:1],
+            jnp.maximum(row_max(scores[0]) - shifts[0], row_max(scores[1]) - shifts[1]),
+        )
+        weights = [
+            jnp.exp2(score - (top + shift)).astype(jnp.bfloat16)
+            for score, shift in zip(scores, shifts)
+        ]
+        far = weighted(weights[0], values[0]) + weighted(weights[1], values[1])
         share = jnp.exp2(band - top)
+        scale = 1.0 / (share + far[:, -DH:])
+        acc = acc_ref[rows, :] * share
         if split:
-            scale = 1.0 / (share[:, 0:1] + row_sum(weights[0] + weights[1]))
             for f in range(FAR):
-                weights_ref[rows, f * BT : (f + 1) * BT] = (weights[f] * scale).astype(jnp.bfloat16)
-            out_ref[rows, :] = acc_ref[rows, :] * (share * scale)
+                weights_ref[rows, f * BT : (f + 1) * BT] = weights[f]
+            out_ref[rows, :] = acc
+            scale_ref[rows, :] = scale
         else:
-            far = weighted(weights[0], values[0]) + weighted(weights[1], values[1])
-            acc = acc_ref[rows, :] * share + far[:, :DH]
-            out_ref[rows, :] = (acc / (share + far[:, DH:])).astype(jnp.bfloat16)
+            out_ref[rows, :] = ((acc + far[:, :DH]) * scale).astype(jnp.bfloat16)
 
 
 def far_attention(meta, slots, far_blocks, slopes, queries, acc, stat, pieces, head, sources):
@@ -325,7 +331,9 @@
         out_shape = [
             pltpu.VMEM((tok_rows, FAR * BT), jnp.bfloat16),
             pltpu.VMEM((tok_rows, DH), jnp.float32),
+            pltpu.VMEM((tok_rows, DH), jnp.float32),
         ]
+        out_specs.append(out_specs[0])
         out_specs.insert(0, pl.BlockSpec((group * BT, FAR * BT), lambda i, *_: (i, 0)))
     return pl.pallas_call(
         functools.partial(
@@ -339,11 +347,11 @@
             out_specs=out_specs,
             scratch_shapes=[
                 pltpu.VMEM((sources, CAP if split else CAP * 2, BT, DH), jnp.bfloat16),
-                pltpu.VMEM((BT, BT), jnp.float32),
+                pltpu.VMEM((3, BT, BT), jnp.float32),
                 pltpu.SemaphoreType.DMA((sources,)),
             ],
         ),
-        compiler_params=pltpu.CompilerParams(vmem_limit_bytes=12 * MIB),
+        compiler_params=pltpu.CompilerParams(vmem_limit_bytes=14 * MIB),
         cost_estimate=pl.CostEstimate(
             flops=2 * 4 * tok_rows * BT * DH,
             transcendentals=2 * tok_rows * BT,
@@ -353,34 +361,38 @@
     )(meta, slots, far_blocks, slopes, queries, acc, stat, *pieces)
 
 
-def value_kernel(me_ref, slot_ref, weights_ref, acc_ref, *refs, sources, blk_dev):
-    pieces = refs[:-2]
-    out_ref, buffer_ref = refs[-2:]
-    for s, piece in enumerate(pieces):
-        buffer_ref[s] = piece[...]
+def value_kernel(me_ref, slot_ref, weights_ref, acc_ref, scale_ref, *refs, sources, blk_dev):
+    pieces = refs[:-3]
+    out_ref, buffer_ref, sems = refs[-3:]
+    for copy in gather_pieces(pieces, buffer_ref, sems, sources):
+        copy.wait()
     for i in range(blk_dev):
         r = pl.ds(i * BT, BT)
         acc = acc_ref[r, :]
         for f in range(FAR):
             source, rank = place_of(slot_ref[f, i], me_ref[0], sources, True)
             acc = acc + weighted(weights_ref[r, f * BT : (f + 1) * BT], buffer_ref[source, rank])
-        out_ref[r, :] = acc.astype(jnp.bfloat16)
-
-
-def far_values(me, slots, weights, acc, pieces, sources):
+        out_ref[r, :] = (acc * scale_ref[r, :]).astype(jnp.bfloat16)
+
+
+def far_values(me, slots, weights, acc, scale, pieces, sources):
     tok_rows = acc.shape[0]
     blk_dev = tok_rows // BT
     smem = pl.BlockSpec(memory_space=pltpu.SMEM)
     vmem = pl.BlockSpec(memory_space=pltpu.VMEM)
+    hbm = pl.BlockSpec(memory_space=pltpu.HBM)
     return pl.pallas_call(
         functools.partial(value_kernel, sources=sources, blk_dev=blk_dev),
         out_shape=pltpu.VMEM((tok_rows, DH), jnp.bfloat16),
-        in_specs=[smem, smem] + [vmem] * (2 + len(pieces)),
+        in_specs=[smem, smem] + [vmem] * 3 + [hbm] * len(pieces),
         out_specs=vmem,
-        scratch_shapes=[pltpu.VMEM((sources, CAP, BT, DH), jnp.bfloat16)],
+        scratch_shapes=[
+            pltpu.VMEM((sources, CAP, BT, DH), jnp.bfloat16),
+            pltpu.SemaphoreType.DMA((sources,)),
+        ],
         compiler_params=pltpu.CompilerParams(vmem_limit_bytes=4 * MIB),
         name="values",
-    )(me, slots, weights, acc, *pieces)
+    )(me, slots, weights, acc, scale, *pieces)
 
 
 def place_kernel(*refs, heads):
@@ -441,13 +453,12 @@
         outgoing = pack(asked, me, keys_hbm, values_hbm, head, split)
         if split:
             pieces = []
-            for which, kind in enumerate(("key", "value")):
+            for which in range(2):
                 arrays = list(outgoing[which * sources : (which + 1) * sources])
                 for shift in range(1, sources):
                     ring = [(i, (i + shift) % sources) for i in range(sources)]
                     arrays[shift] = lax.ppermute(arrays[shift], "seq", ring)
-                space = pltpu.HBM if kind == "key" else pltpu.VMEM
-                pieces.append([pltpu.with_memory_space_constraint(x, space) for x in arrays])
+                pieces.append([pltpu.with_memory_space_constraint(x, pltpu.HBM) for x in arrays])
             incoming.append(pieces)
         else:
             incoming.append(

time: 382 us -> 388 us (1.016)
  Pallas kernels: 99.3 us -> 106 us
  waiting for transfers between devices: 141 us -> 137 us
    pallas_call x1, Pallas kernels: 58.1 us -> 64.8 us  [band_attention(): pl.pallas_call(functools.partial(band_kernel, blk_dev=blk_dev, total_bloc...]
  transfers between devices with their start and end apart: 35 -> 35, of which waited for: 14 -> 14; matrix products, arithmetic and copies ran while one was open for 0% -> 0% of each run, Pallas kernels for 24% -> 25%
where the time goes in v6:
time: 388 us; the launch traced here: 387 us
  waiting for transfers between devices  137 us (35%)
  starting transfers between devices  119 us (31%)
  Pallas kernels  106 us (27%)
  blocking collectives  20 us (5%)
  local copies, waits for them, and re-layouts  4.85 us (1%)
    ppermute x30, waiting for transfers between devices, body(): arrays[shift] = lax.ppermute(arrays[shift], 'seq', ring)  128 us
    ppermute x30, starting transfers between devices, body(): arrays[shift] = lax.ppermute(arrays[shift], 'seq', ring)  89.7 us
    pallas_call x1, Pallas kernels, band_attention(): pl.pallas_call(functools.partial(band_kernel, blk_dev=blk_dev, total_bloc...  64.8 us
    pallas_call x2, Pallas kernels, far_attention(): pl.pallas_call(functools.partial(far_kernel, head=head, blk_dev=blk_dev,...  23.6 us
    all_to_all x1, blocking collectives, body(): lax.all_to_all(attended.reshape(lax.axis_size('head'), -1, DH), 'head', s...  20 us
    pallas_call x2, Pallas kernels, pack(): pl.pallas_call(functools.partial(pack_kernel, shifts=shifts), out_shape=o...  9.76 us
    all_to_all x1, starting transfers between devices, body(): lax.all_to_all(table, 'seq', split_axis=0, concat_axis=0, tiled=True)  9.5 us
  transfers between devices with their start and end apart: 35, of which 14 were waited for; matrix products, arithmetic and copies ran while one was open for 0% of the time, Pallas kernels for 25%

profile of v6, /device:TPU:40, one launch (start us, length us, event | category | flops | bytes accessed | tf_op | source)
XLA Modules:
  0.0 387.4 jit_solution(10305902251319982850)
XLA Ops:
  1.8 9.5 %all-to-all-start = ((s32[16,1,2]{2,1,0:T(1,128)}), s32[16,1,2]{2,1,0:T(1,128)S(1)}, u32[]{:S(2)}, u32[]{:S(2)}) async-start(s32[16,1,2]{2,1,0:T(1,128)} %bitcast.22), calls=%async_computation | async-start | bytes 16384 | tf_op jit(solution)/shard_map/all_to_all | solution.py:440
  11.3 6.2 %all-to-all-done = s32[16,1,2]{2,1,0:T(1,128)S(1)} async-done(((s32[16,1,2]{2,1,0:T(1,128)}), s32[16,1,2]{2,1,0:T(1,128)S(1)}, u32[]{:S(2)}, u32[]{:S(2)}) %all-to-all-start) | async-done | bytes 160 | tf_op jit(solution)/shard_map/all_to_all | solution.py:440
  17.5 4.7 %pack.2 = bf16[16,4,256,128]{3,2,1,0:T(8,128)(2,1)} custom-call(s32[16,2]{1,0:T(8,128)S(1)} %bitcast.17, s32[1]{0:T(128)} %bitcast.me_ref, bf16[3584,256]{1,0:T(8,128)(2,1)} %keys_ref.3, bf16[3584,256]{1,0:T(8,128)(2,1)} %values_ref.3), custom_call_target="tpu_custom_call" | custom-call | tf_op jit(solution)/shard_map/pack/pallas_call | solution.py:87
  22.2 6.6 %all-to-all-start.1 = ((bf16[16,4,256,128]{3,2,1,0:T(8,128)(2,1)}), bf16[16,4,256,128]{3,2,1,0:T(8,128)(2,1)}, u32[]{:S(2)}, u32[]{:S(2)}) async-start(bf16[16,4,256,128]{3,2,1,0:T(8,128)(2,1)} %pack.2), calls=%async_computation.1 | async-start | bytes 8388608 | tf_op jit(solution)/shard_map/all_to_all | solution.py:465
  28.8 5.1 %pack.3 = (bf16[2,256,128]{2,1,0:T(8,128)(2,1)}, bf16[2,256,128]{2,1,0:T(8,128)(2,1)}, bf16[2,256,128]{2,1,0:T(8,128)(2,1)}, bf16[2,256,128]{2,1,0:T(8,128)(2,1)...) custom-call(s32[16,2]{1,0:T(8,128)S(1)} %bitcast.18, ...), custom_call_target="tpu_custom_call" | custom-call | tf_op jit(solution)/shard_map/pack/pallas_call | solution.py:87
  35.9 4.6 %collective-permute-start.11 = (bf16[2,256,128]{2,1,0:T(8,128)(2,1)S(1)}, bf16[2,256,128]{2,1,0:T(8,128)(2,1)S(1)}, u32[]{:S(2)}, u32[]{:S(2)}) collective-permute-start(bf16[2,256,128]{2,1,0:T(8,128)(2,1)S(1)} %copy-done.66), channel_id=1, source_target_pairs={{0,160},{16,176},{32,192},{48,208},{64,224},{80,240},{96,0},{112,1... | collective-permute-start | bytes 393224 | tf_op jit(solution)/shard_map/ppermute | solution.py:460
  41.0 3.2 collective-permute-start.13
  45.8 79.2 %collective-permute-done.10.refs_9_ = bf16[2,256,128]{2,1,0:T(8,128)(2,1)S(1)} collective-permute-done((bf16[2,256,128]{2,1,0:T(8,128)(2,1)}, bf16[2,256,128]{2,1,0:T(8,128)(2,1)S(1)}, u32[]{:S(2)}, u32[]{:S(2)}) %collective-permute-start.10) | collective-permute-done | bytes 131104 | tf_op jit(solution)/shard_map/ppermute | solution.py:460
  127.6 3.2 collective-permute-done.11.refs_10_
  130.8 4.4 %collective-permute-start.1 = (bf16[2,768,256]{2,1,0:T(8,128)(2,1)S(1)}, bf16[2,768,256]{2,1,0:T(8,128)(2,1)S(1)}, u32[]{:S(2)}, u32[]{:S(2)}) collective-permute-start(bf16[2,768,256]{2,1,0:T(8,128)(2,1)S(1)} %pad_maximum_fusion.1), channel_id=1, source_target_pairs={{16,0},{32,16},{48,32},{64,48},{80,64},{96,80},{112,96},{128,112},... | collective-permute-start | bytes 2359304 | tf_op jit(solution)/shard_map/ppermute | solution.py:444
  135.2 3.9 %collective-permute-done.12.refs_11_ = bf16[2,256,128]{2,1,0:T(8,128)(2,1)S(1)} collective-permute-done((bf16[2,256,128]{2,1,0:T(8,128)(2,1)S(1)}, bf16[2,256,128]{2,1,0:T(8,128)(2,1)S(1)}, u32[]{:S(2)}, u32[]{:S(2)}) %collective-permute-start.12) | collective-permute-done | bytes 131104 | tf_op jit(solution)/shard_map/ppermute | solution.py:460
  139.2 3.6 collective-permute-start.16
  142.8 3.0 collective-permute-start.2
  145.9 6.4 %collective-permute-start.4 = (bf16[2,256,128]{2,1,0:T(8,128)(2,1)S(1)}, bf16[2,256,128]{2,1,0:T(8,128)(2,1)S(1)}, u32[]{:S(2)}, u32[]{:S(2)}) collective-permute-start(bf16[2,256,128]{2,1,0:T(8,128)(2,1)S(1)} %copy-done.58), channel_id=1, source_target_pairs={{0,48},{16,64},{32,80},{48,96},{64,112},{80,128},{96,144},{112,160... | collective-permute-start | bytes 393224 | tf_op jit(solution)/shard_map/ppermute | solution.py:460
  152.4 9.2 %collective-permute-done.16.refs_15_ = bf16[2,256,128]{2,1,0:T(8,128)(2,1)S(1)} collective-permute-done((bf16[2,256,128]{2,1,0:T(8,128)(2,1)S(1)}, bf16[2,256,128]{2,1,0:T(8,128)(2,1)S(1)}, u32[]{:S(2)}, u32[]{:S(2)}) %collective-permute-start.16) | collective-permute-done | bytes 131104 | tf_op jit(solution)/shard_map/ppermute | solution.py:460
  163.8 4.6 %collective-permute-start.5 = (bf16[2,256,128]{2,1,0:T(8,128)(2,1)S(1)}, bf16[2,256,128]{2,1,0:T(8,128)(2,1)S(1)}, u32[]{:S(2)}, u32[]{:S(2)}) collective-permute-start(bf16[2,256,128]{2,1,0:T(8,128)(2,1)S(1)} %copy-done.57), channel_id=1, source_target_pairs={{0,64},{16,80},{32,96},{48,112},{64,128},{80,144},{96,160},{112,17... | collective-permute-start | bytes 393224 | tf_op jit(solution)/shard_map/ppermute | solution.py:460
  168.3 4.7 %collective-permute-start.6 = (bf16[2,256,128]{2,1,0:T(8,128)(2,1)S(1)}, bf16[2,256,128]{2,1,0:T(8,128)(2,1)S(1)}, u32[]{:S(2)}, u32[]{:S(2)}) collective-permute-start(bf16[2,256,128]{2,1,0:T(8,128)(2,1)S(1)} %copy-done.56), channel_id=1, source_target_pairs={{0,80},{16,96},{32,112},{48,128},{64,144},{80,160},{96,176},{112,1... | collective-permute-start | bytes 393224 | tf_op jit(solution)/shard_map/ppermute | solution.py:460
  173.7 17.3 %collective-permute-start.8 = (bf16[2,256,128]{2,1,0:T(8,128)(2,1)S(1)}, bf16[2,256,128]{2,1,0:T(8,128)(2,1)S(1)}, u32[]{:S(2)}, u32[]{:S(2)}) collective-permute-start(bf16[2,256,128]{2,1,0:T(8,128)(2,1)S(1)} %copy-done.54), channel_id=1, source_target_pairs={{0,112},{16,128},{32,144},{48,160},{64,176},{80,192},{96,208},{112... | collective-permute-start | bytes 393224 | tf_op jit(solution)/shard_map/ppermute | solution.py:460
  195.1 3.0 collective-permute-done.8.refs_7_
  201.9 5.1 %collective-permute-start.20 = (bf16[2,256,128]{2,1,0:T(8,128)(2,1)S(1)}, bf16[2,256,128]{2,1,0:T(8,128)(2,1)S(1)}, u32[]{:S(2)}, u32[]{:S(2)}) collective-permute-start(bf16[2,256,128]{2,1,0:T(8,128)(2,1)S(1)} %copy-done.49), channel_id=1, source_target_pairs={{0,64},{16,80},{32,96},{48,112},{64,128},{80,144},{96,160},{112,17... | collective-permute-start | bytes 393224 | tf_op jit(solution)/shard_map/ppermute | solution.py:460
  206.9 11.5 %collective-permute-done.18.refs_2_ = bf16[2,256,128]{2,1,0:T(8,128)(2,1)S(1)} collective-permute-done((bf16[2,256,128]{2,1,0:T(8,128)(2,1)S(1)}, bf16[2,256,128]{2,1,0:T(8,128)(2,1)S(1)}, u32[]{:S(2)}, u32[]{:S(2)}) %collective-permute-start.18) | collective-permute-done | bytes 131104 | tf_op jit(solution)/shard_map/ppermute | solution.py:460
  221.3 10.0 %collective-permute-done.21.refs_5_ = bf16[2,256,128]{2,1,0:T(8,128)(2,1)S(1)} collective-permute-done((bf16[2,256,128]{2,1,0:T(8,128)(2,1)S(1)}, bf16[2,256,128]{2,1,0:T(8,128)(2,1)S(1)}, u32[]{:S(2)}, u32[]{:S(2)}) %collective-permute-start.21) | collective-permute-done | bytes 131104 | tf_op jit(solution)/shard_map/ppermute | solution.py:460
  238.3 3.6 collective-permute-start.28
  242.0 3.6 collective-permute-done.26.refs_10_
  247.6 10.8 %collective-permute-start.30 = (bf16[2,256,128]{2,1,0:T(8,128)(2,1)S(1)}, bf16[2,256,128]{2,1,0:T(8,128)(2,1)S(1)}, u32[]{:S(2)}, u32[]{:S(2)}) collective-permute-start(bf16[2,256,128]{2,1,0:T(8,128)(2,1)S(1)} %copy-done.39), channel_id=1, source_target_pairs={{0,224},{16,240},{32,0},{48,16},{64,32},{80,48},{96,64},{112,80},{... | collective-permute-start | bytes 393224 | tf_op jit(solution)/shard_map/ppermute | solution.py:460
  258.7 64.8 %band.1 = (f32[3584,256]{1,0:T(8,128)S(1)}, f32[3584,256]{1,0:T(8,128)S(1)}) custom-call(s32[15]{0:T(128)S(1)} %pad_add_fusion.meta_ref, f32[2]{0:T(128)S(1)} %copy-done.7, bf16[3584,256]{1,0:T(8,128)(2,1)S(1)} %copy-done.4, bf16[3584,256]{1,0:T(8,128)(2,1)S(1)} %copy-done.2, bf16[3584,256]{1,0:T(8,128)(2,1)S(1)} %copy-done.3, ...), custom_call_target="tpu_custom_call" | custom-call | flops 6576668672 | bytes 31457280 | tf_op jit(solution)/shard_map/band/pallas_call | solution.py:210
  327.5 10.4 %far.3 = (bf16[3584,512]{1,0:T(8,128)(2,1)S(1)}, f32[3584,128]{1,0:T(8,128)S(1)}, f32[3584,128]{1,0:T(8,128)S(1)}) custom-call(s32[15]{0:T(128)S(1)} %pad_add_fusion.meta_ref, s32[2,14]{1,0:T(2,128)S(1)} %copy-done.5, s32[2,14]{1,0:T(2,128)S(1)} %bitcast.20, f32[2]{0:T(128)S(1)} %copy-done.7, bf16[3584,256]{1,0:T(8,128)(2,1)} %query_ref.5, ...), custom_call_target="tpu_custom_call" | custom-call | flops 939524096 | bytes 14680064 | tf_op jit(solution)/shard_map/far/pallas_call | solution.py:338
  338.7 4.3 %values.1 = bf16[3584,128]{1,0:T(8,128)(2,1)} custom-call(s32[1]{0:T(128)} %bitcast.me_ref, s32[2,14]{1,0:T(2,128)S(1)} %copy-done.5, bf16[3584,512]{1,0:T(8,128)(2,1)S(1)} %get-tuple-element.64.weights_ref, f32[3584,128]{1,0:T(8,128)S(1)} %get-tuple-element.65.acc_ref, f32[3584,128]{1,0:T(8,128)S(1)} %get-tuple-element.66.scale_ref, ...), custom_call_target="tpu_custom_call" | custom-call | tf_op jit(solution)/shard_map/values/pallas_call | solution.py:384
  343.1 6.1 %all-to-all-start.3 = ((bf16[16,224,128]{2,1,0:T(8,128)(2,1)}), bf16[16,224,128]{2,1,0:T(8,128)(2,1)S(1)}, u32[]{:S(2)}, u32[]{:S(2)}) async-start(bf16[16,224,128]{2,1,0:T(8,128)(2,1)} %bitcast.9), calls=%async_computation.3 | async-start | bytes 1835008 | tf_op jit(solution)/shard_map/all_to_all | solution.py:487
  349.2 13.2 %far.2 = bf16[3584,128]{1,0:T(8,128)(2,1)S(1)} custom-call(s32[15]{0:T(128)S(1)} %pad_add_fusion.meta_ref, s32[2,14]{1,0:T(2,128)S(1)} %copy-done.5, s32[2,14]{1,0:T(2,128)S(1)} %bitcast.21, f32[2]{0:T(128)S(1)} %copy-done.7, bf16[3584,256]{1,0:T(8,128)(2,1)} %query_ref.5, f32[3584,256]{1,0:T(8,128)} %copy-done, f32[3584,256]{1,0:T(8,128)} %copy-done.1, ...), custom_call_target="tpu_custom_call" | custom-call | flops 939524096 | bytes 14680064 | tf_op jit(solution)/shard_map/far/pallas_call | solution.py:338
  362.4 3.4 all-to-all-done.3.refs_1_
  365.8 20.0 %all_to_all.26.refs_0_ = bf16[16,224,128]{2,1,0:T(8,128)(2,1)S(1)} all-to-all(bf16[16,224,128]{2,1,0:T(8,128)(2,1)S(1)} %bitcast.16), channel_id=1, replica_groups=mesh['seq'=16,'head'=16] {'head'}, dimensions={0} | all-to-all | bytes 1835008 | tf_op jit(solution)/shard_map/all_to_all | solution.py:487
  (187 shorter events, 37.1 us)
Async XLA Ops:
  1.8 15.7 %all-to-all-start = ((s32[16,1,2]{2,1,0:T(1,128)}), s32[16,1,2]{2,1,0:T(1,128)S(1)}, u32[]{:S(2)}, u32[]{:S(2)}) async-start(s32[16,1,2]{2,1,0:T(1,128)} %bitcast.22), calls=%async_computation | async-start | bytes 16384 | tf_op jit(solution)/shard_map/all_to_all | solution.py:440
  22.2 320.9 %all-to-all-start.1 = ((bf16[16,4,256,128]{3,2,1,0:T(8,128)(2,1)}), bf16[16,4,256,128]{3,2,1,0:T(8,128)(2,1)}, u32[]{:S(2)}, u32[]{:S(2)}) async-start(bf16[16,4,256,128]{3,2,1,0:T(8,128)(2,1)} %pack.2), calls=%async_computation.1 | async-start | bytes 8388608 | tf_op jit(solution)/shard_map/all_to_all | solution.py:465
  34.0 91.0 %collective-permute-start.10 = (bf16[2,256,128]{2,1,0:T(8,128)(2,1)}, bf16[2,256,128]{2,1,0:T(8,128)(2,1)S(1)}, u32[]{:S(2)}, u32[]{:S(2)}) collective-permute-start(bf16[2,256,128]{2,1,0:T(8,128)(2,1)} %get-tuple-element.57), channel_id=1, source_target_pairs={{0,144},{16,160},{32,176},{48,192},{64,208},{80,224},{96,240},{112... | collective-permute-start | bytes 393224 | tf_op jit(solution)/shard_map/ppermute | solution.py:460
  35.9 94.9 %collective-permute-start.11 = (bf16[2,256,128]{2,1,0:T(8,128)(2,1)S(1)}, bf16[2,256,128]{2,1,0:T(8,128)(2,1)S(1)}, u32[]{:S(2)}, u32[]{:S(2)}) collective-permute-start(bf16[2,256,128]{2,1,0:T(8,128)(2,1)S(1)} %copy-done.66), channel_id=1, source_target_pairs={{0,160},{16,176},{32,192},{48,208},{64,224},{80,240},{96,0},{112,1... | collective-permute-start | bytes 393224 | tf_op jit(solution)/shard_map/ppermute | solution.py:460
  40.5 98.7 %collective-permute-start.12 = (bf16[2,256,128]{2,1,0:T(8,128)(2,1)S(1)}, bf16[2,256,128]{2,1,0:T(8,128)(2,1)S(1)}, u32[]{:S(2)}, u32[]{:S(2)}) collective-permute-start(bf16[2,256,128]{2,1,0:T(8,128)(2,1)S(1)} %copy-done.65), channel_id=1, source_target_pairs={{0,176},{16,192},{32,208},{48,224},{64,240},{80,0},{96,16},{112,32... | collective-permute-start | bytes 393224 | tf_op jit(solution)/shard_map/ppermute | solution.py:460
  41.0 101.8 %collective-permute-start.13 = (bf16[2,256,128]{2,1,0:T(8,128)(2,1)S(1)}, bf16[2,256,128]{2,1,0:T(8,128)(2,1)S(1)}, u32[]{:S(2)}, u32[]{:S(2)}) collective-permute-start(bf16[2,256,128]{2,1,0:T(8,128)(2,1)S(1)} %copy-done.64), channel_id=1, source_target_pairs={{0,192},{16,208},{32,224},{48,240},{64,0},{80,16},{96,32},{112,48}... | collective-permute-start | bytes 393224 | tf_op jit(solution)/shard_map/ppermute | solution.py:460
  44.2 101.6 %collective-permute-start.14 = (bf16[2,256,128]{2,1,0:T(8,128)(2,1)S(1)}, bf16[2,256,128]{2,1,0:T(8,128)(2,1)S(1)}, u32[]{:S(2)}, u32[]{:S(2)}) collective-permute-start(bf16[2,256,128]{2,1,0:T(8,128)(2,1)S(1)} %copy-done.63), channel_id=1, source_target_pairs={{0,208},{16,224},{32,240},{48,0},{64,16},{80,32},{96,48},{112,64},... | collective-permute-start | bytes 393224 | tf_op jit(solution)/shard_map/ppermute | solution.py:460
  125.0 20.9 %collective-permute-start.15 = (bf16[2,256,128]{2,1,0:T(8,128)(2,1)S(1)}, bf16[2,256,128]{2,1,0:T(8,128)(2,1)S(1)}, u32[]{:S(2)}, u32[]{:S(2)}) collective-permute-start(bf16[2,256,128]{2,1,0:T(8,128)(2,1)S(1)} %copy-done.62), channel_id=1, source_target_pairs={{0,224},{16,240},{32,0},{48,16},{64,32},{80,48},{96,64},{112,80},{... | collective-permute-start | bytes 393224 | tf_op jit(solution)/shard_map/ppermute | solution.py:460
  130.8 116.8 %collective-permute-start.1 = (bf16[2,768,256]{2,1,0:T(8,128)(2,1)S(1)}, bf16[2,768,256]{2,1,0:T(8,128)(2,1)S(1)}, u32[]{:S(2)}, u32[]{:S(2)}) collective-permute-start(bf16[2,768,256]{2,1,0:T(8,128)(2,1)S(1)} %pad_maximum_fusion.1), channel_id=1, source_target_pairs={{16,0},{32,16},{48,32},{64,48},{80,64},{96,80},{112,96},{128,112},... | collective-permute-start | bytes 2359304 | tf_op jit(solution)/shard_map/ppermute | solution.py:444
  139.2 22.5 %collective-permute-start.16 = (bf16[2,256,128]{2,1,0:T(8,128)(2,1)S(1)}, bf16[2,256,128]{2,1,0:T(8,128)(2,1)S(1)}, u32[]{:S(2)}, u32[]{:S(2)}) collective-permute-start(bf16[2,256,128]{2,1,0:T(8,128)(2,1)S(1)} %copy-done.61), channel_id=1, source_target_pairs={{0,240},{16,0},{32,16},{48,32},{64,48},{80,64},{96,80},{112,96},{1... | collective-permute-start | bytes 393224 | tf_op jit(solution)/shard_map/ppermute | solution.py:460
  142.8 20.9 %collective-permute-start.2 = (bf16[2,256,128]{2,1,0:T(8,128)(2,1)S(1)}, bf16[2,256,128]{2,1,0:T(8,128)(2,1)S(1)}, u32[]{:S(2)}, u32[]{:S(2)}) collective-permute-start(bf16[2,256,128]{2,1,0:T(8,128)(2,1)S(1)} %copy-done.60), channel_id=1, source_target_pairs={{0,16},{16,32},{32,48},{48,64},{64,80},{80,96},{96,112},{112,128},... | collective-permute-start | bytes 393224 | tf_op jit(solution)/shard_map/ppermute | solution.py:460
  145.8 22.5 %collective-permute-start.3 = (bf16[2,256,128]{2,1,0:T(8,128)(2,1)S(1)}, bf16[2,256,128]{2,1,0:T(8,128)(2,1)S(1)}, u32[]{:S(2)}, u32[]{:S(2)}) collective-permute-start(bf16[2,256,128]{2,1,0:T(8,128)(2,1)S(1)} %copy-done.59), channel_id=1, source_target_pairs={{0,32},{16,48},{32,64},{48,80},{64,96},{80,112},{96,128},{112,144}... | collective-permute-start | bytes 393224 | tf_op jit(solution)/shard_map/ppermute | solution.py:460
  145.9 27.1 %collective-permute-start.4 = (bf16[2,256,128]{2,1,0:T(8,128)(2,1)S(1)}, bf16[2,256,128]{2,1,0:T(8,128)(2,1)S(1)}, u32[]{:S(2)}, u32[]{:S(2)}) collective-permute-start(bf16[2,256,128]{2,1,0:T(8,128)(2,1)S(1)} %copy-done.58), channel_id=1, source_target_pairs={{0,48},{16,64},{32,80},{48,96},{64,112},{80,128},{96,144},{112,160... | collective-permute-start | bytes 393224 | tf_op jit(solution)/shard_map/ppermute | solution.py:460
  161.6 96.8 %collective-permute-start = (bf16[2,768,256]{2,1,0:T(8,128)(2,1)S(1)}, bf16[2,768,256]{2,1,0:T(8,128)(2,1)S(1)}, u32[]{:S(2)}, u32[]{:S(2)}) collective-permute-start(bf16[2,768,256]{2,1,0:T(8,128)(2,1)S(1)} %pad_maximum_fusion), channel_id=1, source_target_pairs={{0,16},{16,32},{32,48},{48,64},{64,80},{80,96},{96,112},{112,128},... | collective-permute-start | bytes 2359304 | tf_op jit(solution)/shard_map/ppermute | solution.py:443
  163.8 10.0 %collective-permute-start.5 = (bf16[2,256,128]{2,1,0:T(8,128)(2,1)S(1)}, bf16[2,256,128]{2,1,0:T(8,128)(2,1)S(1)}, u32[]{:S(2)}, u32[]{:S(2)}) collective-permute-start(bf16[2,256,128]{2,1,0:T(8,128)(2,1)S(1)} %copy-done.57), channel_id=1, source_target_pairs={{0,64},{16,80},{32,96},{48,112},{64,128},{80,144},{96,160},{112,17... | collective-permute-start | bytes 393224 | tf_op jit(solution)/shard_map/ppermute | solution.py:460
  168.3 22.7 %collective-permute-start.6 = (bf16[2,256,128]{2,1,0:T(8,128)(2,1)S(1)}, bf16[2,256,128]{2,1,0:T(8,128)(2,1)S(1)}, u32[]{:S(2)}, u32[]{:S(2)}) collective-permute-start(bf16[2,256,128]{2,1,0:T(8,128)(2,1)S(1)} %copy-done.56), channel_id=1, source_target_pairs={{0,80},{16,96},{32,112},{48,128},{64,144},{80,160},{96,176},{112,1... | collective-permute-start | bytes 393224 | tf_op jit(solution)/shard_map/ppermute | solution.py:460
  173.0 20.4 %collective-permute-start.7 = (bf16[2,256,128]{2,1,0:T(8,128)(2,1)S(1)}, bf16[2,256,128]{2,1,0:T(8,128)(2,1)S(1)}, u32[]{:S(2)}, u32[]{:S(2)}) collective-permute-start(bf16[2,256,128]{2,1,0:T(8,128)(2,1)S(1)} %copy-done.55), channel_id=1, source_target_pairs={{0,96},{16,112},{32,128},{48,144},{64,160},{80,176},{96,192},{112,... | collective-permute-start | bytes 393224 | tf_op jit(solution)/shard_map/ppermute | solution.py:460
  173.7 24.5 %collective-permute-start.8 = (bf16[2,256,128]{2,1,0:T(8,128)(2,1)S(1)}, bf16[2,256,128]{2,1,0:T(8,128)(2,1)S(1)}, u32[]{:S(2)}, u32[]{:S(2)}) collective-permute-start(bf16[2,256,128]{2,1,0:T(8,128)(2,1)S(1)} %copy-done.54), channel_id=1, source_target_pairs={{0,112},{16,128},{32,144},{48,160},{64,176},{80,192},{96,208},{112... | collective-permute-start | bytes 393224 | tf_op jit(solution)/shard_map/ppermute | solution.py:460
  193.5 8.4 %collective-permute-start.17 = (bf16[2,256,128]{2,1,0:T(8,128)(2,1)S(1)}, bf16[2,256,128]{2,1,0:T(8,128)(2,1)S(1)}, u32[]{:S(2)}, u32[]{:S(2)}) collective-permute-start(bf16[2,256,128]{2,1,0:T(8,128)(2,1)S(1)} %copy-done.52), channel_id=1, source_target_pairs={{0,16},{16,32},{32,48},{48,64},{64,80},{80,96},{96,112},{112,128},... | collective-permute-start | bytes 393224 | tf_op jit(solution)/shard_map/ppermute | solution.py:460
  198.2 20.2 %collective-permute-start.18 = (bf16[2,256,128]{2,1,0:T(8,128)(2,1)S(1)}, bf16[2,256,128]{2,1,0:T(8,128)(2,1)S(1)}, u32[]{:S(2)}, u32[]{:S(2)}) collective-permute-start(bf16[2,256,128]{2,1,0:T(8,128)(2,1)S(1)} %copy-done.51), channel_id=1, source_target_pairs={{0,32},{16,48},{32,64},{48,80},{64,96},{80,112},{96,128},{112,144}... | collective-permute-start | bytes 393224 | tf_op jit(solution)/shard_map/ppermute | solution.py:460
  199.2 19.2 %collective-permute-start.19 = (bf16[2,256,128]{2,1,0:T(8,128)(2,1)S(1)}, bf16[2,256,128]{2,1,0:T(8,128)(2,1)S(1)}, u32[]{:S(2)}, u32[]{:S(2)}) collective-permute-start(bf16[2,256,128]{2,1,0:T(8,128)(2,1)S(1)} %copy-done.50), channel_id=1, source_target_pairs={{0,48},{16,64},{32,80},{48,96},{64,112},{80,128},{96,144},{112,160... | collective-permute-start | bytes 393224 | tf_op jit(solution)/shard_map/ppermute | solution.py:460
  201.9 19.0 %collective-permute-start.20 = (bf16[2,256,128]{2,1,0:T(8,128)(2,1)S(1)}, bf16[2,256,128]{2,1,0:T(8,128)(2,1)S(1)}, u32[]{:S(2)}, u32[]{:S(2)}) collective-permute-start(bf16[2,256,128]{2,1,0:T(8,128)(2,1)S(1)} %copy-done.49), channel_id=1, source_target_pairs={{0,64},{16,80},{32,96},{48,112},{64,128},{80,144},{96,160},{112,17... | collective-permute-start | bytes 393224 | tf_op jit(solution)/shard_map/ppermute | solution.py:460
  218.5 12.8 %collective-permute-start.21 = (bf16[2,256,128]{2,1,0:T(8,128)(2,1)S(1)}, bf16[2,256,128]{2,1,0:T(8,128)(2,1)S(1)}, u32[]{:S(2)}, u32[]{:S(2)}) collective-permute-start(bf16[2,256,128]{2,1,0:T(8,128)(2,1)S(1)} %copy-done.48), channel_id=1, source_target_pairs={{0,80},{16,96},{32,112},{48,128},{64,144},{80,160},{96,176},{112,1... | collective-permute-start | bytes 393224 | tf_op jit(solution)/shard_map/ppermute | solution.py:460
  218.5 12.8 %collective-permute-start.22 = (bf16[2,256,128]{2,1,0:T(8,128)(2,1)S(1)}, bf16[2,256,128]{2,1,0:T(8,128)(2,1)S(1)}, u32[]{:S(2)}, u32[]{:S(2)}) collective-permute-start(bf16[2,256,128]{2,1,0:T(8,128)(2,1)S(1)} %copy-done.47), channel_id=1, source_target_pairs={{0,96},{16,112},{32,128},{48,144},{64,160},{80,176},{96,192},{112,... | collective-permute-start | bytes 393224 | tf_op jit(solution)/shard_map/ppermute | solution.py:460
  220.9 12.6 %collective-permute-start.23 = (bf16[2,256,128]{2,1,0:T(8,128)(2,1)S(1)}, bf16[2,256,128]{2,1,0:T(8,128)(2,1)S(1)}, u32[]{:S(2)}, u32[]{:S(2)}) collective-permute-start(bf16[2,256,128]{2,1,0:T(8,128)(2,1)S(1)} %copy-done.46), channel_id=1, source_target_pairs={{0,112},{16,128},{32,144},{48,160},{64,176},{80,192},{96,208},{112... | collective-permute-start | bytes 393224 | tf_op jit(solution)/shard_map/ppermute | solution.py:460
  233.5 12.0 %collective-permute-start.26 = (bf16[2,256,128]{2,1,0:T(8,128)(2,1)S(1)}, bf16[2,256,128]{2,1,0:T(8,128)(2,1)S(1)}, u32[]{:S(2)}, u32[]{:S(2)}) collective-permute-start(bf16[2,256,128]{2,1,0:T(8,128)(2,1)S(1)} %copy-done.43), channel_id=1, source_target_pairs={{0,160},{16,176},{32,192},{48,208},{64,224},{80,240},{96,0},{112,1... | collective-permute-start | bytes 393224 | tf_op jit(solution)/shard_map/ppermute | solution.py:460
  237.4 100.5 %collective-permute-start.27 = (bf16[2,256,128]{2,1,0:T(8,128)(2,1)S(1)}, bf16[2,256,128]{2,1,0:T(8,128)(2,1)S(1)}, u32[]{:S(2)}, u32[]{:S(2)}) collective-permute-start(bf16[2,256,128]{2,1,0:T(8,128)(2,1)S(1)} %copy-done.42), channel_id=1, source_target_pairs={{0,176},{16,192},{32,208},{48,224},{64,240},{80,0},{96,16},{112,32... | collective-permute-start | bytes 393224 | tf_op jit(solution)/shard_map/ppermute | solution.py:460
  238.3 99.5 %collective-permute-start.28 = (bf16[2,256,128]{2,1,0:T(8,128)(2,1)S(1)}, bf16[2,256,128]{2,1,0:T(8,128)(2,1)S(1)}, u32[]{:S(2)}, u32[]{:S(2)}) collective-permute-start(bf16[2,256,128]{2,1,0:T(8,128)(2,1)S(1)} %copy-done.41), channel_id=1, source_target_pairs={{0,192},{16,208},{32,224},{48,240},{64,0},{80,16},{96,32},{112,48}... | collective-permute-start | bytes 393224 | tf_op jit(solution)/shard_map/ppermute | solution.py:460
  245.5 92.4 %collective-permute-start.29 = (bf16[2,256,128]{2,1,0:T(8,128)(2,1)S(1)}, bf16[2,256,128]{2,1,0:T(8,128)(2,1)S(1)}, u32[]{:S(2)}, u32[]{:S(2)}) collective-permute-start(bf16[2,256,128]{2,1,0:T(8,128)(2,1)S(1)} %copy-done.40), channel_id=1, source_target_pairs={{0,208},{16,224},{32,240},{48,0},{64,16},{80,32},{96,48},{112,64},... | collective-permute-start | bytes 393224 | tf_op jit(solution)/shard_map/ppermute | solution.py:460
  247.6 90.4 %collective-permute-start.30 = (bf16[2,256,128]{2,1,0:T(8,128)(2,1)S(1)}, bf16[2,256,128]{2,1,0:T(8,128)(2,1)S(1)}, u32[]{:S(2)}, u32[]{:S(2)}) collective-permute-start(bf16[2,256,128]{2,1,0:T(8,128)(2,1)S(1)} %copy-done.39), channel_id=1, source_target_pairs={{0,224},{16,240},{32,0},{48,16},{64,32},{80,48},{96,64},{112,80},{... | collective-permute-start | bytes 393224 | tf_op jit(solution)/shard_map/ppermute | solution.py:460
  258.4 79.6 %collective-permute-start.31 = (bf16[2,256,128]{2,1,0:T(8,128)(2,1)S(1)}, bf16[2,256,128]{2,1,0:T(8,128)(2,1)S(1)}, u32[]{:S(2)}, u32[]{:S(2)}) collective-permute-start(bf16[2,256,128]{2,1,0:T(8,128)(2,1)S(1)} %copy-done.38), channel_id=1, source_target_pairs={{0,240},{16,0},{32,16},{48,32},{64,48},{80,64},{96,80},{112,96},{1... | collective-permute-start | bytes 393224 | tf_op jit(solution)/shard_map/ppermute | solution.py:460
  343.1 22.7 %all-to-all-start.3 = ((bf16[16,224,128]{2,1,0:T(8,128)(2,1)}), bf16[16,224,128]{2,1,0:T(8,128)(2,1)S(1)}, u32[]{:S(2)}, u32[]{:S(2)}) async-start(bf16[16,224,128]{2,1,0:T(8,128)(2,1)} %bitcast.9), calls=%async_computation.3 | async-start | bytes 1835008 | tf_op jit(solution)/shard_map/all_to_all | solution.py:487
  (71 other events, 8272.3 us)

commit v7 on v6

--- a/solution.py
+++ b/solution.py
@@ -19,7 +19,21 @@
 MIB = 1 << 20
 
 
-def route_kernel(far_ref, table_ref, slot_ref, count_ref, *, sources, blk_dev):
+def route_kernel(
+    far_ref, keys_hbm, values_hbm, table_ref, slot_ref, last_ref, first_ref, count_ref, sems,
+    *, sources, blk_dev,
+):
+    margin = BAND * BT
+    copies = []
+    for which, ref in enumerate((keys_hbm, values_hbm)):
+        copies += [
+            pltpu.make_async_copy(
+                ref.at[pl.ds(blk_dev * BT - margin, margin)], last_ref.at[which], sems.at[which, 0]
+            ),
+            pltpu.make_async_copy(ref.at[pl.ds(0, margin)], first_ref.at[which], sems.at[which, 1]),
+        ]
+    for copy in copies:
+        copy.start()
     for s in range(sources):
         count_ref[s] = 0
         for r in range(CAP):
@@ -36,22 +50,30 @@
         return carry
 
     lax.fori_loop(0, blk_dev, step, 0)
-
-
-def route(far_list, sources):
+    for copy in copies:
+        copy.wait()
+
+
+def route(far_list, key_rows, value_rows, sources):
     blk_dev = far_list.shape[0]
     smem = pl.BlockSpec(memory_space=pltpu.SMEM)
+    vmem = pl.BlockSpec(memory_space=pltpu.VMEM)
+    hbm = pl.BlockSpec(memory_space=pltpu.HBM)
+    halo = pltpu.VMEM((2, BAND * BT, key_rows.shape[1]), key_rows.dtype)
     return pl.pallas_call(
         functools.partial(route_kernel, sources=sources, blk_dev=blk_dev),
         out_shape=(
             jax.ShapeDtypeStruct((sources, CAP), jnp.int32),
             jax.ShapeDtypeStruct((FAR, blk_dev), jnp.int32),
-        ),
-        in_specs=[smem],
-        out_specs=(smem, smem),
-        scratch_shapes=[pltpu.SMEM((sources,), jnp.int32)],
+            halo,
+            halo,
+        ),
+        in_specs=[smem, hbm, hbm],
+        out_specs=(smem, smem, vmem, vmem),
+        scratch_shapes=[pltpu.SMEM((sources,), jnp.int32), pltpu.SemaphoreType.DMA((2, 2))],
+        compiler_params=pltpu.CompilerParams(vmem_limit_bytes=4 * MIB),
         name="route",
-    )(far_list.T)
+    )(far_list.T, key_rows, value_rows)
 
 
 def pack_kernel(asked_ref, me_ref, keys_ref, values_ref, *refs, shifts):
@@ -362,10 +384,10 @@
 
 
 def value_kernel(me_ref, slot_ref, weights_ref, acc_ref, scale_ref, *refs, sources, blk_dev):
-    pieces = refs[:-3]
-    out_ref, buffer_ref, sems = refs[-3:]
-    for copy in gather_pieces(pieces, buffer_ref, sems, sources):
-        copy.wait()
+    pieces = refs[:-2]
+    out_ref, buffer_ref = refs[-2:]
+    for s, piece in enumerate(pieces):
+        buffer_ref[s] = piece[...]
     for i in range(blk_dev):
         r = pl.ds(i * BT, BT)
         acc = acc_ref[r, :]
@@ -380,16 +402,12 @@
     blk_dev = tok_rows // BT
     smem = pl.BlockSpec(memory_space=pltpu.SMEM)
     vmem = pl.BlockSpec(memory_space=pltpu.VMEM)
-    hbm = pl.BlockSpec(memory_space=pltpu.HBM)
     return pl.pallas_call(
         functools.partial(value_kernel, sources=sources, blk_dev=blk_dev),
         out_shape=pltpu.VMEM((tok_rows, DH), jnp.bfloat16),
-        in_specs=[smem, smem] + [vmem] * 3 + [hbm] * len(pieces),
+        in_specs=[smem, smem] + [vmem] * (3 + len(pieces)),
         out_specs=vmem,
-        scratch_shapes=[
-            pltpu.VMEM((sources, CAP, BT, DH), jnp.bfloat16),
-            pltpu.SemaphoreType.DMA((sources,)),
-        ],
+        scratch_shapes=[pltpu.VMEM((sources, CAP, BT, DH), jnp.bfloat16)],
         compiler_params=pltpu.CompilerParams(vmem_limit_bytes=4 * MIB),
         name="values",
     )(me, slots, weights, acc, scale, *pieces)
@@ -431,34 +449,32 @@
     sources = lax.axis_size("seq")
     tok_rows, channels = key_rows.shape
     blk_dev = tok_rows // BT
-    margin = BAND * BT
     heads = channels // DH
     up = [(i, i + 1) for i in range(sources - 1)]
     down = [(i + 1, i) for i in range(sources - 1)]
 
-    table, slots = route(far_list, sources)
-    asked = lax.all_to_all(table, "seq", split_axis=0, concat_axis=0, tiled=True)
-    last = jnp.stack([key_rows[tok_rows - margin :], value_rows[tok_rows - margin :]])
-    first = jnp.stack([key_rows[:margin], value_rows[:margin]])
-    before = lax.ppermute(last, "seq", up)
-    after = lax.ppermute(first, "seq", down)
-
-    me = myself[None].astype(jnp.int32)
     keys_hbm, values_hbm = (
         pltpu.with_memory_space_constraint(x, pltpu.HBM) for x in (key_rows, value_rows)
     )
+    table, slots, last, first = route(far_list, keys_hbm, values_hbm, sources)
+    asked = lax.all_to_all(table, "seq", split_axis=0, concat_axis=0, tiled=True)
+    before = lax.ppermute(last, "seq", up)
+    after = lax.ppermute(first, "seq", down)
+
+    me = myself[None].astype(jnp.int32)
     incoming = []
     for head in range(heads):
         split = head == heads - 1
         outgoing = pack(asked, me, keys_hbm, values_hbm, head, split)
         if split:
             pieces = []
-            for which in range(2):
+            for which, kind in enumerate(("key", "value")):
                 arrays = list(outgoing[which * sources : (which + 1) * sources])
                 for shift in range(1, sources):
                     ring = [(i, (i + shift) % sources) for i in range(sources)]
                     arrays[shift] = lax.ppermute(arrays[shift], "seq", ring)
-                pieces.append([pltpu.with_memory_space_constraint(x, pltpu.HBM) for x in arrays])
+                space = pltpu.HBM if kind == "key" else pltpu.VMEM
+                pieces.append([pltpu.with_memory_space_constraint(x, space) for x in arrays])
             incoming.append(pieces)
         else:
             incoming.append(

time: 388 us -> 385 us (level)
  the two profiles are of different devices: /device:TPU:40 before, /device:TPU:64 now
where the time goes in v7:
time: 385 us; the launch traced here: 384 us
  waiting for transfers between devices  158 us (41%)
  Pallas kernels  108 us (28%)
  starting transfers between devices  93.6 us (24%)
  blocking collectives  20 us (5%)
  local copies, waits for them, and re-layouts  4.39 us (1%)
    ppermute x30, waiting for transfers between devices, body(): arrays[shift] = lax.ppermute(arrays[shift], 'seq', ring)  148 us
    pallas_call x1, Pallas kernels, band_attention(): pl.pallas_call(functools.partial(band_kernel, blk_dev=blk_dev, total_bloc...  67.6 us
    ppermute x30, starting transfers between devices, body(): arrays[shift] = lax.ppermute(arrays[shift], 'seq', ring)  61.9 us
    pallas_call x2, Pallas kernels, far_attention(): pl.pallas_call(functools.partial(far_kernel, head=head, blk_dev=blk_dev,...  23.6 us
    all_to_all x1, blocking collectives, body(): lax.all_to_all(attended.reshape(lax.axis_size('head'), -1, DH), 'head', s...  20 us
    pallas_call x2, Pallas kernels, pack(): pl.pallas_call(functools.partial(pack_kernel, shifts=shifts), out_shape=o...  9.78 us
    all_to_all x1, starting transfers between devices, body(): lax.all_to_all(table, 'seq', split_axis=0, concat_axis=0, tiled=True)  9.16 us
  transfers between devices with their start and end apart: 35, of which 20 were waited for; matrix products, arithmetic and copies ran while one was open for 0% of the time, Pallas kernels for 26%

profile of v7, /device:TPU:64, one launch (start us, length us, event | category | flops | bytes accessed | tf_op | source)
XLA Modules:
  0.0 384.3 jit_solution(1487332215623398443)
XLA Ops:
  3.4 9.2 %all-to-all-start = ((s32[16,1,2]{2,1,0:T(1,128)}), s32[16,1,2]{2,1,0:T(1,128)S(1)}, u32[]{:S(2)}, u32[]{:S(2)}) async-start(s32[16,1,2]{2,1,0:T(1,128)} %bitcast.6), calls=%async_computation | async-start | bytes 16384 | tf_op jit(solution)/shard_map/all_to_all | solution.py:460
  12.5 6.2 %all-to-all-done = s32[16,1,2]{2,1,0:T(1,128)S(1)} async-done(((s32[16,1,2]{2,1,0:T(1,128)}), s32[16,1,2]{2,1,0:T(1,128)S(1)}, u32[]{:S(2)}, u32[]{:S(2)}) %all-to-all-start) | async-done | bytes 160 | tf_op jit(solution)/shard_map/all_to_all | solution.py:460
  18.7 4.7 %pack.2 = bf16[16,4,256,128]{3,2,1,0:T(8,128)(2,1)} custom-call(s32[16,2]{1,0:T(8,128)S(1)} %bitcast.9, s32[1]{0:T(128)} %bitcast.me_ref, bf16[3584,256]{1,0:T(8,128)(2,1)} %keys_ref.3, bf16[3584,256]{1,0:T(8,128)(2,1)} %values_ref.3), custom_call_target="tpu_custom_call" | custom-call | tf_op jit(solution)/shard_map/pack/pallas_call | solution.py:109
  23.5 6.7 %all-to-all-start.1 = ((bf16[16,4,256,128]{3,2,1,0:T(8,128)(2,1)}), bf16[16,4,256,128]{3,2,1,0:T(8,128)(2,1)}, u32[]{:S(2)}, u32[]{:S(2)}) async-start(bf16[16,4,256,128]{3,2,1,0:T(8,128)(2,1)} %pack.2), calls=%async_computation.1 | async-start | bytes 8388608 | tf_op jit(solution)/shard_map/all_to_all | solution.py:481
  30.2 5.1 %pack.3 = (bf16[2,256,128]{2,1,0:T(8,128)(2,1)}, bf16[2,256,128]{2,1,0:T(8,128)(2,1)}, bf16[2,256,128]{2,1,0:T(8,128)(2,1)}, bf16[2,256,128]{2,1,0:T(8,128)(2,1)...) custom-call(s32[16,2]{1,0:T(8,128)S(1)} %bitcast.10, ...), custom_call_target="tpu_custom_call" | custom-call | tf_op jit(solution)/shard_map/pack/pallas_call | solution.py:109
  40.7 6.6 %collective-permute-start.13 = (bf16[2,256,128]{2,1,0:T(8,128)(2,1)}, bf16[2,256,128]{2,1,0:T(8,128)(2,1)S(1)}, u32[]{:S(2)}, u32[]{:S(2)}) collective-permute-start(bf16[2,256,128]{2,1,0:T(8,128)(2,1)} %get-tuple-element.64), channel_id=1, source_target_pairs={{0,192},{16,208},{32,224},{48,240},{64,0},{80,16},{96,32},{112,48}... | collective-permute-start | bytes 393224 | tf_op jit(solution)/shard_map/ppermute | solution.py:475
  47.9 82.3 %collective-permute-done.10.refs_9_ = bf16[2,256,128]{2,1,0:T(8,128)(2,1)S(1)} collective-permute-done((bf16[2,256,128]{2,1,0:T(8,128)(2,1)}, bf16[2,256,128]{2,1,0:T(8,128)(2,1)S(1)}, u32[]{:S(2)}, u32[]{:S(2)}) %collective-permute-start.10) | collective-permute-done | bytes 131104 | tf_op jit(solution)/shard_map/ppermute | solution.py:475
  130.1 8.1 %collective-permute-done.11.refs_10_ = bf16[2,256,128]{2,1,0:T(8,128)(2,1)S(1)} collective-permute-done((bf16[2,256,128]{2,1,0:T(8,128)(2,1)}, bf16[2,256,128]{2,1,0:T(8,128)(2,1)S(1)}, u32[]{:S(2)}, u32[]{:S(2)}) %collective-permute-start.11) | collective-permute-done | bytes 131104 | tf_op jit(solution)/shard_map/ppermute | solution.py:475
  138.2 4.8 %collective-permute-done.12.refs_11_ = bf16[2,256,128]{2,1,0:T(8,128)(2,1)S(1)} collective-permute-done((bf16[2,256,128]{2,1,0:T(8,128)(2,1)}, bf16[2,256,128]{2,1,0:T(8,128)(2,1)S(1)}, u32[]{:S(2)}, u32[]{:S(2)}) %collective-permute-start.12) | collective-permute-done | bytes 131104 | tf_op jit(solution)/shard_map/ppermute | solution.py:475
  143.1 3.3 collective-permute-done.13.refs_12_
  146.3 3.7 collective-permute-start.3
  150.0 5.7 %collective-permute-start = (bf16[2,768,256]{2,1,0:T(8,128)(2,1)S(1)}, bf16[2,768,256]{2,1,0:T(8,128)(2,1)S(1)}, u32[]{:S(2)}, u32[]{:S(2)}) collective-permute-start(bf16[2,768,256]{2,1,0:T(8,128)(2,1)S(1)} %get-tuple-element.47), channel_id=1, source_target_pairs={{0,16},{16,32},{32,48},{48,64},{64,80},{80,96},{96,112},{112,128},... | collective-permute-start | bytes 2359304 | tf_op jit(solution)/shard_map/ppermute | solution.py:461
  155.7 3.3 collective-permute-start.1
  160.4 3.8 collective-permute-start.6
  164.9 5.1 %collective-permute-start.7 = (bf16[2,256,128]{2,1,0:T(8,128)(2,1)}, bf16[2,256,128]{2,1,0:T(8,128)(2,1)S(1)}, u32[]{:S(2)}, u32[]{:S(2)}) collective-permute-start(bf16[2,256,128]{2,1,0:T(8,128)(2,1)} %get-tuple-element.58), channel_id=1, source_target_pairs={{0,96},{16,112},{32,128},{48,144},{64,160},{80,176},{96,192},{112,... | collective-permute-start | bytes 393224 | tf_op jit(solution)/shard_map/ppermute | solution.py:475
  170.0 21.2 %collective-permute-done.5.refs_4_ = bf16[2,256,128]{2,1,0:T(8,128)(2,1)S(1)} collective-permute-done((bf16[2,256,128]{2,1,0:T(8,128)(2,1)}, bf16[2,256,128]{2,1,0:T(8,128)(2,1)S(1)}, u32[]{:S(2)}, u32[]{:S(2)}) %collective-permute-start.5) | collective-permute-done | bytes 131104 | tf_op jit(solution)/shard_map/ppermute | solution.py:475
  195.2 3.4 collective-permute-done.7.refs_6_
  201.1 3.7 collective-permute-start.19
  204.8 3.9 %collective-permute-done.17.refs_1_ = bf16[2,256,128]{2,1,0:T(8,128)(2,1)S(1)} collective-permute-done((bf16[2,256,128]{2,1,0:T(8,128)(2,1)}, bf16[2,256,128]{2,1,0:T(8,128)(2,1)S(1)}, u32[]{:S(2)}, u32[]{:S(2)}) %collective-permute-start.17) | collective-permute-done | bytes 131104 | tf_op jit(solution)/shard_map/ppermute | solution.py:475
  213.9 6.1 %collective-permute-done.19.refs_3_ = bf16[2,256,128]{2,1,0:T(8,128)(2,1)S(1)} collective-permute-done((bf16[2,256,128]{2,1,0:T(8,128)(2,1)}, bf16[2,256,128]{2,1,0:T(8,128)(2,1)S(1)}, u32[]{:S(2)}, u32[]{:S(2)}) %collective-permute-start.19) | collective-permute-done | bytes 131104 | tf_op jit(solution)/shard_map/ppermute | solution.py:475
  220.0 4.0 %collective-permute-start.22 = (bf16[2,256,128]{2,1,0:T(8,128)(2,1)}, bf16[2,256,128]{2,1,0:T(8,128)(2,1)S(1)}, u32[]{:S(2)}, u32[]{:S(2)}) collective-permute-start(bf16[2,256,128]{2,1,0:T(8,128)(2,1)} %get-tuple-element.77), channel_id=1, source_target_pairs={{0,96},{16,112},{32,128},{48,144},{64,160},{80,176},{96,192},{112,... | collective-permute-start | bytes 393224 | tf_op jit(solution)/shard_map/ppermute | solution.py:475
  228.1 3.5 collective-permute-done.22.refs_6_
  233.0 3.1 collective-permute-start.26
  239.5 2.7 collective-permute-start.28
  242.3 5.7 %collective-permute-done.26.refs_10_ = bf16[2,256,128]{2,1,0:T(8,128)(2,1)S(1)} collective-permute-done((bf16[2,256,128]{2,1,0:T(8,128)(2,1)}, bf16[2,256,128]{2,1,0:T(8,128)(2,1)S(1)}, u32[]{:S(2)}, u32[]{:S(2)}) %collective-permute-start.26) | collective-permute-done | bytes 131104 | tf_op jit(solution)/shard_map/ppermute | solution.py:475
  247.9 4.9 %collective-permute-start.29 = (bf16[2,256,128]{2,1,0:T(8,128)(2,1)}, bf16[2,256,128]{2,1,0:T(8,128)(2,1)S(1)}, u32[]{:S(2)}, u32[]{:S(2)}) collective-permute-start(bf16[2,256,128]{2,1,0:T(8,128)(2,1)} %get-tuple-element.84), channel_id=1, source_target_pairs={{0,208},{16,224},{32,240},{48,0},{64,16},{80,32},{96,48},{112,64},... | collective-permute-start | bytes 393224 | tf_op jit(solution)/shard_map/ppermute | solution.py:475
  254.8 67.6 %band.1 = (f32[3584,256]{1,0:T(8,128)S(1)}, f32[3584,256]{1,0:T(8,128)S(1)}) custom-call(s32[15]{0:T(128)S(1)} %pad_add_fusion.meta_ref, f32[2]{0:T(128)S(1)} %copy-done.8, bf16[3584,256]{1,0:T(8,128)(2,1)S(1)} %copy-done.4, bf16[3584,256]{1,0:T(8,128)(2,1)S(1)} %copy-done, bf16[3584,256]{1,0:T(8,128)(2,1)S(1)} %copy-done.1, ...), custom_call_target="tpu_custom_call" | custom-call | flops 6576668672 | bytes 31457280 | tf_op jit(solution)/shard_map/band/pallas_call | solution.py:232
  326.2 10.4 %far.3 = (bf16[3584,512]{1,0:T(8,128)(2,1)S(1)}, f32[3584,128]{1,0:T(8,128)S(1)}, f32[3584,128]{1,0:T(8,128)S(1)}) custom-call(s32[15]{0:T(128)S(1)} %pad_add_fusion.meta_ref, s32[2,14]{1,0:T(2,128)S(1)} %get-tuple-element.46.slot_ref, s32[2,14]{1,0:T(2,128)S(1)} %bitcast.12, f32[2]{0:T(128)S(1)} %copy-done.8, bf16[3584,256]{1,0:T(8,128)(2,1)} %query_ref.5, ...), custom_call_target="tpu_custom_call" | custom-call | flops 939524096 | bytes 14680064 | tf_op jit(solution)/shard_map/far/pallas_call | solution.py:360
  339.4 6.8 %all-to-all-start.3 = ((bf16[16,224,128]{2,1,0:T(8,128)(2,1)}), bf16[16,224,128]{2,1,0:T(8,128)(2,1)S(1)}, u32[]{:S(2)}, u32[]{:S(2)}) async-start(bf16[16,224,128]{2,1,0:T(8,128)(2,1)} %bitcast.5), calls=%async_computation.3 | async-start | bytes 1835008 | tf_op jit(solution)/shard_map/all_to_all | solution.py:503
  346.2 13.2 %far.2 = bf16[3584,128]{1,0:T(8,128)(2,1)S(1)} custom-call(s32[15]{0:T(128)S(1)} %pad_add_fusion.meta_ref, s32[2,14]{1,0:T(2,128)S(1)} %get-tuple-element.46.slot_ref, s32[2,14]{1,0:T(2,128)S(1)} %bitcast.13, f32[2]{0:T(128)S(1)} %copy-done.8, bf16[3584,256]{1,0:T(8,128)(2,1)} %query_ref.5, f32[3584,256]{1,0:T(8,128)} %copy-done.2, f32[3584,256]{1,0:T(8,128)} %copy-done.3, ...), custom_call_target="tpu_custom_call" | custom-call | flops 939524096 | bytes 14680064 | tf_op jit(solution)/shard_map/far/pallas_call | solution.py:360
  359.4 3.4 all-to-all-done.3.refs_1_
  362.7 20.0 %all_to_all.26.refs_0_ = bf16[16,224,128]{2,1,0:T(8,128)(2,1)S(1)} all-to-all(bf16[16,224,128]{2,1,0:T(8,128)(2,1)S(1)} %bitcast.8), channel_id=1, replica_groups=mesh['seq'=16,'head'=16] {'head'}, dimensions={0} | all-to-all | bytes 1835008 | tf_op jit(solution)/shard_map/all_to_all | solution.py:503
  (98 shorter events, 41.8 us)
Async XLA Ops:
  3.4 15.4 %all-to-all-start = ((s32[16,1,2]{2,1,0:T(1,128)}), s32[16,1,2]{2,1,0:T(1,128)S(1)}, u32[]{:S(2)}, u32[]{:S(2)}) async-start(s32[16,1,2]{2,1,0:T(1,128)} %bitcast.6), calls=%async_computation | async-start | bytes 16384 | tf_op jit(solution)/shard_map/all_to_all | solution.py:460
  23.5 315.9 %all-to-all-start.1 = ((bf16[16,4,256,128]{3,2,1,0:T(8,128)(2,1)}), bf16[16,4,256,128]{3,2,1,0:T(8,128)(2,1)}, u32[]{:S(2)}, u32[]{:S(2)}) async-start(bf16[16,4,256,128]{3,2,1,0:T(8,128)(2,1)} %pack.2), calls=%async_computation.1 | async-start | bytes 8388608 | tf_op jit(solution)/shard_map/all_to_all | solution.py:481
  35.3 94.8 %collective-permute-start.10 = (bf16[2,256,128]{2,1,0:T(8,128)(2,1)}, bf16[2,256,128]{2,1,0:T(8,128)(2,1)S(1)}, u32[]{:S(2)}, u32[]{:S(2)}) collective-permute-start(bf16[2,256,128]{2,1,0:T(8,128)(2,1)} %get-tuple-element.61), channel_id=1, source_target_pairs={{0,144},{16,160},{32,176},{48,192},{64,208},{80,224},{96,240},{112... | collective-permute-start | bytes 393224 | tf_op jit(solution)/shard_map/ppermute | solution.py:475
  37.8 100.4 %collective-permute-start.11 = (bf16[2,256,128]{2,1,0:T(8,128)(2,1)}, bf16[2,256,128]{2,1,0:T(8,128)(2,1)S(1)}, u32[]{:S(2)}, u32[]{:S(2)}) collective-permute-start(bf16[2,256,128]{2,1,0:T(8,128)(2,1)} %get-tuple-element.62), channel_id=1, source_target_pairs={{0,160},{16,176},{32,192},{48,208},{64,224},{80,240},{96,0},{112,1... | collective-permute-start | bytes 393224 | tf_op jit(solution)/shard_map/ppermute | solution.py:475
  40.4 102.6 %collective-permute-start.12 = (bf16[2,256,128]{2,1,0:T(8,128)(2,1)}, bf16[2,256,128]{2,1,0:T(8,128)(2,1)S(1)}, u32[]{:S(2)}, u32[]{:S(2)}) collective-permute-start(bf16[2,256,128]{2,1,0:T(8,128)(2,1)} %get-tuple-element.63), channel_id=1, source_target_pairs={{0,176},{16,192},{32,208},{48,224},{64,240},{80,0},{96,16},{112,32... | collective-permute-start | bytes 393224 | tf_op jit(solution)/shard_map/ppermute | solution.py:475
  40.7 105.6 %collective-permute-start.13 = (bf16[2,256,128]{2,1,0:T(8,128)(2,1)}, bf16[2,256,128]{2,1,0:T(8,128)(2,1)S(1)}, u32[]{:S(2)}, u32[]{:S(2)}) collective-permute-start(bf16[2,256,128]{2,1,0:T(8,128)(2,1)} %get-tuple-element.64), channel_id=1, source_target_pairs={{0,192},{16,208},{32,224},{48,240},{64,0},{80,16},{96,32},{112,48}... | collective-permute-start | bytes 393224 | tf_op jit(solution)/shard_map/ppermute | solution.py:475
  47.3 102.7 %collective-permute-start.14 = (bf16[2,256,128]{2,1,0:T(8,128)(2,1)}, bf16[2,256,128]{2,1,0:T(8,128)(2,1)S(1)}, u32[]{:S(2)}, u32[]{:S(2)}) collective-permute-start(bf16[2,256,128]{2,1,0:T(8,128)(2,1)} %get-tuple-element.65), channel_id=1, source_target_pairs={{0,208},{16,224},{32,240},{48,0},{64,16},{80,32},{96,48},{112,64},... | collective-permute-start | bytes 393224 | tf_op jit(solution)/shard_map/ppermute | solution.py:475
  130.1 19.9 %collective-permute-start.15 = (bf16[2,256,128]{2,1,0:T(8,128)(2,1)}, bf16[2,256,128]{2,1,0:T(8,128)(2,1)S(1)}, u32[]{:S(2)}, u32[]{:S(2)}) collective-permute-start(bf16[2,256,128]{2,1,0:T(8,128)(2,1)} %get-tuple-element.66), channel_id=1, source_target_pairs={{0,224},{16,240},{32,0},{48,16},{64,32},{80,48},{96,64},{112,80},{... | collective-permute-start | bytes 393224 | tf_op jit(solution)/shard_map/ppermute | solution.py:475
  138.2 17.5 %collective-permute-start.16 = (bf16[2,256,128]{2,1,0:T(8,128)(2,1)}, bf16[2,256,128]{2,1,0:T(8,128)(2,1)S(1)}, u32[]{:S(2)}, u32[]{:S(2)}) collective-permute-start(bf16[2,256,128]{2,1,0:T(8,128)(2,1)} %get-tuple-element.67), channel_id=1, source_target_pairs={{0,240},{16,0},{32,16},{48,32},{64,48},{80,64},{96,80},{112,96},{1... | collective-permute-start | bytes 393224 | tf_op jit(solution)/shard_map/ppermute | solution.py:475
  143.1 16.0 %collective-permute-start.2 = (bf16[2,256,128]{2,1,0:T(8,128)(2,1)}, bf16[2,256,128]{2,1,0:T(8,128)(2,1)S(1)}, u32[]{:S(2)}, u32[]{:S(2)}) collective-permute-start(bf16[2,256,128]{2,1,0:T(8,128)(2,1)} %get-tuple-element.53), channel_id=1, source_target_pairs={{0,16},{16,32},{32,48},{48,64},{64,80},{80,96},{96,112},{112,128},... | collective-permute-start | bytes 393224 | tf_op jit(solution)/shard_map/ppermute | solution.py:475
  146.3 14.0 %collective-permute-start.3 = (bf16[2,256,128]{2,1,0:T(8,128)(2,1)}, bf16[2,256,128]{2,1,0:T(8,128)(2,1)S(1)}, u32[]{:S(2)}, u32[]{:S(2)}) collective-permute-start(bf16[2,256,128]{2,1,0:T(8,128)(2,1)} %get-tuple-element.54), channel_id=1, source_target_pairs={{0,32},{16,48},{32,64},{48,80},{64,96},{80,112},{96,128},{112,144}... | collective-permute-start | bytes 393224 | tf_op jit(solution)/shard_map/ppermute | solution.py:475
  150.0 14.8 %collective-permute-start.4 = (bf16[2,256,128]{2,1,0:T(8,128)(2,1)}, bf16[2,256,128]{2,1,0:T(8,128)(2,1)S(1)}, u32[]{:S(2)}, u32[]{:S(2)}) collective-permute-start(bf16[2,256,128]{2,1,0:T(8,128)(2,1)} %get-tuple-element.55), channel_id=1, source_target_pairs={{0,48},{16,64},{32,80},{48,96},{64,112},{80,128},{96,144},{112,160... | collective-permute-start | bytes 393224 | tf_op jit(solution)/shard_map/ppermute | solution.py:475
  150.0 102.8 %collective-permute-start = (bf16[2,768,256]{2,1,0:T(8,128)(2,1)S(1)}, bf16[2,768,256]{2,1,0:T(8,128)(2,1)S(1)}, u32[]{:S(2)}, u32[]{:S(2)}) collective-permute-start(bf16[2,768,256]{2,1,0:T(8,128)(2,1)S(1)} %get-tuple-element.47), channel_id=1, source_target_pairs={{0,16},{16,32},{32,48},{48,64},{64,80},{80,96},{96,112},{112,128},... | collective-permute-start | bytes 2359304 | tf_op jit(solution)/shard_map/ppermute | solution.py:461
  155.7 98.6 %collective-permute-start.1 = (bf16[2,768,256]{2,1,0:T(8,128)(2,1)S(1)}, bf16[2,768,256]{2,1,0:T(8,128)(2,1)S(1)}, u32[]{:S(2)}, u32[]{:S(2)}) collective-permute-start(bf16[2,768,256]{2,1,0:T(8,128)(2,1)S(1)} %get-tuple-element.48), channel_id=1, source_target_pairs={{16,0},{32,16},{48,32},{64,48},{80,64},{96,80},{112,96},{128,112},... | collective-permute-start | bytes 2359304 | tf_op jit(solution)/shard_map/ppermute | solution.py:462
  159.1 32.1 %collective-permute-start.5 = (bf16[2,256,128]{2,1,0:T(8,128)(2,1)}, bf16[2,256,128]{2,1,0:T(8,128)(2,1)S(1)}, u32[]{:S(2)}, u32[]{:S(2)}) collective-permute-start(bf16[2,256,128]{2,1,0:T(8,128)(2,1)} %get-tuple-element.56), channel_id=1, source_target_pairs={{0,64},{16,80},{32,96},{48,112},{64,128},{80,144},{96,160},{112,17... | collective-permute-start | bytes 393224 | tf_op jit(solution)/shard_map/ppermute | solution.py:475
  160.4 32.7 %collective-permute-start.6 = (bf16[2,256,128]{2,1,0:T(8,128)(2,1)}, bf16[2,256,128]{2,1,0:T(8,128)(2,1)S(1)}, u32[]{:S(2)}, u32[]{:S(2)}) collective-permute-start(bf16[2,256,128]{2,1,0:T(8,128)(2,1)} %get-tuple-element.57), channel_id=1, source_target_pairs={{0,80},{16,96},{32,112},{48,128},{64,144},{80,160},{96,176},{112,1... | collective-permute-start | bytes 393224 | tf_op jit(solution)/shard_map/ppermute | solution.py:475
  164.9 33.7 %collective-permute-start.7 = (bf16[2,256,128]{2,1,0:T(8,128)(2,1)}, bf16[2,256,128]{2,1,0:T(8,128)(2,1)S(1)}, u32[]{:S(2)}, u32[]{:S(2)}) collective-permute-start(bf16[2,256,128]{2,1,0:T(8,128)(2,1)} %get-tuple-element.58), channel_id=1, source_target_pairs={{0,96},{16,112},{32,128},{48,144},{64,160},{80,176},{96,192},{112,... | collective-permute-start | bytes 393224 | tf_op jit(solution)/shard_map/ppermute | solution.py:475
  193.1 8.1 %collective-permute-start.9 = (bf16[2,256,128]{2,1,0:T(8,128)(2,1)}, bf16[2,256,128]{2,1,0:T(8,128)(2,1)S(1)}, u32[]{:S(2)}, u32[]{:S(2)}) collective-permute-start(bf16[2,256,128]{2,1,0:T(8,128)(2,1)} %get-tuple-element.60), channel_id=1, source_target_pairs={{0,128},{16,144},{32,160},{48,176},{64,192},{80,208},{96,224},{112... | collective-permute-start | bytes 393224 | tf_op jit(solution)/shard_map/ppermute | solution.py:475
  198.6 10.2 %collective-permute-start.17 = (bf16[2,256,128]{2,1,0:T(8,128)(2,1)}, bf16[2,256,128]{2,1,0:T(8,128)(2,1)S(1)}, u32[]{:S(2)}, u32[]{:S(2)}) collective-permute-start(bf16[2,256,128]{2,1,0:T(8,128)(2,1)} %get-tuple-element.72), channel_id=1, source_target_pairs={{0,16},{16,32},{32,48},{48,64},{64,80},{80,96},{96,112},{112,128},... | collective-permute-start | bytes 393224 | tf_op jit(solution)/shard_map/ppermute | solution.py:475
  199.0 12.2 %collective-permute-start.18 = (bf16[2,256,128]{2,1,0:T(8,128)(2,1)}, bf16[2,256,128]{2,1,0:T(8,128)(2,1)S(1)}, u32[]{:S(2)}, u32[]{:S(2)}) collective-permute-start(bf16[2,256,128]{2,1,0:T(8,128)(2,1)} %get-tuple-element.73), channel_id=1, source_target_pairs={{0,32},{16,48},{32,64},{48,80},{64,96},{80,112},{96,128},{112,144}... | collective-permute-start | bytes 393224 | tf_op jit(solution)/shard_map/ppermute | solution.py:475
  201.1 18.9 %collective-permute-start.19 = (bf16[2,256,128]{2,1,0:T(8,128)(2,1)}, bf16[2,256,128]{2,1,0:T(8,128)(2,1)S(1)}, u32[]{:S(2)}, u32[]{:S(2)}) collective-permute-start(bf16[2,256,128]{2,1,0:T(8,128)(2,1)} %get-tuple-element.74), channel_id=1, source_target_pairs={{0,48},{16,64},{32,80},{48,96},{64,112},{80,128},{96,144},{112,160... | collective-permute-start | bytes 393224 | tf_op jit(solution)/shard_map/ppermute | solution.py:475
  208.7 17.0 %collective-permute-start.20 = (bf16[2,256,128]{2,1,0:T(8,128)(2,1)}, bf16[2,256,128]{2,1,0:T(8,128)(2,1)S(1)}, u32[]{:S(2)}, u32[]{:S(2)}) collective-permute-start(bf16[2,256,128]{2,1,0:T(8,128)(2,1)} %get-tuple-element.75), channel_id=1, source_target_pairs={{0,64},{16,80},{32,96},{48,112},{64,128},{80,144},{96,160},{112,17... | collective-permute-start | bytes 393224 | tf_op jit(solution)/shard_map/ppermute | solution.py:475
  211.2 14.6 %collective-permute-start.21 = (bf16[2,256,128]{2,1,0:T(8,128)(2,1)}, bf16[2,256,128]{2,1,0:T(8,128)(2,1)S(1)}, u32[]{:S(2)}, u32[]{:S(2)}) collective-permute-start(bf16[2,256,128]{2,1,0:T(8,128)(2,1)} %get-tuple-element.76), channel_id=1, source_target_pairs={{0,80},{16,96},{32,112},{48,128},{64,144},{80,160},{96,176},{112,1... | collective-permute-start | bytes 393224 | tf_op jit(solution)/shard_map/ppermute | solution.py:475
  220.0 11.6 %collective-permute-start.22 = (bf16[2,256,128]{2,1,0:T(8,128)(2,1)}, bf16[2,256,128]{2,1,0:T(8,128)(2,1)S(1)}, u32[]{:S(2)}, u32[]{:S(2)}) collective-permute-start(bf16[2,256,128]{2,1,0:T(8,128)(2,1)} %get-tuple-element.77), channel_id=1, source_target_pairs={{0,96},{16,112},{32,128},{48,144},{64,160},{80,176},{96,192},{112,... | collective-permute-start | bytes 393224 | tf_op jit(solution)/shard_map/ppermute | solution.py:475
  225.7 11.4 %collective-permute-start.24 = (bf16[2,256,128]{2,1,0:T(8,128)(2,1)}, bf16[2,256,128]{2,1,0:T(8,128)(2,1)S(1)}, u32[]{:S(2)}, u32[]{:S(2)}) collective-permute-start(bf16[2,256,128]{2,1,0:T(8,128)(2,1)} %get-tuple-element.79), channel_id=1, source_target_pairs={{0,128},{16,144},{32,160},{48,176},{64,192},{80,208},{96,224},{112... | collective-permute-start | bytes 393224 | tf_op jit(solution)/shard_map/ppermute | solution.py:475
  233.0 14.9 %collective-permute-start.26 = (bf16[2,256,128]{2,1,0:T(8,128)(2,1)}, bf16[2,256,128]{2,1,0:T(8,128)(2,1)S(1)}, u32[]{:S(2)}, u32[]{:S(2)}) collective-permute-start(bf16[2,256,128]{2,1,0:T(8,128)(2,1)} %get-tuple-element.81), channel_id=1, source_target_pairs={{0,160},{16,176},{32,192},{48,208},{64,224},{80,240},{96,0},{112,1... | collective-permute-start | bytes 393224 | tf_op jit(solution)/shard_map/ppermute | solution.py:475
  237.2 99.4 %collective-permute-start.27 = (bf16[2,256,128]{2,1,0:T(8,128)(2,1)}, bf16[2,256,128]{2,1,0:T(8,128)(2,1)S(1)}, u32[]{:S(2)}, u32[]{:S(2)}) collective-permute-start(bf16[2,256,128]{2,1,0:T(8,128)(2,1)} %get-tuple-element.82), channel_id=1, source_target_pairs={{0,176},{16,192},{32,208},{48,224},{64,240},{80,0},{96,16},{112,32... | collective-permute-start | bytes 393224 | tf_op jit(solution)/shard_map/ppermute | solution.py:475
  239.5 97.1 %collective-permute-start.28 = (bf16[2,256,128]{2,1,0:T(8,128)(2,1)}, bf16[2,256,128]{2,1,0:T(8,128)(2,1)S(1)}, u32[]{:S(2)}, u32[]{:S(2)}) collective-permute-start(bf16[2,256,128]{2,1,0:T(8,128)(2,1)} %get-tuple-element.83), channel_id=1, source_target_pairs={{0,192},{16,208},{32,224},{48,240},{64,0},{80,16},{96,32},{112,48}... | collective-permute-start | bytes 393224 | tf_op jit(solution)/shard_map/ppermute | solution.py:475
  247.9 88.7 %collective-permute-start.29 = (bf16[2,256,128]{2,1,0:T(8,128)(2,1)}, bf16[2,256,128]{2,1,0:T(8,128)(2,1)S(1)}, u32[]{:S(2)}, u32[]{:S(2)}) collective-permute-start(bf16[2,256,128]{2,1,0:T(8,128)(2,1)} %get-tuple-element.84), channel_id=1, source_target_pairs={{0,208},{16,224},{32,240},{48,0},{64,16},{80,32},{96,48},{112,64},... | collective-permute-start | bytes 393224 | tf_op jit(solution)/shard_map/ppermute | solution.py:475
  252.8 83.8 %collective-permute-start.30 = (bf16[2,256,128]{2,1,0:T(8,128)(2,1)}, bf16[2,256,128]{2,1,0:T(8,128)(2,1)S(1)}, u32[]{:S(2)}, u32[]{:S(2)}) collective-permute-start(bf16[2,256,128]{2,1,0:T(8,128)(2,1)} %get-tuple-element.85), channel_id=1, source_target_pairs={{0,224},{16,240},{32,0},{48,16},{64,32},{80,48},{96,64},{112,80},{... | collective-permute-start | bytes 393224 | tf_op jit(solution)/shard_map/ppermute | solution.py:475
  254.3 82.3 %collective-permute-start.31 = (bf16[2,256,128]{2,1,0:T(8,128)(2,1)}, bf16[2,256,128]{2,1,0:T(8,128)(2,1)S(1)}, u32[]{:S(2)}, u32[]{:S(2)}) collective-permute-start(bf16[2,256,128]{2,1,0:T(8,128)(2,1)} %get-tuple-element.86), channel_id=1, source_target_pairs={{0,240},{16,0},{32,16},{48,32},{64,48},{80,64},{96,80},{112,96},{1... | collective-permute-start | bytes 393224 | tf_op jit(solution)/shard_map/ppermute | solution.py:475
  339.4 23.4 %all-to-all-start.3 = ((bf16[16,224,128]{2,1,0:T(8,128)(2,1)}), bf16[16,224,128]{2,1,0:T(8,128)(2,1)S(1)}, u32[]{:S(2)}, u32[]{:S(2)}) async-start(bf16[16,224,128]{2,1,0:T(8,128)(2,1)} %bitcast.5), calls=%async_computation.3 | async-start | bytes 1835008 | tf_op jit(solution)/shard_map/all_to_all | solution.py:503
  (28 other events, 3577.0 us)

commit v8 on v6

--- a/solution.py
+++ b/solution.py
@@ -51,7 +51,60 @@
         out_specs=(smem, smem),
         scratch_shapes=[pltpu.SMEM((sources,), jnp.int32)],
         name="route",
-    )(far_list.T)
+    )(pltpu.with_memory_space_constraint(far_list.T, pltpu.HBM))
+
+
+def stage_kernel(*refs, moves):
+    sources, targets, sems = refs[:2], refs[2:-1], refs[-1]
+    copies = [
+        pltpu.make_async_copy(sources[which].at[rows, columns], target, sems.at[i])
+        for i, (which, rows, columns, target) in enumerate(moves(targets))
+    ]
+    for copy in copies:
+        copy.start()
+    for copy in copies:
+        copy.wait()
+
+
+def stage(key_rows, value_rows, shapes, moves, count):
+    vmem = pl.BlockSpec(memory_space=pltpu.VMEM)
+    hbm = pl.BlockSpec(memory_space=pltpu.HBM)
+    staged = pl.pallas_call(
+        functools.partial(stage_kernel, moves=moves),
+        out_shape=tuple(pltpu.VMEM(shape, key_rows.dtype) for shape in shapes),
+        in_specs=[hbm, hbm],
+        out_specs=(vmem,) * len(shapes),
+        scratch_shapes=[pltpu.SemaphoreType.DMA((count,))],
+        compiler_params=pltpu.CompilerParams(vmem_limit_bytes=4 * MIB),
+    )(key_rows, value_rows)
+    return [pltpu.with_memory_space_constraint(x, pltpu.VMEM) for x in staged]
+
+
+def halos(key_rows, value_rows):
+    tok_rows, channels = key_rows.shape
+    margin = BAND * BT
+    whole = pl.ds(0, channels)
+
+    def moves(targets):
+        return [
+            (which, pl.ds(start, margin), whole, target.at[which])
+            for which in range(2)
+            for start, target in zip((tok_rows - margin, 0), targets)
+        ]
+
+    return stage(key_rows, value_rows, [(2, margin, channels)] * 2, moves, 4)
+
+
+def head_columns(key_rows, value_rows, head):
+    tok_rows = key_rows.shape[0]
+
+    def moves(targets):
+        return [
+            (which, pl.ds(0, tok_rows), pl.ds(head * DH, DH), target)
+            for which, target in enumerate(targets)
+        ]
+
+    return stage(key_rows, value_rows, [(tok_rows, DH)] * 2, moves, 2)
 
 
 def pack_kernel(asked_ref, me_ref, keys_ref, values_ref, *refs, shifts):
@@ -75,28 +128,41 @@
         copy.wait()
 
 
-def pack(asked, me, key_rows, value_rows, head, split):
+def pack(asked, me, keys, values, head, split):
     shifts = asked.shape[0]
-    tok_rows = key_rows.shape[0]
+    tok_rows, channels = keys.shape
     hbm = pl.BlockSpec(memory_space=pltpu.HBM)
-    column = pl.BlockSpec((tok_rows, DH), lambda i, *_: (0, head))
     if split:
-        out_shape = (pltpu.HBM((CAP, BT, DH), key_rows.dtype),) * (2 * shifts)
+        out_shape = (pltpu.HBM((CAP, BT, DH), keys.dtype),) * (2 * shifts)
     else:
-        out_shape = (pltpu.HBM((shifts, CAP * 2, BT, DH), key_rows.dtype),)
+        out_shape = (pltpu.HBM((shifts, CAP * 2, BT, DH), keys.dtype),)
+    scratch = [pltpu.SemaphoreType.DMA((shifts, CAP * 2))]
+    if channels == DH:
+        smem = pl.BlockSpec(memory_space=pltpu.SMEM)
+        vmem = pl.BlockSpec(memory_space=pltpu.VMEM)
+        layout = dict(
+            in_specs=[smem, smem, vmem, vmem],
+            out_specs=(hbm,) * len(out_shape),
+            scratch_shapes=scratch,
+        )
+    else:
+        column = pl.BlockSpec((tok_rows, DH), lambda i, *_: (0, head))
+        layout = dict(
+            grid_spec=pltpu.PrefetchScalarGridSpec(
+                num_scalar_prefetch=2,
+                grid=(1,),
+                in_specs=[column, column],
+                out_specs=(hbm,) * len(out_shape),
+                scratch_shapes=scratch,
+            )
+        )
     return pl.pallas_call(
         functools.partial(pack_kernel, shifts=shifts),
         out_shape=out_shape,
-        grid_spec=pltpu.PrefetchScalarGridSpec(
-            num_scalar_prefetch=2,
-            grid=(1,),
-            in_specs=[column, column],
-            out_specs=(hbm,) * len(out_shape),
-            scratch_shapes=[pltpu.SemaphoreType.DMA((shifts, CAP * 2))],
-        ),
         compiler_params=pltpu.CompilerParams(vmem_limit_bytes=16 * MIB),
         name="pack",
-    )(asked, me, key_rows, value_rows)
+        **layout,
+    )(asked, me, keys, values)
 
 
 def fill_bias(bias_ref, slope):
@@ -362,10 +428,10 @@
 
 
 def value_kernel(me_ref, slot_ref, weights_ref, acc_ref, scale_ref, *refs, sources, blk_dev):
-    pieces = refs[:-3]
-    out_ref, buffer_ref, sems = refs[-3:]
-    for copy in gather_pieces(pieces, buffer_ref, sems, sources):
-        copy.wait()
+    pieces = refs[:-2]
+    out_ref, buffer_ref = refs[-2:]
+    for s, piece in enumerate(pieces):
+        buffer_ref[s] = piece[...]
     for i in range(blk_dev):
         r = pl.ds(i * BT, BT)
         acc = acc_ref[r, :]
@@ -380,16 +446,12 @@
     blk_dev = tok_rows // BT
     smem = pl.BlockSpec(memory_space=pltpu.SMEM)
     vmem = pl.BlockSpec(memory_space=pltpu.VMEM)
-    hbm = pl.BlockSpec(memory_space=pltpu.HBM)
     return pl.pallas_call(
         functools.partial(value_kernel, sources=sources, blk_dev=blk_dev),
         out_shape=pltpu.VMEM((tok_rows, DH), jnp.bfloat16),
-        in_specs=[smem, smem] + [vmem] * 3 + [hbm] * len(pieces),
+        in_specs=[smem, smem] + [vmem] * (3 + len(pieces)),
         out_specs=vmem,
-        scratch_shapes=[
-            pltpu.VMEM((sources, CAP, BT, DH), jnp.bfloat16),
-            pltpu.SemaphoreType.DMA((sources,)),
-        ],
+        scratch_shapes=[pltpu.VMEM((sources, CAP, BT, DH), jnp.bfloat16)],
         compiler_params=pltpu.CompilerParams(vmem_limit_bytes=4 * MIB),
         name="values",
     )(me, slots, weights, acc, scale, *pieces)
@@ -431,34 +493,35 @@
     sources = lax.axis_size("seq")
     tok_rows, channels = key_rows.shape
     blk_dev = tok_rows // BT
-    margin = BAND * BT
     heads = channels // DH
     up = [(i, i + 1) for i in range(sources - 1)]
     down = [(i + 1, i) for i in range(sources - 1)]
 
-    table, slots = route(far_list, sources)
-    asked = lax.all_to_all(table, "seq", split_axis=0, concat_axis=0, tiled=True)
-    last = jnp.stack([key_rows[tok_rows - margin :], value_rows[tok_rows - margin :]])
-    first = jnp.stack([key_rows[:margin], value_rows[:margin]])
-    before = lax.ppermute(last, "seq", up)
-    after = lax.ppermute(first, "seq", down)
-
-    me = myself[None].astype(jnp.int32)
     keys_hbm, values_hbm = (
         pltpu.with_memory_space_constraint(x, pltpu.HBM) for x in (key_rows, value_rows)
     )
+    table, slots = route(far_list, sources)
+    last, first = halos(keys_hbm, values_hbm)
+    columns = head_columns(keys_hbm, values_hbm, 0)
+    asked = lax.all_to_all(table, "seq", split_axis=0, concat_axis=0, tiled=True)
+    before = lax.ppermute(last, "seq", up)
+    after = lax.ppermute(first, "seq", down)
+
+    me = myself[None].astype(jnp.int32)
     incoming = []
     for head in range(heads):
         split = head == heads - 1
-        outgoing = pack(asked, me, keys_hbm, values_hbm, head, split)
+        source = columns if head == 0 else (keys_hbm, values_hbm)
+        outgoing = pack(asked, me, *source, head, split)
         if split:
             pieces = []
-            for which in range(2):
+            for which, kind in enumerate(("key", "value")):
                 arrays = list(outgoing[which * sources : (which + 1) * sources])
                 for shift in range(1, sources):
                     ring = [(i, (i + shift) % sources) for i in range(sources)]
                     arrays[shift] = lax.ppermute(arrays[shift], "seq", ring)
-                pieces.append([pltpu.with_memory_space_constraint(x, pltpu.HBM) for x in arrays])
+                space = pltpu.HBM if kind == "key" else pltpu.VMEM
+                pieces.append([pltpu.with_memory_space_constraint(x, space) for x in arrays])
             incoming.append(pieces)
         else:
             incoming.append(

time: 388 us -> 386 us (level)
  the two profiles are of different devices: /device:TPU:40 before, /device:TPU:64 now
where the time goes in v8:
time: 386 us; the launch traced here: 385 us
  waiting for transfers between devices  158 us (41%)
  Pallas kernels  108 us (28%)
  starting transfers between devices  94.6 us (25%)
  blocking collectives  20 us (5%)
    ppermute x30, waiting for transfers between devices, body(): arrays[shift] = lax.ppermute(arrays[shift], 'seq', ring)  150 us
    pallas_call x1, Pallas kernels, band_attention(): pl.pallas_call(functools.partial(band_kernel, blk_dev=blk_dev, total_bloc...  67.6 us
    ppermute x30, starting transfers between devices, body(): arrays[shift] = lax.ppermute(arrays[shift], 'seq', ring)  63.2 us
    pallas_call x2, Pallas kernels, far_attention(): pl.pallas_call(functools.partial(far_kernel, head=head, blk_dev=blk_dev,...  23.6 us
    all_to_all x1, blocking collectives, body(): lax.all_to_all(attended.reshape(lax.axis_size('head'), -1, DH), 'head', s...  20 us
    all_to_all x1, starting transfers between devices, body(): lax.all_to_all(table, 'seq', split_axis=0, concat_axis=0, tiled=True)  9.16 us
    pallas_call x2, Pallas kernels, pack(): pl.pallas_call(functools.partial(pack_kernel, shifts=shifts), out_shape=o...  7.93 us
  transfers between devices with their start and end apart: 35, of which 17 were waited for; matrix products, arithmetic and copies ran while one was open for 0% of the time, Pallas kernels for 26%

profile of v8, /device:TPU:64, one launch (start us, length us, event | category | flops | bytes accessed | tf_op | source)
XLA Modules:
  0.0 385.3 jit_solution(11122037059834125242)
XLA Ops:
  1.8 9.2 %all-to-all-start = ((s32[16,1,2]{2,1,0:T(1,128)}), s32[16,1,2]{2,1,0:T(1,128)S(1)}, u32[]{:S(2)}, u32[]{:S(2)}) async-start(s32[16,1,2]{2,1,0:T(1,128)} %bitcast.14), calls=%async_computation | async-start | bytes 16384 | tf_op jit(solution)/shard_map/all_to_all | solution.py:506
  12.4 4.7 %all-to-all-done = s32[16,1,2]{2,1,0:T(1,128)S(1)} async-done(((s32[16,1,2]{2,1,0:T(1,128)}), s32[16,1,2]{2,1,0:T(1,128)S(1)}, u32[]{:S(2)}, u32[]{:S(2)}) %all-to-all-start) | async-done | bytes 160 | tf_op jit(solution)/shard_map/all_to_all | solution.py:506
  17.1 3.2 pack.2
  20.4 6.6 %all-to-all-start.1 = ((bf16[16,4,256,128]{3,2,1,0:T(8,128)(2,1)}), bf16[16,4,256,128]{3,2,1,0:T(8,128)(2,1)}, u32[]{:S(2)}, u32[]{:S(2)}) async-start(bf16[16,4,256,128]{3,2,1,0:T(8,128)(2,1)} %pack.2), calls=%async_computation.1 | async-start | bytes 8388608 | tf_op jit(solution)/shard_map/all_to_all | solution.py:528
  27.0 4.7 %pack.3 = (bf16[2,256,128]{2,1,0:T(8,128)(2,1)}, bf16[2,256,128]{2,1,0:T(8,128)(2,1)}, bf16[2,256,128]{2,1,0:T(8,128)(2,1)}, bf16[2,256,128]{2,1,0:T(8,128)(2,1)...) custom-call(s32[16,2]{1,0:T(8,128)S(1)} %bitcast.10, ...), custom_call_target="tpu_custom_call" | custom-call | tf_op jit(solution)/shard_map/pack/pallas_call | solution.py:159
  37.1 6.6 %collective-permute-start.13 = (bf16[2,256,128]{2,1,0:T(8,128)(2,1)}, bf16[2,256,128]{2,1,0:T(8,128)(2,1)S(1)}, u32[]{:S(2)}, u32[]{:S(2)}) collective-permute-start(bf16[2,256,128]{2,1,0:T(8,128)(2,1)} %get-tuple-element.68), channel_id=1, source_target_pairs={{0,192},{16,208},{32,224},{48,240},{64,0},{80,16},{96,32},{112,48}... | collective-permute-start | bytes 393224 | tf_op jit(solution)/shard_map/ppermute | solution.py:522
  44.3 82.7 %collective-permute-done.10.refs_9_ = bf16[2,256,128]{2,1,0:T(8,128)(2,1)S(1)} collective-permute-done((bf16[2,256,128]{2,1,0:T(8,128)(2,1)}, bf16[2,256,128]{2,1,0:T(8,128)(2,1)S(1)}, u32[]{:S(2)}, u32[]{:S(2)}) %collective-permute-start.10) | collective-permute-done | bytes 131104 | tf_op jit(solution)/shard_map/ppermute | solution.py:522
  126.9 8.1 %collective-permute-done.11.refs_10_ = bf16[2,256,128]{2,1,0:T(8,128)(2,1)S(1)} collective-permute-done((bf16[2,256,128]{2,1,0:T(8,128)(2,1)}, bf16[2,256,128]{2,1,0:T(8,128)(2,1)S(1)}, u32[]{:S(2)}, u32[]{:S(2)}) %collective-permute-start.11) | collective-permute-done | bytes 131104 | tf_op jit(solution)/shard_map/ppermute | solution.py:522
  135.0 4.8 %collective-permute-done.12.refs_11_ = bf16[2,256,128]{2,1,0:T(8,128)(2,1)S(1)} collective-permute-done((bf16[2,256,128]{2,1,0:T(8,128)(2,1)}, bf16[2,256,128]{2,1,0:T(8,128)(2,1)S(1)}, u32[]{:S(2)}, u32[]{:S(2)}) %collective-permute-start.12) | collective-permute-done | bytes 131104 | tf_op jit(solution)/shard_map/ppermute | solution.py:522
  139.8 3.3 collective-permute-done.13.refs_12_
  143.1 3.7 collective-permute-start.3
  148.5 5.5 %collective-permute-start = (bf16[2,768,256]{2,1,0:T(8,128)(2,1)S(1)}, bf16[2,768,256]{2,1,0:T(8,128)(2,1)S(1)}, u32[]{:S(2)}, u32[]{:S(2)}) collective-permute-start(bf16[2,768,256]{2,1,0:T(8,128)(2,1)S(1)} %get-tuple-element.49), channel_id=1, source_target_pairs={{0,16},{16,32},{32,48},{48,64},{64,80},{80,96},{96,112},{112,128},... | collective-permute-start | bytes 2359304 | tf_op jit(solution)/shard_map/ppermute | solution.py:507
  154.0 3.4 collective-permute-start.1
  158.7 3.7 collective-permute-start.6
  162.5 4.4 %collective-permute-start.7 = (bf16[2,256,128]{2,1,0:T(8,128)(2,1)}, bf16[2,256,128]{2,1,0:T(8,128)(2,1)S(1)}, u32[]{:S(2)}, u32[]{:S(2)}) collective-permute-start(bf16[2,256,128]{2,1,0:T(8,128)(2,1)} %get-tuple-element.62), channel_id=1, source_target_pairs={{0,96},{16,112},{32,128},{48,144},{64,160},{80,176},{96,192},{112,... | collective-permute-start | bytes 393224 | tf_op jit(solution)/shard_map/ppermute | solution.py:522
  166.8 20.9 %collective-permute-done.5.refs_4_ = bf16[2,256,128]{2,1,0:T(8,128)(2,1)S(1)} collective-permute-done((bf16[2,256,128]{2,1,0:T(8,128)(2,1)}, bf16[2,256,128]{2,1,0:T(8,128)(2,1)S(1)}, u32[]{:S(2)}, u32[]{:S(2)}) %collective-permute-start.5) | collective-permute-done | bytes 131104 | tf_op jit(solution)/shard_map/ppermute | solution.py:522
  187.7 3.5 collective-permute-done.6.refs_5_
  193.5 3.6 collective-permute-done.7.refs_6_
  199.5 3.7 collective-permute-start.19
  203.2 6.5 %collective-permute-done.17.refs_1_ = bf16[2,256,128]{2,1,0:T(8,128)(2,1)S(1)} collective-permute-done((bf16[2,256,128]{2,1,0:T(8,128)(2,1)}, bf16[2,256,128]{2,1,0:T(8,128)(2,1)S(1)}, u32[]{:S(2)}, u32[]{:S(2)}) %collective-permute-start.17) | collective-permute-done | bytes 131104 | tf_op jit(solution)/shard_map/ppermute | solution.py:522
  212.1 6.6 %collective-permute-done.19.refs_3_ = bf16[2,256,128]{2,1,0:T(8,128)(2,1)S(1)} collective-permute-done((bf16[2,256,128]{2,1,0:T(8,128)(2,1)}, bf16[2,256,128]{2,1,0:T(8,128)(2,1)S(1)}, u32[]{:S(2)}, u32[]{:S(2)}) %collective-permute-start.19) | collective-permute-done | bytes 131104 | tf_op jit(solution)/shard_map/ppermute | solution.py:522
  218.6 3.8 collective-permute-start.22
  234.6 3.6 collective-permute-start.27
  238.2 3.9 %collective-permute-start.28 = (bf16[2,256,128]{2,1,0:T(8,128)(2,1)}, bf16[2,256,128]{2,1,0:T(8,128)(2,1)S(1)}, u32[]{:S(2)}, u32[]{:S(2)}) collective-permute-start(bf16[2,256,128]{2,1,0:T(8,128)(2,1)} %get-tuple-element.87), channel_id=1, source_target_pairs={{0,192},{16,208},{32,224},{48,240},{64,0},{80,16},{96,32},{112,48}... | collective-permute-start | bytes 393224 | tf_op jit(solution)/shard_map/ppermute | solution.py:522
  245.1 4.3 %collective-permute-start.29 = (bf16[2,256,128]{2,1,0:T(8,128)(2,1)}, bf16[2,256,128]{2,1,0:T(8,128)(2,1)S(1)}, u32[]{:S(2)}, u32[]{:S(2)}) collective-permute-start(bf16[2,256,128]{2,1,0:T(8,128)(2,1)} %get-tuple-element.88), channel_id=1, source_target_pairs={{0,208},{16,224},{32,240},{48,0},{64,16},{80,32},{96,48},{112,64},... | collective-permute-start | bytes 393224 | tf_op jit(solution)/shard_map/ppermute | solution.py:522
  249.4 6.2 %collective-permute-start.30 = (bf16[2,256,128]{2,1,0:T(8,128)(2,1)}, bf16[2,256,128]{2,1,0:T(8,128)(2,1)S(1)}, u32[]{:S(2)}, u32[]{:S(2)}) collective-permute-start(bf16[2,256,128]{2,1,0:T(8,128)(2,1)} %get-tuple-element.89), channel_id=1, source_target_pairs={{0,224},{16,240},{32,0},{48,16},{64,32},{80,48},{96,64},{112,80},{... | collective-permute-start | bytes 393224 | tf_op jit(solution)/shard_map/ppermute | solution.py:522
  255.7 67.6 %band.1 = (f32[3584,256]{1,0:T(8,128)S(1)}, f32[3584,256]{1,0:T(8,128)S(1)}) custom-call(s32[15]{0:T(128)S(1)} %pad_add_fusion.meta_ref, f32[2]{0:T(128)S(1)} %copy-done.8, bf16[3584,256]{1,0:T(8,128)(2,1)S(1)} %copy-done.4, bf16[3584,256]{1,0:T(8,128)(2,1)S(1)} %copy-done, bf16[3584,256]{1,0:T(8,128)(2,1)S(1)} %copy-done.1, ...), custom_call_target="tpu_custom_call" | custom-call | flops 6576668672 | bytes 31457280 | tf_op jit(solution)/shard_map/band/pallas_call | solution.py:276
  327.1 10.4 %far.3 = (bf16[3584,512]{1,0:T(8,128)(2,1)S(1)}, f32[3584,128]{1,0:T(8,128)S(1)}, f32[3584,128]{1,0:T(8,128)S(1)}) custom-call(s32[15]{0:T(128)S(1)} %pad_add_fusion.meta_ref, s32[2,14]{1,0:T(2,128)S(1)} %copy-done.6, s32[2,14]{1,0:T(2,128)S(1)} %bitcast.12, f32[2]{0:T(128)S(1)} %copy-done.8, bf16[3584,256]{1,0:T(8,128)(2,1)} %query_ref.5, ...), custom_call_target="tpu_custom_call" | custom-call | flops 939524096 | bytes 14680064 | tf_op jit(solution)/shard_map/far/pallas_call | solution.py:404
  340.3 6.7 %all-to-all-start.3 = ((bf16[16,224,128]{2,1,0:T(8,128)(2,1)}), bf16[16,224,128]{2,1,0:T(8,128)(2,1)S(1)}, u32[]{:S(2)}, u32[]{:S(2)}) async-start(bf16[16,224,128]{2,1,0:T(8,128)(2,1)} %bitcast.5), calls=%async_computation.3 | async-start | bytes 1835008 | tf_op jit(solution)/shard_map/all_to_all | solution.py:550
  347.1 13.2 %far.2 = bf16[3584,128]{1,0:T(8,128)(2,1)S(1)} custom-call(s32[15]{0:T(128)S(1)} %pad_add_fusion.meta_ref, s32[2,14]{1,0:T(2,128)S(1)} %copy-done.6, s32[2,14]{1,0:T(2,128)S(1)} %bitcast.13, f32[2]{0:T(128)S(1)} %copy-done.8, bf16[3584,256]{1,0:T(8,128)(2,1)} %query_ref.5, f32[3584,256]{1,0:T(8,128)} %copy-done.2, f32[3584,256]{1,0:T(8,128)} %copy-done.3, ...), custom_call_target="tpu_custom_call" | custom-call | flops 939524096 | bytes 14680064 | tf_op jit(solution)/shard_map/far/pallas_call | solution.py:404
  360.3 3.3 all-to-all-done.3.refs_1_
  363.6 20.0 %all_to_all.26.refs_0_ = bf16[16,224,128]{2,1,0:T(8,128)(2,1)S(1)} all-to-all(bf16[16,224,128]{2,1,0:T(8,128)(2,1)S(1)} %bitcast.8), channel_id=1, replica_groups=mesh['seq'=16,'head'=16] {'head'}, dimensions={0} | all-to-all | bytes 1835008 | tf_op jit(solution)/shard_map/all_to_all | solution.py:550
  (100 shorter events, 42.3 us)
Async XLA Ops:
  1.8 15.4 %all-to-all-start = ((s32[16,1,2]{2,1,0:T(1,128)}), s32[16,1,2]{2,1,0:T(1,128)S(1)}, u32[]{:S(2)}, u32[]{:S(2)}) async-start(s32[16,1,2]{2,1,0:T(1,128)} %bitcast.14), calls=%async_computation | async-start | bytes 16384 | tf_op jit(solution)/shard_map/all_to_all | solution.py:506
  20.4 319.9 %all-to-all-start.1 = ((bf16[16,4,256,128]{3,2,1,0:T(8,128)(2,1)}), bf16[16,4,256,128]{3,2,1,0:T(8,128)(2,1)}, u32[]{:S(2)}, u32[]{:S(2)}) async-start(bf16[16,4,256,128]{3,2,1,0:T(8,128)(2,1)} %pack.2), calls=%async_computation.1 | async-start | bytes 8388608 | tf_op jit(solution)/shard_map/all_to_all | solution.py:528
  31.7 95.2 %collective-permute-start.10 = (bf16[2,256,128]{2,1,0:T(8,128)(2,1)}, bf16[2,256,128]{2,1,0:T(8,128)(2,1)S(1)}, u32[]{:S(2)}, u32[]{:S(2)}) collective-permute-start(bf16[2,256,128]{2,1,0:T(8,128)(2,1)} %get-tuple-element.65), channel_id=1, source_target_pairs={{0,144},{16,160},{32,176},{48,192},{64,208},{80,224},{96,240},{112... | collective-permute-start | bytes 393224 | tf_op jit(solution)/shard_map/ppermute | solution.py:522
  34.2 100.8 %collective-permute-start.11 = (bf16[2,256,128]{2,1,0:T(8,128)(2,1)}, bf16[2,256,128]{2,1,0:T(8,128)(2,1)S(1)}, u32[]{:S(2)}, u32[]{:S(2)}) collective-permute-start(bf16[2,256,128]{2,1,0:T(8,128)(2,1)} %get-tuple-element.66), channel_id=1, source_target_pairs={{0,160},{16,176},{32,192},{48,208},{64,224},{80,240},{96,0},{112,1... | collective-permute-start | bytes 393224 | tf_op jit(solution)/shard_map/ppermute | solution.py:522
  36.8 103.0 %collective-permute-start.12 = (bf16[2,256,128]{2,1,0:T(8,128)(2,1)}, bf16[2,256,128]{2,1,0:T(8,128)(2,1)S(1)}, u32[]{:S(2)}, u32[]{:S(2)}) collective-permute-start(bf16[2,256,128]{2,1,0:T(8,128)(2,1)} %get-tuple-element.67), channel_id=1, source_target_pairs={{0,176},{16,192},{32,208},{48,224},{64,240},{80,0},{96,16},{112,32... | collective-permute-start | bytes 393224 | tf_op jit(solution)/shard_map/ppermute | solution.py:522
  37.1 106.0 %collective-permute-start.13 = (bf16[2,256,128]{2,1,0:T(8,128)(2,1)}, bf16[2,256,128]{2,1,0:T(8,128)(2,1)S(1)}, u32[]{:S(2)}, u32[]{:S(2)}) collective-permute-start(bf16[2,256,128]{2,1,0:T(8,128)(2,1)} %get-tuple-element.68), channel_id=1, source_target_pairs={{0,192},{16,208},{32,224},{48,240},{64,0},{80,16},{96,32},{112,48}... | collective-permute-start | bytes 393224 | tf_op jit(solution)/shard_map/ppermute | solution.py:522
  43.7 103.1 %collective-permute-start.14 = (bf16[2,256,128]{2,1,0:T(8,128)(2,1)}, bf16[2,256,128]{2,1,0:T(8,128)(2,1)S(1)}, u32[]{:S(2)}, u32[]{:S(2)}) collective-permute-start(bf16[2,256,128]{2,1,0:T(8,128)(2,1)} %get-tuple-element.69), channel_id=1, source_target_pairs={{0,208},{16,224},{32,240},{48,0},{64,16},{80,32},{96,48},{112,64},... | collective-permute-start | bytes 393224 | tf_op jit(solution)/shard_map/ppermute | solution.py:522
  126.9 21.6 %collective-permute-start.15 = (bf16[2,256,128]{2,1,0:T(8,128)(2,1)}, bf16[2,256,128]{2,1,0:T(8,128)(2,1)S(1)}, u32[]{:S(2)}, u32[]{:S(2)}) collective-permute-start(bf16[2,256,128]{2,1,0:T(8,128)(2,1)} %get-tuple-element.70), channel_id=1, source_target_pairs={{0,224},{16,240},{32,0},{48,16},{64,32},{80,48},{96,64},{112,80},{... | collective-permute-start | bytes 393224 | tf_op jit(solution)/shard_map/ppermute | solution.py:522
  135.0 19.0 %collective-permute-start.16 = (bf16[2,256,128]{2,1,0:T(8,128)(2,1)}, bf16[2,256,128]{2,1,0:T(8,128)(2,1)S(1)}, u32[]{:S(2)}, u32[]{:S(2)}) collective-permute-start(bf16[2,256,128]{2,1,0:T(8,128)(2,1)} %get-tuple-element.71), channel_id=1, source_target_pairs={{0,240},{16,0},{32,16},{48,32},{64,48},{80,64},{96,80},{112,96},{1... | collective-permute-start | bytes 393224 | tf_op jit(solution)/shard_map/ppermute | solution.py:522
  139.8 17.6 %collective-permute-start.2 = (bf16[2,256,128]{2,1,0:T(8,128)(2,1)}, bf16[2,256,128]{2,1,0:T(8,128)(2,1)S(1)}, u32[]{:S(2)}, u32[]{:S(2)}) collective-permute-start(bf16[2,256,128]{2,1,0:T(8,128)(2,1)} %get-tuple-element.57), channel_id=1, source_target_pairs={{0,16},{16,32},{32,48},{48,64},{64,80},{80,96},{96,112},{112,128},... | collective-permute-start | bytes 393224 | tf_op jit(solution)/shard_map/ppermute | solution.py:522
  143.1 15.6 %collective-permute-start.3 = (bf16[2,256,128]{2,1,0:T(8,128)(2,1)}, bf16[2,256,128]{2,1,0:T(8,128)(2,1)S(1)}, u32[]{:S(2)}, u32[]{:S(2)}) collective-permute-start(bf16[2,256,128]{2,1,0:T(8,128)(2,1)} %get-tuple-element.58), channel_id=1, source_target_pairs={{0,32},{16,48},{32,64},{48,80},{64,96},{80,112},{96,128},{112,144}... | collective-permute-start | bytes 393224 | tf_op jit(solution)/shard_map/ppermute | solution.py:522
  146.8 15.6 %collective-permute-start.4 = (bf16[2,256,128]{2,1,0:T(8,128)(2,1)}, bf16[2,256,128]{2,1,0:T(8,128)(2,1)S(1)}, u32[]{:S(2)}, u32[]{:S(2)}) collective-permute-start(bf16[2,256,128]{2,1,0:T(8,128)(2,1)} %get-tuple-element.59), channel_id=1, source_target_pairs={{0,48},{16,64},{32,80},{48,96},{64,112},{80,128},{96,144},{112,160... | collective-permute-start | bytes 393224 | tf_op jit(solution)/shard_map/ppermute | solution.py:522
  148.5 100.9 %collective-permute-start = (bf16[2,768,256]{2,1,0:T(8,128)(2,1)S(1)}, bf16[2,768,256]{2,1,0:T(8,128)(2,1)S(1)}, u32[]{:S(2)}, u32[]{:S(2)}) collective-permute-start(bf16[2,768,256]{2,1,0:T(8,128)(2,1)S(1)} %get-tuple-element.49), channel_id=1, source_target_pairs={{0,16},{16,32},{32,48},{48,64},{64,80},{80,96},{96,112},{112,128},... | collective-permute-start | bytes 2359304 | tf_op jit(solution)/shard_map/ppermute | solution.py:507
  154.0 101.6 %collective-permute-start.1 = (bf16[2,768,256]{2,1,0:T(8,128)(2,1)S(1)}, bf16[2,768,256]{2,1,0:T(8,128)(2,1)S(1)}, u32[]{:S(2)}, u32[]{:S(2)}) collective-permute-start(bf16[2,768,256]{2,1,0:T(8,128)(2,1)S(1)} %get-tuple-element.50), channel_id=1, source_target_pairs={{16,0},{32,16},{48,32},{64,48},{80,64},{96,80},{112,96},{128,112},... | collective-permute-start | bytes 2359304 | tf_op jit(solution)/shard_map/ppermute | solution.py:508
  157.4 30.3 %collective-permute-start.5 = (bf16[2,256,128]{2,1,0:T(8,128)(2,1)}, bf16[2,256,128]{2,1,0:T(8,128)(2,1)S(1)}, u32[]{:S(2)}, u32[]{:S(2)}) collective-permute-start(bf16[2,256,128]{2,1,0:T(8,128)(2,1)} %get-tuple-element.60), channel_id=1, source_target_pairs={{0,64},{16,80},{32,96},{48,112},{64,128},{80,144},{96,160},{112,17... | collective-permute-start | bytes 393224 | tf_op jit(solution)/shard_map/ppermute | solution.py:522
  158.7 32.5 %collective-permute-start.6 = (bf16[2,256,128]{2,1,0:T(8,128)(2,1)}, bf16[2,256,128]{2,1,0:T(8,128)(2,1)S(1)}, u32[]{:S(2)}, u32[]{:S(2)}) collective-permute-start(bf16[2,256,128]{2,1,0:T(8,128)(2,1)} %get-tuple-element.61), channel_id=1, source_target_pairs={{0,80},{16,96},{32,112},{48,128},{64,144},{80,160},{96,176},{112,1... | collective-permute-start | bytes 393224 | tf_op jit(solution)/shard_map/ppermute | solution.py:522
  162.5 34.6 %collective-permute-start.7 = (bf16[2,256,128]{2,1,0:T(8,128)(2,1)}, bf16[2,256,128]{2,1,0:T(8,128)(2,1)S(1)}, u32[]{:S(2)}, u32[]{:S(2)}) collective-permute-start(bf16[2,256,128]{2,1,0:T(8,128)(2,1)} %get-tuple-element.62), channel_id=1, source_target_pairs={{0,96},{16,112},{32,128},{48,144},{64,160},{80,176},{96,192},{112,... | collective-permute-start | bytes 393224 | tf_op jit(solution)/shard_map/ppermute | solution.py:522
  187.7 9.4 %collective-permute-start.8 = (bf16[2,256,128]{2,1,0:T(8,128)(2,1)}, bf16[2,256,128]{2,1,0:T(8,128)(2,1)S(1)}, u32[]{:S(2)}, u32[]{:S(2)}) collective-permute-start(bf16[2,256,128]{2,1,0:T(8,128)(2,1)} %get-tuple-element.63), channel_id=1, source_target_pairs={{0,112},{16,128},{32,144},{48,160},{64,176},{80,192},{96,208},{112... | collective-permute-start | bytes 393224 | tf_op jit(solution)/shard_map/ppermute | solution.py:522
  197.1 12.7 %collective-permute-start.17 = (bf16[2,256,128]{2,1,0:T(8,128)(2,1)}, bf16[2,256,128]{2,1,0:T(8,128)(2,1)S(1)}, u32[]{:S(2)}, u32[]{:S(2)}) collective-permute-start(bf16[2,256,128]{2,1,0:T(8,128)(2,1)} %get-tuple-element.76), channel_id=1, source_target_pairs={{0,16},{16,32},{32,48},{48,64},{64,80},{80,96},{96,112},{112,128},... | collective-permute-start | bytes 393224 | tf_op jit(solution)/shard_map/ppermute | solution.py:522
  197.1 13.7 %collective-permute-start.18 = (bf16[2,256,128]{2,1,0:T(8,128)(2,1)}, bf16[2,256,128]{2,1,0:T(8,128)(2,1)S(1)}, u32[]{:S(2)}, u32[]{:S(2)}) collective-permute-start(bf16[2,256,128]{2,1,0:T(8,128)(2,1)} %get-tuple-element.77), channel_id=1, source_target_pairs={{0,32},{16,48},{32,64},{48,80},{64,96},{80,112},{96,128},{112,144}... | collective-permute-start | bytes 393224 | tf_op jit(solution)/shard_map/ppermute | solution.py:522
  199.5 19.2 %collective-permute-start.19 = (bf16[2,256,128]{2,1,0:T(8,128)(2,1)}, bf16[2,256,128]{2,1,0:T(8,128)(2,1)S(1)}, u32[]{:S(2)}, u32[]{:S(2)}) collective-permute-start(bf16[2,256,128]{2,1,0:T(8,128)(2,1)} %get-tuple-element.78), channel_id=1, source_target_pairs={{0,48},{16,64},{32,80},{48,96},{64,112},{80,128},{96,144},{112,160... | collective-permute-start | bytes 393224 | tf_op jit(solution)/shard_map/ppermute | solution.py:522
  209.7 14.6 %collective-permute-start.20 = (bf16[2,256,128]{2,1,0:T(8,128)(2,1)}, bf16[2,256,128]{2,1,0:T(8,128)(2,1)S(1)}, u32[]{:S(2)}, u32[]{:S(2)}) collective-permute-start(bf16[2,256,128]{2,1,0:T(8,128)(2,1)} %get-tuple-element.79), channel_id=1, source_target_pairs={{0,64},{16,80},{32,96},{48,112},{64,128},{80,144},{96,160},{112,17... | collective-permute-start | bytes 393224 | tf_op jit(solution)/shard_map/ppermute | solution.py:522
  210.8 15.0 %collective-permute-start.21 = (bf16[2,256,128]{2,1,0:T(8,128)(2,1)}, bf16[2,256,128]{2,1,0:T(8,128)(2,1)S(1)}, u32[]{:S(2)}, u32[]{:S(2)}) collective-permute-start(bf16[2,256,128]{2,1,0:T(8,128)(2,1)} %get-tuple-element.80), channel_id=1, source_target_pairs={{0,80},{16,96},{32,112},{48,128},{64,144},{80,160},{96,176},{112,1... | collective-permute-start | bytes 393224 | tf_op jit(solution)/shard_map/ppermute | solution.py:522
  218.6 11.4 %collective-permute-start.22 = (bf16[2,256,128]{2,1,0:T(8,128)(2,1)}, bf16[2,256,128]{2,1,0:T(8,128)(2,1)S(1)}, u32[]{:S(2)}, u32[]{:S(2)}) collective-permute-start(bf16[2,256,128]{2,1,0:T(8,128)(2,1)} %get-tuple-element.81), channel_id=1, source_target_pairs={{0,96},{16,112},{32,128},{48,144},{64,160},{80,176},{96,192},{112,... | collective-permute-start | bytes 393224 | tf_op jit(solution)/shard_map/ppermute | solution.py:522
  225.8 8.8 %collective-permute-start.24 = (bf16[2,256,128]{2,1,0:T(8,128)(2,1)}, bf16[2,256,128]{2,1,0:T(8,128)(2,1)S(1)}, u32[]{:S(2)}, u32[]{:S(2)}) collective-permute-start(bf16[2,256,128]{2,1,0:T(8,128)(2,1)} %get-tuple-element.83), channel_id=1, source_target_pairs={{0,128},{16,144},{32,160},{48,176},{64,192},{80,208},{96,224},{112... | collective-permute-start | bytes 393224 | tf_op jit(solution)/shard_map/ppermute | solution.py:522
  231.4 13.6 %collective-permute-start.26 = (bf16[2,256,128]{2,1,0:T(8,128)(2,1)}, bf16[2,256,128]{2,1,0:T(8,128)(2,1)S(1)}, u32[]{:S(2)}, u32[]{:S(2)}) collective-permute-start(bf16[2,256,128]{2,1,0:T(8,128)(2,1)} %get-tuple-element.85), channel_id=1, source_target_pairs={{0,160},{16,176},{32,192},{48,208},{64,224},{80,240},{96,0},{112,1... | collective-permute-start | bytes 393224 | tf_op jit(solution)/shard_map/ppermute | solution.py:522
  234.6 102.8 %collective-permute-start.27 = (bf16[2,256,128]{2,1,0:T(8,128)(2,1)}, bf16[2,256,128]{2,1,0:T(8,128)(2,1)S(1)}, u32[]{:S(2)}, u32[]{:S(2)}) collective-permute-start(bf16[2,256,128]{2,1,0:T(8,128)(2,1)} %get-tuple-element.86), channel_id=1, source_target_pairs={{0,176},{16,192},{32,208},{48,224},{64,240},{80,0},{96,16},{112,32... | collective-permute-start | bytes 393224 | tf_op jit(solution)/shard_map/ppermute | solution.py:522
  238.2 99.3 %collective-permute-start.28 = (bf16[2,256,128]{2,1,0:T(8,128)(2,1)}, bf16[2,256,128]{2,1,0:T(8,128)(2,1)S(1)}, u32[]{:S(2)}, u32[]{:S(2)}) collective-permute-start(bf16[2,256,128]{2,1,0:T(8,128)(2,1)} %get-tuple-element.87), channel_id=1, source_target_pairs={{0,192},{16,208},{32,224},{48,240},{64,0},{80,16},{96,32},{112,48}... | collective-permute-start | bytes 393224 | tf_op jit(solution)/shard_map/ppermute | solution.py:522
  245.1 92.4 %collective-permute-start.29 = (bf16[2,256,128]{2,1,0:T(8,128)(2,1)}, bf16[2,256,128]{2,1,0:T(8,128)(2,1)S(1)}, u32[]{:S(2)}, u32[]{:S(2)}) collective-permute-start(bf16[2,256,128]{2,1,0:T(8,128)(2,1)} %get-tuple-element.88), channel_id=1, source_target_pairs={{0,208},{16,224},{32,240},{48,0},{64,16},{80,32},{96,48},{112,64},... | collective-permute-start | bytes 393224 | tf_op jit(solution)/shard_map/ppermute | solution.py:522
  249.4 88.0 %collective-permute-start.30 = (bf16[2,256,128]{2,1,0:T(8,128)(2,1)}, bf16[2,256,128]{2,1,0:T(8,128)(2,1)S(1)}, u32[]{:S(2)}, u32[]{:S(2)}) collective-permute-start(bf16[2,256,128]{2,1,0:T(8,128)(2,1)} %get-tuple-element.89), channel_id=1, source_target_pairs={{0,224},{16,240},{32,0},{48,16},{64,32},{80,48},{96,64},{112,80},{... | collective-permute-start | bytes 393224 | tf_op jit(solution)/shard_map/ppermute | solution.py:522
  255.6 81.8 %collective-permute-start.31 = (bf16[2,256,128]{2,1,0:T(8,128)(2,1)}, bf16[2,256,128]{2,1,0:T(8,128)(2,1)S(1)}, u32[]{:S(2)}, u32[]{:S(2)}) collective-permute-start(bf16[2,256,128]{2,1,0:T(8,128)(2,1)} %get-tuple-element.90), channel_id=1, source_target_pairs={{0,240},{16,0},{32,16},{48,32},{64,48},{80,64},{96,80},{112,96},{1... | collective-permute-start | bytes 393224 | tf_op jit(solution)/shard_map/ppermute | solution.py:522
  340.3 23.3 %all-to-all-start.3 = ((bf16[16,224,128]{2,1,0:T(8,128)(2,1)}), bf16[16,224,128]{2,1,0:T(8,128)(2,1)S(1)}, u32[]{:S(2)}, u32[]{:S(2)}) async-start(bf16[16,224,128]{2,1,0:T(8,128)(2,1)} %bitcast.5), calls=%async_computation.3 | async-start | bytes 1835008 | tf_op jit(solution)/shard_map/all_to_all | solution.py:550
  (28 other events, 2353.6 us)

commit v9 on v8

--- a/solution.py
+++ b/solution.py
@@ -19,7 +19,21 @@
 MIB = 1 << 20
 
 
-def route_kernel(far_ref, table_ref, slot_ref, count_ref, *, sources, blk_dev):
+def route_kernel(
+    far_ref, keys_hbm, values_hbm, table_ref, slot_ref, last_ref, first_ref, count_ref, sems,
+    *, sources, blk_dev,
+):
+    margin = BAND * BT
+    copies = []
+    for which, ref in enumerate((keys_hbm, values_hbm)):
+        copies += [
+            pltpu.make_async_copy(
+                ref.at[pl.ds(blk_dev * BT - margin, margin)], last_ref.at[which], sems.at[which, 0]
+            ),
+            pltpu.make_async_copy(ref.at[pl.ds(0, margin)], first_ref.at[which], sems.at[which, 1]),
+        ]
+    for copy in copies:
+        copy.start()
     for s in range(sources):
         count_ref[s] = 0
         for r in range(CAP):
@@ -36,22 +50,30 @@
         return carry
 
     lax.fori_loop(0, blk_dev, step, 0)
-
-
-def route(far_list, sources):
+    for copy in copies:
+        copy.wait()
+
+
+def route(far_list, key_rows, value_rows, sources):
     blk_dev = far_list.shape[0]
     smem = pl.BlockSpec(memory_space=pltpu.SMEM)
+    vmem = pl.BlockSpec(memory_space=pltpu.VMEM)
+    hbm = pl.BlockSpec(memory_space=pltpu.HBM)
+    halo = pltpu.VMEM((2, BAND * BT, key_rows.shape[1]), key_rows.dtype)
     return pl.pallas_call(
         functools.partial(route_kernel, sources=sources, blk_dev=blk_dev),
         out_shape=(
             jax.ShapeDtypeStruct((sources, CAP), jnp.int32),
             jax.ShapeDtypeStruct((FAR, blk_dev), jnp.int32),
-        ),
-        in_specs=[smem],
-        out_specs=(smem, smem),
-        scratch_shapes=[pltpu.SMEM((sources,), jnp.int32)],
+            halo,
+            halo,
+        ),
+        in_specs=[smem, hbm, hbm],
+        out_specs=(smem, smem, vmem, vmem),
+        scratch_shapes=[pltpu.SMEM((sources,), jnp.int32), pltpu.SemaphoreType.DMA((2, 2))],
+        compiler_params=pltpu.CompilerParams(vmem_limit_bytes=4 * MIB),
         name="route",
-    )(pltpu.with_memory_space_constraint(far_list.T, pltpu.HBM))
+    )(pltpu.with_memory_space_constraint(far_list.T, pltpu.HBM), key_rows, value_rows)
 
 
 def stage_kernel(*refs, moves):
@@ -78,21 +100,6 @@
         compiler_params=pltpu.CompilerParams(vmem_limit_bytes=4 * MIB),
     )(key_rows, value_rows)
     return [pltpu.with_memory_space_constraint(x, pltpu.VMEM) for x in staged]
-
-
-def halos(key_rows, value_rows):
-    tok_rows, channels = key_rows.shape
-    margin = BAND * BT
-    whole = pl.ds(0, channels)
-
-    def moves(targets):
-        return [
-            (which, pl.ds(start, margin), whole, target.at[which])
-            for which in range(2)
-            for start, target in zip((tok_rows - margin, 0), targets)
-        ]
-
-    return stage(key_rows, value_rows, [(2, margin, channels)] * 2, moves, 4)
 
 
 def head_columns(key_rows, value_rows, head):
@@ -500,8 +507,7 @@
     keys_hbm, values_hbm = (
         pltpu.with_memory_space_constraint(x, pltpu.HBM) for x in (key_rows, value_rows)
     )
-    table, slots = route(far_list, sources)
-    last, first = halos(keys_hbm, values_hbm)
+    table, slots, last, first = route(far_list, keys_hbm, values_hbm, sources)
     columns = head_columns(keys_hbm, values_hbm, 0)
     asked = lax.all_to_all(table, "seq", split_axis=0, concat_axis=0, tiled=True)
     before = lax.ppermute(last, "seq", up)

time: 386 us -> 383 us (level)
  transfers between devices with their start and end apart: 35 -> 35, of which waited for: 17 -> 20; matrix products, arithmetic and copies ran while one was open for 0% -> 0% of each run, Pallas kernels for 26% -> 26%
where the time goes in v9:
time: 383 us
  waiting for transfers between devices  156 us (41%)
  Pallas kernels  108 us (28%)
  starting transfers between devices  93.6 us (24%)
  blocking collectives  20 us (5%)
    ppermute x30, waiting for transfers between devices, body(): arrays[shift] = lax.ppermute(arrays[shift], 'seq', ring)  148 us
    pallas_call x1, Pallas kernels, band_attention(): pl.pallas_call(functools.partial(band_kernel, blk_dev=blk_dev, total_bloc...  67.7 us
    ppermute x30, starting transfers between devices, body(): arrays[shift] = lax.ppermute(arrays[shift], 'seq', ring)  61.9 us
    pallas_call x2, Pallas kernels, far_attention(): pl.pallas_call(functools.partial(far_kernel, head=head, blk_dev=blk_dev,...  23.6 us
    all_to_all x1, blocking collectives, body(): lax.all_to_all(attended.reshape(lax.axis_size('head'), -1, DH), 'head', s...  20 us
    all_to_all x1, starting transfers between devices, body(): lax.all_to_all(table, 'seq', split_axis=0, concat_axis=0, tiled=True)  9.16 us
    pallas_call x2, Pallas kernels, pack(): pl.pallas_call(functools.partial(pack_kernel, shifts=shifts), out_shape=o...  8.34 us
  transfers between devices with their start and end apart: 35, of which 20 were waited for; matrix products, arithmetic and copies ran while one was open for 0% of the time, Pallas kernels for 26%

profile of v9, /device:TPU:64, one launch (start us, length us, event | category | flops | bytes accessed | tf_op | source)
XLA Modules:
  0.0 382.6 jit_solution(10646504955300775168)
XLA Ops:
  2.8 9.2 %all-to-all-start = ((s32[16,1,2]{2,1,0:T(1,128)}), s32[16,1,2]{2,1,0:T(1,128)S(1)}, u32[]{:S(2)}, u32[]{:S(2)}) async-start(s32[16,1,2]{2,1,0:T(1,128)} %bitcast.6), calls=%async_computation | async-start | bytes 16384 | tf_op jit(solution)/shard_map/all_to_all | solution.py:512
  13.5 4.7 %all-to-all-done = s32[16,1,2]{2,1,0:T(1,128)S(1)} async-done(((s32[16,1,2]{2,1,0:T(1,128)}), s32[16,1,2]{2,1,0:T(1,128)S(1)}, u32[]{:S(2)}, u32[]{:S(2)}) %all-to-all-start) | async-done | bytes 160 | tf_op jit(solution)/shard_map/all_to_all | solution.py:512
  18.2 3.3 pack.2
  21.5 6.7 %all-to-all-start.1 = ((bf16[16,4,256,128]{3,2,1,0:T(8,128)(2,1)}), bf16[16,4,256,128]{3,2,1,0:T(8,128)(2,1)}, u32[]{:S(2)}, u32[]{:S(2)}) async-start(bf16[16,4,256,128]{3,2,1,0:T(8,128)(2,1)} %pack.2), calls=%async_computation.1 | async-start | bytes 8388608 | tf_op jit(solution)/shard_map/all_to_all | solution.py:534
  28.2 5.1 %pack.3 = (bf16[2,256,128]{2,1,0:T(8,128)(2,1)}, bf16[2,256,128]{2,1,0:T(8,128)(2,1)}, bf16[2,256,128]{2,1,0:T(8,128)(2,1)}, bf16[2,256,128]{2,1,0:T(8,128)(2,1)...) custom-call(s32[16,2]{1,0:T(8,128)S(1)} %bitcast.10, ...), custom_call_target="tpu_custom_call" | custom-call | tf_op jit(solution)/shard_map/pack/pallas_call | solution.py:166
  38.7 6.6 %collective-permute-start.13 = (bf16[2,256,128]{2,1,0:T(8,128)(2,1)}, bf16[2,256,128]{2,1,0:T(8,128)(2,1)S(1)}, u32[]{:S(2)}, u32[]{:S(2)}) collective-permute-start(bf16[2,256,128]{2,1,0:T(8,128)(2,1)} %get-tuple-element.68), channel_id=1, source_target_pairs={{0,192},{16,208},{32,224},{48,240},{64,0},{80,16},{96,32},{112,48}... | collective-permute-start | bytes 393224 | tf_op jit(solution)/shard_map/ppermute | solution.py:528
  45.9 82.3 %collective-permute-done.10.refs_9_ = bf16[2,256,128]{2,1,0:T(8,128)(2,1)S(1)} collective-permute-done((bf16[2,256,128]{2,1,0:T(8,128)(2,1)}, bf16[2,256,128]{2,1,0:T(8,128)(2,1)S(1)}, u32[]{:S(2)}, u32[]{:S(2)}) %collective-permute-start.10) | collective-permute-done | bytes 131104 | tf_op jit(solution)/shard_map/ppermute | solution.py:528
  128.2 8.1 %collective-permute-done.11.refs_10_ = bf16[2,256,128]{2,1,0:T(8,128)(2,1)S(1)} collective-permute-done((bf16[2,256,128]{2,1,0:T(8,128)(2,1)}, bf16[2,256,128]{2,1,0:T(8,128)(2,1)S(1)}, u32[]{:S(2)}, u32[]{:S(2)}) %collective-permute-start.11) | collective-permute-done | bytes 131104 | tf_op jit(solution)/shard_map/ppermute | solution.py:528
  136.2 4.8 %collective-permute-done.12.refs_11_ = bf16[2,256,128]{2,1,0:T(8,128)(2,1)S(1)} collective-permute-done((bf16[2,256,128]{2,1,0:T(8,128)(2,1)}, bf16[2,256,128]{2,1,0:T(8,128)(2,1)S(1)}, u32[]{:S(2)}, u32[]{:S(2)}) %collective-permute-start.12) | collective-permute-done | bytes 131104 | tf_op jit(solution)/shard_map/ppermute | solution.py:528
  141.1 3.3 collective-permute-done.13.refs_12_
  144.3 3.7 collective-permute-start.3
  148.0 5.7 %collective-permute-start = (bf16[2,768,256]{2,1,0:T(8,128)(2,1)S(1)}, bf16[2,768,256]{2,1,0:T(8,128)(2,1)S(1)}, u32[]{:S(2)}, u32[]{:S(2)}) collective-permute-start(bf16[2,768,256]{2,1,0:T(8,128)(2,1)S(1)} %get-tuple-element.49), channel_id=1, source_target_pairs={{0,16},{16,32},{32,48},{48,64},{64,80},{80,96},{96,112},{112,128},... | collective-permute-start | bytes 2359304 | tf_op jit(solution)/shard_map/ppermute | solution.py:513
  153.7 3.3 collective-permute-start.1
  158.4 3.8 collective-permute-start.6
  162.9 5.1 %collective-permute-start.7 = (bf16[2,256,128]{2,1,0:T(8,128)(2,1)}, bf16[2,256,128]{2,1,0:T(8,128)(2,1)S(1)}, u32[]{:S(2)}, u32[]{:S(2)}) collective-permute-start(bf16[2,256,128]{2,1,0:T(8,128)(2,1)} %get-tuple-element.62), channel_id=1, source_target_pairs={{0,96},{16,112},{32,128},{48,144},{64,160},{80,176},{96,192},{112,... | collective-permute-start | bytes 393224 | tf_op jit(solution)/shard_map/ppermute | solution.py:528
  168.0 21.2 %collective-permute-done.5.refs_4_ = bf16[2,256,128]{2,1,0:T(8,128)(2,1)S(1)} collective-permute-done((bf16[2,256,128]{2,1,0:T(8,128)(2,1)}, bf16[2,256,128]{2,1,0:T(8,128)(2,1)S(1)}, u32[]{:S(2)}, u32[]{:S(2)}) %collective-permute-start.5) | collective-permute-done | bytes 131104 | tf_op jit(solution)/shard_map/ppermute | solution.py:528
  193.2 3.4 collective-permute-done.7.refs_6_
  199.1 3.7 collective-permute-start.19
  202.8 3.9 %collective-permute-done.17.refs_1_ = bf16[2,256,128]{2,1,0:T(8,128)(2,1)S(1)} collective-permute-done((bf16[2,256,128]{2,1,0:T(8,128)(2,1)}, bf16[2,256,128]{2,1,0:T(8,128)(2,1)S(1)}, u32[]{:S(2)}, u32[]{:S(2)}) %collective-permute-start.17) | collective-permute-done | bytes 131104 | tf_op jit(solution)/shard_map/ppermute | solution.py:528
  211.9 6.1 %collective-permute-done.19.refs_3_ = bf16[2,256,128]{2,1,0:T(8,128)(2,1)S(1)} collective-permute-done((bf16[2,256,128]{2,1,0:T(8,128)(2,1)}, bf16[2,256,128]{2,1,0:T(8,128)(2,1)S(1)}, u32[]{:S(2)}, u32[]{:S(2)}) %collective-permute-start.19) | collective-permute-done | bytes 131104 | tf_op jit(solution)/shard_map/ppermute | solution.py:528
  218.0 4.0 %collective-permute-start.22 = (bf16[2,256,128]{2,1,0:T(8,128)(2,1)}, bf16[2,256,128]{2,1,0:T(8,128)(2,1)S(1)}, u32[]{:S(2)}, u32[]{:S(2)}) collective-permute-start(bf16[2,256,128]{2,1,0:T(8,128)(2,1)} %get-tuple-element.81), channel_id=1, source_target_pairs={{0,96},{16,112},{32,128},{48,144},{64,160},{80,176},{96,192},{112,... | collective-permute-start | bytes 393224 | tf_op jit(solution)/shard_map/ppermute | solution.py:528
  226.1 3.5 collective-permute-done.22.refs_6_
  231.0 3.1 collective-permute-start.26
  240.3 5.7 %collective-permute-done.26.refs_10_ = bf16[2,256,128]{2,1,0:T(8,128)(2,1)S(1)} collective-permute-done((bf16[2,256,128]{2,1,0:T(8,128)(2,1)}, bf16[2,256,128]{2,1,0:T(8,128)(2,1)S(1)}, u32[]{:S(2)}, u32[]{:S(2)}) %collective-permute-start.26) | collective-permute-done | bytes 131104 | tf_op jit(solution)/shard_map/ppermute | solution.py:528
  246.0 4.9 %collective-permute-start.29 = (bf16[2,256,128]{2,1,0:T(8,128)(2,1)}, bf16[2,256,128]{2,1,0:T(8,128)(2,1)S(1)}, u32[]{:S(2)}, u32[]{:S(2)}) collective-permute-start(bf16[2,256,128]{2,1,0:T(8,128)(2,1)} %get-tuple-element.88), channel_id=1, source_target_pairs={{0,208},{16,224},{32,240},{48,0},{64,16},{80,32},{96,48},{112,64},... | collective-permute-start | bytes 393224 | tf_op jit(solution)/shard_map/ppermute | solution.py:528
  252.8 67.7 %band.1 = (f32[3584,256]{1,0:T(8,128)S(1)}, f32[3584,256]{1,0:T(8,128)S(1)}) custom-call(s32[15]{0:T(128)S(1)} %pad_add_fusion.meta_ref, f32[2]{0:T(128)S(1)} %copy-done.7, bf16[3584,256]{1,0:T(8,128)(2,1)S(1)} %copy-done.4, bf16[3584,256]{1,0:T(8,128)(2,1)S(1)} %copy-done, bf16[3584,256]{1,0:T(8,128)(2,1)S(1)} %copy-done.1, ...), custom_call_target="tpu_custom_call" | custom-call | flops 6576668672 | bytes 31457280 | tf_op jit(solution)/shard_map/band/pallas_call | solution.py:283
  324.3 10.4 %far.3 = (bf16[3584,512]{1,0:T(8,128)(2,1)S(1)}, f32[3584,128]{1,0:T(8,128)S(1)}, f32[3584,128]{1,0:T(8,128)S(1)}) custom-call(s32[15]{0:T(128)S(1)} %pad_add_fusion.meta_ref, s32[2,14]{1,0:T(2,128)S(1)} %get-tuple-element.48.slot_ref, s32[2,14]{1,0:T(2,128)S(1)} %bitcast.12, f32[2]{0:T(128)S(1)} %copy-done.7, bf16[3584,256]{1,0:T(8,128)(2,1)} %query_ref.5, ...), custom_call_target="tpu_custom_call" | custom-call | flops 939524096 | bytes 14680064 | tf_op jit(solution)/shard_map/far/pallas_call | solution.py:411
  334.7 2.8 values.1
  337.6 6.8 %all-to-all-start.3 = ((bf16[16,224,128]{2,1,0:T(8,128)(2,1)}), bf16[16,224,128]{2,1,0:T(8,128)(2,1)S(1)}, u32[]{:S(2)}, u32[]{:S(2)}) async-start(bf16[16,224,128]{2,1,0:T(8,128)(2,1)} %bitcast.5), calls=%async_computation.3 | async-start | bytes 1835008 | tf_op jit(solution)/shard_map/all_to_all | solution.py:556
  344.4 13.2 %far.2 = bf16[3584,128]{1,0:T(8,128)(2,1)S(1)} custom-call(s32[15]{0:T(128)S(1)} %pad_add_fusion.meta_ref, s32[2,14]{1,0:T(2,128)S(1)} %get-tuple-element.48.slot_ref, s32[2,14]{1,0:T(2,128)S(1)} %bitcast.13, f32[2]{0:T(128)S(1)} %copy-done.7, bf16[3584,256]{1,0:T(8,128)(2,1)} %query_ref.5, f32[3584,256]{1,0:T(8,128)} %copy-done.2, f32[3584,256]{1,0:T(8,128)} %copy-done.3, ...), custom_call_target="tpu_custom_call" | custom-call | flops 939524096 | bytes 14680064 | tf_op jit(solution)/shard_map/far/pallas_call | solution.py:411
  357.6 3.3 all-to-all-done.3.refs_1_
  360.9 20.0 %all_to_all.26.refs_0_ = bf16[16,224,128]{2,1,0:T(8,128)(2,1)S(1)} all-to-all(bf16[16,224,128]{2,1,0:T(8,128)(2,1)S(1)} %bitcast.8), channel_id=1, replica_groups=mesh['seq'=16,'head'=16] {'head'}, dimensions={0} | all-to-all | bytes 1835008 | tf_op jit(solution)/shard_map/all_to_all | solution.py:556
  (97 shorter events, 42.8 us)
Async XLA Ops:
  2.8 15.4 %all-to-all-start = ((s32[16,1,2]{2,1,0:T(1,128)}), s32[16,1,2]{2,1,0:T(1,128)S(1)}, u32[]{:S(2)}, u32[]{:S(2)}) async-start(s32[16,1,2]{2,1,0:T(1,128)} %bitcast.6), calls=%async_computation | async-start | bytes 16384 | tf_op jit(solution)/shard_map/all_to_all | solution.py:512
  21.5 316.1 %all-to-all-start.1 = ((bf16[16,4,256,128]{3,2,1,0:T(8,128)(2,1)}), bf16[16,4,256,128]{3,2,1,0:T(8,128)(2,1)}, u32[]{:S(2)}, u32[]{:S(2)}) async-start(bf16[16,4,256,128]{3,2,1,0:T(8,128)(2,1)} %pack.2), calls=%async_computation.1 | async-start | bytes 8388608 | tf_op jit(solution)/shard_map/all_to_all | solution.py:534
  33.3 94.8 %collective-permute-start.10 = (bf16[2,256,128]{2,1,0:T(8,128)(2,1)}, bf16[2,256,128]{2,1,0:T(8,128)(2,1)S(1)}, u32[]{:S(2)}, u32[]{:S(2)}) collective-permute-start(bf16[2,256,128]{2,1,0:T(8,128)(2,1)} %get-tuple-element.65), channel_id=1, source_target_pairs={{0,144},{16,160},{32,176},{48,192},{64,208},{80,224},{96,240},{112... | collective-permute-start | bytes 393224 | tf_op jit(solution)/shard_map/ppermute | solution.py:528
  35.8 100.4 %collective-permute-start.11 = (bf16[2,256,128]{2,1,0:T(8,128)(2,1)}, bf16[2,256,128]{2,1,0:T(8,128)(2,1)S(1)}, u32[]{:S(2)}, u32[]{:S(2)}) collective-permute-start(bf16[2,256,128]{2,1,0:T(8,128)(2,1)} %get-tuple-element.66), channel_id=1, source_target_pairs={{0,160},{16,176},{32,192},{48,208},{64,224},{80,240},{96,0},{112,1... | collective-permute-start | bytes 393224 | tf_op jit(solution)/shard_map/ppermute | solution.py:528
  38.5 102.6 %collective-permute-start.12 = (bf16[2,256,128]{2,1,0:T(8,128)(2,1)}, bf16[2,256,128]{2,1,0:T(8,128)(2,1)S(1)}, u32[]{:S(2)}, u32[]{:S(2)}) collective-permute-start(bf16[2,256,128]{2,1,0:T(8,128)(2,1)} %get-tuple-element.67), channel_id=1, source_target_pairs={{0,176},{16,192},{32,208},{48,224},{64,240},{80,0},{96,16},{112,32... | collective-permute-start | bytes 393224 | tf_op jit(solution)/shard_map/ppermute | solution.py:528
  38.7 105.6 %collective-permute-start.13 = (bf16[2,256,128]{2,1,0:T(8,128)(2,1)}, bf16[2,256,128]{2,1,0:T(8,128)(2,1)S(1)}, u32[]{:S(2)}, u32[]{:S(2)}) collective-permute-start(bf16[2,256,128]{2,1,0:T(8,128)(2,1)} %get-tuple-element.68), channel_id=1, source_target_pairs={{0,192},{16,208},{32,224},{48,240},{64,0},{80,16},{96,32},{112,48}... | collective-permute-start | bytes 393224 | tf_op jit(solution)/shard_map/ppermute | solution.py:528
  45.3 102.7 %collective-permute-start.14 = (bf16[2,256,128]{2,1,0:T(8,128)(2,1)}, bf16[2,256,128]{2,1,0:T(8,128)(2,1)S(1)}, u32[]{:S(2)}, u32[]{:S(2)}) collective-permute-start(bf16[2,256,128]{2,1,0:T(8,128)(2,1)} %get-tuple-element.69), channel_id=1, source_target_pairs={{0,208},{16,224},{32,240},{48,0},{64,16},{80,32},{96,48},{112,64},... | collective-permute-start | bytes 393224 | tf_op jit(solution)/shard_map/ppermute | solution.py:528
  128.2 19.9 %collective-permute-start.15 = (bf16[2,256,128]{2,1,0:T(8,128)(2,1)}, bf16[2,256,128]{2,1,0:T(8,128)(2,1)S(1)}, u32[]{:S(2)}, u32[]{:S(2)}) collective-permute-start(bf16[2,256,128]{2,1,0:T(8,128)(2,1)} %get-tuple-element.70), channel_id=1, source_target_pairs={{0,224},{16,240},{32,0},{48,16},{64,32},{80,48},{96,64},{112,80},{... | collective-permute-start | bytes 393224 | tf_op jit(solution)/shard_map/ppermute | solution.py:528
  136.2 17.5 %collective-permute-start.16 = (bf16[2,256,128]{2,1,0:T(8,128)(2,1)}, bf16[2,256,128]{2,1,0:T(8,128)(2,1)S(1)}, u32[]{:S(2)}, u32[]{:S(2)}) collective-permute-start(bf16[2,256,128]{2,1,0:T(8,128)(2,1)} %get-tuple-element.71), channel_id=1, source_target_pairs={{0,240},{16,0},{32,16},{48,32},{64,48},{80,64},{96,80},{112,96},{1... | collective-permute-start | bytes 393224 | tf_op jit(solution)/shard_map/ppermute | solution.py:528
  141.1 16.0 %collective-permute-start.2 = (bf16[2,256,128]{2,1,0:T(8,128)(2,1)}, bf16[2,256,128]{2,1,0:T(8,128)(2,1)S(1)}, u32[]{:S(2)}, u32[]{:S(2)}) collective-permute-start(bf16[2,256,128]{2,1,0:T(8,128)(2,1)} %get-tuple-element.57), channel_id=1, source_target_pairs={{0,16},{16,32},{32,48},{48,64},{64,80},{80,96},{96,112},{112,128},... | collective-permute-start | bytes 393224 | tf_op jit(solution)/shard_map/ppermute | solution.py:528
  144.3 14.0 %collective-permute-start.3 = (bf16[2,256,128]{2,1,0:T(8,128)(2,1)}, bf16[2,256,128]{2,1,0:T(8,128)(2,1)S(1)}, u32[]{:S(2)}, u32[]{:S(2)}) collective-permute-start(bf16[2,256,128]{2,1,0:T(8,128)(2,1)} %get-tuple-element.58), channel_id=1, source_target_pairs={{0,32},{16,48},{32,64},{48,80},{64,96},{80,112},{96,128},{112,144}... | collective-permute-start | bytes 393224 | tf_op jit(solution)/shard_map/ppermute | solution.py:528
  148.0 14.8 %collective-permute-start.4 = (bf16[2,256,128]{2,1,0:T(8,128)(2,1)}, bf16[2,256,128]{2,1,0:T(8,128)(2,1)S(1)}, u32[]{:S(2)}, u32[]{:S(2)}) collective-permute-start(bf16[2,256,128]{2,1,0:T(8,128)(2,1)} %get-tuple-element.59), channel_id=1, source_target_pairs={{0,48},{16,64},{32,80},{48,96},{64,112},{80,128},{96,144},{112,160... | collective-permute-start | bytes 393224 | tf_op jit(solution)/shard_map/ppermute | solution.py:528
  148.0 102.8 %collective-permute-start = (bf16[2,768,256]{2,1,0:T(8,128)(2,1)S(1)}, bf16[2,768,256]{2,1,0:T(8,128)(2,1)S(1)}, u32[]{:S(2)}, u32[]{:S(2)}) collective-permute-start(bf16[2,768,256]{2,1,0:T(8,128)(2,1)S(1)} %get-tuple-element.49), channel_id=1, source_target_pairs={{0,16},{16,32},{32,48},{48,64},{64,80},{80,96},{96,112},{112,128},... | collective-permute-start | bytes 2359304 | tf_op jit(solution)/shard_map/ppermute | solution.py:513
  153.7 98.6 %collective-permute-start.1 = (bf16[2,768,256]{2,1,0:T(8,128)(2,1)S(1)}, bf16[2,768,256]{2,1,0:T(8,128)(2,1)S(1)}, u32[]{:S(2)}, u32[]{:S(2)}) collective-permute-start(bf16[2,768,256]{2,1,0:T(8,128)(2,1)S(1)} %get-tuple-element.50), channel_id=1, source_target_pairs={{16,0},{32,16},{48,32},{64,48},{80,64},{96,80},{112,96},{128,112},... | collective-permute-start | bytes 2359304 | tf_op jit(solution)/shard_map/ppermute | solution.py:514
  157.1 32.1 %collective-permute-start.5 = (bf16[2,256,128]{2,1,0:T(8,128)(2,1)}, bf16[2,256,128]{2,1,0:T(8,128)(2,1)S(1)}, u32[]{:S(2)}, u32[]{:S(2)}) collective-permute-start(bf16[2,256,128]{2,1,0:T(8,128)(2,1)} %get-tuple-element.60), channel_id=1, source_target_pairs={{0,64},{16,80},{32,96},{48,112},{64,128},{80,144},{96,160},{112,17... | collective-permute-start | bytes 393224 | tf_op jit(solution)/shard_map/ppermute | solution.py:528
  158.4 32.7 %collective-permute-start.6 = (bf16[2,256,128]{2,1,0:T(8,128)(2,1)}, bf16[2,256,128]{2,1,0:T(8,128)(2,1)S(1)}, u32[]{:S(2)}, u32[]{:S(2)}) collective-permute-start(bf16[2,256,128]{2,1,0:T(8,128)(2,1)} %get-tuple-element.61), channel_id=1, source_target_pairs={{0,80},{16,96},{32,112},{48,128},{64,144},{80,160},{96,176},{112,1... | collective-permute-start | bytes 393224 | tf_op jit(solution)/shard_map/ppermute | solution.py:528
  162.9 33.7 %collective-permute-start.7 = (bf16[2,256,128]{2,1,0:T(8,128)(2,1)}, bf16[2,256,128]{2,1,0:T(8,128)(2,1)S(1)}, u32[]{:S(2)}, u32[]{:S(2)}) collective-permute-start(bf16[2,256,128]{2,1,0:T(8,128)(2,1)} %get-tuple-element.62), channel_id=1, source_target_pairs={{0,96},{16,112},{32,128},{48,144},{64,160},{80,176},{96,192},{112,... | collective-permute-start | bytes 393224 | tf_op jit(solution)/shard_map/ppermute | solution.py:528
  191.1 8.1 %collective-permute-start.9 = (bf16[2,256,128]{2,1,0:T(8,128)(2,1)}, bf16[2,256,128]{2,1,0:T(8,128)(2,1)S(1)}, u32[]{:S(2)}, u32[]{:S(2)}) collective-permute-start(bf16[2,256,128]{2,1,0:T(8,128)(2,1)} %get-tuple-element.64), channel_id=1, source_target_pairs={{0,128},{16,144},{32,160},{48,176},{64,192},{80,208},{96,224},{112... | collective-permute-start | bytes 393224 | tf_op jit(solution)/shard_map/ppermute | solution.py:528
  196.6 10.2 %collective-permute-start.17 = (bf16[2,256,128]{2,1,0:T(8,128)(2,1)}, bf16[2,256,128]{2,1,0:T(8,128)(2,1)S(1)}, u32[]{:S(2)}, u32[]{:S(2)}) collective-permute-start(bf16[2,256,128]{2,1,0:T(8,128)(2,1)} %get-tuple-element.76), channel_id=1, source_target_pairs={{0,16},{16,32},{32,48},{48,64},{64,80},{80,96},{96,112},{112,128},... | collective-permute-start | bytes 393224 | tf_op jit(solution)/shard_map/ppermute | solution.py:528
  197.0 12.2 %collective-permute-start.18 = (bf16[2,256,128]{2,1,0:T(8,128)(2,1)}, bf16[2,256,128]{2,1,0:T(8,128)(2,1)S(1)}, u32[]{:S(2)}, u32[]{:S(2)}) collective-permute-start(bf16[2,256,128]{2,1,0:T(8,128)(2,1)} %get-tuple-element.77), channel_id=1, source_target_pairs={{0,32},{16,48},{32,64},{48,80},{64,96},{80,112},{96,128},{112,144}... | collective-permute-start | bytes 393224 | tf_op jit(solution)/shard_map/ppermute | solution.py:528
  199.1 18.9 %collective-permute-start.19 = (bf16[2,256,128]{2,1,0:T(8,128)(2,1)}, bf16[2,256,128]{2,1,0:T(8,128)(2,1)S(1)}, u32[]{:S(2)}, u32[]{:S(2)}) collective-permute-start(bf16[2,256,128]{2,1,0:T(8,128)(2,1)} %get-tuple-element.78), channel_id=1, source_target_pairs={{0,48},{16,64},{32,80},{48,96},{64,112},{80,128},{96,144},{112,160... | collective-permute-start | bytes 393224 | tf_op jit(solution)/shard_map/ppermute | solution.py:528
  206.8 17.0 %collective-permute-start.20 = (bf16[2,256,128]{2,1,0:T(8,128)(2,1)}, bf16[2,256,128]{2,1,0:T(8,128)(2,1)S(1)}, u32[]{:S(2)}, u32[]{:S(2)}) collective-permute-start(bf16[2,256,128]{2,1,0:T(8,128)(2,1)} %get-tuple-element.79), channel_id=1, source_target_pairs={{0,64},{16,80},{32,96},{48,112},{64,128},{80,144},{96,160},{112,17... | collective-permute-start | bytes 393224 | tf_op jit(solution)/shard_map/ppermute | solution.py:528
  209.2 14.6 %collective-permute-start.21 = (bf16[2,256,128]{2,1,0:T(8,128)(2,1)}, bf16[2,256,128]{2,1,0:T(8,128)(2,1)S(1)}, u32[]{:S(2)}, u32[]{:S(2)}) collective-permute-start(bf16[2,256,128]{2,1,0:T(8,128)(2,1)} %get-tuple-element.80), channel_id=1, source_target_pairs={{0,80},{16,96},{32,112},{48,128},{64,144},{80,160},{96,176},{112,1... | collective-permute-start | bytes 393224 | tf_op jit(solution)/shard_map/ppermute | solution.py:528
  218.0 11.6 %collective-permute-start.22 = (bf16[2,256,128]{2,1,0:T(8,128)(2,1)}, bf16[2,256,128]{2,1,0:T(8,128)(2,1)S(1)}, u32[]{:S(2)}, u32[]{:S(2)}) collective-permute-start(bf16[2,256,128]{2,1,0:T(8,128)(2,1)} %get-tuple-element.81), channel_id=1, source_target_pairs={{0,96},{16,112},{32,128},{48,144},{64,160},{80,176},{96,192},{112,... | collective-permute-start | bytes 393224 | tf_op jit(solution)/shard_map/ppermute | solution.py:528
  223.8 11.4 %collective-permute-start.24 = (bf16[2,256,128]{2,1,0:T(8,128)(2,1)}, bf16[2,256,128]{2,1,0:T(8,128)(2,1)S(1)}, u32[]{:S(2)}, u32[]{:S(2)}) collective-permute-start(bf16[2,256,128]{2,1,0:T(8,128)(2,1)} %get-tuple-element.83), channel_id=1, source_target_pairs={{0,128},{16,144},{32,160},{48,176},{64,192},{80,208},{96,224},{112... | collective-permute-start | bytes 393224 | tf_op jit(solution)/shard_map/ppermute | solution.py:528
  231.0 14.9 %collective-permute-start.26 = (bf16[2,256,128]{2,1,0:T(8,128)(2,1)}, bf16[2,256,128]{2,1,0:T(8,128)(2,1)S(1)}, u32[]{:S(2)}, u32[]{:S(2)}) collective-permute-start(bf16[2,256,128]{2,1,0:T(8,128)(2,1)} %get-tuple-element.85), channel_id=1, source_target_pairs={{0,160},{16,176},{32,192},{48,208},{64,224},{80,240},{96,0},{112,1... | collective-permute-start | bytes 393224 | tf_op jit(solution)/shard_map/ppermute | solution.py:528
  235.2 99.5 %collective-permute-start.27 = (bf16[2,256,128]{2,1,0:T(8,128)(2,1)}, bf16[2,256,128]{2,1,0:T(8,128)(2,1)S(1)}, u32[]{:S(2)}, u32[]{:S(2)}) collective-permute-start(bf16[2,256,128]{2,1,0:T(8,128)(2,1)} %get-tuple-element.86), channel_id=1, source_target_pairs={{0,176},{16,192},{32,208},{48,224},{64,240},{80,0},{96,16},{112,32... | collective-permute-start | bytes 393224 | tf_op jit(solution)/shard_map/ppermute | solution.py:528
  237.5 97.2 %collective-permute-start.28 = (bf16[2,256,128]{2,1,0:T(8,128)(2,1)}, bf16[2,256,128]{2,1,0:T(8,128)(2,1)S(1)}, u32[]{:S(2)}, u32[]{:S(2)}) collective-permute-start(bf16[2,256,128]{2,1,0:T(8,128)(2,1)} %get-tuple-element.87), channel_id=1, source_target_pairs={{0,192},{16,208},{32,224},{48,240},{64,0},{80,16},{96,32},{112,48}... | collective-permute-start | bytes 393224 | tf_op jit(solution)/shard_map/ppermute | solution.py:528
  246.0 88.7 %collective-permute-start.29 = (bf16[2,256,128]{2,1,0:T(8,128)(2,1)}, bf16[2,256,128]{2,1,0:T(8,128)(2,1)S(1)}, u32[]{:S(2)}, u32[]{:S(2)}) collective-permute-start(bf16[2,256,128]{2,1,0:T(8,128)(2,1)} %get-tuple-element.88), channel_id=1, source_target_pairs={{0,208},{16,224},{32,240},{48,0},{64,16},{80,32},{96,48},{112,64},... | collective-permute-start | bytes 393224 | tf_op jit(solution)/shard_map/ppermute | solution.py:528
  250.8 83.9 %collective-permute-start.30 = (bf16[2,256,128]{2,1,0:T(8,128)(2,1)}, bf16[2,256,128]{2,1,0:T(8,128)(2,1)S(1)}, u32[]{:S(2)}, u32[]{:S(2)}) collective-permute-start(bf16[2,256,128]{2,1,0:T(8,128)(2,1)} %get-tuple-element.89), channel_id=1, source_target_pairs={{0,224},{16,240},{32,0},{48,16},{64,32},{80,48},{96,64},{112,80},{... | collective-permute-start | bytes 393224 | tf_op jit(solution)/shard_map/ppermute | solution.py:528
  252.3 82.4 %collective-permute-start.31 = (bf16[2,256,128]{2,1,0:T(8,128)(2,1)}, bf16[2,256,128]{2,1,0:T(8,128)(2,1)S(1)}, u32[]{:S(2)}, u32[]{:S(2)}) collective-permute-start(bf16[2,256,128]{2,1,0:T(8,128)(2,1)} %get-tuple-element.90), channel_id=1, source_target_pairs={{0,240},{16,0},{32,16},{48,32},{64,48},{80,64},{96,80},{112,96},{1... | collective-permute-start | bytes 393224 | tf_op jit(solution)/shard_map/ppermute | solution.py:528
  337.6 23.4 %all-to-all-start.3 = ((bf16[16,224,128]{2,1,0:T(8,128)(2,1)}), bf16[16,224,128]{2,1,0:T(8,128)(2,1)S(1)}, u32[]{:S(2)}, u32[]{:S(2)}) async-start(bf16[16,224,128]{2,1,0:T(8,128)(2,1)} %bitcast.5), calls=%async_computation.3 | async-start | bytes 1835008 | tf_op jit(solution)/shard_map/all_to_all | solution.py:556
  (27 other events, 3578.0 us)
